TPU v7x, 256 devices: a whole 4x4x8 slice. The times are simulated.
256 devices in a mesh: depth: 4 (over z_lo, core), scan: 64 (over z_hi, x, y).
Axes of the slice: x: 4, y: 4, z: 8 (z_hi: 4, z_lo: 2; z = z_hi * 2 + z_lo), core: 2. Of those that a mesh axis runs over, the one named last changes fastest.
Arguments:
- probe_wave: bfloat16 [2, 512, 512], replicated, may hold values from -6 to 6
- prop_rows: bfloat16 [2, 512, 512], replicated, may hold values from -0.1875 to 0.1875
- prop_cols: bfloat16 [2, 512, 512], replicated, may hold values from -0.1875 to 0.1875
- transmission: bfloat16 [4, 2, 768, 768], P('depth', None, 'scan'), may hold values from -0.5 to 1.3, as said below
- exit_cotangent: bfloat16 [128, 2, 512, 512], P('scan'), may hold values from -1.1953125 to 1.1953125
- window_tiles: int32 [128, 2], P('scan'), may hold values from 0 to 8
- slot_count: int32 [64], P('scan'), may hold values from 1 to 2, as said below
Outputs:
- object_grad: float32 [4, 2, 768, 768], P('depth', None, 'scan')
Inputs may be any that keep to these rules, and one draw needn't show every extreme that they name: `window_tiles`: a window starts 32 times these indices and stays inside the slice. The first slot_count[j] slots of scan index j are used and the others are ignored; some scan index uses all 2 slots and some uses one. `transmission`: real parts lie in 0.6 to 1.3 and imaginary parts in -0.5 to 0.5.
All inputs are finite; a program needn't handle non-finite values.
Results may differ from a plain program's by a relative error of at most 0.014.
Values may be sent and summed in bfloat16 or wider, within the bound.
No kernel may reach another device: no remote copies, remote signals or barrier semaphores. Data moves between devices by JAX's collectives and lax.ppermute only.
A program may use at most 128 MiB of HBM per device.

v0:
```python
import jax
import jax.numpy as jnp
from jax import lax
from jax.sharding import PartitionSpec as P

TILE = 32


def shifted(value, axis, steps):
    count = lax.axis_size(axis)
    leading, last = (max(0, -steps), min(count, count - steps))
    return lax.ppermute(value, axis, [(source, source + steps) for source in range(leading, last)])


def rows_product(matrix, field):
    real = jnp.dot(matrix[0], field[0], preferred_element_type=jnp.float32) - jnp.dot(
        matrix[1], field[1], preferred_element_type=jnp.float32
    )
    imag = jnp.dot(matrix[0], field[1], preferred_element_type=jnp.float32) + jnp.dot(
        matrix[1], field[0], preferred_element_type=jnp.float32
    )
    return jnp.stack([real, imag])


def right_transpose(left, right):
    return lax.dot_general(
        left, right, (((1,), (1,)), ((), ())), preferred_element_type=jnp.float32
    )


def cols_product(field, matrix):
    real = right_transpose(field[0], matrix[0]) - right_transpose(field[1], matrix[1])
    imag = right_transpose(field[1], matrix[0]) + right_transpose(field[0], matrix[1])
    return jnp.stack([real, imag])


def left_transpose(left, right):
    return lax.dot_general(
        left, right, (((0,), (0,)), ((), ())), preferred_element_type=jnp.float32
    )


def adjoint_rows(matrix, field):
    real = left_transpose(matrix[0], field[0]) + left_transpose(matrix[1], field[1])
    imag = left_transpose(matrix[0], field[1]) - left_transpose(matrix[1], field[0])
    return jnp.stack([real, imag])


def conj_cols(field, matrix):
    real = jnp.dot(field[0], matrix[0], preferred_element_type=jnp.float32) + jnp.dot(
        field[1], matrix[1], preferred_element_type=jnp.float32
    )
    imag = jnp.dot(field[1], matrix[0], preferred_element_type=jnp.float32) - jnp.dot(
        field[0], matrix[1], preferred_element_type=jnp.float32
    )
    return jnp.stack([real, imag])


def complex_times(first, second):
    a0 = first[0].astype(jnp.float32)
    a1 = first[1].astype(jnp.float32)
    b0 = second[0].astype(jnp.float32)
    b1 = second[1].astype(jnp.float32)
    return jnp.stack([a0 * b0 - a1 * b1, a0 * b1 + a1 * b0])


def conj_times(first, second):
    a0 = first[0].astype(jnp.float32)
    a1 = first[1].astype(jnp.float32)
    b0 = second[0]
    b1 = second[1]
    return jnp.stack([a0 * b0 + a1 * b1, a0 * b1 - a1 * b0])


def on_device(
    probe_wave, prop_rows, prop_cols, transmission, exit_cotangent, window_tiles, slot_count
):
    depth_count = lax.axis_size("depth")
    depth_index = lax.axis_index("depth")
    slots = exit_cotangent.shape[0]
    width = probe_wave.shape[-1]
    ticks = slots + depth_count - 1
    used_slots = slot_count[0]
    whole = lax.all_gather(transmission[0], "scan", axis=1, tiled=True)
    zero = jnp.zeros((), jnp.int32)

    def window_start(slot):
        return (window_tiles[slot, 0] * TILE, window_tiles[slot, 1] * TILE)

    def patch_of(slot):
        row_start, col_start = window_start(slot)
        return lax.dynamic_slice(whole, (zero, row_start, col_start), (2, width, width))

    empty_wave = jnp.zeros((2, width, width), jnp.bfloat16)
    stored = jnp.zeros((slots, 2, width, width), jnp.bfloat16)
    incoming = empty_wave
    for tick in range(ticks):
        slot = tick - depth_index
        active = (slot >= 0) & (slot < slots) & (slot < used_slots)
        safe = jnp.clip(slot, 0, slots - 1)
        wave = jnp.where(depth_index == 0, probe_wave, incoming)
        kept = jnp.where(active, wave, stored[safe])
        stored = lax.dynamic_update_index_in_dim(stored, kept, safe, 0)

        def advance():
            product = complex_times(wave, patch_of(safe)).astype(jnp.bfloat16)
            swept = rows_product(prop_rows, product).astype(jnp.bfloat16)
            return cols_product(swept, prop_cols).astype(jnp.bfloat16)

        outgoing = lax.cond(active & (depth_index < depth_count - 1), advance, lambda: empty_wave)
        incoming = shifted(outgoing, "depth", 1)
    grad = jnp.zeros(whole.shape, jnp.float32)
    incoming = empty_wave
    empty_term = jnp.zeros((2, width, width), jnp.float32)
    for tick in range(ticks):
        slot = tick - (depth_count - 1 - depth_index)
        active = (slot >= 0) & (slot < slots) & (slot < used_slots)
        safe = jnp.clip(slot, 0, slots - 1)
        upstream = jnp.where(depth_index == depth_count - 1, exit_cotangent[safe], incoming)

        def retreat():
            swept = adjoint_rows(prop_rows, upstream).astype(jnp.bfloat16)
            adjoint = conj_cols(swept, prop_cols)
            contrib = conj_times(stored[safe], adjoint)
            return (contrib, conj_times(patch_of(safe), adjoint).astype(jnp.bfloat16))

        contrib, outgoing = lax.cond(active, retreat, lambda: (empty_term, empty_wave))
        row_start, col_start = window_start(safe)
        current = lax.dynamic_slice(grad, (zero, row_start, col_start), (2, width, width))
        grad = lax.dynamic_update_slice(grad, current + contrib, (zero, row_start, col_start))
        incoming = shifted(outgoing, "depth", -1)
    total = lax.psum_scatter(grad, "scan", scatter_dimension=1, tiled=True)
    return total[None]


def solution(mesh):
    placed = (
        P(),
        P(),
        P(),
        P("depth", None, "scan", None),
        P("scan", None, None, None),
        P("scan", None),
        P("scan"),
    )
    return jax.shard_map(
        on_device,
        mesh=mesh,
        in_specs=placed,
        out_specs=P("depth", None, "scan", None),
        check_vma=False,
    )
```

profile of v0, /device:TPU:8, one launch (start us, length us, event | category | flops | bytes accessed | tf_op | source)
XLA Modules:
  0.0 1588.3 jit_solution(9367382944052077562)
XLA Ops:
  11.3 81.5 %all-gather.3.cloned.1.call-done = bf16[1,2,768,768]{3,1,0,2:T(2,128)(2,1)} async-done(((bf16[1,2,12,768]{3,1,0,2:T(2,128)(2,1)}), bf16[1,2,768,768]{3,1,0,2:T(2,128)(2,1)}) %all-gather.3.cloned.1.call-update) | async-done | bytes 2359312 | tf_op jit(solution)/shard_map/all_gather | solution.py:84
  92.8 12.7 conditional.9
  92.8 3.4 copy.15
  112.3 16.4 %collective-permute-start.1 = (bf16[2,512,512]{2,1,0:T(8,128)(2,1)}, bf16[2,512,512]{2,1,0:T(8,128)(2,1)}, u32[]{:S(2)}, u32[]{:S(2)}) collective-permute-start(bf16[2,512,512]{2,1,0:T(8,128)(2,1)} %get-tuple-element.591), channel_id=1, source_target_pairs={{0,64},{64,128},{128,192},{1,65},{65,129},{129,193},{2,66},{66,130... | collective-permute-start | bytes 3145736 | tf_op jit(solution)/shard_map/ppermute | solution.py:12
  133.1 13.5 collective-permute-start.2
  151.1 27.8 %collective-permute-start.3 = (bf16[2,512,512]{2,1,0:T(8,128)(2,1)}, bf16[2,512,512]{2,1,0:T(8,128)(2,1)}, u32[]{:S(2)}, u32[]{:S(2)}) collective-permute-start(bf16[2,512,512]{2,1,0:T(8,128)(2,1)} %get-tuple-element.593), channel_id=1, source_target_pairs={{0,64},{64,128},{128,192},{1,65},{65,129},{129,193},{2,66},{66,130... | collective-permute-start | bytes 3145736 | tf_op jit(solution)/shard_map/ppermute | solution.py:12
  186.5 16.1 %collective-permute-done.4 = bf16[2,512,512]{2,1,0:T(8,128)(2,1)S(1)} collective-permute-done((bf16[2,512,512]{2,1,0:T(8,128)(2,1)}, bf16[2,512,512]{2,1,0:T(8,128)(2,1)S(1)}, u32[]{:S(2)}, u32[]{:S(2)}) %collective-permute-start.4) | collective-permute-done | bytes 1048608 | tf_op jit(solution)/shard_map/ppermute | solution.py:12
  202.5 3.1 conditional.14
  207.0 15.8 collective-permute-done.5
  222.8 3.5 conditional.15
  227.5 44.8 %collective-permute-done.6 = bf16[2,512,512]{2,1,0:T(8,128)(2,1)S(1)} collective-permute-done((bf16[2,512,512]{2,1,0:T(8,128)(2,1)}, bf16[2,512,512]{2,1,0:T(8,128)(2,1)S(1)}, u32[]{:S(2)}, u32[]{:S(2)}) %collective-permute-start.6) | collective-permute-done | bytes 1048608 | tf_op jit(solution)/shard_map/ppermute | solution.py:12
  272.3 18.9 %conditional.16 = (bf16[2,512,512]{2,1,0:T(8,128)(2,1)}, f32[2,512,512]{2,0,1:T(2,128)}) conditional(s32[]{:T(128)} %convert_element_type.243, () %tuple.81, (s32[]{:T(128)}, bf16[2,2,512,512]{3,2,1,0:T(8,128)(2,1)}, bf16[2,512,512]{2,1,0:T(8,128)(2,1)S(1)}, pred[]{:T(512)}, bf16[2,512,512]{2,1,0:T(8,128)(2,1)S(1)}, ...), branch_computations={%region_14.15_spmd, %region_15.16_spmd.clone.clone} | conditional | flops 2155347968 | bytes 47710424 | solution.py:127
  277.6 3.4 copy.44
  299.8 3.4 broadcast_in_dim.40
  303.2 95.6 %dynamic_update_slice.36 = f32[2,768,768]{2,0,1:T(2,128)} dynamic-update-slice(f32[2,768,768]{2,0,1:T(2,128)} %broadcast_in_dim.40, f32[2,512,512]{2,0,1:T(2,128)} %get-tuple-element.413, s32[]{:T(128)} %constant.173.clone.1, s32[]{:T(128)S(6)} %select_n.250, s32[]{:T(128)S(6)} %select_n.251) | dynamic-update-slice | bytes 4194308 | tf_op jit(solution)/shard_map/dynamic_update_slice | solution.py:130
  398.8 5.9 dynamic-slice_add_fusion.3
  404.7 95.6 %dynamic_update_slice.37 = f32[2,768,768]{2,0,1:T(2,128)} dynamic-update-slice(f32[2,768,768]{2,0,1:T(2,128)} %dynamic_update_slice.36, f32[2,512,512]{2,0,1:T(2,128)} %dynamic-slice_add_fusion.3, s32[]{:T(128)} %constant.173.clone.1, s32[]{:T(128)S(6)} %select_n.252, s32[]{:T(128)S(6)} %select_n.253) | dynamic-update-slice | bytes 4194308 | tf_op jit(solution)/shard_map/dynamic_update_slice | solution.py:130
  500.3 5.9 dynamic-slice_add_fusion.2
  506.2 95.6 %dynamic_update_slice.38 = f32[2,768,768]{2,0,1:T(2,128)} dynamic-update-slice(f32[2,768,768]{2,0,1:T(2,128)} %dynamic_update_slice.37, f32[2,512,512]{2,0,1:T(2,128)} %dynamic-slice_add_fusion.2, s32[]{:T(128)} %constant.173.clone.1, s32[]{:T(128)S(6)} %select_n.256, s32[]{:T(128)S(6)} %select_n.257) | dynamic-update-slice | bytes 4194308 | tf_op jit(solution)/shard_map/dynamic_update_slice | solution.py:130
  601.8 5.9 dynamic-slice_add_fusion.1
  607.7 95.6 %dynamic_update_slice.39 = f32[2,768,768]{2,0,1:T(2,128)} dynamic-update-slice(f32[2,768,768]{2,0,1:T(2,128)} %dynamic_update_slice.38, f32[2,512,512]{2,0,1:T(2,128)} %dynamic-slice_add_fusion.1, s32[]{:T(128)} %constant.173.clone.1, s32[]{:T(128)S(6)} %select_n.259, s32[]{:T(128)S(6)} %select_n.260) | dynamic-update-slice | bytes 4194308 | tf_op jit(solution)/shard_map/dynamic_update_slice | solution.py:130
  705.4 4.6 dynamic-slice_add_fusion
  710.0 96.7 %dynamic_update_slice.40 = f32[2,768,768]{2,0,1:T(2,128)} dynamic-update-slice(f32[2,768,768]{2,0,1:T(2,128)} %dynamic_update_slice.39, f32[2,512,512]{2,0,1:T(2,128)S(1)} %dynamic-slice_add_fusion, s32[]{:T(128)} %constant.173.clone.1, s32[]{:T(128)S(6)} %select_n.262, s32[]{:T(128)S(6)} %select_n.263) | dynamic-update-slice | bytes 4194308 | tf_op jit(solution)/shard_map/dynamic_update_slice | solution.py:130
  808.7 771.0 %all-reduce.3.cloned.1.call-done = f32[2,768,768]{2,0,1:T(2,128)} async-done(((f32[2,768,768]{2,0,1:T(2,128)}), f32[2,768,768]{2,0,1:T(2,128)}) %all-reduce.3.cloned.1.call-update) | async-done | bytes 4718608
  (82 shorter events, 71.5 us)
Async XLA Ops:
  6.5 3.0 copy-start.2
  6.5 86.3 %all-gather.3.cloned.1.call-start = ((), (), s32[]{:S(2)}) async-start(), calls=%async_computation | async-start | bytes 2396160 | tf_op jit(solution)/shard_map/all_gather | solution.py:84
  7.3 1572.4 %all-reduce.3.cloned.1.call-start = ((), (), s32[]{:S(2)}) async-start(), calls=%async_computation.1 | async-start | bytes 9437184
  9.5 83.3 %copy-start = (bf16[2,512,512]{2,1,0:T(8,128)(2,1)S(1)}, bf16[2,512,512]{2,1,0:T(8,128)(2,1)}, u32[]{:S(2)}) copy-start(bf16[2,512,512]{2,1,0:T(8,128)(2,1)} %param.27) | copy-start | bytes 3145732
  9.5 83.3 %copy-start.1 = (bf16[2,512,512]{2,1,0:T(8,128)(2,1)S(1)}, bf16[2,512,512]{2,1,0:T(8,128)(2,1)}, u32[]{:S(2)}) copy-start(bf16[2,512,512]{2,1,0:T(8,128)(2,1)} %param.26) | copy-start | bytes 3145732
  9.5 83.3 %copy-start.9 = (s32[2,2]{1,0:T(2,128)S(1)}, s32[2,2]{1,0:T(2,128)}, u32[]{:S(2)}) copy-start(s32[2,2]{1,0:T(2,128)} %param.30) | copy-start | bytes 52
  105.5 3.9 collective-permute-start
  112.3 17.9 %collective-permute-start.1 = (bf16[2,512,512]{2,1,0:T(8,128)(2,1)}, bf16[2,512,512]{2,1,0:T(8,128)(2,1)}, u32[]{:S(2)}, u32[]{:S(2)}) collective-permute-start(bf16[2,512,512]{2,1,0:T(8,128)(2,1)} %get-tuple-element.591), channel_id=1, source_target_pairs={{0,64},{64,128},{128,192},{1,65},{65,129},{129,193},{2,66},{66,130... | collective-permute-start | bytes 3145736 | tf_op jit(solution)/shard_map/ppermute | solution.py:12
  133.1 15.2 collective-permute-start.2
  151.1 29.5 %collective-permute-start.3 = (bf16[2,512,512]{2,1,0:T(8,128)(2,1)}, bf16[2,512,512]{2,1,0:T(8,128)(2,1)}, u32[]{:S(2)}, u32[]{:S(2)}) collective-permute-start(bf16[2,512,512]{2,1,0:T(8,128)(2,1)} %get-tuple-element.593), channel_id=1, source_target_pairs={{0,64},{64,128},{128,192},{1,65},{65,129},{129,193},{2,66},{66,130... | collective-permute-start | bytes 3145736 | tf_op jit(solution)/shard_map/ppermute | solution.py:12
  180.2 1.8 copy-start.3
  185.2 17.4 %collective-permute-start.4 = (bf16[2,512,512]{2,1,0:T(8,128)(2,1)}, bf16[2,512,512]{2,1,0:T(8,128)(2,1)S(1)}, u32[]{:S(2)}, u32[]{:S(2)}) collective-permute-start(bf16[2,512,512]{2,1,0:T(8,128)(2,1)} %get-tuple-element.200), channel_id=1, source_target_pairs={{64,0},{128,64},{192,128},{65,1},{129,65},{193,129},{66,2},{130,66... | collective-permute-start | bytes 3145736 | tf_op jit(solution)/shard_map/ppermute | solution.py:12
  205.7 17.1 %collective-permute-start.5 = (bf16[2,512,512]{2,1,0:T(8,128)(2,1)}, bf16[2,512,512]{2,1,0:T(8,128)(2,1)S(1)}, u32[]{:S(2)}, u32[]{:S(2)}) collective-permute-start(bf16[2,512,512]{2,1,0:T(8,128)(2,1)} %get-tuple-element.202), channel_id=1, source_target_pairs={{64,0},{128,64},{192,128},{65,1},{129,65},{193,129},{66,2},{130,66... | collective-permute-start | bytes 3145736 | tf_op jit(solution)/shard_map/ppermute | solution.py:12
  226.2 46.1 %collective-permute-start.6 = (bf16[2,512,512]{2,1,0:T(8,128)(2,1)}, bf16[2,512,512]{2,1,0:T(8,128)(2,1)S(1)}, u32[]{:S(2)}, u32[]{:S(2)}) collective-permute-start(bf16[2,512,512]{2,1,0:T(8,128)(2,1)} %get-tuple-element.204), channel_id=1, source_target_pairs={{64,0},{128,64},{192,128},{65,1},{129,65},{193,129},{66,2},{130,66... | collective-permute-start | bytes 3145736 | tf_op jit(solution)/shard_map/ppermute | solution.py:12
  282.9 1.2 copy-start.8
  291.2 412.1 %collective-permute-start.7 = (bf16[2,512,512]{2,1,0:T(8,128)(2,1)}, bf16[2,512,512]{2,1,0:T(8,128)(2,1)S(1)}, u32[]{:S(2)}, u32[]{:S(2)}) collective-permute-start(bf16[2,512,512]{2,1,0:T(8,128)(2,1)} %get-tuple-element.206), channel_id=1, source_target_pairs={{64,0},{128,64},{192,128},{65,1},{129,65},{193,129},{66,2},{130,66... | collective-permute-start | bytes 3145736 | tf_op jit(solution)/shard_map/ppermute | solution.py:12
  704.1 1.3 copy-start.4
  806.7 0.7 copy-start.10
Sparse Core Ops, SparseCore 0:
  10.5 82.2 all-gather.2
  806.9 772.7 all-reduce.2
where the time goes:
time: 1610 us; the launch traced here: 1590 us
  waiting for transfers between devices  931 us (58%)
  local copies, waits for them, and re-layouts  518 us (32%)
  starting transfers between devices  65.4 us (4%)
  other arithmetic  37.2 us (2%)
  between operations  21.6 us (1%)
    unnamed x3, waiting for transfers between devices  772 us
    dynamic_update_slice x5, local copies, waits for them, and re-layouts, on_device(): lax.dynamic_update_slice(grad, current + contrib, (zero, row_start, col_s...  479 us
    all_gather x1, waiting for transfers between devices, on_device(): whole = lax.all_gather(transmission[0], 'scan', axis=1, tiled=True)  81.5 us
    ppermute x8, waiting for transfers between devices, shifted(): lax.ppermute(value, axis, [(source, source + steps) for source in range(l...  77.8 us
    ppermute x8, starting transfers between devices, shifted(): lax.ppermute(value, axis, [(source, source + steps) for source in range(l...  65.4 us
  transfers between devices with their start and end apart: 10, of which 9 were waited for; matrix products, arithmetic and copies ran while one was open for 26% of the time, Pallas kernels for 0%

commit v1 on v0

v1 whole, which is shorter than its diff:
```python
import jax
import jax.numpy as jnp
from jax import lax
from jax.experimental import pallas as pl
from jax.experimental.pallas import tpu as pltpu
from jax.sharding import Mesh, PartitionSpec as P

TILE = 32
W = 512
OBJ = 768
PAD = 64
ROWS = 640
BF = jnp.bfloat16
F32 = jnp.float32


SMEM = pl.BlockSpec(memory_space=pltpu.SMEM)
VMEM = pl.BlockSpec(memory_space=pltpu.VMEM)


def params(mib):
    return pltpu.CompilerParams(vmem_limit_bytes=mib * 1024 * 1024)


def first_interval(row_tile, x):
    return ((row_tile * TILE - 48 * x + 144) >= 192).astype(jnp.int32)


def prep_kernel(info, rows, cols, probe, cot, a1, a1t, b1, b2, wave, grad):
    shift = info[1] * TILE
    ar = rows[0].astype(F32)
    ai = rows[1].astype(F32)
    a1[0:W, 0:W] = rows[0]
    a1[0:W, W:] = (-ai).astype(BF)
    a1[W:, 0:W] = rows[1]
    a1[W:, W:] = rows[0]
    art = ar.T.astype(BF)
    ait = ai.T
    a1t[0:W, 0:W] = art
    a1t[0:W, W:] = ait.astype(BF)
    a1t[W:, 0:W] = (-ait).astype(BF)
    a1t[W:, W:] = art

    def turned(value):
        return pltpu.roll(pltpu.roll(value, shift, 1), shift, 0)

    br = turned(cols[0].astype(F32))
    bi = turned(cols[1].astype(F32))
    b2[0:W, 0:W] = br.astype(BF)
    b2[0:W, W:] = (-bi).astype(BF)
    b2[W:, 0:W] = bi.astype(BF)
    b2[W:, W:] = br.astype(BF)
    brt = br.T.astype(BF)
    bit = bi.T
    b1[0:W, 0:W] = brt
    b1[0:W, W:] = bit.astype(BF)
    b1[W:, 0:W] = (-bit).astype(BF)
    b1[W:, W:] = brt
    slot = info[2]
    for part in range(2):
        wave[:, part * W : (part + 1) * W] = pltpu.roll(probe[part].astype(F32), shift, 1).astype(BF)
        grad[part * W : (part + 1) * W, :] = pltpu.roll(cot[slot, part].astype(F32), shift, 1).astype(BF)


def prep(info, rows, cols, probe, cot):
    square = jax.ShapeDtypeStruct((2 * W, 2 * W), BF)
    return pl.pallas_call(
        prep_kernel,
        out_shape=[square] * 4 + [jax.ShapeDtypeStruct((W, 2 * W), BF), jax.ShapeDtypeStruct((2 * W, W), BF)],
        in_specs=[SMEM] + [VMEM] * 4,
        out_specs=[VMEM] * 6,
        compiler_params=params(48),
        name="prep",
    )(info, rows, cols, probe, cot)


def pack_kernel(info, peers, own, one, two, three, out, held):
    zh = info[3]
    x = info[4]
    for step, piece in enumerate((own, one, two, three)):
        place = lax.rem(zh - step + 4, 4)
        for a in range(2):
            held[a, pl.ds(pl.multiple_of(place * 24, 8), 24), :] = piece[a].astype(F32)
    lane = lax.broadcasted_iota(jnp.int32, (72, 256), 1)

    def target(t, carry):
        first = first_interval(peers[t, 0], x)
        start = pl.multiple_of(first * 24, 8)
        wrapped = lane < peers[t, 1] * TILE
        for a in range(2):
            low = held[a, pl.ds(start, 72), 0:256]
            high = held[a, pl.ds(start, 72), 512:768]
            out[t, a, :, 0:256] = jnp.where(wrapped, high, low).astype(BF)
            out[t, a, :, 256:512] = held[a, pl.ds(start, 72), 256:512].astype(BF)
        return carry

    lax.fori_loop(0, 16, target, 0)


def pack(info, peers, own, others):
    return pl.pallas_call(
        pack_kernel,
        out_shape=jax.ShapeDtypeStruct((16, 2, 72, W), BF),
        in_specs=[SMEM, SMEM] + [VMEM] * 4,
        out_specs=VMEM,
        scratch_shapes=[pltpu.VMEM((2, 96, OBJ), F32)],
        compiler_params=params(32),
        name="pack",
    )(info, peers, own, *others)


def main_kernel(info, own, other, a1, a1t, b1, b2, wave0, grad0, out, patch, waves, left, right, contrib):
    row_tile = info[0]
    used = info[5] > 0
    core = info[6]
    for turn, source in enumerate((own, other)):
        parity = core if turn == 0 else 1 - core

        def place(plane, carry):
            first = first_interval(row_tile, plane)
            for y in range(4):
                part, half = y // 2, y % 2
                for a in range(2):
                    for k in range(3):
                        row = 192 * (first + k) + 48 * plane + 24 * half - TILE * row_tile + PAD
                        patch[2 * a + parity, part, pl.ds(pl.multiple_of(row, 8), 24), :] = source[
                            plane * 4 + y, a, k * 24 : (k + 1) * 24, :
                        ].astype(F32)
            return carry

        lax.fori_loop(0, 4, place, 0)
    waves[0] = wave0[...]
    for s in range(3):
        wr = waves[s, :, 0:W].astype(F32)
        wi = waves[s, :, W:].astype(F32)
        pr = patch[s, 0, PAD : PAD + W, :]
        pi = patch[s, 1, PAD : PAD + W, :]
        left[0:W, :] = (wr * pr - wi * pi).astype(BF)
        left[W:, :] = (wr * pi + wi * pr).astype(BF)
        swept = jnp.dot(a1[...], left[...], preferred_element_type=F32)
        right[:, 0:W] = swept[0:W].astype(BF)
        right[:, W:] = swept[W:].astype(BF)
        waves[s + 1] = jnp.dot(right[...], b1[...], preferred_element_type=F32).astype(BF)
    left[...] = grad0[...]
    contrib[:, 0:PAD, :] = jnp.zeros((2, PAD, W), F32)
    contrib[:, PAD + W :, :] = jnp.zeros((2, PAD, W), F32)
    for s in range(3, -1, -1):
        swept = jnp.dot(a1t[...], left[...], preferred_element_type=F32)
        right[:, 0:W] = swept[0:W].astype(BF)
        right[:, W:] = swept[W:].astype(BF)
        adjoint = jnp.dot(right[...], b2[...], preferred_element_type=F32)
        gr = adjoint[:, 0:W]
        gi = adjoint[:, W:]
        if s > 0:
            pr = patch[s, 0, PAD : PAD + W, :]
            pi = patch[s, 1, PAD : PAD + W, :]
            left[0:W, :] = (pr * gr + pi * gi).astype(BF)
            left[W:, :] = (pr * gi - pi * gr).astype(BF)

        @pl.when(core == s % 2)
        def _():
            wr = waves[s, :, 0:W].astype(F32)
            wi = waves[s, :, W:].astype(F32)
            contrib[0, PAD : PAD + W, :] = jnp.where(used, wr * gr + wi * gi, 0.0)
            contrib[1, PAD : PAD + W, :] = jnp.where(used, wr * gi - wi * gr, 0.0)

            def target(plane, carry):
                first = first_interval(row_tile, plane)
                for y in range(4):
                    part, half = y // 2, y % 2
                    for k in range(3):
                        row = 192 * (first + k) + 48 * plane + 24 * half - TILE * row_tile + PAD
                        out[plane * 4 + y, s // 2, k * 24 : (k + 1) * 24, :] = contrib[
                            part, pl.ds(pl.multiple_of(row, 8), 24), :
                        ].astype(BF)
                return carry

            lax.fori_loop(0, 4, target, 0)


def main(info, own, other, mats):
    return pl.pallas_call(
        main_kernel,
        out_shape=jax.ShapeDtypeStruct((16, 2, 72, W), BF),
        in_specs=[SMEM] + [VMEM] * 8,
        out_specs=VMEM,
        scratch_shapes=[
            pltpu.VMEM((4, 2, ROWS, W), F32),
            pltpu.VMEM((4, W, 2 * W), BF),
            pltpu.VMEM((2 * W, W), BF),
            pltpu.VMEM((W, 2 * W), BF),
            pltpu.VMEM((2, ROWS, W), F32),
        ],
        compiler_params=params(60),
        name="main",
    )(info, own, other, *mats)


def gather_kernel(info, peers, got, out, total):
    x = info[4]
    total[...] = jnp.zeros((2, 96, OBJ), F32)
    lane = lax.broadcasted_iota(jnp.int32, (72, 256), 1)

    def source(t, carry):
        first = first_interval(peers[t, 0], x)
        rows = pl.ds(pl.multiple_of(first * 24, 8), 72)
        wrapped = lane < peers[t, 1] * TILE
        for a in range(2):
            value = got[t, a].astype(F32)
            low = value[:, 0:256]
            total[a, rows, 0:256] += jnp.where(wrapped, 0.0, low)
            total[a, rows, 512:768] += jnp.where(wrapped, low, 0.0)
            total[a, rows, 256:512] += value[:, 256:512]
        return carry

    lax.fori_loop(0, 16, source, 0)
    for a in range(2):
        for k in range(4):
            out[a, k] = total[a, k * 24 : (k + 1) * 24, :].astype(BF)


def gather(info, peers, got):
    return pl.pallas_call(
        gather_kernel,
        out_shape=jax.ShapeDtypeStruct((2, 4, 24, OBJ), BF),
        in_specs=[SMEM, SMEM, VMEM],
        out_specs=VMEM,
        scratch_shapes=[pltpu.VMEM((2, 96, OBJ), F32)],
        compiler_params=params(32),
        name="gather",
    )(info, peers, got)


def turn(value, axis, step, count):
    return lax.ppermute(value, axis, [(i, (i + step) % count) for i in range(count)])


def on_device(probe_wave, prop_rows, prop_cols, transmission, exit_cotangent, window_tiles, slot_count):
    zl = lax.axis_index("zl")
    core = lax.axis_index("core")
    zh = lax.axis_index("zh")
    x = lax.axis_index("x")
    y = lax.axis_index("y")
    tiles = lax.dynamic_index_in_dim(window_tiles, zl, 0, keepdims=False)
    used = (zl < slot_count[0]).astype(jnp.int32)
    info = jnp.stack([tiles[0], tiles[1], zl, zh, x, used, core, y]).astype(jnp.int32)
    mats = prep(info, prop_rows, prop_cols, probe_wave, exit_cotangent)
    asked = jnp.broadcast_to(jnp.pad(tiles, (0, 126))[None, None, :], (16, 1, 128))
    peers = lax.all_to_all(asked, ("x", "y"), 0, 0, tiled=True)[:, 0, 0:2]
    part = transmission[0]
    low = y % 2
    mine = jnp.where(low == 0, part[0], part[1])
    rest = jnp.where(low == 0, part[1], part[0])
    first = lax.ppermute(mine, "y", [(0, 0), (1, 2), (2, 1), (3, 3)])
    second = lax.ppermute(rest, "y", [(0, 2), (1, 0), (2, 3), (3, 1)])
    piece = jnp.where(y < 2, jnp.concatenate([first, second]), jnp.concatenate([second, first]))
    across = turn(piece, "zl", 1, 2)
    pair = jnp.where(zl == 0, jnp.stack([piece, across]), jnp.stack([across, piece]))
    others = [turn(pair, "zh", step, 4) for step in (1, 2, 3)]
    sent = pack(info, peers, pair, others)
    own = lax.all_to_all(sent, ("x", "y"), 0, 0, tiled=True)
    other = turn(own, "core", 1, 2)
    contrib = main(info, own, other, mats)
    got = lax.all_to_all(contrib, ("x", "y"), 0, 0, tiled=True)
    total = gather(info, peers, got)
    kept = jnp.where(zl == 0, total[0], total[1]).astype(F32)
    given = jnp.where(zl == 0, total[1], total[0])
    kept = (kept + turn(given, "zl", 1, 2).astype(F32)).astype(BF)
    here = lax.dynamic_index_in_dim(kept, zh, 0, keepdims=False).astype(F32)
    for step in (1, 2, 3):
        away = lax.dynamic_index_in_dim(kept, (zh + step) % 4, 0, keepdims=False)
        here = here + turn(away, "zh", step, 4).astype(F32)
    up = y < 2
    mine = jnp.where(up, here[0:12], here[12:24])
    rest = jnp.where(up, here[12:24], here[0:12])
    first = lax.ppermute(mine, "y", [(0, 0), (1, 2), (2, 1), (3, 3)])
    second = lax.ppermute(rest, "y", [(0, 1), (1, 3), (2, 0), (3, 2)])
    grad = jnp.where(low == 0, jnp.stack([first, second]), jnp.stack([second, first]))
    return grad[None]


def solution(mesh):
    whole = Mesh(mesh.devices.reshape(2, 2, 4, 4, 4), ("zl", "core", "zh", "x", "y"))
    depth = ("zl", "core")
    scan = ("zh", "x", "y")
    placed = (
        P(),
        P(),
        P(),
        P(depth, None, scan, None),
        P(scan, None, None, None),
        P(scan, None),
        P(scan),
    )
    return jax.shard_map(
        on_device,
        mesh=whole,
        in_specs=placed,
        out_specs=P(depth, None, scan, None),
        check_vma=False,
    )
```

time: 1610 us -> 166 us (0.10)
  the two profiles are of different devices: /device:TPU:8 before, /device:TPU:64 now
where the time goes in v1:
time: 166 us
  blocking collectives  70.2 us (42%)
  Pallas kernels  36.6 us (22%)
  starting transfers between devices  35.4 us (21%)
  waiting for transfers between devices  14.9 us (9%)
  local copies, waits for them, and re-layouts  7.7 us (5%)
    all_to_all x1, blocking collectives, on_device(): own = lax.all_to_all(sent, ('x', 'y'), 0, 0, tiled=True)  35.2 us
    all_to_all x1, blocking collectives, on_device(): got = lax.all_to_all(contrib, ('x', 'y'), 0, 0, tiled=True)  35 us
    pallas_call x1, Pallas kernels, main(): pl.pallas_call(main_kernel, out_shape=jax.ShapeDtypeStruct((16, 2, 72, W)...  25.7 us
    ppermute x9, starting transfers between devices, turn(): lax.ppermute(value, axis, [(i, (i + step) % count) for i in range(count)])  20.2 us
    ppermute x9, waiting for transfers between devices, turn(): lax.ppermute(value, axis, [(i, (i + step) % count) for i in range(count)])  11.9 us
    pallas_call x1, Pallas kernels, prep(): pl.pallas_call(prep_kernel, out_shape=[square] * 4 + [jax.ShapeDtypeStruc...  8.2 us
    all_to_all x1, starting transfers between devices, on_device(): peers = lax.all_to_all(asked, ('x', 'y'), 0, 0, tiled=True)[:, 0, 0:2]  6.02 us
    ppermute x1, starting transfers between devices, on_device(): second = lax.ppermute(rest, 'y', [(0, 2), (1, 0), (2, 3), (3, 1)])  4.97 us
  transfers between devices with their start and end apart: 14, of which 5 were waited for; matrix products, arithmetic and copies ran while one was open for 2% of the time, Pallas kernels for 5%

profile of v1, /device:TPU:64, one launch (start us, length us, event | category | flops | bytes accessed | tf_op | source)
XLA Modules:
  0.0 165.8 jit_solution(12823715518997518337)
XLA Ops:
  1.6 5.0 %collective-permute-start.1 = (bf16[12,768]{1,0:T(8,128)(2,1)S(1)}, bf16[12,768]{1,0:T(8,128)(2,1)S(1)}, u32[]{:S(2)}, u32[]{:S(2)}) collective-permute-start(bf16[12,768]{1,0:T(8,128)(2,1)S(1)} %get-tuple-element.23), channel_id=1, source_target_pairs={{0,2},{1,0},{2,3},{3,1},{4,6},{5,4},{6,7},{7,5},{8,10},{9,8},{10,1... | collective-permute-start | bytes 55304 | tf_op jit(solution)/shard_map/ppermute | solution.py:255
  7.2 6.0 %all-to-all-start = ((s32[16,1,128]{2,1,0:T(1,128)}), s32[16,1,128]{2,1,0:T(1,128)S(1)}, u32[]{:S(2)}, u32[]{:S(2)}) async-start(s32[16,1,128]{2,1,0:T(1,128)} %broadcast_in_dim.2), calls=%async_computation | async-start | bytes 16384 | tf_op jit(solution)/shard_map/all_to_all | solution.py:249
  13.3 2.0 %collective-permute-start.2 = (bf16[24,768]{1,0:T(8,128)(2,1)S(1)}, bf16[24,768]{1,0:T(8,128)(2,1)S(1)}, u32[]{:S(2)}, u32[]{:S(2)}) collective-permute-start(bf16[24,768]{1,0:T(8,128)(2,1)S(1)} %maximum_select_fusion.3), channel_id=1, source_target_pairs={{0,128},{128,0},{1,129},{129,1},{2,130},{130,2},{3,131},{131,3},{4... | collective-permute-start | bytes 110600 | tf_op jit(solution)/shard_map/ppermute | solution.py:235
  15.3 2.0 %collective-permute-done.2 = bf16[24,768]{1,0:T(8,128)(2,1)S(1)} collective-permute-done((bf16[24,768]{1,0:T(8,128)(2,1)S(1)}, bf16[24,768]{1,0:T(8,128)(2,1)S(1)}, u32[]{:S(2)}, u32[]{:S(2)}) %collective-permute-start.2) | collective-permute-done | bytes 36896 | tf_op jit(solution)/shard_map/ppermute | solution.py:235
  17.4 4.6 %collective-permute-start.3 = (bf16[2,24,768]{2,1,0:T(8,128)(2,1)S(1)}, bf16[2,24,768]{2,1,0:T(8,128)(2,1)S(1)}, u32[]{:S(2)}, u32[]{:S(2)}) collective-permute-start(bf16[2,24,768]{2,1,0:T(8,128)(2,1)S(1)} %maximum_select_fusion.1.own), channel_id=1, source_target_pairs={{0,16},{16,32},{32,48},{48,0},{1,17},{17,33},{33,49},{49,1},{2,18}... | collective-permute-start | bytes 221192 | tf_op jit(solution)/shard_map/ppermute | solution.py:235
  21.9 1.0 collective-permute-start.4
  22.9 2.8 %collective-permute-start.5 = (bf16[2,24,768]{2,1,0:T(8,128)(2,1)S(1)}, bf16[2,24,768]{2,1,0:T(8,128)(2,1)S(1)}, u32[]{:S(2)}, u32[]{:S(2)}) collective-permute-start(bf16[2,24,768]{2,1,0:T(8,128)(2,1)S(1)} %maximum_select_fusion.1.own), channel_id=1, source_target_pairs={{0,48},{16,0},{32,16},{48,32},{1,49},{17,1},{33,17},{49,33},{2,50}... | collective-permute-start | bytes 221192 | tf_op jit(solution)/shard_map/ppermute | solution.py:235
  27.1 1.3 stack.57.info
  28.4 2.0 %collective-permute-done.4.two = bf16[2,24,768]{2,1,0:T(8,128)(2,1)S(1)} collective-permute-done((bf16[2,24,768]{2,1,0:T(8,128)(2,1)S(1)}, bf16[2,24,768]{2,1,0:T(8,128)(2,1)S(1)}, u32[]{:S(2)}, u32[]{:S(2)}) %collective-permute-start.4) | collective-permute-done | bytes 73760 | tf_op jit(solution)/shard_map/ppermute | solution.py:235
  30.4 1.2 pack.1
  31.7 35.2 %all_to_all.15.own = bf16[16,2,72,512]{3,2,1,0:T(8,128)(2,1)S(1)} all-to-all(bf16[16,2,72,512]{3,2,1,0:T(8,128)(2,1)S(1)} %pack.1), channel_id=1, replica_groups=mesh['zl'=2,'core'=2,'zh'=4,'x'=4,'y'=4] {'x','y'}, dimensions={0} | all-to-all | bytes 4718592 | tf_op jit(solution)/shard_map/all_to_all | solution.py:261
  67.0 8.2 %prep.1 = (bf16[1024,1024]{1,0:T(8,128)(2,1)}, bf16[1024,1024]{1,0:T(8,128)(2,1)}, bf16[1024,1024]{1,0:T(8,128)(2,1)}, bf16[1024,1024]{1,0:T(8,128)(2,1)}, bf16[...) custom-call(s32[8]{0:T(128)S(1)} %stack.57.info, bf16[2,512,512]{2,1,0:T(8,128)(2,1)S(1)} %copy-done.3, ...), custom_call_target="tpu_custom_call" | custom-call | tf_op jit(solution)/shard_map/prep/pallas_call | solution.py:67
  76.1 1.0 copy-done.2
  77.1 1.5 copy-done.9
  78.6 25.7 %main.1 = bf16[16,2,72,512]{3,2,1,0:T(8,128)(2,1)} custom-call(s32[8]{0:T(128)} %copy-done.6, bf16[16,2,72,512]{3,2,1,0:T(8,128)(2,1)} %copy-done.8, bf16[16,2,72,512]{3,2,1,0:T(8,128)(2,1)} %copy-done.9, bf16[1024,1024]{1,0:T(8,128)(2,1)} %get-tuple-element.11.a1, bf16[1024,1024]{1,0:T(8,128)(2,1)} %get-tuple-element.12.a1t, ...), custom_call_target="tpu_custom_call" | custom-call | tf_op jit(solution)/shard_map/main/pallas_call | solution.py:182
  104.2 35.0 %all_to_all.16.got = bf16[16,2,72,512]{3,2,1,0:T(8,128)(2,1)S(1)} all-to-all(bf16[16,2,72,512]{3,2,1,0:T(8,128)(2,1)} %main.1), channel_id=1, replica_groups=mesh['zl'=2,'core'=2,'zh'=4,'x'=4,'y'=4] {'x','y'}, dimensions={0} | all-to-all | bytes 4718592 | tf_op jit(solution)/shard_map/all_to_all | solution.py:264
  139.2 1.5 gather.1
  140.7 1.4 collective-permute-start.7
  142.1 3.9 %collective-permute-done.7 = bf16[4,24,768]{2,1,0:T(8,128)(2,1)S(1)} collective-permute-done((bf16[4,24,768]{2,1,0:T(8,128)(2,1)S(1)}, bf16[4,24,768]{2,1,0:T(8,128)(2,1)S(1)}, u32[]{:S(2)}, u32[]{:S(2)}) %collective-permute-start.7) | collective-permute-done | bytes 147488 | tf_op jit(solution)/shard_map/ppermute | solution.py:235
  147.0 3.3 %collective-permute-start.8 = (bf16[24,768]{1,0:T(8,128)(2,1)S(1)}, bf16[24,768]{1,0:T(8,128)(2,1)S(1)}, u32[]{:S(2)}, u32[]{:S(2)}) collective-permute-start(bf16[24,768]{1,0:T(8,128)(2,1)S(1)} %get-tuple-element.17), channel_id=1, source_target_pairs={{0,16},{16,32},{32,48},{48,0},{1,17},{17,33},{33,49},{49,1},{2,18}... | collective-permute-start | bytes 110600 | tf_op jit(solution)/shard_map/ppermute | solution.py:235
  150.3 4.2 %collective-permute-start.9 = (bf16[24,768]{1,0:T(8,128)(2,1)S(1)}, bf16[24,768]{1,0:T(8,128)(2,1)S(1)}, u32[]{:S(2)}, u32[]{:S(2)}) collective-permute-start(bf16[24,768]{1,0:T(8,128)(2,1)S(1)} %get-tuple-element.19), channel_id=1, source_target_pairs={{0,32},{16,48},{32,0},{48,16},{1,33},{17,49},{33,1},{49,17},{2,34}... | collective-permute-start | bytes 110600 | tf_op jit(solution)/shard_map/ppermute | solution.py:235
  154.6 4.0 %collective-permute-done.9 = bf16[24,768]{1,0:T(8,128)(2,1)S(1)} collective-permute-done((bf16[24,768]{1,0:T(8,128)(2,1)S(1)}, bf16[24,768]{1,0:T(8,128)(2,1)S(1)}, u32[]{:S(2)}, u32[]{:S(2)}) %collective-permute-start.9) | collective-permute-done | bytes 36896 | tf_op jit(solution)/shard_map/ppermute | solution.py:235
  159.3 2.8 %collective-permute-start.12 = (f32[12,768]{1,0:T(8,128)S(1)}, f32[12,768]{1,0:T(8,128)S(1)}, u32[]{:S(2)}, u32[]{:S(2)}) collective-permute-start(f32[12,768]{1,0:T(8,128)S(1)} %get-tuple-element.21), channel_id=1, source_target_pairs={{0,1},{1,3},{2,0},{3,2},{4,5},{5,7},{6,4},{7,6},{8,9},{9,11},{10,8... | collective-permute-start | bytes 110600 | tf_op jit(solution)/shard_map/ppermute | solution.py:277
  162.1 3.0 %collective-permute-done.12 = f32[12,768]{1,0:T(8,128)S(1)} collective-permute-done((f32[12,768]{1,0:T(8,128)S(1)}, f32[12,768]{1,0:T(8,128)S(1)}, u32[]{:S(2)}, u32[]{:S(2)}) %collective-permute-start.12) | collective-permute-done | bytes 36896 | tf_op jit(solution)/shard_map/ppermute | solution.py:277
  (48 shorter events, 6.4 us)
Async XLA Ops:
  0.0 6.6 %copy-start = (s32[2,2]{1,0:T(2,128)S(1)}, s32[2,2]{1,0:T(2,128)}, u32[]{:S(2)}) copy-start(s32[2,2]{1,0:T(2,128)} %param.12) | copy-start | bytes 52
  0.9 12.3 %collective-permute-start = (bf16[12,768]{1,0:T(8,128)(2,1)S(1)}, bf16[12,768]{1,0:T(8,128)(2,1)S(1)}, u32[]{:S(2)}, u32[]{:S(2)}) collective-permute-start(bf16[12,768]{1,0:T(8,128)(2,1)S(1)} %get-tuple-element.22), channel_id=1, source_target_pairs={{0,0},{1,2},{2,1},{3,3},{4,4},{5,6},{6,5},{7,7},{8,8},{9,10},{10,9... | collective-permute-start | bytes 55304 | tf_op jit(solution)/shard_map/ppermute | solution.py:254
  1.6 11.7 %collective-permute-start.1 = (bf16[12,768]{1,0:T(8,128)(2,1)S(1)}, bf16[12,768]{1,0:T(8,128)(2,1)S(1)}, u32[]{:S(2)}, u32[]{:S(2)}) collective-permute-start(bf16[12,768]{1,0:T(8,128)(2,1)S(1)} %get-tuple-element.23), channel_id=1, source_target_pairs={{0,2},{1,0},{2,3},{3,1},{4,6},{5,4},{6,7},{7,5},{8,10},{9,8},{10,1... | collective-permute-start | bytes 55304 | tf_op jit(solution)/shard_map/ppermute | solution.py:255
  7.2 21.2 %all-to-all-start = ((s32[16,1,128]{2,1,0:T(1,128)}), s32[16,1,128]{2,1,0:T(1,128)S(1)}, u32[]{:S(2)}, u32[]{:S(2)}) async-start(s32[16,1,128]{2,1,0:T(1,128)} %broadcast_in_dim.2), calls=%async_computation | async-start | bytes 16384 | tf_op jit(solution)/shard_map/all_to_all | solution.py:249
  13.3 4.0 %collective-permute-start.2 = (bf16[24,768]{1,0:T(8,128)(2,1)S(1)}, bf16[24,768]{1,0:T(8,128)(2,1)S(1)}, u32[]{:S(2)}, u32[]{:S(2)}) collective-permute-start(bf16[24,768]{1,0:T(8,128)(2,1)S(1)} %maximum_select_fusion.3), channel_id=1, source_target_pairs={{0,128},{128,0},{1,129},{129,1},{2,130},{130,2},{3,131},{131,3},{4... | collective-permute-start | bytes 110600 | tf_op jit(solution)/shard_map/ppermute | solution.py:235
  17.4 11.1 %collective-permute-start.3 = (bf16[2,24,768]{2,1,0:T(8,128)(2,1)S(1)}, bf16[2,24,768]{2,1,0:T(8,128)(2,1)S(1)}, u32[]{:S(2)}, u32[]{:S(2)}) collective-permute-start(bf16[2,24,768]{2,1,0:T(8,128)(2,1)S(1)} %maximum_select_fusion.1.own), channel_id=1, source_target_pairs={{0,16},{16,32},{32,48},{48,0},{1,17},{17,33},{33,49},{49,1},{2,18}... | collective-permute-start | bytes 221192 | tf_op jit(solution)/shard_map/ppermute | solution.py:235
  21.9 8.5 %collective-permute-start.4 = (bf16[2,24,768]{2,1,0:T(8,128)(2,1)S(1)}, bf16[2,24,768]{2,1,0:T(8,128)(2,1)S(1)}, u32[]{:S(2)}, u32[]{:S(2)}) collective-permute-start(bf16[2,24,768]{2,1,0:T(8,128)(2,1)S(1)} %maximum_select_fusion.1.own), channel_id=1, source_target_pairs={{0,32},{16,48},{32,0},{48,16},{1,33},{17,49},{33,1},{49,17},{2,34}... | collective-permute-start | bytes 221192 | tf_op jit(solution)/shard_map/ppermute | solution.py:235
  22.9 7.5 %collective-permute-start.5 = (bf16[2,24,768]{2,1,0:T(8,128)(2,1)S(1)}, bf16[2,24,768]{2,1,0:T(8,128)(2,1)S(1)}, u32[]{:S(2)}, u32[]{:S(2)}) collective-permute-start(bf16[2,24,768]{2,1,0:T(8,128)(2,1)S(1)} %maximum_select_fusion.1.own), channel_id=1, source_target_pairs={{0,48},{16,0},{32,16},{48,32},{1,49},{17,1},{33,17},{49,33},{2,50}... | collective-permute-start | bytes 221192 | tf_op jit(solution)/shard_map/ppermute | solution.py:235
  28.4 38.5 %copy-start.6 = (s32[8]{0:T(128)}, s32[8]{0:T(128)S(1)}, u32[]{:S(2)}) copy-start(s32[8]{0:T(128)S(1)} %stack.57.info) | copy-start | bytes 100
  31.7 35.3 %copy-start.3 = (bf16[2,512,512]{2,1,0:T(8,128)(2,1)S(1)}, bf16[2,512,512]{2,1,0:T(8,128)(2,1)}, u32[]{:S(2)}) copy-start(bf16[2,512,512]{2,1,0:T(8,128)(2,1)} %rows.1) | copy-start | bytes 3145732
  31.7 35.3 %copy-start.4 = (bf16[2,512,512]{2,1,0:T(8,128)(2,1)S(1)}, bf16[2,512,512]{2,1,0:T(8,128)(2,1)}, u32[]{:S(2)}) copy-start(bf16[2,512,512]{2,1,0:T(8,128)(2,1)} %cols.1) | copy-start | bytes 3145732
  31.7 35.3 %copy-start.5 = (bf16[2,512,512]{2,1,0:T(8,128)(2,1)S(1)}, bf16[2,512,512]{2,1,0:T(8,128)(2,1)}, u32[]{:S(2)}) copy-start(bf16[2,512,512]{2,1,0:T(8,128)(2,1)} %probe.1) | copy-start | bytes 3145732
  66.9 8.2 %copy-start.8 = (bf16[16,2,72,512]{3,2,1,0:T(8,128)(2,1)}, bf16[16,2,72,512]{3,2,1,0:T(8,128)(2,1)S(1)}, u32[]{:S(2)}) copy-start(bf16[16,2,72,512]{3,2,1,0:T(8,128)(2,1)S(1)} %all_to_all.15.own) | copy-start | bytes 7077892
  66.9 10.2 %collective-permute-start.6 = (bf16[16,2,72,512]{3,2,1,0:T(8,128)(2,1)S(1)}, bf16[16,2,72,512]{3,2,1,0:T(8,128)(2,1)S(1)}, u32[]{:S(2)}, u32[]{:S(2)}) collective-permute-start(bf16[16,2,72,512]{3,2,1,0:T(8,128)(2,1)S(1)} %all_to_all.15.own), channel_id=1, source_target_pairs={{0,64},{64,0},{1,65},{65,1},{2,66},{66,2},{3,67},{67,3},{4,68},{68... | collective-permute-start | bytes 7077896 | tf_op jit(solution)/shard_map/ppermute | solution.py:235
  75.2 1.0 copy-start.1
  76.1 1.0 copy-start.2
  77.1 1.5 copy-start.9
  104.2 35.0 %copy-start.7 = (s32[8]{0:T(128)S(1)}, s32[8]{0:T(128)}, u32[]{:S(2)}) copy-start(s32[8]{0:T(128)} %copy-done.6) | copy-start | bytes 100
  140.7 5.3 %collective-permute-start.7 = (bf16[4,24,768]{2,1,0:T(8,128)(2,1)S(1)}, bf16[4,24,768]{2,1,0:T(8,128)(2,1)S(1)}, u32[]{:S(2)}, u32[]{:S(2)}) collective-permute-start(bf16[4,24,768]{2,1,0:T(8,128)(2,1)S(1)} %select_bitcast_fusion), channel_id=1, source_target_pairs={{0,128},{128,0},{1,129},{129,1},{2,130},{130,2},{3,131},{131,3},{4... | collective-permute-start | bytes 442376 | tf_op jit(solution)/shard_map/ppermute | solution.py:235
  146.1 8.5 %collective-permute-start.10 = (bf16[24,768]{1,0:T(8,128)(2,1)S(1)}, bf16[24,768]{1,0:T(8,128)(2,1)S(1)}, u32[]{:S(2)}, u32[]{:S(2)}) collective-permute-start(bf16[24,768]{1,0:T(8,128)(2,1)S(1)} %get-tuple-element.18), channel_id=1, source_target_pairs={{0,48},{16,0},{32,16},{48,32},{1,49},{17,1},{33,17},{49,33},{2,50}... | collective-permute-start | bytes 110600 | tf_op jit(solution)/shard_map/ppermute | solution.py:235
  147.0 7.5 %collective-permute-start.8 = (bf16[24,768]{1,0:T(8,128)(2,1)S(1)}, bf16[24,768]{1,0:T(8,128)(2,1)S(1)}, u32[]{:S(2)}, u32[]{:S(2)}) collective-permute-start(bf16[24,768]{1,0:T(8,128)(2,1)S(1)} %get-tuple-element.17), channel_id=1, source_target_pairs={{0,16},{16,32},{32,48},{48,0},{1,17},{17,33},{33,49},{49,1},{2,18}... | collective-permute-start | bytes 110600 | tf_op jit(solution)/shard_map/ppermute | solution.py:235
  150.3 8.3 %collective-permute-start.9 = (bf16[24,768]{1,0:T(8,128)(2,1)S(1)}, bf16[24,768]{1,0:T(8,128)(2,1)S(1)}, u32[]{:S(2)}, u32[]{:S(2)}) collective-permute-start(bf16[24,768]{1,0:T(8,128)(2,1)S(1)} %get-tuple-element.19), channel_id=1, source_target_pairs={{0,32},{16,48},{32,0},{48,16},{1,33},{17,49},{33,1},{49,17},{2,34}... | collective-permute-start | bytes 110600 | tf_op jit(solution)/shard_map/ppermute | solution.py:235
  158.6 3.5 %collective-permute-start.11 = (f32[12,768]{1,0:T(8,128)S(1)}, f32[12,768]{1,0:T(8,128)S(1)}, u32[]{:S(2)}, u32[]{:S(2)}) collective-permute-start(f32[12,768]{1,0:T(8,128)S(1)} %get-tuple-element.20), channel_id=1, source_target_pairs={{0,0},{1,2},{2,1},{3,3},{4,4},{5,6},{6,5},{7,7},{8,8},{9,10},{10,9... | collective-permute-start | bytes 110600 | tf_op jit(solution)/shard_map/ppermute | solution.py:276
  159.3 5.8 %collective-permute-start.12 = (f32[12,768]{1,0:T(8,128)S(1)}, f32[12,768]{1,0:T(8,128)S(1)}, u32[]{:S(2)}, u32[]{:S(2)}) collective-permute-start(f32[12,768]{1,0:T(8,128)S(1)} %get-tuple-element.21), channel_id=1, source_target_pairs={{0,1},{1,3},{2,0},{3,2},{4,5},{5,7},{6,4},{7,6},{8,9},{9,11},{10,8... | collective-permute-start | bytes 110600 | tf_op jit(solution)/shard_map/ppermute | solution.py:277

commit v2 on v1

v2 whole, which is shorter than its diff:
```python
import jax
import jax.numpy as jnp
from jax import lax
from jax.experimental import pallas as pl
from jax.experimental.pallas import tpu as pltpu
from jax.sharding import Mesh, PartitionSpec as P

TILE = 32
W = 512
OBJ = 768
PAD = 64
ROWS = 640
BF = jnp.bfloat16
F32 = jnp.float32


SMEM = pl.BlockSpec(memory_space=pltpu.SMEM)
VMEM = pl.BlockSpec(memory_space=pltpu.VMEM)


def params(mib):
    return pltpu.CompilerParams(vmem_limit_bytes=mib * 1024 * 1024)


def first_interval(row_tile, x):
    return ((row_tile * TILE - 48 * x + 144) >= 192).astype(jnp.int32)


def prep_kernel(info, rows, cols, probe, cot, a1, a1t, b1, b2, wave, grad):
    shift = info[1] * TILE
    ar = rows[0].astype(F32)
    ai = rows[1].astype(F32)
    a1[0:W, 0:W] = rows[0]
    a1[0:W, W:] = (-ai).astype(BF)
    a1[W:, 0:W] = rows[1]
    a1[W:, W:] = rows[0]
    art = ar.T.astype(BF)
    ait = ai.T
    a1t[0:W, 0:W] = art
    a1t[0:W, W:] = ait.astype(BF)
    a1t[W:, 0:W] = (-ait).astype(BF)
    a1t[W:, W:] = art

    def turned(value):
        return pltpu.roll(pltpu.roll(value, shift, 1), shift, 0)

    br = turned(cols[0].astype(F32))
    bi = turned(cols[1].astype(F32))
    b2[0:W, 0:W] = br.astype(BF)
    b2[0:W, W:] = (-bi).astype(BF)
    b2[W:, 0:W] = bi.astype(BF)
    b2[W:, W:] = br.astype(BF)
    brt = br.T.astype(BF)
    bit = bi.T
    b1[0:W, 0:W] = brt
    b1[0:W, W:] = bit.astype(BF)
    b1[W:, 0:W] = (-bit).astype(BF)
    b1[W:, W:] = brt
    slot = info[2]
    for part in range(2):
        wave[:, part * W : (part + 1) * W] = pltpu.roll(probe[part].astype(F32), shift, 1).astype(BF)
        grad[part * W : (part + 1) * W, :] = pltpu.roll(cot[slot, part].astype(F32), shift, 1).astype(BF)


def prep(info, rows, cols, probe, cot):
    square = jax.ShapeDtypeStruct((2 * W, 2 * W), BF)
    return pl.pallas_call(
        prep_kernel,
        out_shape=[square] * 4 + [jax.ShapeDtypeStruct((W, 2 * W), BF), jax.ShapeDtypeStruct((2 * W, W), BF)],
        in_specs=[SMEM] + [VMEM] * 4,
        out_specs=[VMEM] * 6,
        compiler_params=params(48),
        name="prep",
    )(info, rows, cols, probe, cot)


def pack_kernel(info, peers, own, one, two, three, ready, out, held):
    zh = info[3]
    x = info[4]
    for step, piece in enumerate((own, one, two, three)):
        place = lax.rem(zh - step + 4, 4)
        held[pl.ds(pl.multiple_of(place * 24, 8), 24), :] = piece[...].astype(F32)
    lane = lax.broadcasted_iota(jnp.int32, (72, 256), 1)
    for slot in range(2):

        def target(t, carry):
            first = first_interval(peers[t, 2 * slot], x)
            rows = pl.ds(pl.multiple_of(first * 24, 8), 72)
            wrapped = lane < peers[t, 2 * slot + 1] * TILE
            low = held[rows, 0:256]
            high = held[rows, 512:768]
            out[slot * 16 + t, :, 0:256] = jnp.where(wrapped, high, low).astype(BF)
            out[slot * 16 + t, :, 256:512] = held[rows, 256:512].astype(BF)
            return carry

        lax.fori_loop(0, 16, target, 0)


def pack(info, peers, own, others, ready):
    return pl.pallas_call(
        pack_kernel,
        out_shape=jax.ShapeDtypeStruct((32, 72, W), BF),
        in_specs=[SMEM, SMEM] + [VMEM] * 4 + [pl.BlockSpec(memory_space=pl.ANY)],
        out_specs=VMEM,
        scratch_shapes=[pltpu.VMEM((96, OBJ), F32)],
        compiler_params=params(16),
        name="pack",
    )(info, peers, own, *others, ready)


def place_patches(source, patch, slices, row_tile):
    def place(plane, carry):
        start = 192 * first_interval(row_tile, plane) + 48 * plane - TILE * row_tile + PAD
        for a in range(2):
            got = [source[a * 16 + plane * 4 + y].astype(F32) for y in range(4)]
            for k in range(3):
                rows = pl.ds(pl.multiple_of(start + 192 * k, 16), 48)
                for part in range(2):
                    cut = k * 24 + part * 12
                    patch[slices[a], part, rows, :] = jnp.concatenate([g[cut : cut + 12] for g in got])
        return carry

    lax.fori_loop(0, 4, place, 0)


def cut_contrib(contrib, out, a, row_tile):
    def cut(plane, carry):
        start = 192 * first_interval(row_tile, plane) + 48 * plane - TILE * row_tile + PAD
        blocks = [
            contrib[part, pl.ds(pl.multiple_of(start + 192 * k, 16), 48), :] for k in range(3) for part in range(2)
        ]
        for y in range(4):
            out[a * 16 + plane * 4 + y] = jnp.concatenate([b[12 * y : 12 * y + 12] for b in blocks]).astype(BF)
        return carry

    lax.fori_loop(0, 4, cut, 0)


def main_kernel(info, own, other, a1, a1t, b1, b2, wave0, grad0, out, patch, waves, left, right, contrib):
    row_tile = info[0]
    used = info[5] > 0
    core = info[6]
    place_patches(own, patch, (core, core + 2), row_tile)
    place_patches(other, patch, (1 - core, 3 - core), row_tile)
    waves[0] = wave0[...]
    for s in range(3):
        wr = waves[s, :, 0:W].astype(F32)
        wi = waves[s, :, W:].astype(F32)
        pr = patch[s, 0, PAD : PAD + W, :]
        pi = patch[s, 1, PAD : PAD + W, :]
        left[0:W, :] = (wr * pr - wi * pi).astype(BF)
        left[W:, :] = (wr * pi + wi * pr).astype(BF)
        swept = jnp.dot(a1[...], left[...], preferred_element_type=F32)
        right[:, 0:W] = swept[0:W].astype(BF)
        right[:, W:] = swept[W:].astype(BF)
        waves[s + 1] = jnp.dot(right[...], b1[...], preferred_element_type=F32).astype(BF)
    left[...] = grad0[...]
    contrib[:, 0:PAD, :] = jnp.zeros((2, PAD, W), F32)
    contrib[:, PAD + W :, :] = jnp.zeros((2, PAD, W), F32)
    for s in range(3, -1, -1):
        swept = jnp.dot(a1t[...], left[...], preferred_element_type=F32)
        right[:, 0:W] = swept[0:W].astype(BF)
        right[:, W:] = swept[W:].astype(BF)
        adjoint = jnp.dot(right[...], b2[...], preferred_element_type=F32)
        gr = adjoint[:, 0:W]
        gi = adjoint[:, W:]
        if s > 0:
            pr = patch[s, 0, PAD : PAD + W, :]
            pi = patch[s, 1, PAD : PAD + W, :]
            left[0:W, :] = (pr * gr + pi * gi).astype(BF)
            left[W:, :] = (pr * gi - pi * gr).astype(BF)

        @pl.when(core == s % 2)
        def _():
            wr = waves[s, :, 0:W].astype(F32)
            wi = waves[s, :, W:].astype(F32)
            contrib[0, PAD : PAD + W, :] = jnp.where(used, wr * gr + wi * gi, 0.0)
            contrib[1, PAD : PAD + W, :] = jnp.where(used, wr * gi - wi * gr, 0.0)

            cut_contrib(contrib, out, s // 2, row_tile)


def main(info, own, other, mats):
    return pl.pallas_call(
        main_kernel,
        out_shape=jax.ShapeDtypeStruct((32, 72, W), BF),
        in_specs=[SMEM] + [VMEM] * 8,
        out_specs=VMEM,
        scratch_shapes=[
            pltpu.VMEM((4, 2, ROWS, W), F32),
            pltpu.VMEM((4, W, 2 * W), BF),
            pltpu.VMEM((2 * W, W), BF),
            pltpu.VMEM((W, 2 * W), BF),
            pltpu.VMEM((2, ROWS, W), F32),
        ],
        compiler_params=params(40),
        name="main",
    )(info, own, other, *mats)


def gather_kernel(info, peers, got, own, one, two, three, total):
    zh = info[3]
    x = info[4]
    total[...] = jnp.zeros((96, OBJ), F32)
    lane = lax.broadcasted_iota(jnp.int32, (72, 256), 1)
    for slot in range(2):

        def source(t, carry):
            first = first_interval(peers[t, 2 * slot], x)
            rows = pl.ds(pl.multiple_of(first * 24, 8), 72)
            wrapped = lane < peers[t, 2 * slot + 1] * TILE
            value = got[slot * 16 + t].astype(F32)
            low = value[:, 0:256]
            total[rows, 0:256] += jnp.where(wrapped, 0.0, low)
            total[rows, 512:768] += jnp.where(wrapped, low, 0.0)
            total[rows, 256:512] += value[:, 256:512]
            return carry

        lax.fori_loop(0, 16, source, 0)
    for step, out in enumerate((own, one, two, three)):
        place = lax.rem(zh + step, 4)
        out[...] = total[pl.ds(pl.multiple_of(place * 24, 8), 24), :].astype(out.dtype)


def gather(info, peers, got):
    return pl.pallas_call(
        gather_kernel,
        out_shape=[jax.ShapeDtypeStruct((24, OBJ), F32)] + [jax.ShapeDtypeStruct((24, OBJ), BF)] * 3,
        in_specs=[SMEM, SMEM, VMEM],
        out_specs=[VMEM] * 4,
        scratch_shapes=[pltpu.VMEM((96, OBJ), F32)],
        compiler_params=params(16),
        name="gather",
    )(info, peers, got)


def turn(value, axis, step, count):
    return lax.ppermute(value, axis, [(i, (i + step) % count) for i in range(count)])


def on_device(probe_wave, prop_rows, prop_cols, transmission, exit_cotangent, window_tiles, slot_count):
    zl = lax.axis_index("zl")
    core = lax.axis_index("core")
    zh = lax.axis_index("zh")
    x = lax.axis_index("x")
    tiles = lax.dynamic_index_in_dim(window_tiles, zl, 0, keepdims=False)
    used = (zl < slot_count[0]).astype(jnp.int32)
    info = jnp.stack([tiles[0], tiles[1], zl, zh, x, used, core, core]).astype(jnp.int32)
    mats = prep(info, prop_rows, prop_cols, probe_wave, exit_cotangent)
    asked = jnp.broadcast_to(jnp.pad(window_tiles.reshape(4), (0, 124))[None, None, :], (16, 1, 128))
    peers = lax.all_to_all(asked, ("x", "y"), 0, 0, tiled=True)[:, 0, 0:4]
    piece = transmission.reshape(24, OBJ)
    others = [turn(piece, "zh", step, 4) for step in (1, 2, 3)]
    sent = pack(info, peers, piece, others, mats[0])
    own = lax.all_to_all(sent, ("zl", "x", "y"), 0, 0, tiled=True)
    other = turn(own, "core", 1, 2)
    contrib = main(info, own, other, mats)
    got = lax.all_to_all(contrib, ("zl", "x", "y"), 0, 0, tiled=True)
    here, *away = gather(info, peers, got)
    for step in (1, 2, 3):
        here = here + turn(away[step - 1], "zh", step, 4).astype(F32)
    return here.reshape(1, 2, 12, OBJ)


def solution(mesh):
    whole = Mesh(mesh.devices.reshape(2, 2, 4, 4, 4), ("zl", "core", "zh", "x", "y"))
    depth = ("zl", "core")
    scan = ("zh", "x", "y")
    placed = (
        P(),
        P(),
        P(),
        P(depth, None, scan, None),
        P(scan, None, None, None),
        P(scan, None),
        P(scan),
    )
    return jax.shard_map(
        on_device,
        mesh=whole,
        in_specs=placed,
        out_specs=P(depth, None, scan, None),
        check_vma=False,
    )
```

time: 166 us -> 151 us (0.910)
  starting transfers between devices: 35.4 us -> 21.1 us
  Pallas kernels: 36.6 us -> 32.1 us
  local copies, waits for them, and re-layouts: 7.7 us -> 12.2 us
  waiting for transfers between devices: 14.9 us -> 10.5 us
  blocking collectives: 70.2 us -> 73.8 us
    ppermute x4 -> x0, starting transfers between devices: 9.11 us -> none  [the longest x1 4.97 us: on_device(): second = lax.ppermute(rest, 'y', [(0, 2), (1, 0), (2, 3), (3, 1)])]
    ppermute x9 -> x7, starting transfers between devices: 20.2 us -> 14.1 us  [turn(): lax.ppermute(value, axis, [(i, (i + step) % count) for i in range(count)])]
    unnamed x20 -> x21, local copies, waits for them, and re-layouts: 3.44 us -> 7.48 us
    pallas_call x3, Pallas kernels: 28.4 us -> 24.6 us  [the longest x1 21.5 us: main(): pl.pallas_call(main_kernel, out_shape=jax.ShapeDtypeStruct((32, 72, W), B...]
    all_to_all x2, blocking collectives: 70.2 us -> 73.8 us  [the longest x1 38.2 us: on_device(): own = lax.all_to_all(sent, ('zl', 'x', 'y'), 0, 0, tiled=True)]
    ppermute x4 -> x0, waiting for transfers between devices: 2.96 us -> none  [the longest x1 2.95 us: on_device(): second = lax.ppermute(rest, 'y', [(0, 1), (1, 3), (2, 0), (3, 2)])]
    ppermute x9 -> x7, waiting for transfers between devices: 11.9 us -> 10.5 us  [turn(): lax.ppermute(value, axis, [(i, (i + step) % count) for i in range(count)])]
  transfers between devices with their start and end apart: 14 -> 8, of which waited for: 5 -> 4; matrix products, arithmetic and copies ran while one was open for 2% -> 3% of each run, Pallas kernels for 5% -> 5%
where the time goes in v2:
time: 151 us; the launch traced here: 150 us
  blocking collectives  73.8 us (49%)
  Pallas kernels  32.1 us (21%)
  starting transfers between devices  21.1 us (14%)
  local copies, waits for them, and re-layouts  12.2 us (8%)
  waiting for transfers between devices  10.5 us (7%)
    all_to_all x1, blocking collectives, on_device(): own = lax.all_to_all(sent, ('zl', 'x', 'y'), 0, 0, tiled=True)  38.2 us
    all_to_all x1, blocking collectives, on_device(): got = lax.all_to_all(contrib, ('zl', 'x', 'y'), 0, 0, tiled=True)  35.5 us
    pallas_call x1, Pallas kernels, main(): pl.pallas_call(main_kernel, out_shape=jax.ShapeDtypeStruct((32, 72, W), B...  21.5 us
    ppermute x7, starting transfers between devices, turn(): lax.ppermute(value, axis, [(i, (i + step) % count) for i in range(count)])  14.1 us
    ppermute x7, waiting for transfers between devices, turn(): lax.ppermute(value, axis, [(i, (i + step) % count) for i in range(count)])  10.5 us
    pallas_call x1, Pallas kernels, prep(): pl.pallas_call(prep_kernel, out_shape=[square] * 4 + [jax.ShapeDtypeStruc...  7.48 us
    unnamed x21, local copies, waits for them, and re-layouts  7.48 us
    all_to_all x1, starting transfers between devices, on_device(): peers = lax.all_to_all(asked, ('x', 'y'), 0, 0, tiled=True)[:, 0, 0:4]  7.03 us
  transfers between devices with their start and end apart: 8, of which 4 were waited for; matrix products, arithmetic and copies ran while one was open for 3% of the time, Pallas kernels for 5%

profile of v2, /device:TPU:64, one launch (start us, length us, event | category | flops | bytes accessed | tf_op | source)
XLA Modules:
  0.0 150.4 jit_solution(5356070716282290841)
XLA Ops:
  0.0 0.8 copy.17
  0.8 1.5 collective-permute-start.2
  2.3 5.5 %collective-permute-start.1 = (bf16[24,768]{1,0:T(8,128)(2,1)S(1)}, bf16[24,768]{1,0:T(8,128)(2,1)S(1)}, u32[]{:S(2)}, u32[]{:S(2)}) collective-permute-start(bf16[24,768]{1,0:T(8,128)(2,1)S(1)} %reshape.15.own), channel_id=1, source_target_pairs={{0,32},{16,48},{32,0},{48,16},{1,33},{17,49},{33,1},{49,17},{2,34}... | collective-permute-start | bytes 110600 | tf_op jit(solution)/shard_map/ppermute | solution.py:238
  7.7 2.7 %collective-permute-start = (bf16[24,768]{1,0:T(8,128)(2,1)S(1)}, bf16[24,768]{1,0:T(8,128)(2,1)S(1)}, u32[]{:S(2)}, u32[]{:S(2)}) collective-permute-start(bf16[24,768]{1,0:T(8,128)(2,1)S(1)} %reshape.15.own), channel_id=1, source_target_pairs={{0,16},{16,32},{32,48},{48,0},{1,17},{17,33},{33,49},{49,1},{2,18}... | collective-permute-start | bytes 110600 | tf_op jit(solution)/shard_map/ppermute | solution.py:238
  10.4 0.8 reshape.14
  11.8 7.0 %all-to-all-start = ((s32[16,1,128]{2,1,0:T(1,128)}), s32[16,1,128]{2,1,0:T(1,128)S(1)}, u32[]{:S(2)}, u32[]{:S(2)}) async-start(s32[16,1,128]{2,1,0:T(1,128)} %broadcast_in_dim.2), calls=%async_computation | async-start | bytes 16384 | tf_op jit(solution)/shard_map/all_to_all | solution.py:251
  20.8 1.3 stack.28.info
  22.1 1.2 copy-done.5
  23.3 1.2 copy-done.6
  24.6 1.2 copy-done.7
  25.8 7.5 %prep.1 = (bf16[1024,1024]{1,0:T(8,128)(2,1)}, bf16[1024,1024]{1,0:T(8,128)(2,1)}, bf16[1024,1024]{1,0:T(8,128)(2,1)}, bf16[1024,1024]{1,0:T(8,128)(2,1)}, bf16[...) custom-call(s32[8]{0:T(128)S(1)} %stack.28.info, bf16[2,512,512]{2,1,0:T(8,128)(2,1)S(1)} %copy-done.5, ...), custom_call_target="tpu_custom_call" | custom-call | tf_op jit(solution)/shard_map/prep/pallas_call | solution.py:67
  33.3 1.6 %copy-done = bf16[1024,1024]{1,0:T(8,128)(2,1)S(1)} copy-done((bf16[1024,1024]{1,0:T(8,128)(2,1)S(1)}, bf16[1024,1024]{1,0:T(8,128)(2,1)}, u32[]{:S(2)}) %copy-start) | copy-done | bytes 2097176
  34.9 1.4 pack.1
  36.3 38.2 %all_to_all.15.own = bf16[32,72,512]{2,1,0:T(8,128)(2,1)S(1)} all-to-all(bf16[32,72,512]{2,1,0:T(8,128)(2,1)S(1)} %pack.1), channel_id=1, replica_groups=mesh['zl'=2,'core'=2,'zh'=4,'x'=4,'y'=4] {'zl','x','y'}, dimensions={0} | all-to-all | bytes 4718592 | tf_op jit(solution)/shard_map/all_to_all | solution.py:255
  74.5 4.5 %collective-permute-done.3.other = bf16[32,72,512]{2,1,0:T(8,128)(2,1)S(1)} collective-permute-done((bf16[32,72,512]{2,1,0:T(8,128)(2,1)S(1)}, bf16[32,72,512]{2,1,0:T(8,128)(2,1)S(1)}, u32[]{:S(2)}, u32[]{:S(2)}) %collective-permute-start.3) | collective-permute-done | bytes 2359328 | tf_op jit(solution)/shard_map/ppermute | solution.py:238
  79.1 1.4 copy-done.9
  80.5 21.5 %main.1 = bf16[32,72,512]{2,1,0:T(8,128)(2,1)S(1)} custom-call(s32[8]{0:T(128)S(1)} %stack.28.info, bf16[32,72,512]{2,1,0:T(8,128)(2,1)} %copy-done.8, bf16[32,72,512]{2,1,0:T(8,128)(2,1)} %copy-done.9, bf16[1024,1024]{1,0:T(8,128)(2,1)S(1)} %copy-done.1, bf16[1024,1024]{1,0:T(8,128)(2,1)S(1)} %copy-done.2, bf16[1024,1024]{1,0:T(8,128)(2,1)S(1)} %copy-done.3, ...), custom_call_target="tpu_custom_call" | custom-call | tf_op jit(solution)/shard_map/main/pallas_call | solution.py:184
  102.1 35.5 %all_to_all.16.got = bf16[32,72,512]{2,1,0:T(8,128)(2,1)S(1)} all-to-all(bf16[32,72,512]{2,1,0:T(8,128)(2,1)S(1)} %main.1), channel_id=1, replica_groups=mesh['zl'=2,'core'=2,'zh'=4,'x'=4,'y'=4] {'zl','x','y'}, dimensions={0} | all-to-all | bytes 4718592 | tf_op jit(solution)/shard_map/all_to_all | solution.py:258
  137.6 1.6 %gather.1 = (f32[24,768]{1,0:T(8,128)S(1)}, bf16[24,768]{1,0:T(8,128)(2,1)S(1)}, bf16[24,768]{1,0:T(8,128)(2,1)S(1)}, bf16[24,768]{1,0:T(8,128)(2,1)S(1)}) custom-call(s32[8]{0:T(128)S(1)} %stack.28.info, s32[16,4]{1,0:T(8,128)S(1)} %bitcast.12, bf16[32,72,512]{2,1,0:T(8,128)(2,1)S(1)} %all_to_all.16.got), custom_call_target="tpu_custom_call" | custom-call | tf_op jit(solution)/shard_map/gather/pallas_call | solution.py:226
  139.6 3.5 %collective-permute-start.5 = (bf16[24,768]{1,0:T(8,128)(2,1)S(1)}, bf16[24,768]{1,0:T(8,128)(2,1)S(1)}, u32[]{:S(2)}, u32[]{:S(2)}) collective-permute-start(bf16[24,768]{1,0:T(8,128)(2,1)S(1)} %get-tuple-element.23), channel_id=1, source_target_pairs={{0,32},{16,48},{32,0},{48,16},{1,33},{17,49},{33,1},{49,17},{2,34}... | collective-permute-start | bytes 110600 | tf_op jit(solution)/shard_map/ppermute | solution.py:238
  143.7 1.3 collective-permute-done.4
  145.0 2.5 %collective-permute-done.5 = bf16[24,768]{1,0:T(8,128)(2,1)S(1)} collective-permute-done((bf16[24,768]{1,0:T(8,128)(2,1)S(1)}, bf16[24,768]{1,0:T(8,128)(2,1)S(1)}, u32[]{:S(2)}, u32[]{:S(2)}) %collective-permute-start.5) | collective-permute-done | bytes 36896 | tf_op jit(solution)/shard_map/ppermute | solution.py:238
  147.5 2.1 %collective-permute-done.6 = bf16[24,768]{1,0:T(8,128)(2,1)S(1)} collective-permute-done((bf16[24,768]{1,0:T(8,128)(2,1)S(1)}, bf16[24,768]{1,0:T(8,128)(2,1)S(1)}, u32[]{:S(2)}, u32[]{:S(2)}) %collective-permute-start.6) | collective-permute-done | bytes 36896 | tf_op jit(solution)/shard_map/ppermute | solution.py:238
  149.7 0.7 copy.20
  (29 shorter events, 2.9 us)
Async XLA Ops:
  0.8 32.5 %collective-permute-start.2 = (bf16[24,768]{1,0:T(8,128)(2,1)S(1)}, bf16[24,768]{1,0:T(8,128)(2,1)S(1)}, u32[]{:S(2)}, u32[]{:S(2)}) collective-permute-start(bf16[24,768]{1,0:T(8,128)(2,1)S(1)} %reshape.15.own), channel_id=1, source_target_pairs={{0,48},{16,0},{32,16},{48,32},{1,49},{17,1},{33,17},{49,33},{2,50}... | collective-permute-start | bytes 110600 | tf_op jit(solution)/shard_map/ppermute | solution.py:238
  2.3 31.0 %collective-permute-start.1 = (bf16[24,768]{1,0:T(8,128)(2,1)S(1)}, bf16[24,768]{1,0:T(8,128)(2,1)S(1)}, u32[]{:S(2)}, u32[]{:S(2)}) collective-permute-start(bf16[24,768]{1,0:T(8,128)(2,1)S(1)} %reshape.15.own), channel_id=1, source_target_pairs={{0,32},{16,48},{32,0},{48,16},{1,33},{17,49},{33,1},{49,17},{2,34}... | collective-permute-start | bytes 110600 | tf_op jit(solution)/shard_map/ppermute | solution.py:238
  7.7 25.6 %collective-permute-start = (bf16[24,768]{1,0:T(8,128)(2,1)S(1)}, bf16[24,768]{1,0:T(8,128)(2,1)S(1)}, u32[]{:S(2)}, u32[]{:S(2)}) collective-permute-start(bf16[24,768]{1,0:T(8,128)(2,1)S(1)} %reshape.15.own), channel_id=1, source_target_pairs={{0,16},{16,32},{32,48},{48,0},{1,17},{17,33},{33,49},{49,1},{2,18}... | collective-permute-start | bytes 110600 | tf_op jit(solution)/shard_map/ppermute | solution.py:238
  11.8 21.5 %all-to-all-start = ((s32[16,1,128]{2,1,0:T(1,128)}), s32[16,1,128]{2,1,0:T(1,128)S(1)}, u32[]{:S(2)}, u32[]{:S(2)}) async-start(s32[16,1,128]{2,1,0:T(1,128)} %broadcast_in_dim.2), calls=%async_computation | async-start | bytes 16384 | tf_op jit(solution)/shard_map/all_to_all | solution.py:251
  22.1 1.2 copy-start.5
  23.3 1.2 copy-start.6
  24.6 1.2 copy-start.7
  33.3 1.6 %copy-start = (bf16[1024,1024]{1,0:T(8,128)(2,1)S(1)}, bf16[1024,1024]{1,0:T(8,128)(2,1)}, u32[]{:S(2)}) copy-start(bf16[1024,1024]{1,0:T(8,128)(2,1)} %get-tuple-element.15.ready.a1) | copy-start | bytes 6291460
  34.9 45.6 %copy-start.3 = (bf16[1024,1024]{1,0:T(8,128)(2,1)S(1)}, bf16[1024,1024]{1,0:T(8,128)(2,1)}, u32[]{:S(2)}) copy-start(bf16[1024,1024]{1,0:T(8,128)(2,1)} %get-tuple-element.17.b1) | copy-start | bytes 6291460
  34.9 45.6 %copy-start.4 = (bf16[1024,1024]{1,0:T(8,128)(2,1)S(1)}, bf16[1024,1024]{1,0:T(8,128)(2,1)}, u32[]{:S(2)}) copy-start(bf16[1024,1024]{1,0:T(8,128)(2,1)} %get-tuple-element.18.b2) | copy-start | bytes 6291460
  36.3 44.2 %copy-start.1 = (bf16[1024,1024]{1,0:T(8,128)(2,1)S(1)}, bf16[1024,1024]{1,0:T(8,128)(2,1)}, u32[]{:S(2)}) copy-start(bf16[1024,1024]{1,0:T(8,128)(2,1)} %get-tuple-element.15.ready.a1) | copy-start | bytes 6291460
  36.3 44.2 %copy-start.2 = (bf16[1024,1024]{1,0:T(8,128)(2,1)S(1)}, bf16[1024,1024]{1,0:T(8,128)(2,1)}, u32[]{:S(2)}) copy-start(bf16[1024,1024]{1,0:T(8,128)(2,1)} %get-tuple-element.16.a1t) | copy-start | bytes 6291460
  74.5 4.5 %copy-start.8 = (bf16[32,72,512]{2,1,0:T(8,128)(2,1)}, bf16[32,72,512]{2,1,0:T(8,128)(2,1)S(1)}, u32[]{:S(2)}) copy-start(bf16[32,72,512]{2,1,0:T(8,128)(2,1)S(1)} %all_to_all.15.own) | copy-start | bytes 7077892
  74.5 4.5 %collective-permute-start.3 = (bf16[32,72,512]{2,1,0:T(8,128)(2,1)S(1)}, bf16[32,72,512]{2,1,0:T(8,128)(2,1)S(1)}, u32[]{:S(2)}, u32[]{:S(2)}) collective-permute-start(bf16[32,72,512]{2,1,0:T(8,128)(2,1)S(1)} %all_to_all.15.own), channel_id=1, source_target_pairs={{0,64},{64,0},{1,65},{65,1},{2,66},{66,2},{3,67},{67,3},{4,68},{68... | collective-permute-start | bytes 7077896 | tf_op jit(solution)/shard_map/ppermute | solution.py:238
  79.1 1.4 copy-start.9
  139.3 5.7 %collective-permute-start.4 = (bf16[24,768]{1,0:T(8,128)(2,1)S(1)}, bf16[24,768]{1,0:T(8,128)(2,1)S(1)}, u32[]{:S(2)}, u32[]{:S(2)}) collective-permute-start(bf16[24,768]{1,0:T(8,128)(2,1)S(1)} %get-tuple-element.22), channel_id=1, source_target_pairs={{0,16},{16,32},{32,48},{48,0},{1,17},{17,33},{33,49},{49,1},{2,18}... | collective-permute-start | bytes 110600 | tf_op jit(solution)/shard_map/ppermute | solution.py:238
  139.6 7.9 %collective-permute-start.5 = (bf16[24,768]{1,0:T(8,128)(2,1)S(1)}, bf16[24,768]{1,0:T(8,128)(2,1)S(1)}, u32[]{:S(2)}, u32[]{:S(2)}) collective-permute-start(bf16[24,768]{1,0:T(8,128)(2,1)S(1)} %get-tuple-element.23), channel_id=1, source_target_pairs={{0,32},{16,48},{32,0},{48,16},{1,33},{17,49},{33,1},{49,17},{2,34}... | collective-permute-start | bytes 110600 | tf_op jit(solution)/shard_map/ppermute | solution.py:238
  143.2 6.5 %collective-permute-start.6 = (bf16[24,768]{1,0:T(8,128)(2,1)S(1)}, bf16[24,768]{1,0:T(8,128)(2,1)S(1)}, u32[]{:S(2)}, u32[]{:S(2)}) collective-permute-start(bf16[24,768]{1,0:T(8,128)(2,1)S(1)} %get-tuple-element.24), channel_id=1, source_target_pairs={{0,48},{16,0},{32,16},{48,32},{1,49},{17,1},{33,17},{49,33},{2,50}... | collective-permute-start | bytes 110600 | tf_op jit(solution)/shard_map/ppermute | solution.py:238

commit v3 on v2

v3 whole, which is shorter than its diff:
```python
import jax
import jax.numpy as jnp
from jax import lax
from jax.experimental import pallas as pl
from jax.experimental.pallas import tpu as pltpu
from jax.sharding import Mesh, PartitionSpec as P

TILE = 32
W = 512
OBJ = 768
PAD = 64
ROWS = 640
BF = jnp.bfloat16
F32 = jnp.float32


SMEM = pl.BlockSpec(memory_space=pltpu.SMEM)
VMEM = pl.BlockSpec(memory_space=pltpu.VMEM)


def params(mib):
    return pltpu.CompilerParams(vmem_limit_bytes=mib * 1024 * 1024)


def first_interval(row_tile, x):
    return ((row_tile * TILE - 48 * x + 144) >= 192).astype(jnp.int32)


def product(m1, m2, left, right):
    swept = jnp.dot(m1[...], left[...], preferred_element_type=F32)
    right[:, 0:W] = swept[0:W].astype(BF)
    right[:, W:] = swept[W:].astype(BF)
    return jnp.dot(right[...], m2[...], preferred_element_type=F32)


def step(state, patch, sign, m1, m2, left, right):
    sr = state[:, 0:W].astype(F32)
    si = state[:, W:].astype(F32)
    pr = patch[0, PAD : PAD + W, :]
    pi = patch[1, PAD : PAD + W, :] * sign
    left[0:W, :] = (sr * pr - si * pi).astype(BF)
    left[W:, :] = (sr * pi + si * pr).astype(BF)
    return product(m1, m2, left, right)


def prep_kernel(tiles, rows, cols, probe, cot, m1, m2, state, left, right):
    slot = lax.axis_index("zl")
    core = lax.axis_index("core")
    shift = tiles[slot, 1] * TILE

    def turned(value):
        return pltpu.roll(pltpu.roll(value, shift, 1), shift, 0)

    @pl.when(core == 0)
    def _():
        m1[0:W, 0:W] = rows[0]
        m1[0:W, W:] = (-rows[1].astype(F32)).astype(BF)
        m1[W:, 0:W] = rows[1]
        m1[W:, W:] = rows[0]
        br = turned(cols[0].astype(F32)).T.astype(BF)
        bi = turned(cols[1].astype(F32)).T
        m2[0:W, 0:W] = br
        m2[0:W, W:] = bi.astype(BF)
        m2[W:, 0:W] = (-bi).astype(BF)
        m2[W:, W:] = br
        for part in range(2):
            state[:, part * W : (part + 1) * W] = pltpu.roll(probe[part].astype(F32), shift, 1)

    @pl.when(core == 1)
    def _():
        ar = rows[0].astype(F32).T.astype(BF)
        ai = rows[1].astype(F32).T
        m1[0:W, 0:W] = ar
        m1[0:W, W:] = ai.astype(BF)
        m1[W:, 0:W] = (-ai).astype(BF)
        m1[W:, W:] = ar
        br = turned(cols[0].astype(F32))
        bi = turned(cols[1].astype(F32))
        m2[0:W, 0:W] = br.astype(BF)
        m2[0:W, W:] = (-bi).astype(BF)
        m2[W:, 0:W] = bi.astype(BF)
        m2[W:, W:] = br.astype(BF)
        for part in range(2):
            left[part * W : (part + 1) * W, :] = pltpu.roll(cot[slot, part].astype(F32), shift, 1).astype(BF)
        state[...] = product(m1, m2, left, right)


def prep(tiles, rows, cols, probe, cot):
    square = jax.ShapeDtypeStruct((2 * W, 2 * W), BF)
    return pl.pallas_call(
        prep_kernel,
        out_shape=[square, square, jax.ShapeDtypeStruct((W, 2 * W), F32)],
        in_specs=[SMEM] + [VMEM] * 4,
        out_specs=[VMEM] * 3,
        scratch_shapes=[pltpu.VMEM((2 * W, W), BF), pltpu.VMEM((W, 2 * W), BF)],
        compiler_params=params(36),
        cost_estimate=pl.CostEstimate(flops=4 * 10**9, transcendentals=0, bytes_accessed=2 * 10**7),
        name="prep",
    )(tiles, rows, cols, probe, cot)


def pack_kernel(peers, own, one, two, three, out, held):
    zh = lax.axis_index("zh")
    x = lax.axis_index("x")
    for step, piece in enumerate((own, one, two, three)):
        place = lax.rem(zh - step + 4, 4)
        held[pl.ds(pl.multiple_of(place * 24, 8), 24), :] = piece[...].astype(F32)
    lane = lax.broadcasted_iota(jnp.int32, (72, 256), 1)
    for slot in range(2):

        def target(t, carry):
            first = first_interval(peers[t, slot, 0], x)
            rows = pl.ds(pl.multiple_of(first * 24, 8), 72)
            wrapped = lane < peers[t, slot, 1] * TILE
            low = held[rows, 0:256]
            high = held[rows, 512:768]
            out[slot * 16 + t, :, 0:256] = jnp.where(wrapped, high, low).astype(BF)
            out[slot * 16 + t, :, 256:512] = held[rows, 256:512].astype(BF)
            return carry

        lax.fori_loop(0, 16, target, 0)


def pack(peers, own, others):
    return pl.pallas_call(
        pack_kernel,
        out_shape=jax.ShapeDtypeStruct((32, 72, W), BF),
        in_specs=[SMEM] + [VMEM] * 4,
        out_specs=VMEM,
        scratch_shapes=[pltpu.VMEM((96, OBJ), F32)],
        compiler_params=params(16),
        name="pack",
    )(peers, own, *others)


def place_patch(source, base, patch, row_tile):
    def place(plane, carry):
        start = 192 * first_interval(row_tile, plane) + 48 * plane - TILE * row_tile + PAD
        got = [source[base + plane * 4 + y].astype(F32) for y in range(4)]
        for k in range(3):
            rows = pl.ds(pl.multiple_of(start + 192 * k, 16), 48)
            for part in range(2):
                cut = k * 24 + part * 12
                patch[part, rows, :] = jnp.concatenate([g[cut : cut + 12] for g in got])
        return carry

    lax.fori_loop(0, 4, place, 0)


def form_contrib(local, remote, contrib, out, base, sign, used, row_tile):
    ar = local[:, 0:W]
    ai = local[:, W:]
    br = remote[:, 0:W].astype(F32)
    bi = remote[:, W:].astype(F32)
    contrib[:, 0:PAD, :] = jnp.zeros((2, PAD, W), F32)
    contrib[:, PAD + W :, :] = jnp.zeros((2, PAD, W), F32)
    contrib[0, PAD : PAD + W, :] = jnp.where(used, ar * br + ai * bi, 0.0)
    contrib[1, PAD : PAD + W, :] = jnp.where(used, (ar * bi - ai * br) * sign, 0.0)

    def cut(plane, carry):
        start = 192 * first_interval(row_tile, plane) + 48 * plane - TILE * row_tile + PAD
        blocks = [
            contrib[part, pl.ds(pl.multiple_of(start + 192 * k, 16), 48), :] for k in range(3) for part in range(2)
        ]
        for y in range(4):
            out[base + plane * 4 + y] = jnp.concatenate([b[12 * y : 12 * y + 12] for b in blocks]).astype(BF)
        return carry

    lax.fori_loop(0, 4, cut, 0)


def role(tiles):
    core = lax.axis_index("core")
    return core, jnp.where(core == 0, 1.0, -1.0).astype(F32), tiles[lax.axis_index("zl"), 0]


STATE = jax.ShapeDtypeStruct((W, 2 * W), F32)
SENT = jax.ShapeDtypeStruct((W, 2 * W), BF)
WORK = [pltpu.VMEM((2, ROWS, W), F32), pltpu.VMEM((2 * W, W), BF), pltpu.VMEM((W, 2 * W), BF)]
HALF = jax.ShapeDtypeStruct((16, 72, W), BF)


def open_kernel(tiles, own, m1, m2, state, after, sent, patch, left, right):
    core, sign, row_tile = role(tiles)
    place_patch(own, core * 16, patch, row_tile)
    value = step(state, patch, sign, m1, m2, left, right)
    after[...] = value
    sent[...] = value.astype(BF)


def open_step(tiles, own, m1, m2, state):
    return pl.pallas_call(
        open_kernel,
        out_shape=[STATE, SENT],
        in_specs=[SMEM] + [VMEM] * 4,
        out_specs=[VMEM] * 2,
        scratch_shapes=WORK,
        compiler_params=params(32),
        cost_estimate=pl.CostEstimate(flops=4 * 10**9, transcendentals=0, bytes_accessed=10**7),
        name="open_step",
    )(tiles, own, m1, m2, state)


def close_kernel(tiles, own, other, m1, m2, state, middle, sent, patch, left, right):
    core, sign, row_tile = role(tiles)
    place_patch(other, 0, patch, row_tile)
    middle[...] = step(state, patch, sign, m1, m2, left, right)
    place_patch(own, (1 - core) * 16, patch, row_tile)
    sent[...] = step(middle, patch, sign, m1, m2, left, right).astype(BF)


def close_steps(tiles, own, other, m1, m2, state):
    return pl.pallas_call(
        close_kernel,
        out_shape=[STATE, SENT],
        in_specs=[SMEM] + [VMEM] * 5,
        out_specs=[VMEM] * 2,
        scratch_shapes=WORK,
        compiler_params=params(36),
        cost_estimate=pl.CostEstimate(flops=8 * 10**9, transcendentals=0, bytes_accessed=10**7),
        name="close_steps",
    )(tiles, own, other, m1, m2, state)


def early_kernel(tiles, count, local, remote, out, contrib):
    core, sign, row_tile = role(tiles)
    used = lax.axis_index("zl") < count[0]
    form_contrib(local, remote, contrib, out, 0, sign, used, row_tile)


def early(tiles, count, local, remote):
    return pl.pallas_call(
        early_kernel,
        out_shape=HALF,
        in_specs=[SMEM] * 2 + [VMEM] * 2,
        out_specs=VMEM,
        scratch_shapes=WORK[:1],
        compiler_params=params(24),
        cost_estimate=pl.CostEstimate(flops=4 * 10**9, transcendentals=0, bytes_accessed=10**7),
        name="early",
    )(tiles, count, local, remote)


def late_kernel(tiles, count, local, remote, half, out, contrib):
    core, sign, row_tile = role(tiles)
    used = lax.axis_index("zl") < count[0]

    def keep(i, carry):
        out[(1 - core) * 16 + i] = half[i]
        return carry

    lax.fori_loop(0, 16, keep, 0)
    form_contrib(local, remote, contrib, out, core * 16, sign, used, row_tile)


def late(tiles, count, local, remote, half):
    return pl.pallas_call(
        late_kernel,
        out_shape=jax.ShapeDtypeStruct((32, 72, W), BF),
        in_specs=[SMEM] * 2 + [VMEM] * 3,
        out_specs=VMEM,
        scratch_shapes=WORK[:1],
        compiler_params=params(24),
        name="late",
    )(tiles, count, local, remote, half)


def gather_kernel(peers, got, own, one, two, three, total):
    zh = lax.axis_index("zh")
    x = lax.axis_index("x")
    total[...] = jnp.zeros((96, OBJ), F32)
    lane = lax.broadcasted_iota(jnp.int32, (72, 256), 1)
    for slot in range(2):

        def source(t, carry):
            first = first_interval(peers[t, slot, 0], x)
            rows = pl.ds(pl.multiple_of(first * 24, 8), 72)
            wrapped = lane < peers[t, slot, 1] * TILE
            value = got[slot * 16 + t].astype(F32)
            low = value[:, 0:256]
            total[rows, 0:256] += jnp.where(wrapped, 0.0, low)
            total[rows, 512:768] += jnp.where(wrapped, low, 0.0)
            total[rows, 256:512] += value[:, 256:512]
            return carry

        lax.fori_loop(0, 16, source, 0)
    for step, out in enumerate((own, one, two, three)):
        place = lax.rem(zh + step, 4)
        out[...] = total[pl.ds(pl.multiple_of(place * 24, 8), 24), :].astype(out.dtype)


def gather(peers, got):
    return pl.pallas_call(
        gather_kernel,
        out_shape=[jax.ShapeDtypeStruct((24, OBJ), F32)] + [jax.ShapeDtypeStruct((24, OBJ), BF)] * 3,
        in_specs=[SMEM, VMEM],
        out_specs=[VMEM] * 4,
        scratch_shapes=[pltpu.VMEM((96, OBJ), F32)],
        compiler_params=params(16),
        name="gather",
    )(peers, got)


def turn(value, axis, step, count):
    return lax.ppermute(value, axis, [(i, (i + step) % count) for i in range(count)])


def on_device(probe_wave, prop_rows, prop_cols, transmission, exit_cotangent, window_tiles, slot_count):
    core = lax.axis_index("core")
    piece = transmission.reshape(24, OBJ)
    others = [turn(piece, "zh", hops, 4) for hops in (2, 1, 3)]
    others = [others[1], others[0], others[2]]
    peers = lax.all_to_all(jnp.broadcast_to(window_tiles[None], (16, 2, 2)), ("x", "y"), 0, 0, tiled=True)
    sent = pack(peers, piece, others)
    sent, rows = lax.optimization_barrier((sent, prop_rows))
    own = lax.all_to_all(sent, ("zl", "x", "y"), 0, 0, tiled=True)
    mats = prep(window_tiles, rows, prop_cols, probe_wave, exit_cotangent)
    own, m1, m2, state = lax.optimization_barrier((own, *mats))
    given = lax.dynamic_index_in_dim(own.reshape(2, 16, 72, W), 1 - core, 0, keepdims=False)
    other = turn(given, "core", 1, 2)
    after, first = open_step(window_tiles, own, m1, m2, state)
    first_away = turn(first, "core", 1, 2)
    middle, last = close_steps(window_tiles, own, other, m1, m2, after)
    last_away = turn(last, "core", 1, 2)
    half = early(window_tiles, slot_count, middle, first_away)
    contrib = late(window_tiles, slot_count, state, last_away, half)
    got = lax.all_to_all(contrib, ("zl", "x", "y"), 0, 0, tiled=True)
    here, *away = gather(peers, got)
    for hops in (2, 1, 3):
        here = here + turn(away[hops - 1], "zh", hops, 4).astype(F32)
    return here.reshape(1, 2, 12, OBJ)


def solution(mesh):
    whole = Mesh(mesh.devices.reshape(2, 2, 4, 4, 4), ("zl", "core", "zh", "x", "y"))
    depth = ("zl", "core")
    scan = ("zh", "x", "y")
    placed = (
        P(),
        P(),
        P(),
        P(depth, None, scan, None),
        P(scan, None, None, None),
        P(scan, None),
        P(scan),
    )
    return jax.shard_map(
        on_device,
        mesh=whole,
        in_specs=placed,
        out_specs=P(depth, None, scan, None),
        check_vma=False,
    )
```

time: 151 us -> 132 us (0.87)
  blocking collectives: 73.8 us -> 52.1 us
  waiting for transfers between devices: 10.5 us -> 24.1 us
  Pallas kernels: 32.1 us -> 19.7 us
  local copies, waits for them, and re-layouts: 12.2 us -> 15 us
    all_to_all x1, blocking collectives: 38.2 us -> 14.4 us  [on_device(): lax.all_to_all(jnp.broadcast_to(window_tiles[None], (16, 2, 2)), ('x', 'y...]
    all_to_all x1, waiting for transfers between devices: 0.01 us -> 17.3 us  [on_device(): own = lax.all_to_all(sent, ('zl', 'x', 'y'), 0, 0, tiled=True)]
    pallas_call x2 -> x5, Pallas kernels: 29 us -> 15 us  [the longest x1 6.01 us: close_steps(): pl.pallas_call(close_kernel, out_shape=[STATE, SENT], in_specs=[SMEM] + [...]
    unnamed x21 -> x27, local copies, waits for them, and re-layouts: 7.48 us -> 13.5 us
    ppermute x7 -> x9, waiting for transfers between devices: 10.5 us -> 6.84 us  [turn(): lax.ppermute(value, axis, [(i, (i + step) % count) for i in range(count)])]
    all_to_all x1, starting transfers between devices: 7.03 us -> 4.19 us  [on_device(): own = lax.all_to_all(sent, ('zl', 'x', 'y'), 0, 0, tiled=True)]
    all_to_all x1, blocking collectives: 35.5 us -> 37.7 us  [on_device(): got = lax.all_to_all(contrib, ('zl', 'x', 'y'), 0, 0, tiled=True)]
    ppermute x7 -> x9, starting transfers between devices: 14.1 us -> 15.6 us  [turn(): lax.ppermute(value, axis, [(i, (i + step) % count) for i in range(count)])]
  transfers between devices with their start and end apart: 8 -> 10, of which waited for: 4 -> 4; matrix products, arithmetic and copies ran while one was open for 3% -> 1% of each run, Pallas kernels for 5% -> 10%
where the time goes in v3:
time: 132 us
  blocking collectives  52.1 us (39%)
  waiting for transfers between devices  24.1 us (18%)
  starting transfers between devices  19.8 us (15%)
  Pallas kernels  19.7 us (15%)
  local copies, waits for them, and re-layouts  15 us (11%)
    all_to_all x1, blocking collectives, on_device(): got = lax.all_to_all(contrib, ('zl', 'x', 'y'), 0, 0, tiled=True)  37.7 us
    all_to_all x1, waiting for transfers between devices, on_device(): own = lax.all_to_all(sent, ('zl', 'x', 'y'), 0, 0, tiled=True)  17.3 us
    ppermute x9, starting transfers between devices, turn(): lax.ppermute(value, axis, [(i, (i + step) % count) for i in range(count)])  15.6 us
    all_to_all x1, blocking collectives, on_device(): lax.all_to_all(jnp.broadcast_to(window_tiles[None], (16, 2, 2)), ('x', 'y...  14.4 us
    unnamed x27, local copies, waits for them, and re-layouts  13.5 us
    ppermute x9, waiting for transfers between devices, turn(): lax.ppermute(value, axis, [(i, (i + step) % count) for i in range(count)])  6.84 us
    pallas_call x1, Pallas kernels, close_steps(): pl.pallas_call(close_kernel, out_shape=[STATE, SENT], in_specs=[SMEM] + [...  6.01 us
    all_to_all x1, starting transfers between devices, on_device(): own = lax.all_to_all(sent, ('zl', 'x', 'y'), 0, 0, tiled=True)  4.19 us
  transfers between devices with their start and end apart: 10, of which 4 were waited for; matrix products, arithmetic and copies ran while one was open for 1% of the time, Pallas kernels for 10%

profile of v3, /device:TPU:64, one launch (start us, length us, event | category | flops | bytes accessed | tf_op | source)
XLA Modules:
  0.0 131.7 jit_solution(9913611760258539234)
XLA Ops:
  0.8 4.6 %collective-permute-start = (bf16[24,768]{1,0:T(8,128)(2,1)S(1)}, bf16[24,768]{1,0:T(8,128)(2,1)S(1)}, u32[]{:S(2)}, u32[]{:S(2)}) collective-permute-start(bf16[24,768]{1,0:T(8,128)(2,1)S(1)} %reshape.10.own), channel_id=1, source_target_pairs={{0,16},{16,32},{32,48},{48,0},{1,17},{17,33},{33,49},{49,1},{2,18}... | collective-permute-start | bytes 110600 | tf_op jit(solution)/shard_map/ppermute | solution.py:305
  6.4 2.8 %collective-permute-start.2 = (bf16[24,768]{1,0:T(8,128)(2,1)S(1)}, bf16[24,768]{1,0:T(8,128)(2,1)S(1)}, u32[]{:S(2)}, u32[]{:S(2)}) collective-permute-start(bf16[24,768]{1,0:T(8,128)(2,1)S(1)} %reshape.10.own), channel_id=1, source_target_pairs={{0,48},{16,0},{32,16},{48,32},{1,49},{17,1},{33,17},{49,33},{2,50}... | collective-permute-start | bytes 110600 | tf_op jit(solution)/shard_map/ppermute | solution.py:305
  9.9 14.4 %all_to_all.15.peers = s32[16,2,2]{2,1,0:T(2,128)S(1)} all-to-all(s32[16,2,2]{2,1,0:T(2,128)S(1)} %broadcast_in_dim.2), channel_id=1, replica_groups=mesh['zl'=2,'core'=2,'zh'=4,'x'=4,'y'=4] {'x','y'}, dimensions={0} | all-to-all | bytes 512 | tf_op jit(solution)/shard_map/all_to_all | solution.py:313
  24.3 3.0 %pack.1 = bf16[32,72,512]{2,1,0:T(8,128)(2,1)} custom-call(s32[16,2,2]{2,1,0:T(2,128)S(1)} %all_to_all.15.peers, bf16[24,768]{1,0:T(8,128)(2,1)S(1)} %reshape.10.own, bf16[24,768]{1,0:T(8,128)(2,1)S(1)} %collective-permute-done.one, bf16[24,768]{1,0:T(8,128)(2,1)S(1)} %collective-permute-done.1.two, bf16[24,768]{1,0:T(8,128)(2,1)S(1)} %collective-permute-done.2.three), custom_call_target="tpu_custom_call" | custom-call | tf_op jit(solution)/shard_map/pack/pallas_call | solution.py:125
  27.3 4.2 %all-to-all-start.1 = ((bf16[32,72,512]{2,1,0:T(8,128)(2,1)}), bf16[32,72,512]{2,1,0:T(8,128)(2,1)S(1)}, u32[]{:S(2)}, u32[]{:S(2)}) async-start(bf16[32,72,512]{2,1,0:T(8,128)(2,1)} %pack.1), calls=%async_computation.1 | async-start | bytes 4718592 | tf_op jit(solution)/shard_map/all_to_all | solution.py:316
  31.5 1.6 %copy-done.3 = bf16[2,2,512,512]{3,2,1,0:T(8,128)(2,1)S(1)} copy-done((bf16[2,2,512,512]{3,2,1,0:T(8,128)(2,1)S(1)}, bf16[2,2,512,512]{3,2,1,0:T(8,128)(2,1)}, u32[]{:S(2)}) %copy-start.3) | copy-done | bytes 2097176
  35.5 3.1 %prep.1 = (bf16[1024,1024]{1,0:T(8,128)(2,1)S(1)}, bf16[1024,1024]{1,0:T(8,128)(2,1)S(1)}, f32[512,1024]{1,0:T(8,128)S(1)}) custom-call(s32[2,2]{1,0:T(2,128)S(1)} %copy-done.2, bf16[2,512,512]{2,1,0:T(8,128)(2,1)S(1)} %copy-done.4, bf16[2,512,512]{2,1,0:T(8,128)(2,1)S(1)} %copy-done.5, bf16[2,512,512]{2,1,0:T(8,128)(2,1)S(1)} %copy-done.6, ...), custom_call_target="tpu_custom_call" | custom-call | flops 4000000000 | bytes 20000000 | tf_op jit(solution)/shard_map/prep/pallas_call | solution.py:90
  38.7 1.3 copy-done
  40.0 1.4 %copy-done.7 = bf16[1024,1024]{1,0:T(8,128)(2,1)} copy-done((bf16[1024,1024]{1,0:T(8,128)(2,1)}, bf16[1024,1024]{1,0:T(8,128)(2,1)S(1)}, u32[]{:S(2)}) %copy-start.7) | copy-done | bytes 2097176
  41.4 1.4 %copy-done.10 = bf16[1024,1024]{1,0:T(8,128)(2,1)} copy-done((bf16[1024,1024]{1,0:T(8,128)(2,1)}, bf16[1024,1024]{1,0:T(8,128)(2,1)S(1)}, u32[]{:S(2)}) %copy-start.10) | copy-done | bytes 2097176
  42.8 17.3 %all-to-all-done.1.own = bf16[32,72,512]{2,1,0:T(8,128)(2,1)S(1)} async-done(((bf16[32,72,512]{2,1,0:T(8,128)(2,1)}), bf16[32,72,512]{2,1,0:T(8,128)(2,1)S(1)}, u32[]{:S(2)}, u32[]{:S(2)}) %all-to-all-start.1) | async-done | bytes 2359328 | tf_op jit(solution)/shard_map/all_to_all | solution.py:316
  60.2 1.4 %copy-done.1 = f32[512,1024]{1,0:T(8,128)S(1)} copy-done((f32[512,1024]{1,0:T(8,128)S(1)}, f32[512,1024]{1,0:T(8,128)}, u32[]{:S(2)}) %copy-start.1) | copy-done | bytes 2097176
  61.7 1.6 %copy-done.8 = bf16[1024,1024]{1,0:T(8,128)(2,1)S(1)} copy-done((bf16[1024,1024]{1,0:T(8,128)(2,1)S(1)}, bf16[1024,1024]{1,0:T(8,128)(2,1)}, u32[]{:S(2)}) %copy-start.8) | copy-done | bytes 2097176
  63.3 1.6 %copy-done.11 = bf16[1024,1024]{1,0:T(8,128)(2,1)S(1)} copy-done((bf16[1024,1024]{1,0:T(8,128)(2,1)S(1)}, bf16[1024,1024]{1,0:T(8,128)(2,1)}, u32[]{:S(2)}) %copy-start.11) | copy-done | bytes 2097176
  64.8 3.3 %open_step.1 = (f32[512,1024]{1,0:T(8,128)S(1)}, bf16[512,1024]{1,0:T(8,128)(2,1)S(1)}) custom-call(s32[2,2]{1,0:T(2,128)S(1)} %copy-done.2, bf16[32,72,512]{2,1,0:T(8,128)(2,1)S(1)} %all-to-all-done.1.own, bf16[1024,1024]{1,0:T(8,128)(2,1)S(1)} %copy-done.8, bf16[1024,1024]{1,0:T(8,128)(2,1)S(1)} %copy-done.11, f32[512,1024]{1,0:T(8,128)S(1)} %copy-done.1), custom_call_target="tpu_custom_call" | custom-call | flops 4000000000 | bytes 10000000 | tf_op jit(solution)/shard_map/open_step/pallas_call | solution.py:192
  68.4 6.0 %close_steps.1 = (f32[512,1024]{1,0:T(8,128)S(1)}, bf16[512,1024]{1,0:T(8,128)(2,1)S(1)}) custom-call(s32[2,2]{1,0:T(2,128)S(1)} %copy-done.2, bf16[32,72,512]{2,1,0:T(8,128)(2,1)S(1)} %all-to-all-done.1.own, bf16[16,72,512]{2,1,0:T(8,128)(2,1)S(1)} %collective-permute-done.3.other, bf16[1024,1024]{1,0:T(8,128)(2,1)S(1)} %copy-done.9, ...), custom_call_target="tpu_custom_call" | custom-call | flops 8000000000 | bytes 10000000 | tf_op jit(solution)/shard_map/close_steps/pallas_call | solution.py:213
  75.7 1.2 early.1.half
  77.3 1.4 %late.1 = bf16[32,72,512]{2,1,0:T(8,128)(2,1)S(1)} custom-call(s32[2,2]{1,0:T(2,128)S(1)} %copy-done.2, s32[1]{0:T(128)S(6)} %copy.12.count, f32[512,1024]{1,0:T(8,128)S(1)} %copy-done.1, bf16[512,1024]{1,0:T(8,128)(2,1)S(1)} %collective-permute-done.4.remote, bf16[16,72,512]{2,1,0:T(8,128)(2,1)S(1)} %early.1.half), custom_call_target="tpu_custom_call" | custom-call | tf_op jit(solution)/shard_map/late/pallas_call | solution.py:257
  78.7 37.7 %all_to_all.16.got = bf16[32,72,512]{2,1,0:T(8,128)(2,1)S(1)} all-to-all(bf16[32,72,512]{2,1,0:T(8,128)(2,1)S(1)} %late.1), channel_id=1, replica_groups=mesh['zl'=2,'core'=2,'zh'=4,'x'=4,'y'=4] {'zl','x','y'}, dimensions={0} | all-to-all | bytes 4718592 | tf_op jit(solution)/shard_map/all_to_all | solution.py:327
  116.4 1.8 %gather.1 = (f32[24,768]{1,0:T(8,128)S(1)}, bf16[24,768]{1,0:T(8,128)(2,1)S(1)}, bf16[24,768]{1,0:T(8,128)(2,1)S(1)}, bf16[24,768]{1,0:T(8,128)(2,1)S(1)}) custom-call(s32[16,2,2]{2,1,0:T(2,128)S(1)} %all_to_all.15.peers, bf16[32,72,512]{2,1,0:T(8,128)(2,1)S(1)} %all_to_all.16.got), custom_call_target="tpu_custom_call" | custom-call | tf_op jit(solution)/shard_map/gather/pallas_call | solution.py:293
  118.1 2.2 %collective-permute-start.6 = (bf16[24,768]{1,0:T(8,128)(2,1)S(1)}, bf16[24,768]{1,0:T(8,128)(2,1)S(1)}, u32[]{:S(2)}, u32[]{:S(2)}) collective-permute-start(bf16[24,768]{1,0:T(8,128)(2,1)S(1)} %get-tuple-element.36), channel_id=1, source_target_pairs={{0,32},{16,48},{32,0},{48,16},{1,33},{17,49},{33,1},{49,17},{2,34}... | collective-permute-start | bytes 110600 | tf_op jit(solution)/shard_map/ppermute | solution.py:305
  120.3 4.1 %collective-permute-start.7 = (bf16[24,768]{1,0:T(8,128)(2,1)S(1)}, bf16[24,768]{1,0:T(8,128)(2,1)S(1)}, u32[]{:S(2)}, u32[]{:S(2)}) collective-permute-start(bf16[24,768]{1,0:T(8,128)(2,1)S(1)} %get-tuple-element.37), channel_id=1, source_target_pairs={{0,16},{16,32},{32,48},{48,0},{1,17},{17,33},{33,49},{49,1},{2,18}... | collective-permute-start | bytes 110600 | tf_op jit(solution)/shard_map/ppermute | solution.py:305
  124.5 2.0 %collective-permute-done.6 = bf16[24,768]{1,0:T(8,128)(2,1)S(1)} collective-permute-done((bf16[24,768]{1,0:T(8,128)(2,1)S(1)}, bf16[24,768]{1,0:T(8,128)(2,1)S(1)}, u32[]{:S(2)}, u32[]{:S(2)}) %collective-permute-start.6) | collective-permute-done | bytes 36896 | tf_op jit(solution)/shard_map/ppermute | solution.py:305
  126.4 4.5 %collective-permute-done.8 = bf16[24,768]{1,0:T(8,128)(2,1)S(1)} collective-permute-done((bf16[24,768]{1,0:T(8,128)(2,1)S(1)}, bf16[24,768]{1,0:T(8,128)(2,1)S(1)}, u32[]{:S(2)}, u32[]{:S(2)}) %collective-permute-start.8) | collective-permute-done | bytes 36896 | tf_op jit(solution)/shard_map/ppermute | solution.py:305
  (38 shorter events, 7.1 us)
Async XLA Ops:
  0.8 23.5 %collective-permute-start = (bf16[24,768]{1,0:T(8,128)(2,1)S(1)}, bf16[24,768]{1,0:T(8,128)(2,1)S(1)}, u32[]{:S(2)}, u32[]{:S(2)}) collective-permute-start(bf16[24,768]{1,0:T(8,128)(2,1)S(1)} %reshape.10.own), channel_id=1, source_target_pairs={{0,16},{16,32},{32,48},{48,0},{1,17},{17,33},{33,49},{49,1},{2,18}... | collective-permute-start | bytes 110600 | tf_op jit(solution)/shard_map/ppermute | solution.py:305
  5.4 18.9 %collective-permute-start.1 = (bf16[24,768]{1,0:T(8,128)(2,1)S(1)}, bf16[24,768]{1,0:T(8,128)(2,1)S(1)}, u32[]{:S(2)}, u32[]{:S(2)}) collective-permute-start(bf16[24,768]{1,0:T(8,128)(2,1)S(1)} %reshape.10.own), channel_id=1, source_target_pairs={{0,32},{16,48},{32,0},{48,16},{1,33},{17,49},{33,1},{49,17},{2,34}... | collective-permute-start | bytes 110600 | tf_op jit(solution)/shard_map/ppermute | solution.py:305
  6.4 17.9 %collective-permute-start.2 = (bf16[24,768]{1,0:T(8,128)(2,1)S(1)}, bf16[24,768]{1,0:T(8,128)(2,1)S(1)}, u32[]{:S(2)}, u32[]{:S(2)}) collective-permute-start(bf16[24,768]{1,0:T(8,128)(2,1)S(1)} %reshape.10.own), channel_id=1, source_target_pairs={{0,48},{16,0},{32,16},{48,32},{1,49},{17,1},{33,17},{49,33},{2,50}... | collective-permute-start | bytes 110600 | tf_op jit(solution)/shard_map/ppermute | solution.py:305
  27.3 4.2 %copy-start.2 = (s32[2,2]{1,0:T(2,128)S(1)}, s32[2,2]{1,0:T(2,128)}, u32[]{:S(2)}) copy-start(s32[2,2]{1,0:T(2,128)} %tiles.9) | copy-start | bytes 52
  27.3 4.2 %copy-start.4 = (bf16[2,512,512]{2,1,0:T(8,128)(2,1)S(1)}, bf16[2,512,512]{2,1,0:T(8,128)(2,1)}, u32[]{:S(2)}) copy-start(bf16[2,512,512]{2,1,0:T(8,128)(2,1)} %rows) | copy-start | bytes 3145732
  27.3 32.8 %all-to-all-start.1 = ((bf16[32,72,512]{2,1,0:T(8,128)(2,1)}), bf16[32,72,512]{2,1,0:T(8,128)(2,1)S(1)}, u32[]{:S(2)}, u32[]{:S(2)}) async-start(bf16[32,72,512]{2,1,0:T(8,128)(2,1)} %pack.1), calls=%async_computation.1 | async-start | bytes 4718592 | tf_op jit(solution)/shard_map/all_to_all | solution.py:316
  31.5 1.6 %copy-start.3 = (bf16[2,2,512,512]{3,2,1,0:T(8,128)(2,1)S(1)}, bf16[2,2,512,512]{3,2,1,0:T(8,128)(2,1)}, u32[]{:S(2)}) copy-start(bf16[2,2,512,512]{3,2,1,0:T(8,128)(2,1)} %cot.1) | copy-start | bytes 6291460
  33.1 1.2 copy-start.5
  34.3 1.2 copy-start.6
  38.6 1.3 %copy-start = (f32[512,1024]{1,0:T(8,128)}, f32[512,1024]{1,0:T(8,128)S(1)}, u32[]{:S(2)}) copy-start(f32[512,1024]{1,0:T(8,128)S(1)} %get-tuple-element.27.state.local) | copy-start | bytes 6291460
  40.0 1.4 %copy-start.7 = (bf16[1024,1024]{1,0:T(8,128)(2,1)}, bf16[1024,1024]{1,0:T(8,128)(2,1)S(1)}, u32[]{:S(2)}) copy-start(bf16[1024,1024]{1,0:T(8,128)(2,1)S(1)} %get-tuple-element.29.m1) | copy-start | bytes 6291460
  41.4 1.4 %copy-start.10 = (bf16[1024,1024]{1,0:T(8,128)(2,1)}, bf16[1024,1024]{1,0:T(8,128)(2,1)S(1)}, u32[]{:S(2)}) copy-start(bf16[1024,1024]{1,0:T(8,128)(2,1)S(1)} %get-tuple-element.30.m2) | copy-start | bytes 6291460
  60.1 1.6 %copy-start.1 = (f32[512,1024]{1,0:T(8,128)S(1)}, f32[512,1024]{1,0:T(8,128)}, u32[]{:S(2)}) copy-start(f32[512,1024]{1,0:T(8,128)} %copy-done) | copy-start | bytes 6291460
  60.1 8.3 %collective-permute-start.3 = (bf16[16,72,512]{2,1,0:T(8,128)(2,1)S(1)}, bf16[16,72,512]{2,1,0:T(8,128)(2,1)S(1)}, u32[]{:S(2)}, u32[]{:S(2)}) collective-permute-start(bf16[16,72,512]{2,1,0:T(8,128)(2,1)S(1)} %dynamic-slice_bitcast_fusion), channel_id=1, source_target_pairs={{0,64},{64,0},{1,65},{65,1},{2,66},{66,2},{3,67},{67,3},{4,68},{68... | collective-permute-start | bytes 3538952 | tf_op jit(solution)/shard_map/ppermute | solution.py:305
  61.7 1.6 %copy-start.8 = (bf16[1024,1024]{1,0:T(8,128)(2,1)S(1)}, bf16[1024,1024]{1,0:T(8,128)(2,1)}, u32[]{:S(2)}) copy-start(bf16[1024,1024]{1,0:T(8,128)(2,1)} %copy-done.7) | copy-start | bytes 6291460
  63.2 1.6 %copy-start.11 = (bf16[1024,1024]{1,0:T(8,128)(2,1)S(1)}, bf16[1024,1024]{1,0:T(8,128)(2,1)}, u32[]{:S(2)}) copy-start(bf16[1024,1024]{1,0:T(8,128)(2,1)} %copy-done.10) | copy-start | bytes 6291460
  64.8 3.6 %copy-start.9 = (bf16[1024,1024]{1,0:T(8,128)(2,1)S(1)}, bf16[1024,1024]{1,0:T(8,128)(2,1)}, u32[]{:S(2)}) copy-start(bf16[1024,1024]{1,0:T(8,128)(2,1)} %copy-done.7) | copy-start | bytes 6291460
  64.8 3.6 %copy-start.12 = (bf16[1024,1024]{1,0:T(8,128)(2,1)S(1)}, bf16[1024,1024]{1,0:T(8,128)(2,1)}, u32[]{:S(2)}) copy-start(bf16[1024,1024]{1,0:T(8,128)(2,1)} %copy-done.10) | copy-start | bytes 6291460
  68.1 7.5 %collective-permute-start.5 = (bf16[512,1024]{1,0:T(8,128)(2,1)S(1)}, bf16[512,1024]{1,0:T(8,128)(2,1)S(1)}, u32[]{:S(2)}, u32[]{:S(2)}) collective-permute-start(bf16[512,1024]{1,0:T(8,128)(2,1)S(1)} %get-tuple-element.34), channel_id=1, source_target_pairs={{0,64},{64,0},{1,65},{65,1},{2,66},{66,2},{3,67},{67,3},{4,68},{68... | collective-permute-start | bytes 3145736 | tf_op jit(solution)/shard_map/ppermute | solution.py:305
  74.4 2.9 %collective-permute-start.4 = (bf16[512,1024]{1,0:T(8,128)(2,1)S(1)}, bf16[512,1024]{1,0:T(8,128)(2,1)S(1)}, u32[]{:S(2)}, u32[]{:S(2)}) collective-permute-start(bf16[512,1024]{1,0:T(8,128)(2,1)S(1)} %get-tuple-element.32), channel_id=1, source_target_pairs={{0,64},{64,0},{1,65},{65,1},{2,66},{66,2},{3,67},{67,3},{4,68},{68... | collective-permute-start | bytes 3145736 | tf_op jit(solution)/shard_map/ppermute | solution.py:305
  118.1 8.3 %collective-permute-start.6 = (bf16[24,768]{1,0:T(8,128)(2,1)S(1)}, bf16[24,768]{1,0:T(8,128)(2,1)S(1)}, u32[]{:S(2)}, u32[]{:S(2)}) collective-permute-start(bf16[24,768]{1,0:T(8,128)(2,1)S(1)} %get-tuple-element.36), channel_id=1, source_target_pairs={{0,32},{16,48},{32,0},{48,16},{1,33},{17,49},{33,1},{49,17},{2,34}... | collective-permute-start | bytes 110600 | tf_op jit(solution)/shard_map/ppermute | solution.py:305
  120.3 6.1 %collective-permute-start.7 = (bf16[24,768]{1,0:T(8,128)(2,1)S(1)}, bf16[24,768]{1,0:T(8,128)(2,1)S(1)}, u32[]{:S(2)}, u32[]{:S(2)}) collective-permute-start(bf16[24,768]{1,0:T(8,128)(2,1)S(1)} %get-tuple-element.37), channel_id=1, source_target_pairs={{0,16},{16,32},{32,48},{48,0},{1,17},{17,33},{33,49},{49,1},{2,18}... | collective-permute-start | bytes 110600 | tf_op jit(solution)/shard_map/ppermute | solution.py:305
  124.5 6.5 %collective-permute-start.8 = (bf16[24,768]{1,0:T(8,128)(2,1)S(1)}, bf16[24,768]{1,0:T(8,128)(2,1)S(1)}, u32[]{:S(2)}, u32[]{:S(2)}) collective-permute-start(bf16[24,768]{1,0:T(8,128)(2,1)S(1)} %get-tuple-element.38), channel_id=1, source_target_pairs={{0,48},{16,0},{32,16},{48,32},{1,49},{17,1},{33,17},{49,33},{2,50}... | collective-permute-start | bytes 110600 | tf_op jit(solution)/shard_map/ppermute | solution.py:305

commit v4 on v3

--- a/solution.py
+++ b/solution.py
@@ -16,6 +16,7 @@
 
 SMEM = pl.BlockSpec(memory_space=pltpu.SMEM)
 VMEM = pl.BlockSpec(memory_space=pltpu.VMEM)
+HBM = pl.BlockSpec(memory_space=pltpu.HBM)
 
 
 def params(mib):
@@ -26,21 +27,19 @@
     return ((row_tile * TILE - 48 * x + 144) >= 192).astype(jnp.int32)
 
 
-def product(m1, m2, left, right):
+def sweep(m1, left, right):
     swept = jnp.dot(m1[...], left[...], preferred_element_type=F32)
     right[:, 0:W] = swept[0:W].astype(BF)
     right[:, W:] = swept[W:].astype(BF)
-    return jnp.dot(right[...], m2[...], preferred_element_type=F32)
-
-
-def step(state, patch, sign, m1, m2, left, right):
-    sr = state[:, 0:W].astype(F32)
-    si = state[:, W:].astype(F32)
+
+
+def form_left(state, patch, sign, left):
+    sr = state[:, 0:W]
+    si = state[:, W:]
     pr = patch[0, PAD : PAD + W, :]
     pi = patch[1, PAD : PAD + W, :] * sign
     left[0:W, :] = (sr * pr - si * pi).astype(BF)
     left[W:, :] = (sr * pi + si * pr).astype(BF)
-    return product(m1, m2, left, right)
 
 
 def prep_kernel(tiles, rows, cols, probe, cot, m1, m2, state, left, right):
@@ -82,7 +81,8 @@
         m2[W:, W:] = br.astype(BF)
         for part in range(2):
             left[part * W : (part + 1) * W, :] = pltpu.roll(cot[slot, part].astype(F32), shift, 1).astype(BF)
-        state[...] = product(m1, m2, left, right)
+        sweep(m1, left, right)
+        state[...] = jnp.dot(right[...], m2[...], preferred_element_type=F32)
 
 
 def prep(tiles, rows, cols, probe, cot):
@@ -93,7 +93,7 @@
         in_specs=[SMEM] + [VMEM] * 4,
         out_specs=[VMEM] * 3,
         scratch_shapes=[pltpu.VMEM((2 * W, W), BF), pltpu.VMEM((W, 2 * W), BF)],
-        compiler_params=params(36),
+        compiler_params=params(24),
         cost_estimate=pl.CostEstimate(flops=4 * 10**9, transcendentals=0, bytes_accessed=2 * 10**7),
         name="prep",
     )(tiles, rows, cols, probe, cot)
@@ -106,19 +106,22 @@
         place = lax.rem(zh - step + 4, 4)
         held[pl.ds(pl.multiple_of(place * 24, 8), 24), :] = piece[...].astype(F32)
     lane = lax.broadcasted_iota(jnp.int32, (72, 256), 1)
-    for slot in range(2):
-
-        def target(t, carry):
-            first = first_interval(peers[t, slot, 0], x)
+    y = lax.axis_index("y")
+
+    def target(t, carry):
+        ahead, below = t // 4, lax.rem(t, 4)
+        place = lax.rem(x - ahead + 4, 4) * 4 + lax.rem(y - below + 4, 4)
+        for slot in range(2):
+            first = first_interval(peers[ahead, below, slot, 0], x)
             rows = pl.ds(pl.multiple_of(first * 24, 8), 72)
-            wrapped = lane < peers[t, slot, 1] * TILE
+            wrapped = lane < peers[ahead, below, slot, 1] * TILE
             low = held[rows, 0:256]
             high = held[rows, 512:768]
-            out[slot * 16 + t, :, 0:256] = jnp.where(wrapped, high, low).astype(BF)
-            out[slot * 16 + t, :, 256:512] = held[rows, 256:512].astype(BF)
-            return carry
-
-        lax.fori_loop(0, 16, target, 0)
+            out[slot * 16 + place, :, 0:256] = jnp.where(wrapped, high, low).astype(BF)
+            out[slot * 16 + place, :, 256:512] = held[rows, 256:512].astype(BF)
+        return carry
+
+    lax.fori_loop(0, 16, target, 0)
 
 
 def pack(peers, own, others):
@@ -177,13 +180,22 @@
 STATE = jax.ShapeDtypeStruct((W, 2 * W), F32)
 SENT = jax.ShapeDtypeStruct((W, 2 * W), BF)
 WORK = [pltpu.VMEM((2, ROWS, W), F32), pltpu.VMEM((2 * W, W), BF), pltpu.VMEM((W, 2 * W), BF)]
+HELD = [pltpu.VMEM((2 * W, 2 * W), BF)] * 2
 HALF = jax.ShapeDtypeStruct((16, 72, W), BF)
 
 
-def open_kernel(tiles, own, m1, m2, state, after, sent, patch, left, right):
+def open_kernel(tiles, own, m1, m2, state, after, sent, patch, left, right, v1, v2, held, sems):
     core, sign, row_tile = role(tiles)
+    copies = [pltpu.make_async_copy(a, b, sems.at[i]) for i, (a, b) in enumerate([(state, held), (m1, v1), (m2, v2)])]
+    for copy in copies:
+        copy.start()
     place_patch(own, core * 16, patch, row_tile)
-    value = step(state, patch, sign, m1, m2, left, right)
+    copies[0].wait()
+    form_left(held, patch, sign, left)
+    copies[1].wait()
+    sweep(v1, left, right)
+    copies[2].wait()
+    value = jnp.dot(right[...], v2[...], preferred_element_type=F32)
     after[...] = value
     sent[...] = value.astype(BF)
 
@@ -192,31 +204,40 @@
     return pl.pallas_call(
         open_kernel,
         out_shape=[STATE, SENT],
-        in_specs=[SMEM] + [VMEM] * 4,
+        in_specs=[SMEM, VMEM] + [HBM] * 3,
         out_specs=[VMEM] * 2,
-        scratch_shapes=WORK,
-        compiler_params=params(32),
+        scratch_shapes=WORK + HELD + [pltpu.VMEM((W, 2 * W), F32), pltpu.SemaphoreType.DMA((3,))],
+        compiler_params=params(24),
         cost_estimate=pl.CostEstimate(flops=4 * 10**9, transcendentals=0, bytes_accessed=10**7),
         name="open_step",
     )(tiles, own, m1, m2, state)
 
 
-def close_kernel(tiles, own, other, m1, m2, state, middle, sent, patch, left, right):
+def close_kernel(tiles, own, other, m1, m2, state, middle, sent, patch, left, right, v1, v2, sems):
     core, sign, row_tile = role(tiles)
+    copies = [pltpu.make_async_copy(a, b, sems.at[i]) for i, (a, b) in enumerate([(m1, v1), (m2, v2)])]
+    for copy in copies:
+        copy.start()
     place_patch(other, 0, patch, row_tile)
-    middle[...] = step(state, patch, sign, m1, m2, left, right)
+    form_left(state, patch, sign, left)
+    copies[0].wait()
+    sweep(v1, left, right)
+    copies[1].wait()
+    middle[...] = jnp.dot(right[...], v2[...], preferred_element_type=F32)
     place_patch(own, (1 - core) * 16, patch, row_tile)
-    sent[...] = step(middle, patch, sign, m1, m2, left, right).astype(BF)
+    form_left(middle, patch, sign, left)
+    sweep(v1, left, right)
+    sent[...] = jnp.dot(right[...], v2[...], preferred_element_type=F32).astype(BF)
 
 
 def close_steps(tiles, own, other, m1, m2, state):
     return pl.pallas_call(
         close_kernel,
         out_shape=[STATE, SENT],
-        in_specs=[SMEM] + [VMEM] * 5,
+        in_specs=[SMEM, VMEM, VMEM, HBM, HBM, VMEM],
         out_specs=[VMEM] * 2,
-        scratch_shapes=WORK,
-        compiler_params=params(36),
+        scratch_shapes=WORK + HELD + [pltpu.SemaphoreType.DMA((2,))],
+        compiler_params=params(24),
         cost_estimate=pl.CostEstimate(flops=8 * 10**9, transcendentals=0, bytes_accessed=10**7),
         name="close_steps",
     )(tiles, own, other, m1, m2, state)
@@ -270,20 +291,23 @@
     x = lax.axis_index("x")
     total[...] = jnp.zeros((96, OBJ), F32)
     lane = lax.broadcasted_iota(jnp.int32, (72, 256), 1)
-    for slot in range(2):
-
-        def source(t, carry):
-            first = first_interval(peers[t, slot, 0], x)
+    y = lax.axis_index("y")
+
+    def source(t, carry):
+        ahead, below = t // 4, lax.rem(t, 4)
+        place = lax.rem(x - ahead + 4, 4) * 4 + lax.rem(y - below + 4, 4)
+        for slot in range(2):
+            first = first_interval(peers[ahead, below, slot, 0], x)
             rows = pl.ds(pl.multiple_of(first * 24, 8), 72)
-            wrapped = lane < peers[t, slot, 1] * TILE
-            value = got[slot * 16 + t].astype(F32)
+            wrapped = lane < peers[ahead, below, slot, 1] * TILE
+            value = got[slot * 16 + place].astype(F32)
             low = value[:, 0:256]
             total[rows, 0:256] += jnp.where(wrapped, 0.0, low)
             total[rows, 512:768] += jnp.where(wrapped, low, 0.0)
             total[rows, 256:512] += value[:, 256:512]
-            return carry
-
-        lax.fori_loop(0, 16, source, 0)
+        return carry
+
+    lax.fori_loop(0, 16, source, 0)
     for step, out in enumerate((own, one, two, three)):
         place = lax.rem(zh + step, 4)
         out[...] = total[pl.ds(pl.multiple_of(place * 24, 8), 24), :].astype(out.dtype)
@@ -310,15 +334,19 @@
     piece = transmission.reshape(24, OBJ)
     others = [turn(piece, "zh", hops, 4) for hops in (2, 1, 3)]
     others = [others[1], others[0], others[2]]
-    peers = lax.all_to_all(jnp.broadcast_to(window_tiles[None], (16, 2, 2)), ("x", "y"), 0, 0, tiled=True)
+    line = jnp.stack([window_tiles] + [turn(window_tiles, "y", hops, 4) for hops in (1, 2, 3)])
+    peers = jnp.stack([line] + [turn(line, "x", hops, 4) for hops in (1, 2, 3)])
     sent = pack(peers, piece, others)
     sent, rows = lax.optimization_barrier((sent, prop_rows))
     own = lax.all_to_all(sent, ("zl", "x", "y"), 0, 0, tiled=True)
     mats = prep(window_tiles, rows, prop_cols, probe_wave, exit_cotangent)
     own, m1, m2, state = lax.optimization_barrier((own, *mats))
+    m1 = pltpu.with_memory_space_constraint(m1, pltpu.HBM)
+    m2 = pltpu.with_memory_space_constraint(m2, pltpu.HBM)
+    kept = pltpu.with_memory_space_constraint(state, pltpu.HBM)
     given = lax.dynamic_index_in_dim(own.reshape(2, 16, 72, W), 1 - core, 0, keepdims=False)
     other = turn(given, "core", 1, 2)
-    after, first = open_step(window_tiles, own, m1, m2, state)
+    after, first = open_step(window_tiles, own, m1, m2, kept)
     first_away = turn(first, "core", 1, 2)
     middle, last = close_steps(window_tiles, own, other, m1, m2, after)
     last_away = turn(last, "core", 1, 2)

time: 132 us -> 131 us (level)
  blocking collectives: 52.1 us -> 37.9 us
  starting transfers between devices: 19.8 us -> 32.3 us
  local copies, waits for them, and re-layouts: 15 us -> 9.71 us
  Pallas kernels: 19.7 us -> 23.3 us
  other arithmetic: 0.02 us -> 1.4 us
    all_to_all x1 -> x0, blocking collectives: 14.4 us -> none  [on_device(): lax.all_to_all(jnp.broadcast_to(window_tiles[None], (16, 2, 2)), ('x', 'y...]
    ppermute x9 -> x15, starting transfers between devices: 15.6 us -> 27.2 us  [turn(): lax.ppermute(value, axis, [(i, (i + step) % count) for i in range(count)])]
    unnamed x27 -> x19, local copies, waits for them, and re-layouts: 13.5 us -> 8.92 us
    pallas_call x2, Pallas kernels: 9.27 us -> 12.7 us  [the longest x1 7.39 us: close_steps(): pl.pallas_call(close_kernel, out_shape=[STATE, SENT], in_specs=[SMEM, VME...]
    ppermute x9 -> x15, waiting for transfers between devices: 6.84 us -> 9.35 us  [turn(): lax.ppermute(value, axis, [(i, (i + step) % count) for i in range(count)])]
    another operation x0 -> x3, other arithmetic: none -> 1.38 us  [the longest x2 0.69 us: on_device(): peers = jnp.stack([line] + [turn(line, 'x', hops, 4) for hops in (1, 2, 3)])]
  transfers between devices with their start and end apart: 10 -> 16, of which waited for: 4 -> 6; matrix products, arithmetic and copies ran while one was open for 1% -> 2% of each run, Pallas kernels for 10% -> 13%
where the time goes in v4:
time: 131 us
  blocking collectives  37.9 us (29%)
  starting transfers between devices  32.3 us (25%)
  waiting for transfers between devices  25.3 us (19%)
  Pallas kernels  23.3 us (18%)
  local copies, waits for them, and re-layouts  9.71 us (7%)
  other arithmetic  1.4 us (1%)
    all_to_all x1, blocking collectives, on_device(): got = lax.all_to_all(contrib, ('zl', 'x', 'y'), 0, 0, tiled=True)  37.9 us
    ppermute x15, starting transfers between devices, turn(): lax.ppermute(value, axis, [(i, (i + step) % count) for i in range(count)])  27.2 us
    all_to_all x1, waiting for transfers between devices, on_device(): own = lax.all_to_all(sent, ('zl', 'x', 'y'), 0, 0, tiled=True)  16 us
    ppermute x15, waiting for transfers between devices, turn(): lax.ppermute(value, axis, [(i, (i + step) % count) for i in range(count)])  9.35 us
    unnamed x19, local copies, waits for them, and re-layouts  8.92 us
    pallas_call x1, Pallas kernels, close_steps(): pl.pallas_call(close_kernel, out_shape=[STATE, SENT], in_specs=[SMEM, VME...  7.39 us
    pallas_call x1, Pallas kernels, open_step(): pl.pallas_call(open_kernel, out_shape=[STATE, SENT], in_specs=[SMEM, VMEM...  5.32 us
    all_to_all x1, starting transfers between devices, on_device(): own = lax.all_to_all(sent, ('zl', 'x', 'y'), 0, 0, tiled=True)  5.03 us
  transfers between devices with their start and end apart: 16, of which 6 were waited for; matrix products, arithmetic and copies ran while one was open for 2% of the time, Pallas kernels for 13%

profile of v4, /device:TPU:64, one launch (start us, length us, event | category | flops | bytes accessed | tf_op | source)
XLA Modules:
  0.0 130.7 jit_solution(13620060601168160088)
XLA Ops:
  0.0 1.6 %collective-permute-start = (s32[2,2]{1,0:T(2,128)}, s32[2,2]{1,0:T(2,128)S(1)}, u32[]{:S(2)}, u32[]{:S(2)}) collective-permute-start(s32[2,2]{1,0:T(2,128)} %tiles.9), channel_id=1, source_target_pairs={{0,1},{1,2},{2,3},{3,0},{4,5},{5,6},{6,7},{7,4},{8,9},{9,10},{10,1... | collective-permute-start | bytes 56 | tf_op jit(solution)/shard_map/ppermute | solution.py:329
  1.6 2.9 %collective-permute-start.1 = (s32[2,2]{1,0:T(2,128)}, s32[2,2]{1,0:T(2,128)S(1)}, u32[]{:S(2)}, u32[]{:S(2)}) collective-permute-start(s32[2,2]{1,0:T(2,128)} %tiles.9), channel_id=1, source_target_pairs={{0,2},{1,3},{2,0},{3,1},{4,6},{5,7},{6,4},{7,5},{8,10},{9,11},{10,... | collective-permute-start | bytes 56 | tf_op jit(solution)/shard_map/ppermute | solution.py:329
  6.6 4.6 %collective-permute-start.6 = (bf16[24,768]{1,0:T(8,128)(2,1)S(1)}, bf16[24,768]{1,0:T(8,128)(2,1)S(1)}, u32[]{:S(2)}, u32[]{:S(2)}) collective-permute-start(bf16[24,768]{1,0:T(8,128)(2,1)S(1)} %reshape.9.own), channel_id=1, source_target_pairs={{0,16},{16,32},{32,48},{48,0},{1,17},{17,33},{33,49},{49,1},{2,18}... | collective-permute-start | bytes 110600 | tf_op jit(solution)/shard_map/ppermute | solution.py:329
  12.2 2.8 %collective-permute-start.8 = (bf16[24,768]{1,0:T(8,128)(2,1)S(1)}, bf16[24,768]{1,0:T(8,128)(2,1)S(1)}, u32[]{:S(2)}, u32[]{:S(2)}) collective-permute-start(bf16[24,768]{1,0:T(8,128)(2,1)S(1)} %reshape.9.own), channel_id=1, source_target_pairs={{0,48},{16,0},{32,16},{48,32},{1,49},{17,1},{33,17},{49,33},{2,50}... | collective-permute-start | bytes 110600 | tf_op jit(solution)/shard_map/ppermute | solution.py:329
  15.7 1.5 %collective-permute-start.3 = (s32[4,2,2]{2,1,0:T(2,128)S(1)}, s32[4,2,2]{2,1,0:T(2,128)S(1)}, u32[]{:S(2)}, u32[]{:S(2)}) collective-permute-start(s32[4,2,2]{2,1,0:T(2,128)S(1)} %pad_add_fusion.1), channel_id=1, source_target_pairs={{0,4},{4,8},{8,12},{12,0},{1,5},{5,9},{9,13},{13,1},{2,6},{6,10},{... | collective-permute-start | bytes 200 | tf_op jit(solution)/shard_map/ppermute | solution.py:329
  17.2 2.7 %collective-permute-start.4 = (s32[4,2,2]{2,1,0:T(2,128)S(1)}, s32[4,2,2]{2,1,0:T(2,128)S(1)}, u32[]{:S(2)}, u32[]{:S(2)}) collective-permute-start(s32[4,2,2]{2,1,0:T(2,128)S(1)} %pad_add_fusion.1), channel_id=1, source_target_pairs={{0,8},{4,12},{8,0},{12,4},{1,9},{5,13},{9,1},{13,5},{2,10},{6,14},... | collective-permute-start | bytes 200 | tf_op jit(solution)/shard_map/ppermute | solution.py:329
  20.6 1.5 %collective-permute-start.5 = (s32[4,2,2]{2,1,0:T(2,128)S(1)}, s32[4,2,2]{2,1,0:T(2,128)S(1)}, u32[]{:S(2)}, u32[]{:S(2)}) collective-permute-start(s32[4,2,2]{2,1,0:T(2,128)S(1)} %pad_add_fusion.1), channel_id=1, source_target_pairs={{0,12},{4,0},{8,4},{12,8},{1,13},{5,1},{9,5},{13,9},{2,14},{6,2},{... | collective-permute-start | bytes 200 | tf_op jit(solution)/shard_map/ppermute | solution.py:329
  22.3 1.9 %collective-permute-done.5 = s32[4,2,2]{2,1,0:T(2,128)S(1)} collective-permute-done((s32[4,2,2]{2,1,0:T(2,128)S(1)}, s32[4,2,2]{2,1,0:T(2,128)S(1)}, u32[]{:S(2)}, u32[]{:S(2)}) %collective-permute-start.5) | collective-permute-done | bytes 96 | tf_op jit(solution)/shard_map/ppermute | solution.py:329
  24.3 2.9 %pack.1 = bf16[32,72,512]{2,1,0:T(8,128)(2,1)} custom-call(s32[4,4,2,2]{3,2,1,0:T(2,128)S(1)} %pad_add_fusion.peers, bf16[24,768]{1,0:T(8,128)(2,1)S(1)} %reshape.9.own, bf16[24,768]{1,0:T(8,128)(2,1)S(1)} %collective-permute-done.6.one, bf16[24,768]{1,0:T(8,128)(2,1)S(1)} %collective-permute-done.7.two, bf16[24,768]{1,0:T(8,128)(2,1)S(1)} %collective-permute-done.8.three), custom_call_target="tpu_custom_call" | custom-call | tf_op jit(solution)/shard_map/pack/pallas_call | solution.py:128
  27.2 5.0 %all-to-all-start = ((bf16[32,72,512]{2,1,0:T(8,128)(2,1)}), bf16[32,72,512]{2,1,0:T(8,128)(2,1)S(1)}, u32[]{:S(2)}, u32[]{:S(2)}) async-start(bf16[32,72,512]{2,1,0:T(8,128)(2,1)} %pack.1), calls=%async_computation | async-start | bytes 4718592 | tf_op jit(solution)/shard_map/all_to_all | solution.py:341
  32.3 1.6 %copy-done.3 = bf16[2,2,512,512]{3,2,1,0:T(8,128)(2,1)S(1)} copy-done((bf16[2,2,512,512]{3,2,1,0:T(8,128)(2,1)S(1)}, bf16[2,2,512,512]{3,2,1,0:T(8,128)(2,1)}, u32[]{:S(2)}) %copy-start.3) | copy-done | bytes 2097176
  36.3 3.3 %prep.1 = (bf16[1024,1024]{1,0:T(8,128)(2,1)S(1)}, bf16[1024,1024]{1,0:T(8,128)(2,1)S(1)}, f32[512,1024]{1,0:T(8,128)S(1)}) custom-call(s32[2,2]{1,0:T(2,128)S(1)} %copy-done.2, bf16[2,512,512]{2,1,0:T(8,128)(2,1)S(1)} %copy-done.4, bf16[2,512,512]{2,1,0:T(8,128)(2,1)S(1)} %copy-done.5, bf16[2,512,512]{2,1,0:T(8,128)(2,1)S(1)} %copy-done.6, ...), custom_call_target="tpu_custom_call" | custom-call | flops 4000000000 | bytes 20000000 | tf_op jit(solution)/shard_map/prep/pallas_call | solution.py:90
  40.9 1.4 %copy-done.7 = bf16[1024,1024]{1,0:T(8,128)(2,1)} copy-done((bf16[1024,1024]{1,0:T(8,128)(2,1)}, bf16[1024,1024]{1,0:T(8,128)(2,1)S(1)}, u32[]{:S(2)}) %copy-start.7) | copy-done | bytes 2097176
  42.3 1.4 %copy-done.8 = bf16[1024,1024]{1,0:T(8,128)(2,1)} copy-done((bf16[1024,1024]{1,0:T(8,128)(2,1)}, bf16[1024,1024]{1,0:T(8,128)(2,1)S(1)}, u32[]{:S(2)}) %copy-start.8) | copy-done | bytes 2097176
  43.7 16.0 %all-to-all-done.own = bf16[32,72,512]{2,1,0:T(8,128)(2,1)S(1)} async-done(((bf16[32,72,512]{2,1,0:T(8,128)(2,1)}), bf16[32,72,512]{2,1,0:T(8,128)(2,1)S(1)}, u32[]{:S(2)}, u32[]{:S(2)}) %all-to-all-start) | async-done | bytes 2359328 | tf_op jit(solution)/shard_map/all_to_all | solution.py:341
  59.9 5.3 %open_step.1 = (f32[512,1024]{1,0:T(8,128)S(1)}, bf16[512,1024]{1,0:T(8,128)(2,1)S(1)}) custom-call(s32[2,2]{1,0:T(2,128)S(1)} %copy-done.2, bf16[32,72,512]{2,1,0:T(8,128)(2,1)S(1)} %all-to-all-done.own, bf16[1024,1024]{1,0:T(8,128)(2,1)} %copy-done.7, bf16[1024,1024]{1,0:T(8,128)(2,1)} %copy-done.8, f32[512,1024]{1,0:T(8,128)} %copy-done), custom_call_target="tpu_custom_call" | custom-call | flops 4000000000 | bytes 10000000 | tf_op jit(solution)/shard_map/open_step/pallas_call | solution.py:204
  65.8 7.4 %close_steps.1 = (f32[512,1024]{1,0:T(8,128)S(1)}, bf16[512,1024]{1,0:T(8,128)(2,1)S(1)}) custom-call(s32[2,2]{1,0:T(2,128)S(1)} %copy-done.2, bf16[32,72,512]{2,1,0:T(8,128)(2,1)S(1)} %all-to-all-done.own, bf16[16,72,512]{2,1,0:T(8,128)(2,1)S(1)} %collective-permute-done.9.other, bf16[1024,1024]{1,0:T(8,128)(2,1)} %copy-done.7, ...), custom_call_target="tpu_custom_call" | custom-call | flops 8000000000 | bytes 10000000 | tf_op jit(solution)/shard_map/close_steps/pallas_call | solution.py:234
  76.1 1.4 %late.1 = bf16[32,72,512]{2,1,0:T(8,128)(2,1)S(1)} custom-call(s32[2,2]{1,0:T(2,128)S(1)} %copy-done.2, s32[1]{0:T(128)S(6)} %copy.32.count, f32[512,1024]{1,0:T(8,128)S(1)} %copy-done.1, bf16[512,1024]{1,0:T(8,128)(2,1)S(1)} %collective-permute-done.10.remote, bf16[16,72,512]{2,1,0:T(8,128)(2,1)S(1)} %early.1.half), custom_call_target="tpu_custom_call" | custom-call | tf_op jit(solution)/shard_map/late/pallas_call | solution.py:278
  77.5 37.9 %all_to_all.10.got = bf16[32,72,512]{2,1,0:T(8,128)(2,1)S(1)} all-to-all(bf16[32,72,512]{2,1,0:T(8,128)(2,1)S(1)} %late.1), channel_id=1, replica_groups=mesh['zl'=2,'core'=2,'zh'=4,'x'=4,'y'=4] {'zl','x','y'}, dimensions={0} | all-to-all | bytes 4718592 | tf_op jit(solution)/shard_map/all_to_all | solution.py:355
  115.4 1.8 %gather.1 = (f32[24,768]{1,0:T(8,128)S(1)}, bf16[24,768]{1,0:T(8,128)(2,1)S(1)}, bf16[24,768]{1,0:T(8,128)(2,1)S(1)}, bf16[24,768]{1,0:T(8,128)(2,1)S(1)}) custom-call(s32[4,4,2,2]{3,2,1,0:T(2,128)S(1)} %pad_add_fusion.peers, bf16[32,72,512]{2,1,0:T(8,128)(2,1)S(1)} %all_to_all.10.got), custom_call_target="tpu_custom_call" | custom-call | tf_op jit(solution)/shard_map/gather/pallas_call | solution.py:317
  117.2 2.7 %collective-permute-start.12 = (bf16[24,768]{1,0:T(8,128)(2,1)S(1)}, bf16[24,768]{1,0:T(8,128)(2,1)S(1)}, u32[]{:S(2)}, u32[]{:S(2)}) collective-permute-start(bf16[24,768]{1,0:T(8,128)(2,1)S(1)} %get-tuple-element.36), channel_id=1, source_target_pairs={{0,32},{16,48},{32,0},{48,16},{1,33},{17,49},{33,1},{49,17},{2,34}... | collective-permute-start | bytes 110600 | tf_op jit(solution)/shard_map/ppermute | solution.py:329
  119.9 3.7 %collective-permute-start.13 = (bf16[24,768]{1,0:T(8,128)(2,1)S(1)}, bf16[24,768]{1,0:T(8,128)(2,1)S(1)}, u32[]{:S(2)}, u32[]{:S(2)}) collective-permute-start(bf16[24,768]{1,0:T(8,128)(2,1)S(1)} %get-tuple-element.37), channel_id=1, source_target_pairs={{0,16},{16,32},{32,48},{48,0},{1,17},{17,33},{33,49},{49,1},{2,18}... | collective-permute-start | bytes 110600 | tf_op jit(solution)/shard_map/ppermute | solution.py:329
  123.5 1.8 %collective-permute-done.12 = bf16[24,768]{1,0:T(8,128)(2,1)S(1)} collective-permute-done((bf16[24,768]{1,0:T(8,128)(2,1)S(1)}, bf16[24,768]{1,0:T(8,128)(2,1)S(1)}, u32[]{:S(2)}, u32[]{:S(2)}) %collective-permute-start.12) | collective-permute-done | bytes 36896 | tf_op jit(solution)/shard_map/ppermute | solution.py:329
  125.3 4.6 %collective-permute-done.14 = bf16[24,768]{1,0:T(8,128)(2,1)S(1)} collective-permute-done((bf16[24,768]{1,0:T(8,128)(2,1)S(1)}, bf16[24,768]{1,0:T(8,128)(2,1)S(1)}, u32[]{:S(2)}, u32[]{:S(2)}) %collective-permute-start.14) | collective-permute-done | bytes 36896 | tf_op jit(solution)/shard_map/ppermute | solution.py:329
  (43 shorter events, 12.3 us)
Async XLA Ops:
  0.0 12.2 %collective-permute-start = (s32[2,2]{1,0:T(2,128)}, s32[2,2]{1,0:T(2,128)S(1)}, u32[]{:S(2)}, u32[]{:S(2)}) collective-permute-start(s32[2,2]{1,0:T(2,128)} %tiles.9), channel_id=1, source_target_pairs={{0,1},{1,2},{2,3},{3,0},{4,5},{5,6},{6,7},{7,4},{8,9},{9,10},{10,1... | collective-permute-start | bytes 56 | tf_op jit(solution)/shard_map/ppermute | solution.py:329
  1.6 13.4 %collective-permute-start.1 = (s32[2,2]{1,0:T(2,128)}, s32[2,2]{1,0:T(2,128)S(1)}, u32[]{:S(2)}, u32[]{:S(2)}) collective-permute-start(s32[2,2]{1,0:T(2,128)} %tiles.9), channel_id=1, source_target_pairs={{0,2},{1,3},{2,0},{3,1},{4,6},{5,7},{6,4},{7,5},{8,10},{9,11},{10,... | collective-permute-start | bytes 56 | tf_op jit(solution)/shard_map/ppermute | solution.py:329
  4.5 10.5 %collective-permute-start.2 = (s32[2,2]{1,0:T(2,128)}, s32[2,2]{1,0:T(2,128)S(1)}, u32[]{:S(2)}, u32[]{:S(2)}) collective-permute-start(s32[2,2]{1,0:T(2,128)} %tiles.9), channel_id=1, source_target_pairs={{0,3},{1,0},{2,1},{3,2},{4,7},{5,4},{6,5},{7,6},{8,11},{9,8},{10,9... | collective-permute-start | bytes 56 | tf_op jit(solution)/shard_map/ppermute | solution.py:329
  6.6 17.6 %collective-permute-start.6 = (bf16[24,768]{1,0:T(8,128)(2,1)S(1)}, bf16[24,768]{1,0:T(8,128)(2,1)S(1)}, u32[]{:S(2)}, u32[]{:S(2)}) collective-permute-start(bf16[24,768]{1,0:T(8,128)(2,1)S(1)} %reshape.9.own), channel_id=1, source_target_pairs={{0,16},{16,32},{32,48},{48,0},{1,17},{17,33},{33,49},{49,1},{2,18}... | collective-permute-start | bytes 110600 | tf_op jit(solution)/shard_map/ppermute | solution.py:329
  11.2 13.1 %collective-permute-start.7 = (bf16[24,768]{1,0:T(8,128)(2,1)S(1)}, bf16[24,768]{1,0:T(8,128)(2,1)S(1)}, u32[]{:S(2)}, u32[]{:S(2)}) collective-permute-start(bf16[24,768]{1,0:T(8,128)(2,1)S(1)} %reshape.9.own), channel_id=1, source_target_pairs={{0,32},{16,48},{32,0},{48,16},{1,33},{17,49},{33,1},{49,17},{2,34}... | collective-permute-start | bytes 110600 | tf_op jit(solution)/shard_map/ppermute | solution.py:329
  12.2 12.1 %collective-permute-start.8 = (bf16[24,768]{1,0:T(8,128)(2,1)S(1)}, bf16[24,768]{1,0:T(8,128)(2,1)S(1)}, u32[]{:S(2)}, u32[]{:S(2)}) collective-permute-start(bf16[24,768]{1,0:T(8,128)(2,1)S(1)} %reshape.9.own), channel_id=1, source_target_pairs={{0,48},{16,0},{32,16},{48,32},{1,49},{17,1},{33,17},{49,33},{2,50}... | collective-permute-start | bytes 110600 | tf_op jit(solution)/shard_map/ppermute | solution.py:329
  15.7 4.9 %collective-permute-start.3 = (s32[4,2,2]{2,1,0:T(2,128)S(1)}, s32[4,2,2]{2,1,0:T(2,128)S(1)}, u32[]{:S(2)}, u32[]{:S(2)}) collective-permute-start(s32[4,2,2]{2,1,0:T(2,128)S(1)} %pad_add_fusion.1), channel_id=1, source_target_pairs={{0,4},{4,8},{8,12},{12,0},{1,5},{5,9},{9,13},{13,1},{2,6},{6,10},{... | collective-permute-start | bytes 200 | tf_op jit(solution)/shard_map/ppermute | solution.py:329
  17.2 5.1 %collective-permute-start.4 = (s32[4,2,2]{2,1,0:T(2,128)S(1)}, s32[4,2,2]{2,1,0:T(2,128)S(1)}, u32[]{:S(2)}, u32[]{:S(2)}) collective-permute-start(s32[4,2,2]{2,1,0:T(2,128)S(1)} %pad_add_fusion.1), channel_id=1, source_target_pairs={{0,8},{4,12},{8,0},{12,4},{1,9},{5,13},{9,1},{13,5},{2,10},{6,14},... | collective-permute-start | bytes 200 | tf_op jit(solution)/shard_map/ppermute | solution.py:329
  20.6 3.6 %collective-permute-start.5 = (s32[4,2,2]{2,1,0:T(2,128)S(1)}, s32[4,2,2]{2,1,0:T(2,128)S(1)}, u32[]{:S(2)}, u32[]{:S(2)}) collective-permute-start(s32[4,2,2]{2,1,0:T(2,128)S(1)} %pad_add_fusion.1), channel_id=1, source_target_pairs={{0,12},{4,0},{8,4},{12,8},{1,13},{5,1},{9,5},{13,9},{2,14},{6,2},{... | collective-permute-start | bytes 200 | tf_op jit(solution)/shard_map/ppermute | solution.py:329
  27.2 5.1 %copy-start.2 = (s32[2,2]{1,0:T(2,128)S(1)}, s32[2,2]{1,0:T(2,128)}, u32[]{:S(2)}) copy-start(s32[2,2]{1,0:T(2,128)} %tiles.9) | copy-start | bytes 52
  27.2 5.1 %copy-start.4 = (bf16[2,512,512]{2,1,0:T(8,128)(2,1)S(1)}, bf16[2,512,512]{2,1,0:T(8,128)(2,1)}, u32[]{:S(2)}) copy-start(bf16[2,512,512]{2,1,0:T(8,128)(2,1)} %rows) | copy-start | bytes 3145732
  27.2 32.5 %all-to-all-start = ((bf16[32,72,512]{2,1,0:T(8,128)(2,1)}), bf16[32,72,512]{2,1,0:T(8,128)(2,1)S(1)}, u32[]{:S(2)}, u32[]{:S(2)}) async-start(bf16[32,72,512]{2,1,0:T(8,128)(2,1)} %pack.1), calls=%async_computation | async-start | bytes 4718592 | tf_op jit(solution)/shard_map/all_to_all | solution.py:341
  32.3 1.6 %copy-start.3 = (bf16[2,2,512,512]{3,2,1,0:T(8,128)(2,1)S(1)}, bf16[2,2,512,512]{3,2,1,0:T(8,128)(2,1)}, u32[]{:S(2)}) copy-start(bf16[2,2,512,512]{3,2,1,0:T(8,128)(2,1)} %cot.1) | copy-start | bytes 6291460
  33.9 1.2 copy-start.5
  39.6 1.3 %copy-start = (f32[512,1024]{1,0:T(8,128)}, f32[512,1024]{1,0:T(8,128)S(1)}, u32[]{:S(2)}) copy-start(f32[512,1024]{1,0:T(8,128)S(1)} %get-tuple-element.27.state.local) | copy-start | bytes 6291460
  40.9 1.4 %copy-start.7 = (bf16[1024,1024]{1,0:T(8,128)(2,1)}, bf16[1024,1024]{1,0:T(8,128)(2,1)S(1)}, u32[]{:S(2)}) copy-start(bf16[1024,1024]{1,0:T(8,128)(2,1)S(1)} %get-tuple-element.29.m1) | copy-start | bytes 6291460
  42.3 1.4 %copy-start.8 = (bf16[1024,1024]{1,0:T(8,128)(2,1)}, bf16[1024,1024]{1,0:T(8,128)(2,1)S(1)}, u32[]{:S(2)}) copy-start(bf16[1024,1024]{1,0:T(8,128)(2,1)S(1)} %get-tuple-element.30.m2) | copy-start | bytes 6291460
  59.8 6.0 %collective-permute-start.9 = (bf16[16,72,512]{2,1,0:T(8,128)(2,1)S(1)}, bf16[16,72,512]{2,1,0:T(8,128)(2,1)S(1)}, u32[]{:S(2)}, u32[]{:S(2)}) collective-permute-start(bf16[16,72,512]{2,1,0:T(8,128)(2,1)S(1)} %dynamic-slice_bitcast_fusion), channel_id=1, source_target_pairs={{0,64},{64,0},{1,65},{65,1},{2,66},{66,2},{3,67},{67,3},{4,68},{68... | collective-permute-start | bytes 3538952 | tf_op jit(solution)/shard_map/ppermute | solution.py:329
  65.2 9.0 %collective-permute-start.11 = (bf16[512,1024]{1,0:T(8,128)(2,1)S(1)}, bf16[512,1024]{1,0:T(8,128)(2,1)S(1)}, u32[]{:S(2)}, u32[]{:S(2)}) collective-permute-start(bf16[512,1024]{1,0:T(8,128)(2,1)S(1)} %get-tuple-element.34), channel_id=1, source_target_pairs={{0,64},{64,0},{1,65},{65,1},{2,66},{66,2},{3,67},{67,3},{4,68},{68... | collective-permute-start | bytes 3145736 | tf_op jit(solution)/shard_map/ppermute | solution.py:329
  73.2 3.0 %collective-permute-start.10 = (bf16[512,1024]{1,0:T(8,128)(2,1)S(1)}, bf16[512,1024]{1,0:T(8,128)(2,1)S(1)}, u32[]{:S(2)}, u32[]{:S(2)}) collective-permute-start(bf16[512,1024]{1,0:T(8,128)(2,1)S(1)} %get-tuple-element.32), channel_id=1, source_target_pairs={{0,64},{64,0},{1,65},{65,1},{2,66},{66,2},{3,67},{67,3},{4,68},{68... | collective-permute-start | bytes 3145736 | tf_op jit(solution)/shard_map/ppermute | solution.py:329
  74.2 2.0 %copy-start.1 = (f32[512,1024]{1,0:T(8,128)S(1)}, f32[512,1024]{1,0:T(8,128)}, u32[]{:S(2)}) copy-start(f32[512,1024]{1,0:T(8,128)} %copy-done) | copy-start | bytes 6291460
  117.2 8.2 %collective-permute-start.12 = (bf16[24,768]{1,0:T(8,128)(2,1)S(1)}, bf16[24,768]{1,0:T(8,128)(2,1)S(1)}, u32[]{:S(2)}, u32[]{:S(2)}) collective-permute-start(bf16[24,768]{1,0:T(8,128)(2,1)S(1)} %get-tuple-element.36), channel_id=1, source_target_pairs={{0,32},{16,48},{32,0},{48,16},{1,33},{17,49},{33,1},{49,17},{2,34}... | collective-permute-start | bytes 110600 | tf_op jit(solution)/shard_map/ppermute | solution.py:329
  119.9 5.5 %collective-permute-start.13 = (bf16[24,768]{1,0:T(8,128)(2,1)S(1)}, bf16[24,768]{1,0:T(8,128)(2,1)S(1)}, u32[]{:S(2)}, u32[]{:S(2)}) collective-permute-start(bf16[24,768]{1,0:T(8,128)(2,1)S(1)} %get-tuple-element.37), channel_id=1, source_target_pairs={{0,16},{16,32},{32,48},{48,0},{1,17},{17,33},{33,49},{49,1},{2,18}... | collective-permute-start | bytes 110600 | tf_op jit(solution)/shard_map/ppermute | solution.py:329
  123.5 6.5 %collective-permute-start.14 = (bf16[24,768]{1,0:T(8,128)(2,1)S(1)}, bf16[24,768]{1,0:T(8,128)(2,1)S(1)}, u32[]{:S(2)}, u32[]{:S(2)}) collective-permute-start(bf16[24,768]{1,0:T(8,128)(2,1)S(1)} %get-tuple-element.38), channel_id=1, source_target_pairs={{0,48},{16,0},{32,16},{48,32},{1,49},{17,1},{33,17},{49,33},{2,50}... | collective-permute-start | bytes 110600 | tf_op jit(solution)/shard_map/ppermute | solution.py:329
  (1 other events, 1.2 us)

commit v5 on v4

--- a/solution.py
+++ b/solution.py
@@ -86,10 +86,9 @@
 
 
 def prep(tiles, rows, cols, probe, cot):
-    square = jax.ShapeDtypeStruct((2 * W, 2 * W), BF)
     return pl.pallas_call(
         prep_kernel,
-        out_shape=[square, square, jax.ShapeDtypeStruct((W, 2 * W), F32)],
+        out_shape=[SQUARE, SQUARE, jax.ShapeDtypeStruct((W, 2 * W), F32)],
         in_specs=[SMEM] + [VMEM] * 4,
         out_specs=[VMEM] * 3,
         scratch_shapes=[pltpu.VMEM((2 * W, W), BF), pltpu.VMEM((W, 2 * W), BF)],
@@ -99,7 +98,7 @@
     )(tiles, rows, cols, probe, cot)
 
 
-def pack_kernel(peers, own, one, two, three, out, held):
+def pack_kernel(peers, own, one, two, three, out, held, chunks, sems):
     zh = lax.axis_index("zh")
     x = lax.axis_index("x")
     for step, piece in enumerate((own, one, two, three)):
@@ -107,6 +106,9 @@
         held[pl.ds(pl.multiple_of(place * 24, 8), 24), :] = piece[...].astype(F32)
     lane = lax.broadcasted_iota(jnp.int32, (72, 256), 1)
     y = lax.axis_index("y")
+
+    def moved(i):
+        return pltpu.make_async_copy(chunks.at[i], out.at[i], sems.at[i])
 
     def target(t, carry):
         ahead, below = t // 4, lax.rem(t, 4)
@@ -117,11 +119,17 @@
             wrapped = lane < peers[ahead, below, slot, 1] * TILE
             low = held[rows, 0:256]
             high = held[rows, 512:768]
-            out[slot * 16 + place, :, 0:256] = jnp.where(wrapped, high, low).astype(BF)
-            out[slot * 16 + place, :, 256:512] = held[rows, 256:512].astype(BF)
+            chunks[slot * 16 + place, :, 0:256] = jnp.where(wrapped, high, low).astype(BF)
+            chunks[slot * 16 + place, :, 256:512] = held[rows, 256:512].astype(BF)
+            moved(slot * 16 + place).start()
+        return carry
+
+    def settle(i, carry):
+        moved(i).wait()
         return carry
 
     lax.fori_loop(0, 16, target, 0)
+    lax.fori_loop(0, 32, settle, 0)
 
 
 def pack(peers, own, others):
@@ -129,8 +137,12 @@
         pack_kernel,
         out_shape=jax.ShapeDtypeStruct((32, 72, W), BF),
         in_specs=[SMEM] + [VMEM] * 4,
-        out_specs=VMEM,
-        scratch_shapes=[pltpu.VMEM((96, OBJ), F32)],
+        out_specs=HBM,
+        scratch_shapes=[
+            pltpu.VMEM((96, OBJ), F32),
+            pltpu.VMEM((32, 72, W), BF),
+            pltpu.SemaphoreType.DMA((32,)),
+        ],
         compiler_params=params(16),
         name="pack",
     )(peers, own, *others)
@@ -150,7 +162,7 @@
     lax.fori_loop(0, 4, place, 0)
 
 
-def form_contrib(local, remote, contrib, out, base, sign, used, row_tile):
+def form_contrib(local, remote, contrib, out, sign, used, row_tile, formed=None):
     ar = local[:, 0:W]
     ai = local[:, W:]
     br = remote[:, 0:W].astype(F32)
@@ -166,7 +178,9 @@
             contrib[part, pl.ds(pl.multiple_of(start + 192 * k, 16), 48), :] for k in range(3) for part in range(2)
         ]
         for y in range(4):
-            out[base + plane * 4 + y] = jnp.concatenate([b[12 * y : 12 * y + 12] for b in blocks]).astype(BF)
+            out[plane * 4 + y] = jnp.concatenate([b[12 * y : 12 * y + 12] for b in blocks]).astype(BF)
+            if formed is not None:
+                formed(plane * 4 + y)
         return carry
 
     lax.fori_loop(0, 4, cut, 0)
@@ -180,11 +194,11 @@
 STATE = jax.ShapeDtypeStruct((W, 2 * W), F32)
 SENT = jax.ShapeDtypeStruct((W, 2 * W), BF)
 WORK = [pltpu.VMEM((2, ROWS, W), F32), pltpu.VMEM((2 * W, W), BF), pltpu.VMEM((W, 2 * W), BF)]
-HELD = [pltpu.VMEM((2 * W, 2 * W), BF)] * 2
+SQUARE = jax.ShapeDtypeStruct((2 * W, 2 * W), BF)
 HALF = jax.ShapeDtypeStruct((16, 72, W), BF)
 
 
-def open_kernel(tiles, own, m1, m2, state, after, sent, patch, left, right, v1, v2, held, sems):
+def open_kernel(tiles, own, m1, m2, state, after, sent, v1, v2, patch, left, right, held, sems):
     core, sign, row_tile = role(tiles)
     copies = [pltpu.make_async_copy(a, b, sems.at[i]) for i, (a, b) in enumerate([(state, held), (m1, v1), (m2, v2)])]
     for copy in copies:
@@ -203,26 +217,21 @@
 def open_step(tiles, own, m1, m2, state):
     return pl.pallas_call(
         open_kernel,
-        out_shape=[STATE, SENT],
+        out_shape=[STATE, SENT, SQUARE, SQUARE],
         in_specs=[SMEM, VMEM] + [HBM] * 3,
-        out_specs=[VMEM] * 2,
-        scratch_shapes=WORK + HELD + [pltpu.VMEM((W, 2 * W), F32), pltpu.SemaphoreType.DMA((3,))],
+        out_specs=[VMEM] * 4,
+        scratch_shapes=WORK + [pltpu.VMEM((W, 2 * W), F32), pltpu.SemaphoreType.DMA((3,))],
         compiler_params=params(24),
         cost_estimate=pl.CostEstimate(flops=4 * 10**9, transcendentals=0, bytes_accessed=10**7),
         name="open_step",
     )(tiles, own, m1, m2, state)
 
 
-def close_kernel(tiles, own, other, m1, m2, state, middle, sent, patch, left, right, v1, v2, sems):
+def close_kernel(tiles, own, other, v1, v2, state, middle, sent, patch, left, right):
     core, sign, row_tile = role(tiles)
-    copies = [pltpu.make_async_copy(a, b, sems.at[i]) for i, (a, b) in enumerate([(m1, v1), (m2, v2)])]
-    for copy in copies:
-        copy.start()
     place_patch(other, 0, patch, row_tile)
     form_left(state, patch, sign, left)
-    copies[0].wait()
     sweep(v1, left, right)
-    copies[1].wait()
     middle[...] = jnp.dot(right[...], v2[...], preferred_element_type=F32)
     place_patch(own, (1 - core) * 16, patch, row_tile)
     form_left(middle, patch, sign, left)
@@ -234,9 +243,9 @@
     return pl.pallas_call(
         close_kernel,
         out_shape=[STATE, SENT],
-        in_specs=[SMEM, VMEM, VMEM, HBM, HBM, VMEM],
+        in_specs=[SMEM] + [VMEM] * 5,
         out_specs=[VMEM] * 2,
-        scratch_shapes=WORK + HELD + [pltpu.SemaphoreType.DMA((2,))],
+        scratch_shapes=WORK,
         compiler_params=params(24),
         cost_estimate=pl.CostEstimate(flops=8 * 10**9, transcendentals=0, bytes_accessed=10**7),
         name="close_steps",
@@ -246,7 +255,7 @@
 def early_kernel(tiles, count, local, remote, out, contrib):
     core, sign, row_tile = role(tiles)
     used = lax.axis_index("zl") < count[0]
-    form_contrib(local, remote, contrib, out, 0, sign, used, row_tile)
+    form_contrib(local, remote, contrib, out, sign, used, row_tile)
 
 
 def early(tiles, count, local, remote):
@@ -262,16 +271,23 @@
     )(tiles, count, local, remote)
 
 
-def late_kernel(tiles, count, local, remote, half, out, contrib):
+def late_kernel(tiles, count, local, remote, half, out, contrib, chunks, sems):
     core, sign, row_tile = role(tiles)
     used = lax.axis_index("zl") < count[0]
-
-    def keep(i, carry):
-        out[(1 - core) * 16 + i] = half[i]
-        return carry
-
-    lax.fori_loop(0, 16, keep, 0)
-    form_contrib(local, remote, contrib, out, core * 16, sign, used, row_tile)
+    whole = pltpu.make_async_copy(half, out.at[pl.ds((1 - core) * 16, 16)], sems.at[16])
+    whole.start()
+
+    def moved(i):
+        return pltpu.make_async_copy(chunks.at[i], out.at[core * 16 + i], sems.at[i])
+
+    form_contrib(local, remote, contrib, chunks, sign, used, row_tile, lambda i: moved(i).start())
+
+    def settle(i, carry):
+        moved(i).wait()
+        return carry
+
+    lax.fori_loop(0, 16, settle, 0)
+    whole.wait()
 
 
 def late(tiles, count, local, remote, half):
@@ -279,17 +295,33 @@
         late_kernel,
         out_shape=jax.ShapeDtypeStruct((32, 72, W), BF),
         in_specs=[SMEM] * 2 + [VMEM] * 3,
-        out_specs=VMEM,
-        scratch_shapes=WORK[:1],
+        out_specs=HBM,
+        scratch_shapes=WORK[:1] + [pltpu.VMEM((16, 72, W), BF), pltpu.SemaphoreType.DMA((17,))],
         compiler_params=params(24),
         name="late",
     )(tiles, count, local, remote, half)
 
 
-def gather_kernel(peers, got, own, one, two, three, total):
+def blank_kernel(tiles, out):
+    out[...] = jnp.zeros((96, OBJ), F32)
+
+
+def blank(tiles):
+    return pl.pallas_call(
+        blank_kernel,
+        out_shape=jax.ShapeDtypeStruct((96, OBJ), F32),
+        in_specs=[SMEM],
+        out_specs=VMEM,
+        compiler_params=params(4),
+        cost_estimate=pl.CostEstimate(flops=4 * 10**9, transcendentals=0, bytes_accessed=10**7),
+        name="blank",
+    )(tiles)
+
+
+def gather_kernel(peers, got, start, own, one, two, three, total):
     zh = lax.axis_index("zh")
     x = lax.axis_index("x")
-    total[...] = jnp.zeros((96, OBJ), F32)
+    total[...] = start[...]
     lane = lax.broadcasted_iota(jnp.int32, (72, 256), 1)
     y = lax.axis_index("y")
 
@@ -313,16 +345,16 @@
         out[...] = total[pl.ds(pl.multiple_of(place * 24, 8), 24), :].astype(out.dtype)
 
 
-def gather(peers, got):
+def gather(peers, got, start):
     return pl.pallas_call(
         gather_kernel,
         out_shape=[jax.ShapeDtypeStruct((24, OBJ), F32)] + [jax.ShapeDtypeStruct((24, OBJ), BF)] * 3,
-        in_specs=[SMEM, VMEM],
+        in_specs=[SMEM, VMEM, VMEM],
         out_specs=[VMEM] * 4,
         scratch_shapes=[pltpu.VMEM((96, OBJ), F32)],
         compiler_params=params(16),
         name="gather",
-    )(peers, got)
+    )(peers, got, start)
 
 
 def turn(value, axis, step, count):
@@ -346,14 +378,17 @@
     kept = pltpu.with_memory_space_constraint(state, pltpu.HBM)
     given = lax.dynamic_index_in_dim(own.reshape(2, 16, 72, W), 1 - core, 0, keepdims=False)
     other = turn(given, "core", 1, 2)
-    after, first = open_step(window_tiles, own, m1, m2, kept)
+    after, first, m1, m2 = open_step(window_tiles, own, m1, m2, kept)
     first_away = turn(first, "core", 1, 2)
     middle, last = close_steps(window_tiles, own, other, m1, m2, after)
     last_away = turn(last, "core", 1, 2)
     half = early(window_tiles, slot_count, middle, first_away)
     contrib = late(window_tiles, slot_count, state, last_away, half)
+    contrib = pltpu.with_memory_space_constraint(contrib, pltpu.HBM)
+    contrib, tiles = lax.optimization_barrier((contrib, window_tiles))
     got = lax.all_to_all(contrib, ("zl", "x", "y"), 0, 0, tiled=True)
-    here, *away = gather(peers, got)
+    got, start = lax.optimization_barrier((got, blank(tiles)))
+    here, *away = gather(peers, got, start)
     for hops in (2, 1, 3):
         here = here + turn(away[hops - 1], "zh", hops, 4).astype(F32)
     return here.reshape(1, 2, 12, OBJ)

time: 131 us -> 131 us (level)
  blocking collectives: 37.9 us -> 0 us
  waiting for transfers between devices: 25.3 us -> 56.4 us
  starting transfers between devices: 32.3 us -> 38.6 us
    all_to_all x1 -> x0, blocking collectives: 37.9 us -> none  [on_device(): got = lax.all_to_all(contrib, ('zl', 'x', 'y'), 0, 0, tiled=True)]
    all_to_all x0 -> x1, waiting for transfers between devices: none -> 31.4 us  [on_device(): got = lax.all_to_all(contrib, ('zl', 'x', 'y'), 0, 0, tiled=True)]
    all_to_all x0 -> x1, starting transfers between devices: none -> 6.32 us  [on_device(): got = lax.all_to_all(contrib, ('zl', 'x', 'y'), 0, 0, tiled=True)]
    pallas_call x3 -> x4, Pallas kernels: 16 us -> 15 us  [the longest x1 5.86 us: close_steps(): pl.pallas_call(close_kernel, out_shape=[STATE, SENT], in_specs=[SMEM] + [...]
  transfers between devices with their start and end apart: 16 -> 17, of which waited for: 6 -> 7; matrix products, arithmetic and copies ran while one was open for 2% -> 2% of each run, Pallas kernels for 13% -> 12%
where the time goes in v5:
time: 131 us
  waiting for transfers between devices  56.4 us (43%)
  starting transfers between devices  38.6 us (29%)
  Pallas kernels  23.8 us (18%)
  local copies, waits for them, and re-layouts  9.72 us (7%)
  other arithmetic  1.4 us (1%)
    all_to_all x1, waiting for transfers between devices, on_device(): got = lax.all_to_all(contrib, ('zl', 'x', 'y'), 0, 0, tiled=True)  31.4 us
    ppermute x15, starting transfers between devices, turn(): lax.ppermute(value, axis, [(i, (i + step) % count) for i in range(count)])  27.2 us
    all_to_all x1, waiting for transfers between devices, on_device(): own = lax.all_to_all(sent, ('zl', 'x', 'y'), 0, 0, tiled=True)  16 us
    ppermute x15, waiting for transfers between devices, turn(): lax.ppermute(value, axis, [(i, (i + step) % count) for i in range(count)])  9.03 us
    unnamed x19, local copies, waits for them, and re-layouts  8.93 us
    all_to_all x1, starting transfers between devices, on_device(): got = lax.all_to_all(contrib, ('zl', 'x', 'y'), 0, 0, tiled=True)  6.32 us
    pallas_call x1, Pallas kernels, close_steps(): pl.pallas_call(close_kernel, out_shape=[STATE, SENT], in_specs=[SMEM] + [...  5.86 us
    pallas_call x1, Pallas kernels, open_step(): pl.pallas_call(open_kernel, out_shape=[STATE, SENT, SQUARE, SQUARE], in_s...  5.32 us
  transfers between devices with their start and end apart: 17, of which 7 were waited for; matrix products, arithmetic and copies ran while one was open for 2% of the time, Pallas kernels for 12%

profile of v5, /device:TPU:64, one launch (start us, length us, event | category | flops | bytes accessed | tf_op | source)
XLA Modules:
  0.0 130.8 jit_solution(1199837131271060414)
XLA Ops:
  0.0 1.6 %collective-permute-start = (s32[2,2]{1,0:T(2,128)}, s32[2,2]{1,0:T(2,128)S(1)}, u32[]{:S(2)}, u32[]{:S(2)}) collective-permute-start(s32[2,2]{1,0:T(2,128)} %tiles.10), channel_id=1, source_target_pairs={{0,1},{1,2},{2,3},{3,0},{4,5},{5,6},{6,7},{7,4},{8,9},{9,10},{10,1... | collective-permute-start | bytes 56 | tf_op jit(solution)/shard_map/ppermute | solution.py:361
  1.6 2.9 %collective-permute-start.1 = (s32[2,2]{1,0:T(2,128)}, s32[2,2]{1,0:T(2,128)S(1)}, u32[]{:S(2)}, u32[]{:S(2)}) collective-permute-start(s32[2,2]{1,0:T(2,128)} %tiles.10), channel_id=1, source_target_pairs={{0,2},{1,3},{2,0},{3,1},{4,6},{5,7},{6,4},{7,5},{8,10},{9,11},{10,... | collective-permute-start | bytes 56 | tf_op jit(solution)/shard_map/ppermute | solution.py:361
  6.6 4.6 %collective-permute-start.6 = (bf16[24,768]{1,0:T(8,128)(2,1)S(1)}, bf16[24,768]{1,0:T(8,128)(2,1)S(1)}, u32[]{:S(2)}, u32[]{:S(2)}) collective-permute-start(bf16[24,768]{1,0:T(8,128)(2,1)S(1)} %reshape.9.own), channel_id=1, source_target_pairs={{0,16},{16,32},{32,48},{48,0},{1,17},{17,33},{33,49},{49,1},{2,18}... | collective-permute-start | bytes 110600 | tf_op jit(solution)/shard_map/ppermute | solution.py:361
  12.2 2.8 %collective-permute-start.8 = (bf16[24,768]{1,0:T(8,128)(2,1)S(1)}, bf16[24,768]{1,0:T(8,128)(2,1)S(1)}, u32[]{:S(2)}, u32[]{:S(2)}) collective-permute-start(bf16[24,768]{1,0:T(8,128)(2,1)S(1)} %reshape.9.own), channel_id=1, source_target_pairs={{0,48},{16,0},{32,16},{48,32},{1,49},{17,1},{33,17},{49,33},{2,50}... | collective-permute-start | bytes 110600 | tf_op jit(solution)/shard_map/ppermute | solution.py:361
  15.7 1.5 %collective-permute-start.3 = (s32[4,2,2]{2,1,0:T(2,128)S(1)}, s32[4,2,2]{2,1,0:T(2,128)S(1)}, u32[]{:S(2)}, u32[]{:S(2)}) collective-permute-start(s32[4,2,2]{2,1,0:T(2,128)S(1)} %pad_add_fusion.1), channel_id=1, source_target_pairs={{0,4},{4,8},{8,12},{12,0},{1,5},{5,9},{9,13},{13,1},{2,6},{6,10},{... | collective-permute-start | bytes 200 | tf_op jit(solution)/shard_map/ppermute | solution.py:361
  17.2 2.7 %collective-permute-start.4 = (s32[4,2,2]{2,1,0:T(2,128)S(1)}, s32[4,2,2]{2,1,0:T(2,128)S(1)}, u32[]{:S(2)}, u32[]{:S(2)}) collective-permute-start(s32[4,2,2]{2,1,0:T(2,128)S(1)} %pad_add_fusion.1), channel_id=1, source_target_pairs={{0,8},{4,12},{8,0},{12,4},{1,9},{5,13},{9,1},{13,5},{2,10},{6,14},... | collective-permute-start | bytes 200 | tf_op jit(solution)/shard_map/ppermute | solution.py:361
  20.6 1.5 %collective-permute-start.5 = (s32[4,2,2]{2,1,0:T(2,128)S(1)}, s32[4,2,2]{2,1,0:T(2,128)S(1)}, u32[]{:S(2)}, u32[]{:S(2)}) collective-permute-start(s32[4,2,2]{2,1,0:T(2,128)S(1)} %pad_add_fusion.1), channel_id=1, source_target_pairs={{0,12},{4,0},{8,4},{12,8},{1,13},{5,1},{9,5},{13,9},{2,14},{6,2},{... | collective-permute-start | bytes 200 | tf_op jit(solution)/shard_map/ppermute | solution.py:361
  22.3 1.9 %collective-permute-done.5 = s32[4,2,2]{2,1,0:T(2,128)S(1)} collective-permute-done((s32[4,2,2]{2,1,0:T(2,128)S(1)}, s32[4,2,2]{2,1,0:T(2,128)S(1)}, u32[]{:S(2)}, u32[]{:S(2)}) %collective-permute-start.5) | collective-permute-done | bytes 96 | tf_op jit(solution)/shard_map/ppermute | solution.py:361
  24.3 2.7 %pack.1 = bf16[32,72,512]{2,1,0:T(8,128)(2,1)} custom-call(s32[4,4,2,2]{3,2,1,0:T(2,128)S(1)} %pad_add_fusion.peers, bf16[24,768]{1,0:T(8,128)(2,1)S(1)} %reshape.9.own, bf16[24,768]{1,0:T(8,128)(2,1)S(1)} %collective-permute-done.6.one, bf16[24,768]{1,0:T(8,128)(2,1)S(1)} %collective-permute-done.7.two, bf16[24,768]{1,0:T(8,128)(2,1)S(1)} %collective-permute-done.8.three), custom_call_target="tpu_custom_call" | custom-call | tf_op jit(solution)/shard_map/pack/pallas_call | solution.py:136
  27.0 5.1 %all-to-all-start = ((bf16[32,72,512]{2,1,0:T(8,128)(2,1)}), bf16[32,72,512]{2,1,0:T(8,128)(2,1)S(1)}, u32[]{:S(2)}, u32[]{:S(2)}) async-start(bf16[32,72,512]{2,1,0:T(8,128)(2,1)} %pack.1), calls=%async_computation | async-start | bytes 4718592 | tf_op jit(solution)/shard_map/all_to_all | solution.py:373
  32.1 1.6 %copy-done.3 = bf16[2,2,512,512]{3,2,1,0:T(8,128)(2,1)S(1)} copy-done((bf16[2,2,512,512]{3,2,1,0:T(8,128)(2,1)S(1)}, bf16[2,2,512,512]{3,2,1,0:T(8,128)(2,1)}, u32[]{:S(2)}) %copy-start.3) | copy-done | bytes 2097176
  36.1 3.3 %prep.1 = (bf16[1024,1024]{1,0:T(8,128)(2,1)S(1)}, bf16[1024,1024]{1,0:T(8,128)(2,1)S(1)}, f32[512,1024]{1,0:T(8,128)S(1)}) custom-call(s32[2,2]{1,0:T(2,128)S(1)} %copy-done.2, bf16[2,512,512]{2,1,0:T(8,128)(2,1)S(1)} %copy-done.4, bf16[2,512,512]{2,1,0:T(8,128)(2,1)S(1)} %copy-done.5, bf16[2,512,512]{2,1,0:T(8,128)(2,1)S(1)} %copy-done.6, ...), custom_call_target="tpu_custom_call" | custom-call | flops 4000000000 | bytes 20000000 | tf_op jit(solution)/shard_map/prep/pallas_call | solution.py:89
  42.1 1.4 %copy-done.8 = bf16[1024,1024]{1,0:T(8,128)(2,1)} copy-done((bf16[1024,1024]{1,0:T(8,128)(2,1)}, bf16[1024,1024]{1,0:T(8,128)(2,1)S(1)}, u32[]{:S(2)}) %copy-start.8) | copy-done | bytes 2097176
  43.5 16.0 %all-to-all-done.own = bf16[32,72,512]{2,1,0:T(8,128)(2,1)S(1)} async-done(((bf16[32,72,512]{2,1,0:T(8,128)(2,1)}), bf16[32,72,512]{2,1,0:T(8,128)(2,1)S(1)}, u32[]{:S(2)}, u32[]{:S(2)}) %all-to-all-start) | async-done | bytes 2359328 | tf_op jit(solution)/shard_map/all_to_all | solution.py:373
  59.7 5.3 %open_step.1 = (f32[512,1024]{1,0:T(8,128)S(1)}, bf16[512,1024]{1,0:T(8,128)(2,1)S(1)}, bf16[1024,1024]{1,0:T(8,128)(2,1)S(1)}, bf16[1024,1024]{1,0:T(8,128)(2,1)S(1)}) custom-call(s32[2,2]{1,0:T(2,128)S(1)} %copy-done.2, bf16[32,72,512]{2,1,0:T(8,128)(2,1)S(1)} %all-to-all-done.own, bf16[1024,1024]{1,0:T(8,128)(2,1)} %copy-done.7, ...), custom_call_target="tpu_custom_call" | custom-call | flops 4000000000 | bytes 10000000 | tf_op jit(solution)/shard_map/open_step/pallas_call | solution.py:218
  65.6 5.9 %close_steps.1 = (f32[512,1024]{1,0:T(8,128)S(1)}, bf16[512,1024]{1,0:T(8,128)(2,1)S(1)}) custom-call(s32[2,2]{1,0:T(2,128)S(1)} %copy-done.2, bf16[32,72,512]{2,1,0:T(8,128)(2,1)S(1)} %all-to-all-done.own, bf16[16,72,512]{2,1,0:T(8,128)(2,1)S(1)} %collective-permute-done.9.other, bf16[1024,1024]{1,0:T(8,128)(2,1)S(1)} %get-tuple-element.37.v1, ...), custom_call_target="tpu_custom_call" | custom-call | flops 8000000000 | bytes 10000000 | tf_op jit(solution)/shard_map/close_steps/pallas_call | solution.py:243
  74.4 2.2 %late.1 = bf16[32,72,512]{2,1,0:T(8,128)(2,1)} custom-call(s32[2,2]{1,0:T(2,128)S(1)} %copy-done.2, s32[1]{0:T(128)S(6)} %copy.32.count, f32[512,1024]{1,0:T(8,128)S(1)} %copy-done.1, bf16[512,1024]{1,0:T(8,128)(2,1)S(1)} %collective-permute-done.10.remote, bf16[16,72,512]{2,1,0:T(8,128)(2,1)S(1)} %early.1.half), custom_call_target="tpu_custom_call" | custom-call | tf_op jit(solution)/shard_map/late/pallas_call | solution.py:294
  76.7 6.3 %all-to-all-start.1 = ((bf16[32,72,512]{2,1,0:T(8,128)(2,1)}), bf16[32,72,512]{2,1,0:T(8,128)(2,1)}, u32[]{:S(2)}, u32[]{:S(2)}) async-start(bf16[32,72,512]{2,1,0:T(8,128)(2,1)} %late.1), calls=%async_computation.1 | async-start | bytes 4718592 | tf_op jit(solution)/shard_map/all_to_all | solution.py:389
  83.6 31.4 %all-to-all-done.1.got = bf16[32,72,512]{2,1,0:T(8,128)(2,1)} async-done(((bf16[32,72,512]{2,1,0:T(8,128)(2,1)}), bf16[32,72,512]{2,1,0:T(8,128)(2,1)}, u32[]{:S(2)}, u32[]{:S(2)}) %all-to-all-start.1) | async-done | bytes 2359328 | tf_op jit(solution)/shard_map/all_to_all | solution.py:389
  115.0 2.6 %gather.1 = (f32[24,768]{1,0:T(8,128)S(1)}, bf16[24,768]{1,0:T(8,128)(2,1)S(1)}, bf16[24,768]{1,0:T(8,128)(2,1)S(1)}, bf16[24,768]{1,0:T(8,128)(2,1)S(1)}) custom-call(s32[4,4,2,2]{3,2,1,0:T(2,128)S(1)} %pad_add_fusion.peers, bf16[32,72,512]{2,1,0:T(8,128)(2,1)} %all-to-all-done.1.got, f32[96,768]{1,0:T(8,128)S(1)} %blank.1.start), custom_call_target="tpu_custom_call" | custom-call | tf_op jit(solution)/shard_map/gather/pallas_call | solution.py:349
  117.6 2.7 %collective-permute-start.12 = (bf16[24,768]{1,0:T(8,128)(2,1)S(1)}, bf16[24,768]{1,0:T(8,128)(2,1)S(1)}, u32[]{:S(2)}, u32[]{:S(2)}) collective-permute-start(bf16[24,768]{1,0:T(8,128)(2,1)S(1)} %get-tuple-element.48), channel_id=1, source_target_pairs={{0,32},{16,48},{32,0},{48,16},{1,33},{17,49},{33,1},{49,17},{2,34}... | collective-permute-start | bytes 110600 | tf_op jit(solution)/shard_map/ppermute | solution.py:361
  120.3 3.7 %collective-permute-start.13 = (bf16[24,768]{1,0:T(8,128)(2,1)S(1)}, bf16[24,768]{1,0:T(8,128)(2,1)S(1)}, u32[]{:S(2)}, u32[]{:S(2)}) collective-permute-start(bf16[24,768]{1,0:T(8,128)(2,1)S(1)} %get-tuple-element.49), channel_id=1, source_target_pairs={{0,16},{16,32},{32,48},{48,0},{1,17},{17,33},{33,49},{49,1},{2,18}... | collective-permute-start | bytes 110600 | tf_op jit(solution)/shard_map/ppermute | solution.py:361
  124.0 2.0 %collective-permute-done.12 = bf16[24,768]{1,0:T(8,128)(2,1)S(1)} collective-permute-done((bf16[24,768]{1,0:T(8,128)(2,1)S(1)}, bf16[24,768]{1,0:T(8,128)(2,1)S(1)}, u32[]{:S(2)}, u32[]{:S(2)}) %collective-permute-start.12) | collective-permute-done | bytes 36896 | tf_op jit(solution)/shard_map/ppermute | solution.py:361
  126.0 4.1 %collective-permute-done.14 = bf16[24,768]{1,0:T(8,128)(2,1)S(1)} collective-permute-done((bf16[24,768]{1,0:T(8,128)(2,1)S(1)}, bf16[24,768]{1,0:T(8,128)(2,1)S(1)}, u32[]{:S(2)}, u32[]{:S(2)}) %collective-permute-start.14) | collective-permute-done | bytes 36896 | tf_op jit(solution)/shard_map/ppermute | solution.py:361
  (45 shorter events, 14.3 us)
Async XLA Ops:
  0.0 12.2 %collective-permute-start = (s32[2,2]{1,0:T(2,128)}, s32[2,2]{1,0:T(2,128)S(1)}, u32[]{:S(2)}, u32[]{:S(2)}) collective-permute-start(s32[2,2]{1,0:T(2,128)} %tiles.10), channel_id=1, source_target_pairs={{0,1},{1,2},{2,3},{3,0},{4,5},{5,6},{6,7},{7,4},{8,9},{9,10},{10,1... | collective-permute-start | bytes 56 | tf_op jit(solution)/shard_map/ppermute | solution.py:361
  1.6 13.4 %collective-permute-start.1 = (s32[2,2]{1,0:T(2,128)}, s32[2,2]{1,0:T(2,128)S(1)}, u32[]{:S(2)}, u32[]{:S(2)}) collective-permute-start(s32[2,2]{1,0:T(2,128)} %tiles.10), channel_id=1, source_target_pairs={{0,2},{1,3},{2,0},{3,1},{4,6},{5,7},{6,4},{7,5},{8,10},{9,11},{10,... | collective-permute-start | bytes 56 | tf_op jit(solution)/shard_map/ppermute | solution.py:361
  4.5 10.5 %collective-permute-start.2 = (s32[2,2]{1,0:T(2,128)}, s32[2,2]{1,0:T(2,128)S(1)}, u32[]{:S(2)}, u32[]{:S(2)}) collective-permute-start(s32[2,2]{1,0:T(2,128)} %tiles.10), channel_id=1, source_target_pairs={{0,3},{1,0},{2,1},{3,2},{4,7},{5,4},{6,5},{7,6},{8,11},{9,8},{10,9... | collective-permute-start | bytes 56 | tf_op jit(solution)/shard_map/ppermute | solution.py:361
  6.6 17.6 %collective-permute-start.6 = (bf16[24,768]{1,0:T(8,128)(2,1)S(1)}, bf16[24,768]{1,0:T(8,128)(2,1)S(1)}, u32[]{:S(2)}, u32[]{:S(2)}) collective-permute-start(bf16[24,768]{1,0:T(8,128)(2,1)S(1)} %reshape.9.own), channel_id=1, source_target_pairs={{0,16},{16,32},{32,48},{48,0},{1,17},{17,33},{33,49},{49,1},{2,18}... | collective-permute-start | bytes 110600 | tf_op jit(solution)/shard_map/ppermute | solution.py:361
  11.2 13.1 %collective-permute-start.7 = (bf16[24,768]{1,0:T(8,128)(2,1)S(1)}, bf16[24,768]{1,0:T(8,128)(2,1)S(1)}, u32[]{:S(2)}, u32[]{:S(2)}) collective-permute-start(bf16[24,768]{1,0:T(8,128)(2,1)S(1)} %reshape.9.own), channel_id=1, source_target_pairs={{0,32},{16,48},{32,0},{48,16},{1,33},{17,49},{33,1},{49,17},{2,34}... | collective-permute-start | bytes 110600 | tf_op jit(solution)/shard_map/ppermute | solution.py:361
  12.2 12.1 %collective-permute-start.8 = (bf16[24,768]{1,0:T(8,128)(2,1)S(1)}, bf16[24,768]{1,0:T(8,128)(2,1)S(1)}, u32[]{:S(2)}, u32[]{:S(2)}) collective-permute-start(bf16[24,768]{1,0:T(8,128)(2,1)S(1)} %reshape.9.own), channel_id=1, source_target_pairs={{0,48},{16,0},{32,16},{48,32},{1,49},{17,1},{33,17},{49,33},{2,50}... | collective-permute-start | bytes 110600 | tf_op jit(solution)/shard_map/ppermute | solution.py:361
  15.7 4.9 %collective-permute-start.3 = (s32[4,2,2]{2,1,0:T(2,128)S(1)}, s32[4,2,2]{2,1,0:T(2,128)S(1)}, u32[]{:S(2)}, u32[]{:S(2)}) collective-permute-start(s32[4,2,2]{2,1,0:T(2,128)S(1)} %pad_add_fusion.1), channel_id=1, source_target_pairs={{0,4},{4,8},{8,12},{12,0},{1,5},{5,9},{9,13},{13,1},{2,6},{6,10},{... | collective-permute-start | bytes 200 | tf_op jit(solution)/shard_map/ppermute | solution.py:361
  17.2 5.1 %collective-permute-start.4 = (s32[4,2,2]{2,1,0:T(2,128)S(1)}, s32[4,2,2]{2,1,0:T(2,128)S(1)}, u32[]{:S(2)}, u32[]{:S(2)}) collective-permute-start(s32[4,2,2]{2,1,0:T(2,128)S(1)} %pad_add_fusion.1), channel_id=1, source_target_pairs={{0,8},{4,12},{8,0},{12,4},{1,9},{5,13},{9,1},{13,5},{2,10},{6,14},... | collective-permute-start | bytes 200 | tf_op jit(solution)/shard_map/ppermute | solution.py:361
  20.6 3.6 %collective-permute-start.5 = (s32[4,2,2]{2,1,0:T(2,128)S(1)}, s32[4,2,2]{2,1,0:T(2,128)S(1)}, u32[]{:S(2)}, u32[]{:S(2)}) collective-permute-start(s32[4,2,2]{2,1,0:T(2,128)S(1)} %pad_add_fusion.1), channel_id=1, source_target_pairs={{0,12},{4,0},{8,4},{12,8},{1,13},{5,1},{9,5},{13,9},{2,14},{6,2},{... | collective-permute-start | bytes 200 | tf_op jit(solution)/shard_map/ppermute | solution.py:361
  26.9 5.1 %copy-start.2 = (s32[2,2]{1,0:T(2,128)S(1)}, s32[2,2]{1,0:T(2,128)}, u32[]{:S(2)}) copy-start(s32[2,2]{1,0:T(2,128)} %tiles.10) | copy-start | bytes 52
  26.9 5.1 %copy-start.4 = (bf16[2,512,512]{2,1,0:T(8,128)(2,1)S(1)}, bf16[2,512,512]{2,1,0:T(8,128)(2,1)}, u32[]{:S(2)}) copy-start(bf16[2,512,512]{2,1,0:T(8,128)(2,1)} %rows) | copy-start | bytes 3145732
  27.0 32.5 %all-to-all-start = ((bf16[32,72,512]{2,1,0:T(8,128)(2,1)}), bf16[32,72,512]{2,1,0:T(8,128)(2,1)S(1)}, u32[]{:S(2)}, u32[]{:S(2)}) async-start(bf16[32,72,512]{2,1,0:T(8,128)(2,1)} %pack.1), calls=%async_computation | async-start | bytes 4718592 | tf_op jit(solution)/shard_map/all_to_all | solution.py:373
  32.1 1.6 %copy-start.3 = (bf16[2,2,512,512]{3,2,1,0:T(8,128)(2,1)S(1)}, bf16[2,2,512,512]{3,2,1,0:T(8,128)(2,1)}, u32[]{:S(2)}) copy-start(bf16[2,2,512,512]{3,2,1,0:T(8,128)(2,1)} %cot.1) | copy-start | bytes 6291460
  39.4 1.3 %copy-start = (f32[512,1024]{1,0:T(8,128)}, f32[512,1024]{1,0:T(8,128)S(1)}, u32[]{:S(2)}) copy-start(f32[512,1024]{1,0:T(8,128)S(1)} %get-tuple-element.33.state.local) | copy-start | bytes 6291460
  40.7 1.4 %copy-start.7 = (bf16[1024,1024]{1,0:T(8,128)(2,1)}, bf16[1024,1024]{1,0:T(8,128)(2,1)S(1)}, u32[]{:S(2)}) copy-start(bf16[1024,1024]{1,0:T(8,128)(2,1)S(1)} %get-tuple-element.35.m1) | copy-start | bytes 6291460
  42.1 1.4 %copy-start.8 = (bf16[1024,1024]{1,0:T(8,128)(2,1)}, bf16[1024,1024]{1,0:T(8,128)(2,1)S(1)}, u32[]{:S(2)}) copy-start(bf16[1024,1024]{1,0:T(8,128)(2,1)S(1)} %get-tuple-element.36.m2) | copy-start | bytes 6291460
  59.6 6.0 %collective-permute-start.9 = (bf16[16,72,512]{2,1,0:T(8,128)(2,1)S(1)}, bf16[16,72,512]{2,1,0:T(8,128)(2,1)S(1)}, u32[]{:S(2)}, u32[]{:S(2)}) collective-permute-start(bf16[16,72,512]{2,1,0:T(8,128)(2,1)S(1)} %dynamic-slice_bitcast_fusion), channel_id=1, source_target_pairs={{0,64},{64,0},{1,65},{65,1},{2,66},{66,2},{3,67},{67,3},{4,68},{68... | collective-permute-start | bytes 3538952 | tf_op jit(solution)/shard_map/ppermute | solution.py:361
  65.0 7.4 %collective-permute-start.11 = (bf16[512,1024]{1,0:T(8,128)(2,1)S(1)}, bf16[512,1024]{1,0:T(8,128)(2,1)S(1)}, u32[]{:S(2)}, u32[]{:S(2)}) collective-permute-start(bf16[512,1024]{1,0:T(8,128)(2,1)S(1)} %get-tuple-element.42), channel_id=1, source_target_pairs={{0,64},{64,0},{1,65},{65,1},{2,66},{66,2},{3,67},{67,3},{4,68},{68... | collective-permute-start | bytes 3145736 | tf_op jit(solution)/shard_map/ppermute | solution.py:361
  71.4 3.0 %collective-permute-start.10 = (bf16[512,1024]{1,0:T(8,128)(2,1)S(1)}, bf16[512,1024]{1,0:T(8,128)(2,1)S(1)}, u32[]{:S(2)}, u32[]{:S(2)}) collective-permute-start(bf16[512,1024]{1,0:T(8,128)(2,1)S(1)} %get-tuple-element.40), channel_id=1, source_target_pairs={{0,64},{64,0},{1,65},{65,1},{2,66},{66,2},{3,67},{67,3},{4,68},{68... | collective-permute-start | bytes 3145736 | tf_op jit(solution)/shard_map/ppermute | solution.py:361
  72.4 2.0 %copy-start.1 = (f32[512,1024]{1,0:T(8,128)S(1)}, f32[512,1024]{1,0:T(8,128)}, u32[]{:S(2)}) copy-start(f32[512,1024]{1,0:T(8,128)} %copy-done) | copy-start | bytes 6291460
  76.7 38.3 %all-to-all-start.1 = ((bf16[32,72,512]{2,1,0:T(8,128)(2,1)}), bf16[32,72,512]{2,1,0:T(8,128)(2,1)}, u32[]{:S(2)}, u32[]{:S(2)}) async-start(bf16[32,72,512]{2,1,0:T(8,128)(2,1)} %late.1), calls=%async_computation.1 | async-start | bytes 4718592 | tf_op jit(solution)/shard_map/all_to_all | solution.py:389
  117.6 8.3 %collective-permute-start.12 = (bf16[24,768]{1,0:T(8,128)(2,1)S(1)}, bf16[24,768]{1,0:T(8,128)(2,1)S(1)}, u32[]{:S(2)}, u32[]{:S(2)}) collective-permute-start(bf16[24,768]{1,0:T(8,128)(2,1)S(1)} %get-tuple-element.48), channel_id=1, source_target_pairs={{0,32},{16,48},{32,0},{48,16},{1,33},{17,49},{33,1},{49,17},{2,34}... | collective-permute-start | bytes 110600 | tf_op jit(solution)/shard_map/ppermute | solution.py:361
  120.3 5.7 %collective-permute-start.13 = (bf16[24,768]{1,0:T(8,128)(2,1)S(1)}, bf16[24,768]{1,0:T(8,128)(2,1)S(1)}, u32[]{:S(2)}, u32[]{:S(2)}) collective-permute-start(bf16[24,768]{1,0:T(8,128)(2,1)S(1)} %get-tuple-element.49), channel_id=1, source_target_pairs={{0,16},{16,32},{32,48},{48,0},{1,17},{17,33},{33,49},{49,1},{2,18}... | collective-permute-start | bytes 110600 | tf_op jit(solution)/shard_map/ppermute | solution.py:361
  124.0 6.2 %collective-permute-start.14 = (bf16[24,768]{1,0:T(8,128)(2,1)S(1)}, bf16[24,768]{1,0:T(8,128)(2,1)S(1)}, u32[]{:S(2)}, u32[]{:S(2)}) collective-permute-start(bf16[24,768]{1,0:T(8,128)(2,1)S(1)} %get-tuple-element.50), channel_id=1, source_target_pairs={{0,48},{16,0},{32,16},{48,32},{1,49},{17,1},{33,17},{49,33},{2,50}... | collective-permute-start | bytes 110600 | tf_op jit(solution)/shard_map/ppermute | solution.py:361
  (2 other events, 2.4 us)

commit v6 on v5

--- a/solution.py
+++ b/solution.py
@@ -98,30 +98,42 @@
     )(tiles, rows, cols, probe, cot)
 
 
-def pack_kernel(peers, own, one, two, three, out, held, chunks, sems):
+def spread_kernel(own, one, two, three, held):
     zh = lax.axis_index("zh")
+    for hops, piece in enumerate((own, one, two, three)):
+        place = lax.rem(zh - hops + 4, 4)
+        held[pl.ds(pl.multiple_of(place * 24, 8), 24), :] = piece[...].astype(F32)
+
+
+def spread(own, others):
+    return pl.pallas_call(
+        spread_kernel,
+        out_shape=jax.ShapeDtypeStruct((96, OBJ), F32),
+        in_specs=[VMEM] * 4,
+        out_specs=VMEM,
+        compiler_params=params(4),
+        cost_estimate=pl.CostEstimate(flops=4 * 10**9, transcendentals=0, bytes_accessed=10**7),
+        name="spread",
+    )(own, *others)
+
+
+def pack_kernel(peers, held, out, chunks, sems):
     x = lax.axis_index("x")
-    for step, piece in enumerate((own, one, two, three)):
-        place = lax.rem(zh - step + 4, 4)
-        held[pl.ds(pl.multiple_of(place * 24, 8), 24), :] = piece[...].astype(F32)
     lane = lax.broadcasted_iota(jnp.int32, (72, 256), 1)
-    y = lax.axis_index("y")
 
     def moved(i):
         return pltpu.make_async_copy(chunks.at[i], out.at[i], sems.at[i])
 
     def target(t, carry):
-        ahead, below = t // 4, lax.rem(t, 4)
-        place = lax.rem(x - ahead + 4, 4) * 4 + lax.rem(y - below + 4, 4)
         for slot in range(2):
-            first = first_interval(peers[ahead, below, slot, 0], x)
+            first = first_interval(peers[t, slot, 0], x)
             rows = pl.ds(pl.multiple_of(first * 24, 8), 72)
-            wrapped = lane < peers[ahead, below, slot, 1] * TILE
+            wrapped = lane < peers[t, slot, 1] * TILE
             low = held[rows, 0:256]
             high = held[rows, 512:768]
-            chunks[slot * 16 + place, :, 0:256] = jnp.where(wrapped, high, low).astype(BF)
-            chunks[slot * 16 + place, :, 256:512] = held[rows, 256:512].astype(BF)
-            moved(slot * 16 + place).start()
+            chunks[slot * 16 + t, :, 0:256] = jnp.where(wrapped, high, low).astype(BF)
+            chunks[slot * 16 + t, :, 256:512] = held[rows, 256:512].astype(BF)
+            moved(slot * 16 + t).start()
         return carry
 
     def settle(i, carry):
@@ -132,20 +144,19 @@
     lax.fori_loop(0, 32, settle, 0)
 
 
-def pack(peers, own, others):
+def pack(peers, held):
     return pl.pallas_call(
         pack_kernel,
         out_shape=jax.ShapeDtypeStruct((32, 72, W), BF),
-        in_specs=[SMEM] + [VMEM] * 4,
+        in_specs=[SMEM, VMEM],
         out_specs=HBM,
         scratch_shapes=[
-            pltpu.VMEM((96, OBJ), F32),
             pltpu.VMEM((32, 72, W), BF),
             pltpu.SemaphoreType.DMA((32,)),
         ],
         compiler_params=params(16),
         name="pack",
-    )(peers, own, *others)
+    )(peers, held)
 
 
 def place_patch(source, base, patch, row_tile):
@@ -162,7 +173,7 @@
     lax.fori_loop(0, 4, place, 0)
 
 
-def form_contrib(local, remote, contrib, out, sign, used, row_tile, formed=None):
+def form_contrib(local, remote, contrib, out, sign, used, row_tile):
     ar = local[:, 0:W]
     ai = local[:, W:]
     br = remote[:, 0:W].astype(F32)
@@ -179,8 +190,6 @@
         ]
         for y in range(4):
             out[plane * 4 + y] = jnp.concatenate([b[12 * y : 12 * y + 12] for b in blocks]).astype(BF)
-            if formed is not None:
-                formed(plane * 4 + y)
         return carry
 
     lax.fori_loop(0, 4, cut, 0)
@@ -271,23 +280,11 @@
     )(tiles, count, local, remote)
 
 
-def late_kernel(tiles, count, local, remote, half, out, contrib, chunks, sems):
+def late_kernel(tiles, count, local, remote, half, out, contrib):
     core, sign, row_tile = role(tiles)
     used = lax.axis_index("zl") < count[0]
-    whole = pltpu.make_async_copy(half, out.at[pl.ds((1 - core) * 16, 16)], sems.at[16])
-    whole.start()
-
-    def moved(i):
-        return pltpu.make_async_copy(chunks.at[i], out.at[core * 16 + i], sems.at[i])
-
-    form_contrib(local, remote, contrib, chunks, sign, used, row_tile, lambda i: moved(i).start())
-
-    def settle(i, carry):
-        moved(i).wait()
-        return carry
-
-    lax.fori_loop(0, 16, settle, 0)
-    whole.wait()
+    out[pl.ds((1 - core) * 16, 16)] = half[...]
+    form_contrib(local, remote, contrib, out.at[pl.ds(core * 16, 16)], sign, used, row_tile)
 
 
 def late(tiles, count, local, remote, half):
@@ -295,44 +292,25 @@
         late_kernel,
         out_shape=jax.ShapeDtypeStruct((32, 72, W), BF),
         in_specs=[SMEM] * 2 + [VMEM] * 3,
-        out_specs=HBM,
-        scratch_shapes=WORK[:1] + [pltpu.VMEM((16, 72, W), BF), pltpu.SemaphoreType.DMA((17,))],
+        out_specs=VMEM,
+        scratch_shapes=WORK[:1],
         compiler_params=params(24),
         name="late",
     )(tiles, count, local, remote, half)
 
 
-def blank_kernel(tiles, out):
-    out[...] = jnp.zeros((96, OBJ), F32)
-
-
-def blank(tiles):
-    return pl.pallas_call(
-        blank_kernel,
-        out_shape=jax.ShapeDtypeStruct((96, OBJ), F32),
-        in_specs=[SMEM],
-        out_specs=VMEM,
-        compiler_params=params(4),
-        cost_estimate=pl.CostEstimate(flops=4 * 10**9, transcendentals=0, bytes_accessed=10**7),
-        name="blank",
-    )(tiles)
-
-
-def gather_kernel(peers, got, start, own, one, two, three, total):
+def gather_kernel(peers, got, own, one, two, three, total):
     zh = lax.axis_index("zh")
     x = lax.axis_index("x")
-    total[...] = start[...]
+    total[...] = jnp.zeros((96, OBJ), F32)
     lane = lax.broadcasted_iota(jnp.int32, (72, 256), 1)
-    y = lax.axis_index("y")
 
     def source(t, carry):
-        ahead, below = t // 4, lax.rem(t, 4)
-        place = lax.rem(x - ahead + 4, 4) * 4 + lax.rem(y - below + 4, 4)
         for slot in range(2):
-            first = first_interval(peers[ahead, below, slot, 0], x)
+            first = first_interval(peers[t, slot, 0], x)
             rows = pl.ds(pl.multiple_of(first * 24, 8), 72)
-            wrapped = lane < peers[ahead, below, slot, 1] * TILE
-            value = got[slot * 16 + place].astype(F32)
+            wrapped = lane < peers[t, slot, 1] * TILE
+            value = got[slot * 16 + t].astype(F32)
             low = value[:, 0:256]
             total[rows, 0:256] += jnp.where(wrapped, 0.0, low)
             total[rows, 512:768] += jnp.where(wrapped, low, 0.0)
@@ -345,16 +323,33 @@
         out[...] = total[pl.ds(pl.multiple_of(place * 24, 8), 24), :].astype(out.dtype)
 
 
-def gather(peers, got, start):
+def gather(peers, got):
     return pl.pallas_call(
         gather_kernel,
         out_shape=[jax.ShapeDtypeStruct((24, OBJ), F32)] + [jax.ShapeDtypeStruct((24, OBJ), BF)] * 3,
-        in_specs=[SMEM, VMEM, VMEM],
+        in_specs=[SMEM, VMEM],
         out_specs=[VMEM] * 4,
         scratch_shapes=[pltpu.VMEM((96, OBJ), F32)],
         compiler_params=params(16),
         name="gather",
-    )(peers, got, start)
+    )(peers, got)
+
+
+def last_kernel(own, one, two, three, out):
+    total = own[...] + one[...].astype(F32) + two[...].astype(F32) + three[...].astype(F32)
+    out[:, 0, :] = total[0:12]
+    out[:, 1, :] = total[12:24]
+
+
+def last_sum(own, others):
+    return pl.pallas_call(
+        last_kernel,
+        out_shape=jax.ShapeDtypeStruct((12, 2, OBJ), F32),
+        in_specs=[VMEM] * 4,
+        out_specs=VMEM,
+        compiler_params=params(4),
+        name="last_sum",
+    )(own, *others)
 
 
 def turn(value, axis, step, count):
@@ -366,9 +361,9 @@
     piece = transmission.reshape(24, OBJ)
     others = [turn(piece, "zh", hops, 4) for hops in (2, 1, 3)]
     others = [others[1], others[0], others[2]]
-    line = jnp.stack([window_tiles] + [turn(window_tiles, "y", hops, 4) for hops in (1, 2, 3)])
-    peers = jnp.stack([line] + [turn(line, "x", hops, 4) for hops in (1, 2, 3)])
-    sent = pack(peers, piece, others)
+    peers = lax.all_to_all(jnp.broadcast_to(window_tiles[None], (16, 2, 2)), ("x", "y"), 0, 0, tiled=True)
+    peers, held = lax.optimization_barrier((peers, spread(piece, others)))
+    sent = pack(peers, held)
     sent, rows = lax.optimization_barrier((sent, prop_rows))
     own = lax.all_to_all(sent, ("zl", "x", "y"), 0, 0, tiled=True)
     mats = prep(window_tiles, rows, prop_cols, probe_wave, exit_cotangent)
@@ -384,14 +379,10 @@
     last_away = turn(last, "core", 1, 2)
     half = early(window_tiles, slot_count, middle, first_away)
     contrib = late(window_tiles, slot_count, state, last_away, half)
-    contrib = pltpu.with_memory_space_constraint(contrib, pltpu.HBM)
-    contrib, tiles = lax.optimization_barrier((contrib, window_tiles))
     got = lax.all_to_all(contrib, ("zl", "x", "y"), 0, 0, tiled=True)
-    got, start = lax.optimization_barrier((got, blank(tiles)))
-    here, *away = gather(peers, got, start)
-    for hops in (2, 1, 3):
-        here = here + turn(away[hops - 1], "zh", hops, 4).astype(F32)
-    return here.reshape(1, 2, 12, OBJ)
+    here, *away = gather(peers, got)
+    total = last_sum(here, [turn(away[hops - 1], "zh", hops, 4) for hops in (2, 1, 3)])
+    return jnp.transpose(total, (1, 0, 2))[None]
 
 
 def solution(mesh):

time: 131 us -> 130 us (level)
  blocking collectives: 0 us -> 37.4 us
  waiting for transfers between devices: 56.4 us -> 32 us
  starting transfers between devices: 38.6 us -> 26.9 us
  Pallas kernels: 23.8 us -> 21.7 us
  other arithmetic: 1.4 us -> 0 us
    all_to_all x0 -> x1, blocking collectives: none -> 37.4 us  [on_device(): got = lax.all_to_all(contrib, ('zl', 'x', 'y'), 0, 0, tiled=True)]
    all_to_all x1, waiting for transfers between devices: 31.4 us -> 7.52 us  [on_device(): lax.all_to_all(jnp.broadcast_to(window_tiles[None], (16, 2, 2)), ('x', 'y...]
    ppermute x15 -> x9, starting transfers between devices: 27.2 us -> 15.7 us  [turn(): lax.ppermute(value, axis, [(i, (i + step) % count) for i in range(count)])]
    ppermute x15 -> x9, waiting for transfers between devices: 9.03 us -> 7.18 us  [turn(): lax.ppermute(value, axis, [(i, (i + step) % count) for i in range(count)])]
    another operation x3 -> x0, other arithmetic: 1.38 us -> none  [the longest x2 0.69 us: on_device(): peers = jnp.stack([line] + [turn(line, 'x', hops, 4) for hops in (1, 2, 3)])]
    all_to_all x1, waiting for transfers between devices: 16 us -> 17.3 us  [on_device(): own = lax.all_to_all(sent, ('zl', 'x', 'y'), 0, 0, tiled=True)]
  transfers between devices with their start and end apart: 17 -> 11, of which waited for: 7 -> 5; matrix products, arithmetic and copies ran while one was open for 2% -> 1% of each run, Pallas kernels for 12% -> 12%
where the time goes in v6:
time: 130 us; the launch traced here: 129 us
  blocking collectives  37.4 us (29%)
  waiting for transfers between devices  32 us (25%)
  starting transfers between devices  26.9 us (21%)
  Pallas kernels  21.7 us (17%)
  local copies, waits for them, and re-layouts  10.3 us (8%)
    all_to_all x1, blocking collectives, on_device(): got = lax.all_to_all(contrib, ('zl', 'x', 'y'), 0, 0, tiled=True)  37.4 us
    all_to_all x1, waiting for transfers between devices, on_device(): own = lax.all_to_all(sent, ('zl', 'x', 'y'), 0, 0, tiled=True)  17.3 us
    ppermute x9, starting transfers between devices, turn(): lax.ppermute(value, axis, [(i, (i + step) % count) for i in range(count)])  15.7 us
    unnamed x19, local copies, waits for them, and re-layouts  8.95 us
    all_to_all x1, waiting for transfers between devices, on_device(): lax.all_to_all(jnp.broadcast_to(window_tiles[None], (16, 2, 2)), ('x', 'y...  7.52 us
    ppermute x9, waiting for transfers between devices, turn(): lax.ppermute(value, axis, [(i, (i + step) % count) for i in range(count)])  7.18 us
    all_to_all x1, starting transfers between devices, on_device(): lax.all_to_all(jnp.broadcast_to(window_tiles[None], (16, 2, 2)), ('x', 'y...  7.03 us
    pallas_call x1, Pallas kernels, close_steps(): pl.pallas_call(close_kernel, out_shape=[STATE, SENT], in_specs=[SMEM] + [...  5.86 us
  transfers between devices with their start and end apart: 11, of which 5 were waited for; matrix products, arithmetic and copies ran while one was open for 1% of the time, Pallas kernels for 12%

profile of v6, /device:TPU:64, one launch (start us, length us, event | category | flops | bytes accessed | tf_op | source)
XLA Modules:
  0.0 129.2 jit_solution(651456473778838166)
XLA Ops:
  0.8 4.6 %collective-permute-start = (bf16[24,768]{1,0:T(8,128)(2,1)S(1)}, bf16[24,768]{1,0:T(8,128)(2,1)S(1)}, u32[]{:S(2)}, u32[]{:S(2)}) collective-permute-start(bf16[24,768]{1,0:T(8,128)(2,1)S(1)} %reshape.7.own), channel_id=1, source_target_pairs={{0,16},{16,32},{32,48},{48,0},{1,17},{17,33},{33,49},{49,1},{2,18}... | collective-permute-start | bytes 110600 | tf_op jit(solution)/shard_map/ppermute | solution.py:356
  6.4 2.8 %collective-permute-start.2 = (bf16[24,768]{1,0:T(8,128)(2,1)S(1)}, bf16[24,768]{1,0:T(8,128)(2,1)S(1)}, u32[]{:S(2)}, u32[]{:S(2)}) collective-permute-start(bf16[24,768]{1,0:T(8,128)(2,1)S(1)} %reshape.7.own), channel_id=1, source_target_pairs={{0,48},{16,0},{32,16},{48,32},{1,49},{17,1},{33,17},{49,33},{2,50}... | collective-permute-start | bytes 110600 | tf_op jit(solution)/shard_map/ppermute | solution.py:356
  9.2 1.3 broadcast_in_dim.4
  10.5 7.0 %all-to-all-start = ((s32[16,2,2]{2,1,0:T(2,128)}), s32[16,2,2]{2,1,0:T(2,128)S(1)}, u32[]{:S(2)}, u32[]{:S(2)}) async-start(s32[16,2,2]{2,1,0:T(2,128)} %broadcast_in_dim.4), calls=%async_computation | async-start | bytes 32768 | tf_op jit(solution)/shard_map/all_to_all | solution.py:364
  17.6 7.5 %all-to-all-done.peers = s32[16,2,2]{2,1,0:T(2,128)S(1)} async-done(((s32[16,2,2]{2,1,0:T(2,128)}), s32[16,2,2]{2,1,0:T(2,128)S(1)}, u32[]{:S(2)}, u32[]{:S(2)}) %all-to-all-start) | async-done | bytes 288 | tf_op jit(solution)/shard_map/all_to_all | solution.py:364
  25.1 2.6 %pack.1 = bf16[32,72,512]{2,1,0:T(8,128)(2,1)} custom-call(s32[16,2,2]{2,1,0:T(2,128)S(1)} %all-to-all-done.peers, f32[96,768]{1,0:T(8,128)S(1)} %spread.1.held), custom_call_target="tpu_custom_call" | custom-call | tf_op jit(solution)/shard_map/pack/pallas_call | solution.py:148
  27.7 4.2 %all-to-all-start.1 = ((bf16[32,72,512]{2,1,0:T(8,128)(2,1)}), bf16[32,72,512]{2,1,0:T(8,128)(2,1)S(1)}, u32[]{:S(2)}, u32[]{:S(2)}) async-start(bf16[32,72,512]{2,1,0:T(8,128)(2,1)} %pack.1), calls=%async_computation.1 | async-start | bytes 4718592 | tf_op jit(solution)/shard_map/all_to_all | solution.py:368
  32.0 1.6 %copy-done.3 = bf16[2,2,512,512]{3,2,1,0:T(8,128)(2,1)S(1)} copy-done((bf16[2,2,512,512]{3,2,1,0:T(8,128)(2,1)S(1)}, bf16[2,2,512,512]{3,2,1,0:T(8,128)(2,1)}, u32[]{:S(2)}) %copy-start.3) | copy-done | bytes 2097176
  33.5 1.2 copy-done.5
  36.0 3.1 %prep.1 = (bf16[1024,1024]{1,0:T(8,128)(2,1)S(1)}, bf16[1024,1024]{1,0:T(8,128)(2,1)S(1)}, f32[512,1024]{1,0:T(8,128)S(1)}) custom-call(s32[2,2]{1,0:T(2,128)S(1)} %copy-done.2, bf16[2,512,512]{2,1,0:T(8,128)(2,1)S(1)} %copy-done.4, bf16[2,512,512]{2,1,0:T(8,128)(2,1)S(1)} %copy-done.5, bf16[2,512,512]{2,1,0:T(8,128)(2,1)S(1)} %copy-done.6, ...), custom_call_target="tpu_custom_call" | custom-call | flops 4000000000 | bytes 20000000 | tf_op jit(solution)/shard_map/prep/pallas_call | solution.py:89
  39.1 1.3 %copy-done = f32[512,1024]{1,0:T(8,128)} copy-done((f32[512,1024]{1,0:T(8,128)}, f32[512,1024]{1,0:T(8,128)S(1)}, u32[]{:S(2)}) %copy-start) | copy-done | bytes 2097176
  40.4 1.4 %copy-done.7 = bf16[1024,1024]{1,0:T(8,128)(2,1)} copy-done((bf16[1024,1024]{1,0:T(8,128)(2,1)}, bf16[1024,1024]{1,0:T(8,128)(2,1)S(1)}, u32[]{:S(2)}) %copy-start.7) | copy-done | bytes 2097176
  41.8 1.4 %copy-done.8 = bf16[1024,1024]{1,0:T(8,128)(2,1)} copy-done((bf16[1024,1024]{1,0:T(8,128)(2,1)}, bf16[1024,1024]{1,0:T(8,128)(2,1)S(1)}, u32[]{:S(2)}) %copy-start.8) | copy-done | bytes 2097176
  43.2 17.3 %all-to-all-done.1.own = bf16[32,72,512]{2,1,0:T(8,128)(2,1)S(1)} async-done(((bf16[32,72,512]{2,1,0:T(8,128)(2,1)}), bf16[32,72,512]{2,1,0:T(8,128)(2,1)S(1)}, u32[]{:S(2)}, u32[]{:S(2)}) %all-to-all-start.1) | async-done | bytes 2359328 | tf_op jit(solution)/shard_map/all_to_all | solution.py:368
  60.9 5.3 %open_step.1 = (f32[512,1024]{1,0:T(8,128)S(1)}, bf16[512,1024]{1,0:T(8,128)(2,1)S(1)}, bf16[1024,1024]{1,0:T(8,128)(2,1)S(1)}, bf16[1024,1024]{1,0:T(8,128)(2,1)S(1)}) custom-call(s32[2,2]{1,0:T(2,128)S(1)} %copy-done.2, bf16[32,72,512]{2,1,0:T(8,128)(2,1)S(1)} %all-to-all-done.1.own, bf16[1024,1024]{1,0:T(8,128)(2,1)} %copy-done.7, ...), custom_call_target="tpu_custom_call" | custom-call | flops 4000000000 | bytes 10000000 | tf_op jit(solution)/shard_map/open_step/pallas_call | solution.py:227
  66.8 5.9 %close_steps.1 = (f32[512,1024]{1,0:T(8,128)S(1)}, bf16[512,1024]{1,0:T(8,128)(2,1)S(1)}) custom-call(s32[2,2]{1,0:T(2,128)S(1)} %copy-done.2, bf16[32,72,512]{2,1,0:T(8,128)(2,1)S(1)} %all-to-all-done.1.own, bf16[16,72,512]{2,1,0:T(8,128)(2,1)S(1)} %collective-permute-done.3.other, bf16[1024,1024]{1,0:T(8,128)(2,1)S(1)} %get-tuple-element.37.v1, ...), custom_call_target="tpu_custom_call" | custom-call | flops 8000000000 | bytes 10000000 | tf_op jit(solution)/shard_map/close_steps/pallas_call | solution.py:252
  73.4 1.2 early.1.half
  75.4 1.3 %late.1 = bf16[32,72,512]{2,1,0:T(8,128)(2,1)S(1)} custom-call(s32[2,2]{1,0:T(2,128)S(1)} %copy-done.2, s32[1]{0:T(128)S(6)} %copy.10.count, f32[512,1024]{1,0:T(8,128)S(1)} %copy-done.1, bf16[512,1024]{1,0:T(8,128)(2,1)S(1)} %collective-permute-done.4.remote, bf16[16,72,512]{2,1,0:T(8,128)(2,1)S(1)} %early.1.half), custom_call_target="tpu_custom_call" | custom-call | tf_op jit(solution)/shard_map/late/pallas_call | solution.py:291
  76.7 37.4 %all_to_all.15.got = bf16[32,72,512]{2,1,0:T(8,128)(2,1)S(1)} all-to-all(bf16[32,72,512]{2,1,0:T(8,128)(2,1)S(1)} %late.1), channel_id=1, replica_groups=mesh['zl'=2,'core'=2,'zh'=4,'x'=4,'y'=4] {'zl','x','y'}, dimensions={0} | all-to-all | bytes 4718592 | tf_op jit(solution)/shard_map/all_to_all | solution.py:382
  114.1 1.6 %gather.1 = (f32[24,768]{1,0:T(8,128)S(1)}, bf16[24,768]{1,0:T(8,128)(2,1)S(1)}, bf16[24,768]{1,0:T(8,128)(2,1)S(1)}, bf16[24,768]{1,0:T(8,128)(2,1)S(1)}) custom-call(s32[16,2,2]{2,1,0:T(2,128)S(1)} %all-to-all-done.peers, bf16[32,72,512]{2,1,0:T(8,128)(2,1)S(1)} %all_to_all.15.got), custom_call_target="tpu_custom_call" | custom-call | tf_op jit(solution)/shard_map/gather/pallas_call | solution.py:327
  115.8 2.2 %collective-permute-start.6 = (bf16[24,768]{1,0:T(8,128)(2,1)S(1)}, bf16[24,768]{1,0:T(8,128)(2,1)S(1)}, u32[]{:S(2)}, u32[]{:S(2)}) collective-permute-start(bf16[24,768]{1,0:T(8,128)(2,1)S(1)} %get-tuple-element.44), channel_id=1, source_target_pairs={{0,32},{16,48},{32,0},{48,16},{1,33},{17,49},{33,1},{49,17},{2,34}... | collective-permute-start | bytes 110600 | tf_op jit(solution)/shard_map/ppermute | solution.py:356
  118.0 4.1 %collective-permute-start.7 = (bf16[24,768]{1,0:T(8,128)(2,1)S(1)}, bf16[24,768]{1,0:T(8,128)(2,1)S(1)}, u32[]{:S(2)}, u32[]{:S(2)}) collective-permute-start(bf16[24,768]{1,0:T(8,128)(2,1)S(1)} %get-tuple-element.45), channel_id=1, source_target_pairs={{0,16},{16,32},{32,48},{48,0},{1,17},{17,33},{33,49},{49,1},{2,18}... | collective-permute-start | bytes 110600 | tf_op jit(solution)/shard_map/ppermute | solution.py:356
  122.1 2.0 %collective-permute-done.6.one = bf16[24,768]{1,0:T(8,128)(2,1)S(1)} collective-permute-done((bf16[24,768]{1,0:T(8,128)(2,1)S(1)}, bf16[24,768]{1,0:T(8,128)(2,1)S(1)}, u32[]{:S(2)}, u32[]{:S(2)}) %collective-permute-start.6) | collective-permute-done | bytes 36896 | tf_op jit(solution)/shard_map/ppermute | solution.py:356
  124.1 4.5 %collective-permute-done.8.three = bf16[24,768]{1,0:T(8,128)(2,1)S(1)} collective-permute-done((bf16[24,768]{1,0:T(8,128)(2,1)S(1)}, bf16[24,768]{1,0:T(8,128)(2,1)S(1)}, u32[]{:S(2)}, u32[]{:S(2)}) %collective-permute-start.8) | collective-permute-done | bytes 36896 | tf_op jit(solution)/shard_map/ppermute | solution.py:356
  (30 shorter events, 5.5 us)
Async XLA Ops:
  0.8 16.7 %collective-permute-start = (bf16[24,768]{1,0:T(8,128)(2,1)S(1)}, bf16[24,768]{1,0:T(8,128)(2,1)S(1)}, u32[]{:S(2)}, u32[]{:S(2)}) collective-permute-start(bf16[24,768]{1,0:T(8,128)(2,1)S(1)} %reshape.7.own), channel_id=1, source_target_pairs={{0,16},{16,32},{32,48},{48,0},{1,17},{17,33},{33,49},{49,1},{2,18}... | collective-permute-start | bytes 110600 | tf_op jit(solution)/shard_map/ppermute | solution.py:356
  5.4 12.2 %collective-permute-start.1 = (bf16[24,768]{1,0:T(8,128)(2,1)S(1)}, bf16[24,768]{1,0:T(8,128)(2,1)S(1)}, u32[]{:S(2)}, u32[]{:S(2)}) collective-permute-start(bf16[24,768]{1,0:T(8,128)(2,1)S(1)} %reshape.7.own), channel_id=1, source_target_pairs={{0,32},{16,48},{32,0},{48,16},{1,33},{17,49},{33,1},{49,17},{2,34}... | collective-permute-start | bytes 110600 | tf_op jit(solution)/shard_map/ppermute | solution.py:356
  6.4 11.2 %collective-permute-start.2 = (bf16[24,768]{1,0:T(8,128)(2,1)S(1)}, bf16[24,768]{1,0:T(8,128)(2,1)S(1)}, u32[]{:S(2)}, u32[]{:S(2)}) collective-permute-start(bf16[24,768]{1,0:T(8,128)(2,1)S(1)} %reshape.7.own), channel_id=1, source_target_pairs={{0,48},{16,0},{32,16},{48,32},{1,49},{17,1},{33,17},{49,33},{2,50}... | collective-permute-start | bytes 110600 | tf_op jit(solution)/shard_map/ppermute | solution.py:356
  10.5 14.6 %all-to-all-start = ((s32[16,2,2]{2,1,0:T(2,128)}), s32[16,2,2]{2,1,0:T(2,128)S(1)}, u32[]{:S(2)}, u32[]{:S(2)}) async-start(s32[16,2,2]{2,1,0:T(2,128)} %broadcast_in_dim.4), calls=%async_computation | async-start | bytes 32768 | tf_op jit(solution)/shard_map/all_to_all | solution.py:364
  27.7 4.2 %copy-start.2 = (s32[2,2]{1,0:T(2,128)S(1)}, s32[2,2]{1,0:T(2,128)}, u32[]{:S(2)}) copy-start(s32[2,2]{1,0:T(2,128)} %tiles.9) | copy-start | bytes 52
  27.7 4.2 %copy-start.4 = (bf16[2,512,512]{2,1,0:T(8,128)(2,1)S(1)}, bf16[2,512,512]{2,1,0:T(8,128)(2,1)}, u32[]{:S(2)}) copy-start(bf16[2,512,512]{2,1,0:T(8,128)(2,1)} %rows) | copy-start | bytes 3145732
  27.7 32.8 %all-to-all-start.1 = ((bf16[32,72,512]{2,1,0:T(8,128)(2,1)}), bf16[32,72,512]{2,1,0:T(8,128)(2,1)S(1)}, u32[]{:S(2)}, u32[]{:S(2)}) async-start(bf16[32,72,512]{2,1,0:T(8,128)(2,1)} %pack.1), calls=%async_computation.1 | async-start | bytes 4718592 | tf_op jit(solution)/shard_map/all_to_all | solution.py:368
  31.9 1.6 %copy-start.3 = (bf16[2,2,512,512]{3,2,1,0:T(8,128)(2,1)S(1)}, bf16[2,2,512,512]{3,2,1,0:T(8,128)(2,1)}, u32[]{:S(2)}) copy-start(bf16[2,2,512,512]{3,2,1,0:T(8,128)(2,1)} %cot.1) | copy-start | bytes 6291460
  33.5 1.2 copy-start.5
  34.8 1.2 copy-start.6
  39.1 1.3 %copy-start = (f32[512,1024]{1,0:T(8,128)}, f32[512,1024]{1,0:T(8,128)S(1)}, u32[]{:S(2)}) copy-start(f32[512,1024]{1,0:T(8,128)S(1)} %get-tuple-element.33.state.local) | copy-start | bytes 6291460
  40.4 1.4 %copy-start.7 = (bf16[1024,1024]{1,0:T(8,128)(2,1)}, bf16[1024,1024]{1,0:T(8,128)(2,1)S(1)}, u32[]{:S(2)}) copy-start(bf16[1024,1024]{1,0:T(8,128)(2,1)S(1)} %get-tuple-element.35.m1) | copy-start | bytes 6291460
  41.8 1.4 %copy-start.8 = (bf16[1024,1024]{1,0:T(8,128)(2,1)}, bf16[1024,1024]{1,0:T(8,128)(2,1)S(1)}, u32[]{:S(2)}) copy-start(bf16[1024,1024]{1,0:T(8,128)(2,1)S(1)} %get-tuple-element.36.m2) | copy-start | bytes 6291460
  60.6 6.2 %collective-permute-start.3 = (bf16[16,72,512]{2,1,0:T(8,128)(2,1)S(1)}, bf16[16,72,512]{2,1,0:T(8,128)(2,1)S(1)}, u32[]{:S(2)}, u32[]{:S(2)}) collective-permute-start(bf16[16,72,512]{2,1,0:T(8,128)(2,1)S(1)} %dynamic-slice_bitcast_fusion), channel_id=1, source_target_pairs={{0,64},{64,0},{1,65},{65,1},{2,66},{66,2},{3,67},{67,3},{4,68},{68... | collective-permute-start | bytes 3538952 | tf_op jit(solution)/shard_map/ppermute | solution.py:356
  66.2 7.2 %collective-permute-start.5 = (bf16[512,1024]{1,0:T(8,128)(2,1)S(1)}, bf16[512,1024]{1,0:T(8,128)(2,1)S(1)}, u32[]{:S(2)}, u32[]{:S(2)}) collective-permute-start(bf16[512,1024]{1,0:T(8,128)(2,1)S(1)} %get-tuple-element.42), channel_id=1, source_target_pairs={{0,64},{64,0},{1,65},{65,1},{2,66},{66,2},{3,67},{67,3},{4,68},{68... | collective-permute-start | bytes 3145736 | tf_op jit(solution)/shard_map/ppermute | solution.py:356
  72.7 2.7 %collective-permute-start.4 = (bf16[512,1024]{1,0:T(8,128)(2,1)S(1)}, bf16[512,1024]{1,0:T(8,128)(2,1)S(1)}, u32[]{:S(2)}, u32[]{:S(2)}) collective-permute-start(bf16[512,1024]{1,0:T(8,128)(2,1)S(1)} %get-tuple-element.40), channel_id=1, source_target_pairs={{0,64},{64,0},{1,65},{65,1},{2,66},{66,2},{3,67},{67,3},{4,68},{68... | collective-permute-start | bytes 3145736 | tf_op jit(solution)/shard_map/ppermute | solution.py:356
  73.4 2.0 %copy-start.1 = (f32[512,1024]{1,0:T(8,128)S(1)}, f32[512,1024]{1,0:T(8,128)}, u32[]{:S(2)}) copy-start(f32[512,1024]{1,0:T(8,128)} %copy-done) | copy-start | bytes 6291460
  115.8 8.3 %collective-permute-start.6 = (bf16[24,768]{1,0:T(8,128)(2,1)S(1)}, bf16[24,768]{1,0:T(8,128)(2,1)S(1)}, u32[]{:S(2)}, u32[]{:S(2)}) collective-permute-start(bf16[24,768]{1,0:T(8,128)(2,1)S(1)} %get-tuple-element.44), channel_id=1, source_target_pairs={{0,32},{16,48},{32,0},{48,16},{1,33},{17,49},{33,1},{49,17},{2,34}... | collective-permute-start | bytes 110600 | tf_op jit(solution)/shard_map/ppermute | solution.py:356
  118.0 6.1 %collective-permute-start.7 = (bf16[24,768]{1,0:T(8,128)(2,1)S(1)}, bf16[24,768]{1,0:T(8,128)(2,1)S(1)}, u32[]{:S(2)}, u32[]{:S(2)}) collective-permute-start(bf16[24,768]{1,0:T(8,128)(2,1)S(1)} %get-tuple-element.45), channel_id=1, source_target_pairs={{0,16},{16,32},{32,48},{48,0},{1,17},{17,33},{33,49},{49,1},{2,18}... | collective-permute-start | bytes 110600 | tf_op jit(solution)/shard_map/ppermute | solution.py:356
  122.1 6.5 %collective-permute-start.8 = (bf16[24,768]{1,0:T(8,128)(2,1)S(1)}, bf16[24,768]{1,0:T(8,128)(2,1)S(1)}, u32[]{:S(2)}, u32[]{:S(2)}) collective-permute-start(bf16[24,768]{1,0:T(8,128)(2,1)S(1)} %get-tuple-element.46), channel_id=1, source_target_pairs={{0,48},{16,0},{32,16},{48,32},{1,49},{17,1},{33,17},{49,33},{2,50}... | collective-permute-start | bytes 110600 | tf_op jit(solution)/shard_map/ppermute | solution.py:356

commit v7 on v6

--- a/solution.py
+++ b/solution.py
@@ -34,15 +34,15 @@
 
 
 def form_left(state, patch, sign, left):
-    sr = state[:, 0:W]
-    si = state[:, W:]
+    sr = state[:, 0:W].astype(F32)
+    si = state[:, W:].astype(F32)
     pr = patch[0, PAD : PAD + W, :]
     pi = patch[1, PAD : PAD + W, :] * sign
     left[0:W, :] = (sr * pr - si * pi).astype(BF)
     left[W:, :] = (sr * pi + si * pr).astype(BF)
 
 
-def prep_kernel(tiles, rows, cols, probe, cot, m1, m2, state, left, right):
+def prep_kernel(tiles, rows, cols, probe, cot, upper1, upper2, state, m1, m2, left, right):
     slot = lax.axis_index("zl")
     core = lax.axis_index("core")
     shift = tiles[slot, 1] * TILE
@@ -63,7 +63,7 @@
         m2[W:, 0:W] = (-bi).astype(BF)
         m2[W:, W:] = br
         for part in range(2):
-            state[:, part * W : (part + 1) * W] = pltpu.roll(probe[part].astype(F32), shift, 1)
+            state[:, part * W : (part + 1) * W] = pltpu.roll(probe[part].astype(F32), shift, 1).astype(BF)
 
     @pl.when(core == 1)
     def _():
@@ -82,58 +82,55 @@
         for part in range(2):
             left[part * W : (part + 1) * W, :] = pltpu.roll(cot[slot, part].astype(F32), shift, 1).astype(BF)
         sweep(m1, left, right)
-        state[...] = jnp.dot(right[...], m2[...], preferred_element_type=F32)
+        state[...] = jnp.dot(right[...], m2[...], preferred_element_type=F32).astype(BF)
+
+    upper1[...] = m1[0:W]
+    upper2[...] = m2[0:W]
 
 
 def prep(tiles, rows, cols, probe, cot):
     return pl.pallas_call(
         prep_kernel,
-        out_shape=[SQUARE, SQUARE, jax.ShapeDtypeStruct((W, 2 * W), F32)],
+        out_shape=[SENT] * 3,
         in_specs=[SMEM] + [VMEM] * 4,
         out_specs=[VMEM] * 3,
-        scratch_shapes=[pltpu.VMEM((2 * W, W), BF), pltpu.VMEM((W, 2 * W), BF)],
+        scratch_shapes=[pltpu.VMEM((2 * W, 2 * W), BF)] * 2 + [pltpu.VMEM((2 * W, W), BF), pltpu.VMEM((W, 2 * W), BF)],
         compiler_params=params(24),
         cost_estimate=pl.CostEstimate(flops=4 * 10**9, transcendentals=0, bytes_accessed=2 * 10**7),
         name="prep",
     )(tiles, rows, cols, probe, cot)
 
 
-def spread_kernel(own, one, two, three, held):
+def flipped(place, bit):
+    if bit == 1:
+        return place + 1 - 2 * lax.rem(place, 2)
+    return lax.rem(place + 2, 4)
+
+
+def pack_kernel(peers, own, across, far, out, held, chunks, sems):
     zh = lax.axis_index("zh")
-    for hops, piece in enumerate((own, one, two, three)):
-        place = lax.rem(zh - hops + 4, 4)
+    x = lax.axis_index("x")
+    near = flipped(zh, 1)
+    for place, piece in ((zh, own), (near, across), (flipped(zh, 2), far.at[0]), (flipped(near, 2), far.at[1])):
         held[pl.ds(pl.multiple_of(place * 24, 8), 24), :] = piece[...].astype(F32)
-
-
-def spread(own, others):
-    return pl.pallas_call(
-        spread_kernel,
-        out_shape=jax.ShapeDtypeStruct((96, OBJ), F32),
-        in_specs=[VMEM] * 4,
-        out_specs=VMEM,
-        compiler_params=params(4),
-        cost_estimate=pl.CostEstimate(flops=4 * 10**9, transcendentals=0, bytes_accessed=10**7),
-        name="spread",
-    )(own, *others)
-
-
-def pack_kernel(peers, held, out, chunks, sems):
-    x = lax.axis_index("x")
     lane = lax.broadcasted_iota(jnp.int32, (72, 256), 1)
+    y = lax.axis_index("y")
 
     def moved(i):
         return pltpu.make_async_copy(chunks.at[i], out.at[i], sems.at[i])
 
     def target(t, carry):
+        ahead, below = t // 4, lax.rem(t, 4)
+        place = lax.rem(x - ahead + 4, 4) * 4 + lax.rem(y - below + 4, 4)
         for slot in range(2):
-            first = first_interval(peers[t, slot, 0], x)
+            first = first_interval(peers[ahead, below, slot, 0], x)
             rows = pl.ds(pl.multiple_of(first * 24, 8), 72)
-            wrapped = lane < peers[t, slot, 1] * TILE
+            wrapped = lane < peers[ahead, below, slot, 1] * TILE
             low = held[rows, 0:256]
             high = held[rows, 512:768]
-            chunks[slot * 16 + t, :, 0:256] = jnp.where(wrapped, high, low).astype(BF)
-            chunks[slot * 16 + t, :, 256:512] = held[rows, 256:512].astype(BF)
-            moved(slot * 16 + t).start()
+            chunks[slot * 16 + place, :, 0:256] = jnp.where(wrapped, high, low).astype(BF)
+            chunks[slot * 16 + place, :, 256:512] = held[rows, 256:512].astype(BF)
+            moved(slot * 16 + place).start()
         return carry
 
     def settle(i, carry):
@@ -144,19 +141,20 @@
     lax.fori_loop(0, 32, settle, 0)
 
 
-def pack(peers, held):
+def pack(peers, own, across, far):
     return pl.pallas_call(
         pack_kernel,
         out_shape=jax.ShapeDtypeStruct((32, 72, W), BF),
-        in_specs=[SMEM, VMEM],
+        in_specs=[SMEM] + [VMEM] * 3,
         out_specs=HBM,
         scratch_shapes=[
+            pltpu.VMEM((96, OBJ), F32),
             pltpu.VMEM((32, 72, W), BF),
             pltpu.SemaphoreType.DMA((32,)),
         ],
         compiler_params=params(16),
         name="pack",
-    )(peers, held)
+    )(peers, own, across, far)
 
 
 def place_patch(source, base, patch, row_tile):
@@ -174,8 +172,8 @@
 
 
 def form_contrib(local, remote, contrib, out, sign, used, row_tile):
-    ar = local[:, 0:W]
-    ai = local[:, W:]
+    ar = local[:, 0:W].astype(F32)
+    ai = local[:, W:].astype(F32)
     br = remote[:, 0:W].astype(F32)
     bi = remote[:, W:].astype(F32)
     contrib[:, 0:PAD, :] = jnp.zeros((2, PAD, W), F32)
@@ -207,17 +205,24 @@
 HALF = jax.ShapeDtypeStruct((16, 72, W), BF)
 
 
+def complete(m):
+    m[W:, 0:W] = (-m[0:W, W:].astype(F32)).astype(BF)
+    m[W:, W:] = m[0:W, 0:W]
+
+
 def open_kernel(tiles, own, m1, m2, state, after, sent, v1, v2, patch, left, right, held, sems):
     core, sign, row_tile = role(tiles)
-    copies = [pltpu.make_async_copy(a, b, sems.at[i]) for i, (a, b) in enumerate([(state, held), (m1, v1), (m2, v2)])]
+    copies = [pltpu.make_async_copy(a, b, sems.at[i]) for i, (a, b) in enumerate([(state, held), (m1, v1.at[0:W]), (m2, v2.at[0:W])])]
     for copy in copies:
         copy.start()
     place_patch(own, core * 16, patch, row_tile)
     copies[0].wait()
     form_left(held, patch, sign, left)
     copies[1].wait()
+    complete(v1)
     sweep(v1, left, right)
     copies[2].wait()
+    complete(v2)
     value = jnp.dot(right[...], v2[...], preferred_element_type=F32)
     after[...] = value
     sent[...] = value.astype(BF)
@@ -229,7 +234,7 @@
         out_shape=[STATE, SENT, SQUARE, SQUARE],
         in_specs=[SMEM, VMEM] + [HBM] * 3,
         out_specs=[VMEM] * 4,
-        scratch_shapes=WORK + [pltpu.VMEM((W, 2 * W), F32), pltpu.SemaphoreType.DMA((3,))],
+        scratch_shapes=WORK + [pltpu.VMEM((W, 2 * W), BF), pltpu.SemaphoreType.DMA((3,))],
         compiler_params=params(24),
         cost_estimate=pl.CostEstimate(flops=4 * 10**9, transcendentals=0, bytes_accessed=10**7),
         name="open_step",
@@ -238,7 +243,7 @@
 
 def close_kernel(tiles, own, other, v1, v2, state, middle, sent, patch, left, right):
     core, sign, row_tile = role(tiles)
-    place_patch(other, 0, patch, row_tile)
+    place_patch(other, core * 16, patch, row_tile)
     form_left(state, patch, sign, left)
     sweep(v1, left, right)
     middle[...] = jnp.dot(right[...], v2[...], preferred_element_type=F32)
@@ -299,18 +304,21 @@
     )(tiles, count, local, remote, half)
 
 
-def gather_kernel(peers, got, own, one, two, three, total):
+def gather_kernel(peers, got, kept, given, total):
     zh = lax.axis_index("zh")
     x = lax.axis_index("x")
     total[...] = jnp.zeros((96, OBJ), F32)
     lane = lax.broadcasted_iota(jnp.int32, (72, 256), 1)
+    y = lax.axis_index("y")
 
     def source(t, carry):
+        ahead, below = t // 4, lax.rem(t, 4)
+        place = lax.rem(x - ahead + 4, 4) * 4 + lax.rem(y - below + 4, 4)
         for slot in range(2):
-            first = first_interval(peers[t, slot, 0], x)
+            first = first_interval(peers[ahead, below, slot, 0], x)
             rows = pl.ds(pl.multiple_of(first * 24, 8), 72)
-            wrapped = lane < peers[t, slot, 1] * TILE
-            value = got[slot * 16 + t].astype(F32)
+            wrapped = lane < peers[ahead, below, slot, 1] * TILE
+            value = got[slot * 16 + place].astype(F32)
             low = value[:, 0:256]
             total[rows, 0:256] += jnp.where(wrapped, 0.0, low)
             total[rows, 512:768] += jnp.where(wrapped, low, 0.0)
@@ -318,38 +326,60 @@
         return carry
 
     lax.fori_loop(0, 16, source, 0)
-    for step, out in enumerate((own, one, two, three)):
-        place = lax.rem(zh + step, 4)
-        out[...] = total[pl.ds(pl.multiple_of(place * 24, 8), 24), :].astype(out.dtype)
+    near = flipped(zh, 1)
+    for i, place in enumerate((zh, near)):
+        kept[i] = total[pl.ds(pl.multiple_of(place * 24, 8), 24), :]
+        there = pl.multiple_of(flipped(place, 2) * 24, 8)
+        given[i] = total[pl.ds(there, 24), :].astype(BF)
 
 
 def gather(peers, got):
     return pl.pallas_call(
         gather_kernel,
-        out_shape=[jax.ShapeDtypeStruct((24, OBJ), F32)] + [jax.ShapeDtypeStruct((24, OBJ), BF)] * 3,
+        out_shape=[jax.ShapeDtypeStruct((2, 24, OBJ), F32), jax.ShapeDtypeStruct((2, 24, OBJ), BF)],
         in_specs=[SMEM, VMEM],
-        out_specs=[VMEM] * 4,
+        out_specs=[VMEM] * 2,
         scratch_shapes=[pltpu.VMEM((96, OBJ), F32)],
         compiler_params=params(16),
         name="gather",
     )(peers, got)
 
 
-def last_kernel(own, one, two, three, out):
-    total = own[...] + one[...].astype(F32) + two[...].astype(F32) + three[...].astype(F32)
+def half_kernel(kept, far, own, given):
+    own[...] = kept[0] + far[0].astype(F32)
+    given[...] = (kept[1] + far[1].astype(F32)).astype(BF)
+
+
+def half_sum(kept, far):
+    return pl.pallas_call(
+        half_kernel,
+        out_shape=[jax.ShapeDtypeStruct((24, OBJ), F32), jax.ShapeDtypeStruct((24, OBJ), BF)],
+        in_specs=[VMEM] * 2,
+        out_specs=[VMEM] * 2,
+        compiler_params=params(4),
+        name="half_sum",
+    )(kept, far)
+
+
+def last_kernel(own, away, out):
+    total = own[...] + away[...].astype(F32)
     out[:, 0, :] = total[0:12]
     out[:, 1, :] = total[12:24]
 
 
-def last_sum(own, others):
+def last_sum(own, away):
     return pl.pallas_call(
         last_kernel,
         out_shape=jax.ShapeDtypeStruct((12, 2, OBJ), F32),
-        in_specs=[VMEM] * 4,
+        in_specs=[VMEM] * 2,
         out_specs=VMEM,
         compiler_params=params(4),
         name="last_sum",
-    )(own, *others)
+    )(own, away)
+
+
+def swap(value, axis, bit):
+    return lax.ppermute(value, axis, [(i, i ^ bit) for i in range(4)])
 
 
 def turn(value, axis, step, count):
@@ -357,13 +387,12 @@
 
 
 def on_device(probe_wave, prop_rows, prop_cols, transmission, exit_cotangent, window_tiles, slot_count):
-    core = lax.axis_index("core")
+    line = jnp.stack([window_tiles] + [turn(window_tiles, "y", hops, 4) for hops in (1, 2, 3)])
     piece = transmission.reshape(24, OBJ)
-    others = [turn(piece, "zh", hops, 4) for hops in (2, 1, 3)]
-    others = [others[1], others[0], others[2]]
-    peers = lax.all_to_all(jnp.broadcast_to(window_tiles[None], (16, 2, 2)), ("x", "y"), 0, 0, tiled=True)
-    peers, held = lax.optimization_barrier((peers, spread(piece, others)))
-    sent = pack(peers, held)
+    across = swap(piece, "zh", 1)
+    far = swap(jnp.stack([piece, across]), "zh", 2)
+    peers = jnp.stack([line] + [turn(line, "x", hops, 4) for hops in (1, 2, 3)])
+    sent = pack(peers, piece, across, far)
     sent, rows = lax.optimization_barrier((sent, prop_rows))
     own = lax.all_to_all(sent, ("zl", "x", "y"), 0, 0, tiled=True)
     mats = prep(window_tiles, rows, prop_cols, probe_wave, exit_cotangent)
@@ -371,8 +400,7 @@
     m1 = pltpu.with_memory_space_constraint(m1, pltpu.HBM)
     m2 = pltpu.with_memory_space_constraint(m2, pltpu.HBM)
     kept = pltpu.with_memory_space_constraint(state, pltpu.HBM)
-    given = lax.dynamic_index_in_dim(own.reshape(2, 16, 72, W), 1 - core, 0, keepdims=False)
-    other = turn(given, "core", 1, 2)
+    other = turn(own, "core", 1, 2)
     after, first, m1, m2 = open_step(window_tiles, own, m1, m2, kept)
     first_away = turn(first, "core", 1, 2)
     middle, last = close_steps(window_tiles, own, other, m1, m2, after)
@@ -380,8 +408,9 @@
     half = early(window_tiles, slot_count, middle, first_away)
     contrib = late(window_tiles, slot_count, state, last_away, half)
     got = lax.all_to_all(contrib, ("zl", "x", "y"), 0, 0, tiled=True)
-    here, *away = gather(peers, got)
-    total = last_sum(here, [turn(away[hops - 1], "zh", hops, 4) for hops in (2, 1, 3)])
+    kept, given = gather(peers, got)
+    own, given = half_sum(kept, swap(given, "zh", 2))
+    total = last_sum(own, swap(given, "zh", 1))
     return jnp.transpose(total, (1, 0, 2))[None]
 
 

time: 130 us -> 130 us (level)
  local copies, waits for them, and re-layouts: 10.3 us -> 7.81 us
  starting transfers between devices: 26.9 us -> 29.2 us
  waiting for transfers between devices: 32 us -> 30.6 us
  other arithmetic: 0 us -> 1.39 us
    ppermute x0 -> x4, waiting for transfers between devices: none -> 11.6 us  [swap(): return lax.ppermute(value, axis, [(i, i ^ bit) for i in range(4)])]
    ppermute x0 -> x4, starting transfers between devices: none -> 10.9 us  [swap(): return lax.ppermute(value, axis, [(i, i ^ bit) for i in range(4)])]
    all_to_all x1 -> x0, waiting for transfers between devices: 7.52 us -> none  [on_device(): lax.all_to_all(jnp.broadcast_to(window_tiles[None], (16, 2, 2)), ('x', 'y...]
    all_to_all x1 -> x0, starting transfers between devices: 7.03 us -> none  [on_device(): lax.all_to_all(jnp.broadcast_to(window_tiles[None], (16, 2, 2)), ('x', 'y...]
    ppermute x9, waiting for transfers between devices: 7.18 us -> 2.24 us  [turn(): lax.ppermute(value, axis, [(i, (i + step) % count) for i in range(count)])]
    ppermute x9, starting transfers between devices: 15.7 us -> 12.4 us  [turn(): lax.ppermute(value, axis, [(i, (i + step) % count) for i in range(count)])]
    all_to_all x1, starting transfers between devices: 4.2 us -> 5.86 us  [on_device(): own = lax.all_to_all(sent, ('zl', 'x', 'y'), 0, 0, tiled=True)]
    another operation x0 -> x4, other arithmetic: none -> 1.39 us  [the longest x2 0.69 us: on_device(): peers = jnp.stack([line] + [turn(line, 'x', hops, 4) for hops in (1, 2, 3)])]
  transfers between devices with their start and end apart: 11 -> 14, of which waited for: 5 -> 7; matrix products, arithmetic and copies ran while one was open for 1% -> 2% of each run, Pallas kernels for 12% -> 12%
where the time goes in v7:
time: 130 us; the launch traced here: 129 us
  blocking collectives  37.4 us (29%)
  waiting for transfers between devices  30.6 us (24%)
  starting transfers between devices  29.2 us (22%)
  Pallas kernels  22 us (17%)
  local copies, waits for them, and re-layouts  7.81 us (6%)
  other arithmetic  1.39 us (1%)
    all_to_all x1, blocking collectives, on_device(): got = lax.all_to_all(contrib, ('zl', 'x', 'y'), 0, 0, tiled=True)  37.4 us
    all_to_all x1, waiting for transfers between devices, on_device(): own = lax.all_to_all(sent, ('zl', 'x', 'y'), 0, 0, tiled=True)  16.8 us
    ppermute x9, starting transfers between devices, turn(): lax.ppermute(value, axis, [(i, (i + step) % count) for i in range(count)])  12.4 us
    ppermute x4, waiting for transfers between devices, swap(): return lax.ppermute(value, axis, [(i, i ^ bit) for i in range(4)])  11.6 us
    ppermute x4, starting transfers between devices, swap(): return lax.ppermute(value, axis, [(i, i ^ bit) for i in range(4)])  10.9 us
    unnamed x19, local copies, waits for them, and re-layouts  7.78 us
    pallas_call x1, Pallas kernels, close_steps(): pl.pallas_call(close_kernel, out_shape=[STATE, SENT], in_specs=[SMEM] + [...  5.87 us
    all_to_all x1, starting transfers between devices, on_device(): own = lax.all_to_all(sent, ('zl', 'x', 'y'), 0, 0, tiled=True)  5.86 us
  transfers between devices with their start and end apart: 14, of which 7 were waited for; matrix products, arithmetic and copies ran while one was open for 2% of the time, Pallas kernels for 12%

profile of v7, /device:TPU:64, one launch (start us, length us, event | category | flops | bytes accessed | tf_op | source)
XLA Modules:
  0.0 129.3 jit_solution(16958079702881500835)
XLA Ops:
  0.0 1.6 %collective-permute-start = (s32[2,2]{1,0:T(2,128)}, s32[2,2]{1,0:T(2,128)S(1)}, u32[]{:S(2)}, u32[]{:S(2)}) collective-permute-start(s32[2,2]{1,0:T(2,128)} %tiles.9), channel_id=1, source_target_pairs={{0,1},{1,2},{2,3},{3,0},{4,5},{5,6},{6,7},{7,4},{8,9},{9,10},{10,1... | collective-permute-start | bytes 56 | tf_op jit(solution)/shard_map/ppermute | solution.py:386
  1.6 2.9 %collective-permute-start.1 = (s32[2,2]{1,0:T(2,128)}, s32[2,2]{1,0:T(2,128)S(1)}, u32[]{:S(2)}, u32[]{:S(2)}) collective-permute-start(s32[2,2]{1,0:T(2,128)} %tiles.9), channel_id=1, source_target_pairs={{0,2},{1,3},{2,0},{3,1},{4,6},{5,7},{6,4},{7,5},{8,10},{9,11},{10,... | collective-permute-start | bytes 56 | tf_op jit(solution)/shard_map/ppermute | solution.py:386
  4.5 1.3 %collective-permute-start.2 = (s32[2,2]{1,0:T(2,128)}, s32[2,2]{1,0:T(2,128)S(1)}, u32[]{:S(2)}, u32[]{:S(2)}) collective-permute-start(s32[2,2]{1,0:T(2,128)} %tiles.9), channel_id=1, source_target_pairs={{0,3},{1,0},{2,1},{3,2},{4,7},{5,4},{6,5},{7,6},{8,11},{9,8},{10,9... | collective-permute-start | bytes 56 | tf_op jit(solution)/shard_map/ppermute | solution.py:386
  6.9 1.4 %collective-permute-done.2 = s32[2,2]{1,0:T(2,128)S(1)} collective-permute-done((s32[2,2]{1,0:T(2,128)}, s32[2,2]{1,0:T(2,128)S(1)}, u32[]{:S(2)}, u32[]{:S(2)}) %collective-permute-start.2) | collective-permute-done | bytes 48 | tf_op jit(solution)/shard_map/ppermute | solution.py:386
  8.9 1.5 %collective-permute-start.3 = (s32[4,2,2]{2,1,0:T(2,128)S(1)}, s32[4,2,2]{2,1,0:T(2,128)S(1)}, u32[]{:S(2)}, u32[]{:S(2)}) collective-permute-start(s32[4,2,2]{2,1,0:T(2,128)S(1)} %pad_add_fusion.1), channel_id=1, source_target_pairs={{0,4},{4,8},{8,12},{12,0},{1,5},{5,9},{9,13},{13,1},{2,6},{6,10},{... | collective-permute-start | bytes 200 | tf_op jit(solution)/shard_map/ppermute | solution.py:386
  10.4 2.7 %collective-permute-start.4 = (s32[4,2,2]{2,1,0:T(2,128)S(1)}, s32[4,2,2]{2,1,0:T(2,128)S(1)}, u32[]{:S(2)}, u32[]{:S(2)}) collective-permute-start(s32[4,2,2]{2,1,0:T(2,128)S(1)} %pad_add_fusion.1), channel_id=1, source_target_pairs={{0,8},{4,12},{8,0},{12,4},{1,9},{5,13},{9,1},{13,5},{2,10},{6,14},... | collective-permute-start | bytes 200 | tf_op jit(solution)/shard_map/ppermute | solution.py:386
  13.2 1.4 %collective-permute-start.5 = (s32[4,2,2]{2,1,0:T(2,128)S(1)}, s32[4,2,2]{2,1,0:T(2,128)S(1)}, u32[]{:S(2)}, u32[]{:S(2)}) collective-permute-start(s32[4,2,2]{2,1,0:T(2,128)S(1)} %pad_add_fusion.1), channel_id=1, source_target_pairs={{0,12},{4,0},{8,4},{12,8},{1,13},{5,1},{9,5},{13,9},{2,14},{6,2},{... | collective-permute-start | bytes 200 | tf_op jit(solution)/shard_map/ppermute | solution.py:386
  15.3 5.5 %collective-permute-start.7 = (bf16[2,24,768]{2,1,0:T(8,128)(2,1)S(1)}, bf16[2,24,768]{2,1,0:T(8,128)(2,1)S(1)}, u32[]{:S(2)}, u32[]{:S(2)}) collective-permute-start(bf16[2,24,768]{2,1,0:T(8,128)(2,1)S(1)} %pad_maximum_fusion), channel_id=1, source_target_pairs={{0,32},{16,48},{32,0},{48,16},{1,33},{17,49},{33,1},{49,17},{2,34}... | collective-permute-start | bytes 221192 | tf_op jit(solution)/shard_map/ppermute | solution.py:382
  20.8 2.8 %collective-permute-done.7.far = bf16[2,24,768]{2,1,0:T(8,128)(2,1)S(1)} collective-permute-done((bf16[2,24,768]{2,1,0:T(8,128)(2,1)S(1)}, bf16[2,24,768]{2,1,0:T(8,128)(2,1)S(1)}, u32[]{:S(2)}, u32[]{:S(2)}) %collective-permute-start.7) | collective-permute-done | bytes 73760 | tf_op jit(solution)/shard_map/ppermute | solution.py:382
  23.6 2.7 %pack.1 = bf16[32,72,512]{2,1,0:T(8,128)(2,1)} custom-call(s32[4,4,2,2]{3,2,1,0:T(2,128)S(1)} %pad_add_fusion.peers, bf16[24,768]{1,0:T(8,128)(2,1)S(1)} %reshape.3.own, bf16[24,768]{1,0:T(8,128)(2,1)S(1)} %collective-permute-done.6.across, bf16[2,24,768]{2,1,0:T(8,128)(2,1)S(1)} %collective-permute-done.7.far), custom_call_target="tpu_custom_call" | custom-call | tf_op jit(solution)/shard_map/pack/pallas_call | solution.py:145
  26.3 5.9 %all-to-all-start = ((bf16[32,72,512]{2,1,0:T(8,128)(2,1)}), bf16[32,72,512]{2,1,0:T(8,128)(2,1)S(1)}, u32[]{:S(2)}, u32[]{:S(2)}) async-start(bf16[32,72,512]{2,1,0:T(8,128)(2,1)} %pack.1), calls=%async_computation | async-start | bytes 4718592 | tf_op jit(solution)/shard_map/all_to_all | solution.py:397
  32.2 1.6 %copy-done.3 = bf16[2,2,512,512]{3,2,1,0:T(8,128)(2,1)S(1)} copy-done((bf16[2,2,512,512]{3,2,1,0:T(8,128)(2,1)S(1)}, bf16[2,2,512,512]{3,2,1,0:T(8,128)(2,1)}, u32[]{:S(2)}) %copy-start.3) | copy-done | bytes 2097176
  33.8 1.2 copy-done.5
  36.3 3.4 %prep.1 = (bf16[512,1024]{1,0:T(8,128)(2,1)S(1)}, bf16[512,1024]{1,0:T(8,128)(2,1)S(1)}, bf16[512,1024]{1,0:T(8,128)(2,1)S(1)}) custom-call(s32[2,2]{1,0:T(2,128)S(1)} %copy-done.2, bf16[2,512,512]{2,1,0:T(8,128)(2,1)S(1)} %copy-done.4, bf16[2,512,512]{2,1,0:T(8,128)(2,1)S(1)} %copy-done.5, bf16[2,512,512]{2,1,0:T(8,128)(2,1)S(1)} %copy-done.6, ...), custom_call_target="tpu_custom_call" | custom-call | flops 4000000000 | bytes 20000000 | tf_op jit(solution)/shard_map/prep/pallas_call | solution.py:92
  42.6 16.8 %all-to-all-done.own = bf16[32,72,512]{2,1,0:T(8,128)(2,1)S(1)} async-done(((bf16[32,72,512]{2,1,0:T(8,128)(2,1)}), bf16[32,72,512]{2,1,0:T(8,128)(2,1)S(1)}, u32[]{:S(2)}, u32[]{:S(2)}) %all-to-all-start) | async-done | bytes 2359328 | tf_op jit(solution)/shard_map/all_to_all | solution.py:397
  59.4 5.0 %open_step.1 = (f32[512,1024]{1,0:T(8,128)S(1)}, bf16[512,1024]{1,0:T(8,128)(2,1)S(1)}, bf16[1024,1024]{1,0:T(8,128)(2,1)S(1)}, bf16[1024,1024]{1,0:T(8,128)(2,1)S(1)}) custom-call(s32[2,2]{1,0:T(2,128)S(1)} %copy-done.2, bf16[32,72,512]{2,1,0:T(8,128)(2,1)S(1)} %all-to-all-done.own, bf16[512,1024]{1,0:T(8,128)(2,1)} %copy-done.7, ...), custom_call_target="tpu_custom_call" | custom-call | flops 4000000000 | bytes 10000000 | tf_op jit(solution)/shard_map/open_step/pallas_call | solution.py:232
  65.1 5.9 %close_steps.1 = (f32[512,1024]{1,0:T(8,128)S(1)}, bf16[512,1024]{1,0:T(8,128)(2,1)S(1)}) custom-call(s32[2,2]{1,0:T(2,128)S(1)} %copy-done.2, bf16[32,72,512]{2,1,0:T(8,128)(2,1)S(1)} %all-to-all-done.own, bf16[32,72,512]{2,1,0:T(8,128)(2,1)S(1)} %collective-permute-done.8.other, bf16[1024,1024]{1,0:T(8,128)(2,1)S(1)} %get-tuple-element.33.v1, ...), custom_call_target="tpu_custom_call" | custom-call | flops 8000000000 | bytes 10000000 | tf_op jit(solution)/shard_map/close_steps/pallas_call | solution.py:257
  71.9 1.2 early.1.half
  73.9 1.4 %late.1 = bf16[32,72,512]{2,1,0:T(8,128)(2,1)S(1)} custom-call(s32[2,2]{1,0:T(2,128)S(1)} %copy-done.2, s32[1]{0:T(128)S(6)} %copy.32.count, bf16[512,1024]{1,0:T(8,128)(2,1)S(1)} %copy-done.1, bf16[512,1024]{1,0:T(8,128)(2,1)S(1)} %collective-permute-done.9.remote, bf16[16,72,512]{2,1,0:T(8,128)(2,1)S(1)} %early.1.half), custom_call_target="tpu_custom_call" | custom-call | tf_op jit(solution)/shard_map/late/pallas_call | solution.py:296
  75.3 37.4 %all_to_all.10.got = bf16[32,72,512]{2,1,0:T(8,128)(2,1)S(1)} all-to-all(bf16[32,72,512]{2,1,0:T(8,128)(2,1)S(1)} %late.1), channel_id=1, replica_groups=mesh['zl'=2,'core'=2,'zh'=4,'x'=4,'y'=4] {'zl','x','y'}, dimensions={0} | all-to-all | bytes 4718592 | tf_op jit(solution)/shard_map/all_to_all | solution.py:410
  112.8 1.8 %gather.1 = (f32[2,24,768]{2,1,0:T(8,128)S(1)}, bf16[2,24,768]{2,1,0:T(8,128)(2,1)S(1)}) custom-call(s32[4,4,2,2]{3,2,1,0:T(2,128)S(1)} %pad_add_fusion.peers, bf16[32,72,512]{2,1,0:T(8,128)(2,1)S(1)} %all_to_all.10.got), custom_call_target="tpu_custom_call" | custom-call | tf_op jit(solution)/shard_map/gather/pallas_call | solution.py:337
  114.5 4.8 %collective-permute-start.11 = (bf16[2,24,768]{2,1,0:T(8,128)(2,1)S(1)}, bf16[2,24,768]{2,1,0:T(8,128)(2,1)S(1)}, u32[]{:S(2)}, u32[]{:S(2)}) collective-permute-start(bf16[2,24,768]{2,1,0:T(8,128)(2,1)S(1)} %get-tuple-element.40), channel_id=1, source_target_pairs={{0,32},{16,48},{32,0},{48,16},{1,33},{17,49},{33,1},{49,17},{2,34}... | collective-permute-start | bytes 221192 | tf_op jit(solution)/shard_map/ppermute | solution.py:382
  119.4 4.3 %collective-permute-done.11.far = bf16[2,24,768]{2,1,0:T(8,128)(2,1)S(1)} collective-permute-done((bf16[2,24,768]{2,1,0:T(8,128)(2,1)S(1)}, bf16[2,24,768]{2,1,0:T(8,128)(2,1)S(1)}, u32[]{:S(2)}, u32[]{:S(2)}) %collective-permute-start.11) | collective-permute-done | bytes 73760 | tf_op jit(solution)/shard_map/ppermute | solution.py:382
  124.2 4.5 %collective-permute-done.12.away = bf16[24,768]{1,0:T(8,128)(2,1)S(1)} collective-permute-done((bf16[24,768]{1,0:T(8,128)(2,1)S(1)}, bf16[24,768]{1,0:T(8,128)(2,1)S(1)}, u32[]{:S(2)}, u32[]{:S(2)}) %collective-permute-start.12) | collective-permute-done | bytes 36896 | tf_op jit(solution)/shard_map/ppermute | solution.py:382
  (39 shorter events, 9.4 us)
Async XLA Ops:
  0.0 6.7 %collective-permute-start = (s32[2,2]{1,0:T(2,128)}, s32[2,2]{1,0:T(2,128)S(1)}, u32[]{:S(2)}, u32[]{:S(2)}) collective-permute-start(s32[2,2]{1,0:T(2,128)} %tiles.9), channel_id=1, source_target_pairs={{0,1},{1,2},{2,3},{3,0},{4,5},{5,6},{6,7},{7,4},{8,9},{9,10},{10,1... | collective-permute-start | bytes 56 | tf_op jit(solution)/shard_map/ppermute | solution.py:386
  1.6 5.3 %collective-permute-start.1 = (s32[2,2]{1,0:T(2,128)}, s32[2,2]{1,0:T(2,128)S(1)}, u32[]{:S(2)}, u32[]{:S(2)}) collective-permute-start(s32[2,2]{1,0:T(2,128)} %tiles.9), channel_id=1, source_target_pairs={{0,2},{1,3},{2,0},{3,1},{4,6},{5,7},{6,4},{7,5},{8,10},{9,11},{10,... | collective-permute-start | bytes 56 | tf_op jit(solution)/shard_map/ppermute | solution.py:386
  4.5 3.8 %collective-permute-start.2 = (s32[2,2]{1,0:T(2,128)}, s32[2,2]{1,0:T(2,128)S(1)}, u32[]{:S(2)}, u32[]{:S(2)}) collective-permute-start(s32[2,2]{1,0:T(2,128)} %tiles.9), channel_id=1, source_target_pairs={{0,3},{1,0},{2,1},{3,2},{4,7},{5,4},{6,5},{7,6},{8,11},{9,8},{10,9... | collective-permute-start | bytes 56 | tf_op jit(solution)/shard_map/ppermute | solution.py:386
  6.6 8.7 %collective-permute-start.6 = (bf16[24,768]{1,0:T(8,128)(2,1)S(1)}, bf16[24,768]{1,0:T(8,128)(2,1)S(1)}, u32[]{:S(2)}, u32[]{:S(2)}) collective-permute-start(bf16[24,768]{1,0:T(8,128)(2,1)S(1)} %reshape.3.own), channel_id=1, source_target_pairs={{0,16},{16,0},{32,48},{48,32},{1,17},{17,1},{33,49},{49,33},{2,18}... | collective-permute-start | bytes 110600 | tf_op jit(solution)/shard_map/ppermute | solution.py:382
  8.9 11.8 %collective-permute-start.3 = (s32[4,2,2]{2,1,0:T(2,128)S(1)}, s32[4,2,2]{2,1,0:T(2,128)S(1)}, u32[]{:S(2)}, u32[]{:S(2)}) collective-permute-start(s32[4,2,2]{2,1,0:T(2,128)S(1)} %pad_add_fusion.1), channel_id=1, source_target_pairs={{0,4},{4,8},{8,12},{12,0},{1,5},{5,9},{9,13},{13,1},{2,6},{6,10},{... | collective-permute-start | bytes 200 | tf_op jit(solution)/shard_map/ppermute | solution.py:386
  10.4 10.3 %collective-permute-start.4 = (s32[4,2,2]{2,1,0:T(2,128)S(1)}, s32[4,2,2]{2,1,0:T(2,128)S(1)}, u32[]{:S(2)}, u32[]{:S(2)}) collective-permute-start(s32[4,2,2]{2,1,0:T(2,128)S(1)} %pad_add_fusion.1), channel_id=1, source_target_pairs={{0,8},{4,12},{8,0},{12,4},{1,9},{5,13},{9,1},{13,5},{2,10},{6,14},... | collective-permute-start | bytes 200 | tf_op jit(solution)/shard_map/ppermute | solution.py:386
  13.2 7.6 %collective-permute-start.5 = (s32[4,2,2]{2,1,0:T(2,128)S(1)}, s32[4,2,2]{2,1,0:T(2,128)S(1)}, u32[]{:S(2)}, u32[]{:S(2)}) collective-permute-start(s32[4,2,2]{2,1,0:T(2,128)S(1)} %pad_add_fusion.1), channel_id=1, source_target_pairs={{0,12},{4,0},{8,4},{12,8},{1,13},{5,1},{9,5},{13,9},{2,14},{6,2},{... | collective-permute-start | bytes 200 | tf_op jit(solution)/shard_map/ppermute | solution.py:386
  15.3 8.3 %collective-permute-start.7 = (bf16[2,24,768]{2,1,0:T(8,128)(2,1)S(1)}, bf16[2,24,768]{2,1,0:T(8,128)(2,1)S(1)}, u32[]{:S(2)}, u32[]{:S(2)}) collective-permute-start(bf16[2,24,768]{2,1,0:T(8,128)(2,1)S(1)} %pad_maximum_fusion), channel_id=1, source_target_pairs={{0,32},{16,48},{32,0},{48,16},{1,33},{17,49},{33,1},{49,17},{2,34}... | collective-permute-start | bytes 221192 | tf_op jit(solution)/shard_map/ppermute | solution.py:382
  26.3 5.9 %copy-start.2 = (s32[2,2]{1,0:T(2,128)S(1)}, s32[2,2]{1,0:T(2,128)}, u32[]{:S(2)}) copy-start(s32[2,2]{1,0:T(2,128)} %tiles.9) | copy-start | bytes 52
  26.3 5.9 %copy-start.4 = (bf16[2,512,512]{2,1,0:T(8,128)(2,1)S(1)}, bf16[2,512,512]{2,1,0:T(8,128)(2,1)}, u32[]{:S(2)}) copy-start(bf16[2,512,512]{2,1,0:T(8,128)(2,1)} %rows) | copy-start | bytes 3145732
  26.3 33.1 %all-to-all-start = ((bf16[32,72,512]{2,1,0:T(8,128)(2,1)}), bf16[32,72,512]{2,1,0:T(8,128)(2,1)S(1)}, u32[]{:S(2)}, u32[]{:S(2)}) async-start(bf16[32,72,512]{2,1,0:T(8,128)(2,1)} %pack.1), calls=%async_computation | async-start | bytes 4718592 | tf_op jit(solution)/shard_map/all_to_all | solution.py:397
  32.2 1.6 %copy-start.3 = (bf16[2,2,512,512]{3,2,1,0:T(8,128)(2,1)S(1)}, bf16[2,2,512,512]{3,2,1,0:T(8,128)(2,1)}, u32[]{:S(2)}) copy-start(bf16[2,2,512,512]{3,2,1,0:T(8,128)(2,1)} %cot.1) | copy-start | bytes 6291460
  33.8 1.2 copy-start.5
  35.0 1.2 copy-start.6
  39.6 1.0 copy-start
  40.6 1.0 copy-start.7
  41.6 1.0 copy-start.8
  59.4 5.6 %collective-permute-start.8 = (bf16[32,72,512]{2,1,0:T(8,128)(2,1)S(1)}, bf16[32,72,512]{2,1,0:T(8,128)(2,1)S(1)}, u32[]{:S(2)}, u32[]{:S(2)}) collective-permute-start(bf16[32,72,512]{2,1,0:T(8,128)(2,1)S(1)} %all-to-all-done.own), channel_id=1, source_target_pairs={{0,64},{64,0},{1,65},{65,1},{2,66},{66,2},{3,67},{67,3},{4,68},{68... | collective-permute-start | bytes 7077896 | tf_op jit(solution)/shard_map/ppermute | solution.py:386
  64.5 7.5 %collective-permute-start.10 = (bf16[512,1024]{1,0:T(8,128)(2,1)S(1)}, bf16[512,1024]{1,0:T(8,128)(2,1)S(1)}, u32[]{:S(2)}, u32[]{:S(2)}) collective-permute-start(bf16[512,1024]{1,0:T(8,128)(2,1)S(1)} %get-tuple-element.38), channel_id=1, source_target_pairs={{0,64},{64,0},{1,65},{65,1},{2,66},{66,2},{3,67},{67,3},{4,68},{68... | collective-permute-start | bytes 3145736 | tf_op jit(solution)/shard_map/ppermute | solution.py:386
  70.9 3.0 %collective-permute-start.9 = (bf16[512,1024]{1,0:T(8,128)(2,1)S(1)}, bf16[512,1024]{1,0:T(8,128)(2,1)S(1)}, u32[]{:S(2)}, u32[]{:S(2)}) collective-permute-start(bf16[512,1024]{1,0:T(8,128)(2,1)S(1)} %get-tuple-element.36), channel_id=1, source_target_pairs={{0,64},{64,0},{1,65},{65,1},{2,66},{66,2},{3,67},{67,3},{4,68},{68... | collective-permute-start | bytes 3145736 | tf_op jit(solution)/shard_map/ppermute | solution.py:386
  71.9 2.0 %copy-start.1 = (bf16[512,1024]{1,0:T(8,128)(2,1)S(1)}, bf16[512,1024]{1,0:T(8,128)(2,1)}, u32[]{:S(2)}) copy-start(bf16[512,1024]{1,0:T(8,128)(2,1)} %copy-done) | copy-start | bytes 3145732
  114.5 9.1 %collective-permute-start.11 = (bf16[2,24,768]{2,1,0:T(8,128)(2,1)S(1)}, bf16[2,24,768]{2,1,0:T(8,128)(2,1)S(1)}, u32[]{:S(2)}, u32[]{:S(2)}) collective-permute-start(bf16[2,24,768]{2,1,0:T(8,128)(2,1)S(1)} %get-tuple-element.40), channel_id=1, source_target_pairs={{0,32},{16,48},{32,0},{48,16},{1,33},{17,49},{33,1},{49,17},{2,34}... | collective-permute-start | bytes 221192 | tf_op jit(solution)/shard_map/ppermute | solution.py:382
  123.7 4.9 %collective-permute-start.12 = (bf16[24,768]{1,0:T(8,128)(2,1)S(1)}, bf16[24,768]{1,0:T(8,128)(2,1)S(1)}, u32[]{:S(2)}, u32[]{:S(2)}) collective-permute-start(bf16[24,768]{1,0:T(8,128)(2,1)S(1)} %get-tuple-element.42), channel_id=1, source_target_pairs={{0,16},{16,0},{32,48},{48,32},{1,17},{17,1},{33,49},{49,33},{2,18}... | collective-permute-start | bytes 110600 | tf_op jit(solution)/shard_map/ppermute | solution.py:382

commit v8 on v7

--- a/solution.py
+++ b/solution.py
@@ -101,17 +101,11 @@
     )(tiles, rows, cols, probe, cot)
 
 
-def flipped(place, bit):
-    if bit == 1:
-        return place + 1 - 2 * lax.rem(place, 2)
-    return lax.rem(place + 2, 4)
-
-
-def pack_kernel(peers, own, across, far, out, held, chunks, sems):
+def pack_kernel(peers, own, one, two, three, out, held, chunks, sems):
     zh = lax.axis_index("zh")
     x = lax.axis_index("x")
-    near = flipped(zh, 1)
-    for place, piece in ((zh, own), (near, across), (flipped(zh, 2), far.at[0]), (flipped(near, 2), far.at[1])):
+    for hops, piece in enumerate((own, one, two, three)):
+        place = lax.rem(zh - hops + 4, 4)
         held[pl.ds(pl.multiple_of(place * 24, 8), 24), :] = piece[...].astype(F32)
     lane = lax.broadcasted_iota(jnp.int32, (72, 256), 1)
     y = lax.axis_index("y")
@@ -141,11 +135,11 @@
     lax.fori_loop(0, 32, settle, 0)
 
 
-def pack(peers, own, across, far):
+def pack(peers, own, others):
     return pl.pallas_call(
         pack_kernel,
         out_shape=jax.ShapeDtypeStruct((32, 72, W), BF),
-        in_specs=[SMEM] + [VMEM] * 3,
+        in_specs=[SMEM] + [VMEM] * 4,
         out_specs=HBM,
         scratch_shapes=[
             pltpu.VMEM((96, OBJ), F32),
@@ -154,7 +148,7 @@
         ],
         compiler_params=params(16),
         name="pack",
-    )(peers, own, across, far)
+    )(peers, own, *others)
 
 
 def place_patch(source, base, patch, row_tile):
@@ -304,7 +298,7 @@
     )(tiles, count, local, remote, half)
 
 
-def gather_kernel(peers, got, kept, given, total):
+def gather_kernel(peers, got, own, one, two, three, total):
     zh = lax.axis_index("zh")
     x = lax.axis_index("x")
     total[...] = jnp.zeros((96, OBJ), F32)
@@ -326,60 +320,38 @@
         return carry
 
     lax.fori_loop(0, 16, source, 0)
-    near = flipped(zh, 1)
-    for i, place in enumerate((zh, near)):
-        kept[i] = total[pl.ds(pl.multiple_of(place * 24, 8), 24), :]
-        there = pl.multiple_of(flipped(place, 2) * 24, 8)
-        given[i] = total[pl.ds(there, 24), :].astype(BF)
+    for step, out in enumerate((own, one, two, three)):
+        place = lax.rem(zh + step, 4)
+        out[...] = total[pl.ds(pl.multiple_of(place * 24, 8), 24), :].astype(out.dtype)
 
 
 def gather(peers, got):
     return pl.pallas_call(
         gather_kernel,
-        out_shape=[jax.ShapeDtypeStruct((2, 24, OBJ), F32), jax.ShapeDtypeStruct((2, 24, OBJ), BF)],
+        out_shape=[jax.ShapeDtypeStruct((24, OBJ), F32)] + [jax.ShapeDtypeStruct((24, OBJ), BF)] * 3,
         in_specs=[SMEM, VMEM],
-        out_specs=[VMEM] * 2,
+        out_specs=[VMEM] * 4,
         scratch_shapes=[pltpu.VMEM((96, OBJ), F32)],
         compiler_params=params(16),
         name="gather",
     )(peers, got)
 
 
-def half_kernel(kept, far, own, given):
-    own[...] = kept[0] + far[0].astype(F32)
-    given[...] = (kept[1] + far[1].astype(F32)).astype(BF)
-
-
-def half_sum(kept, far):
-    return pl.pallas_call(
-        half_kernel,
-        out_shape=[jax.ShapeDtypeStruct((24, OBJ), F32), jax.ShapeDtypeStruct((24, OBJ), BF)],
-        in_specs=[VMEM] * 2,
-        out_specs=[VMEM] * 2,
-        compiler_params=params(4),
-        name="half_sum",
-    )(kept, far)
-
-
-def last_kernel(own, away, out):
-    total = own[...] + away[...].astype(F32)
+def last_kernel(own, one, two, three, out):
+    total = own[...] + one[...].astype(F32) + two[...].astype(F32) + three[...].astype(F32)
     out[:, 0, :] = total[0:12]
     out[:, 1, :] = total[12:24]
 
 
-def last_sum(own, away):
+def last_sum(own, others):
     return pl.pallas_call(
         last_kernel,
         out_shape=jax.ShapeDtypeStruct((12, 2, OBJ), F32),
-        in_specs=[VMEM] * 2,
+        in_specs=[VMEM] * 4,
         out_specs=VMEM,
         compiler_params=params(4),
         name="last_sum",
-    )(own, away)
-
-
-def swap(value, axis, bit):
-    return lax.ppermute(value, axis, [(i, i ^ bit) for i in range(4)])
+    )(own, *others)
 
 
 def turn(value, axis, step, count):
@@ -389,10 +361,9 @@
 def on_device(probe_wave, prop_rows, prop_cols, transmission, exit_cotangent, window_tiles, slot_count):
     line = jnp.stack([window_tiles] + [turn(window_tiles, "y", hops, 4) for hops in (1, 2, 3)])
     piece = transmission.reshape(24, OBJ)
-    across = swap(piece, "zh", 1)
-    far = swap(jnp.stack([piece, across]), "zh", 2)
+    others = [turn(piece, "zh", hops, 4) for hops in (1, 2, 3)]
     peers = jnp.stack([line] + [turn(line, "x", hops, 4) for hops in (1, 2, 3)])
-    sent = pack(peers, piece, across, far)
+    sent = pack(peers, piece, others)
     sent, rows = lax.optimization_barrier((sent, prop_rows))
     own = lax.all_to_all(sent, ("zl", "x", "y"), 0, 0, tiled=True)
     mats = prep(window_tiles, rows, prop_cols, probe_wave, exit_cotangent)
@@ -408,9 +379,8 @@
     half = early(window_tiles, slot_count, middle, first_away)
     contrib = late(window_tiles, slot_count, state, last_away, half)
     got = lax.all_to_all(contrib, ("zl", "x", "y"), 0, 0, tiled=True)
-    kept, given = gather(peers, got)
-    own, given = half_sum(kept, swap(given, "zh", 2))
-    total = last_sum(own, swap(given, "zh", 1))
+    here, *away = gather(peers, got)
+    total = last_sum(here, [turn(away[hops - 1], "zh", hops, 4) for hops in (2, 1, 3)])
     return jnp.transpose(total, (1, 0, 2))[None]
 
 

time: 130 us -> 129 us (level)
  waiting for transfers between devices: 30.6 us -> 26.4 us
  starting transfers between devices: 29.2 us -> 32.2 us
    ppermute x9 -> x15, starting transfers between devices: 12.4 us -> 27.1 us  [turn(): lax.ppermute(value, axis, [(i, (i + step) % count) for i in range(count)])]
    ppermute x4 -> x0, waiting for transfers between devices: 11.6 us -> none  [swap(): return lax.ppermute(value, axis, [(i, i ^ bit) for i in range(4)])]
    ppermute x4 -> x0, starting transfers between devices: 10.9 us -> none  [swap(): return lax.ppermute(value, axis, [(i, i ^ bit) for i in range(4)])]
    ppermute x9 -> x15, waiting for transfers between devices: 2.24 us -> 9.34 us  [turn(): lax.ppermute(value, axis, [(i, (i + step) % count) for i in range(count)])]
  transfers between devices with their start and end apart: 14 -> 16, of which waited for: 7 -> 6; matrix products, arithmetic and copies ran while one was open for 2% -> 2% of each run, Pallas kernels for 12% -> 12%
where the time goes in v8:
time: 129 us; the launch traced here: 128 us
  blocking collectives  37.9 us (29%)
  starting transfers between devices  32.2 us (25%)
  waiting for transfers between devices  26.4 us (20%)
  Pallas kernels  22 us (17%)
  local copies, waits for them, and re-layouts  7.79 us (6%)
  other arithmetic  1.38 us (1%)
    all_to_all x1, blocking collectives, on_device(): got = lax.all_to_all(contrib, ('zl', 'x', 'y'), 0, 0, tiled=True)  37.9 us
    ppermute x15, starting transfers between devices, turn(): lax.ppermute(value, axis, [(i, (i + step) % count) for i in range(count)])  27.1 us
    all_to_all x1, waiting for transfers between devices, on_device(): own = lax.all_to_all(sent, ('zl', 'x', 'y'), 0, 0, tiled=True)  17 us
    ppermute x15, waiting for transfers between devices, turn(): lax.ppermute(value, axis, [(i, (i + step) % count) for i in range(count)])  9.34 us
    unnamed x19, local copies, waits for them, and re-layouts  7.77 us
    pallas_call x1, Pallas kernels, close_steps(): pl.pallas_call(close_kernel, out_shape=[STATE, SENT], in_specs=[SMEM] + [...  5.87 us
    pallas_call x1, Pallas kernels, open_step(): pl.pallas_call(open_kernel, out_shape=[STATE, SENT, SQUARE, SQUARE], in_s...  5.02 us
    all_to_all x1, starting transfers between devices, on_device(): own = lax.all_to_all(sent, ('zl', 'x', 'y'), 0, 0, tiled=True)  5 us
  transfers between devices with their start and end apart: 16, of which 6 were waited for; matrix products, arithmetic and copies ran while one was open for 2% of the time, Pallas kernels for 12%

profile of v8, /device:TPU:64, one launch (start us, length us, event | category | flops | bytes accessed | tf_op | source)
XLA Modules:
  0.0 128.5 jit_solution(115982845164420688)
XLA Ops:
  0.0 1.6 %collective-permute-start = (s32[2,2]{1,0:T(2,128)}, s32[2,2]{1,0:T(2,128)S(1)}, u32[]{:S(2)}, u32[]{:S(2)}) collective-permute-start(s32[2,2]{1,0:T(2,128)} %tiles.9), channel_id=1, source_target_pairs={{0,1},{1,2},{2,3},{3,0},{4,5},{5,6},{6,7},{7,4},{8,9},{9,10},{10,1... | collective-permute-start | bytes 56 | tf_op jit(solution)/shard_map/ppermute | solution.py:358
  1.6 2.9 %collective-permute-start.1 = (s32[2,2]{1,0:T(2,128)}, s32[2,2]{1,0:T(2,128)S(1)}, u32[]{:S(2)}, u32[]{:S(2)}) collective-permute-start(s32[2,2]{1,0:T(2,128)} %tiles.9), channel_id=1, source_target_pairs={{0,2},{1,3},{2,0},{3,1},{4,6},{5,7},{6,4},{7,5},{8,10},{9,11},{10,... | collective-permute-start | bytes 56 | tf_op jit(solution)/shard_map/ppermute | solution.py:358
  4.5 1.3 %collective-permute-start.2 = (s32[2,2]{1,0:T(2,128)}, s32[2,2]{1,0:T(2,128)S(1)}, u32[]{:S(2)}, u32[]{:S(2)}) collective-permute-start(s32[2,2]{1,0:T(2,128)} %tiles.9), channel_id=1, source_target_pairs={{0,3},{1,0},{2,1},{3,2},{4,7},{5,4},{6,5},{7,6},{8,11},{9,8},{10,9... | collective-permute-start | bytes 56 | tf_op jit(solution)/shard_map/ppermute | solution.py:358
  6.6 4.6 %collective-permute-start.6 = (bf16[24,768]{1,0:T(8,128)(2,1)S(1)}, bf16[24,768]{1,0:T(8,128)(2,1)S(1)}, u32[]{:S(2)}, u32[]{:S(2)}) collective-permute-start(bf16[24,768]{1,0:T(8,128)(2,1)S(1)} %reshape.3.own), channel_id=1, source_target_pairs={{0,16},{16,32},{32,48},{48,0},{1,17},{17,33},{33,49},{49,1},{2,18}... | collective-permute-start | bytes 110600 | tf_op jit(solution)/shard_map/ppermute | solution.py:358
  12.2 2.8 %collective-permute-start.8 = (bf16[24,768]{1,0:T(8,128)(2,1)S(1)}, bf16[24,768]{1,0:T(8,128)(2,1)S(1)}, u32[]{:S(2)}, u32[]{:S(2)}) collective-permute-start(bf16[24,768]{1,0:T(8,128)(2,1)S(1)} %reshape.3.own), channel_id=1, source_target_pairs={{0,48},{16,0},{32,16},{48,32},{1,49},{17,1},{33,17},{49,33},{2,50}... | collective-permute-start | bytes 110600 | tf_op jit(solution)/shard_map/ppermute | solution.py:358
  15.7 1.5 %collective-permute-start.3 = (s32[4,2,2]{2,1,0:T(2,128)S(1)}, s32[4,2,2]{2,1,0:T(2,128)S(1)}, u32[]{:S(2)}, u32[]{:S(2)}) collective-permute-start(s32[4,2,2]{2,1,0:T(2,128)S(1)} %pad_add_fusion.1), channel_id=1, source_target_pairs={{0,4},{4,8},{8,12},{12,0},{1,5},{5,9},{9,13},{13,1},{2,6},{6,10},{... | collective-permute-start | bytes 200 | tf_op jit(solution)/shard_map/ppermute | solution.py:358
  17.2 2.7 %collective-permute-start.4 = (s32[4,2,2]{2,1,0:T(2,128)S(1)}, s32[4,2,2]{2,1,0:T(2,128)S(1)}, u32[]{:S(2)}, u32[]{:S(2)}) collective-permute-start(s32[4,2,2]{2,1,0:T(2,128)S(1)} %pad_add_fusion.1), channel_id=1, source_target_pairs={{0,8},{4,12},{8,0},{12,4},{1,9},{5,13},{9,1},{13,5},{2,10},{6,14},... | collective-permute-start | bytes 200 | tf_op jit(solution)/shard_map/ppermute | solution.py:358
  20.6 1.5 %collective-permute-start.5 = (s32[4,2,2]{2,1,0:T(2,128)S(1)}, s32[4,2,2]{2,1,0:T(2,128)S(1)}, u32[]{:S(2)}, u32[]{:S(2)}) collective-permute-start(s32[4,2,2]{2,1,0:T(2,128)S(1)} %pad_add_fusion.1), channel_id=1, source_target_pairs={{0,12},{4,0},{8,4},{12,8},{1,13},{5,1},{9,5},{13,9},{2,14},{6,2},{... | collective-permute-start | bytes 200 | tf_op jit(solution)/shard_map/ppermute | solution.py:358
  22.3 1.9 %collective-permute-done.5 = s32[4,2,2]{2,1,0:T(2,128)S(1)} collective-permute-done((s32[4,2,2]{2,1,0:T(2,128)S(1)}, s32[4,2,2]{2,1,0:T(2,128)S(1)}, u32[]{:S(2)}, u32[]{:S(2)}) %collective-permute-start.5) | collective-permute-done | bytes 96 | tf_op jit(solution)/shard_map/ppermute | solution.py:358
  24.3 2.7 %pack.1 = bf16[32,72,512]{2,1,0:T(8,128)(2,1)} custom-call(s32[4,4,2,2]{3,2,1,0:T(2,128)S(1)} %pad_add_fusion.peers, bf16[24,768]{1,0:T(8,128)(2,1)S(1)} %reshape.3.own, bf16[24,768]{1,0:T(8,128)(2,1)S(1)} %collective-permute-done.6.one, bf16[24,768]{1,0:T(8,128)(2,1)S(1)} %collective-permute-done.7.two, bf16[24,768]{1,0:T(8,128)(2,1)S(1)} %collective-permute-done.8.three), custom_call_target="tpu_custom_call" | custom-call | tf_op jit(solution)/shard_map/pack/pallas_call | solution.py:139
  27.0 5.0 %all-to-all-start = ((bf16[32,72,512]{2,1,0:T(8,128)(2,1)}), bf16[32,72,512]{2,1,0:T(8,128)(2,1)S(1)}, u32[]{:S(2)}, u32[]{:S(2)}) async-start(bf16[32,72,512]{2,1,0:T(8,128)(2,1)} %pack.1), calls=%async_computation | async-start | bytes 4718592 | tf_op jit(solution)/shard_map/all_to_all | solution.py:368
  32.0 1.6 %copy-done.3 = bf16[2,2,512,512]{3,2,1,0:T(8,128)(2,1)S(1)} copy-done((bf16[2,2,512,512]{3,2,1,0:T(8,128)(2,1)S(1)}, bf16[2,2,512,512]{3,2,1,0:T(8,128)(2,1)}, u32[]{:S(2)}) %copy-start.3) | copy-done | bytes 2097176
  36.1 3.4 %prep.1 = (bf16[512,1024]{1,0:T(8,128)(2,1)S(1)}, bf16[512,1024]{1,0:T(8,128)(2,1)S(1)}, bf16[512,1024]{1,0:T(8,128)(2,1)S(1)}) custom-call(s32[2,2]{1,0:T(2,128)S(1)} %copy-done.2, bf16[2,512,512]{2,1,0:T(8,128)(2,1)S(1)} %copy-done.4, bf16[2,512,512]{2,1,0:T(8,128)(2,1)S(1)} %copy-done.5, bf16[2,512,512]{2,1,0:T(8,128)(2,1)S(1)} %copy-done.6, ...), custom_call_target="tpu_custom_call" | custom-call | flops 4000000000 | bytes 20000000 | tf_op jit(solution)/shard_map/prep/pallas_call | solution.py:92
  42.4 17.0 %all-to-all-done.own = bf16[32,72,512]{2,1,0:T(8,128)(2,1)S(1)} async-done(((bf16[32,72,512]{2,1,0:T(8,128)(2,1)}), bf16[32,72,512]{2,1,0:T(8,128)(2,1)S(1)}, u32[]{:S(2)}, u32[]{:S(2)}) %all-to-all-start) | async-done | bytes 2359328 | tf_op jit(solution)/shard_map/all_to_all | solution.py:368
  59.5 5.0 %open_step.1 = (f32[512,1024]{1,0:T(8,128)S(1)}, bf16[512,1024]{1,0:T(8,128)(2,1)S(1)}, bf16[1024,1024]{1,0:T(8,128)(2,1)S(1)}, bf16[1024,1024]{1,0:T(8,128)(2,1)S(1)}) custom-call(s32[2,2]{1,0:T(2,128)S(1)} %copy-done.2, bf16[32,72,512]{2,1,0:T(8,128)(2,1)S(1)} %all-to-all-done.own, bf16[512,1024]{1,0:T(8,128)(2,1)} %copy-done.7, ...), custom_call_target="tpu_custom_call" | custom-call | flops 4000000000 | bytes 10000000 | tf_op jit(solution)/shard_map/open_step/pallas_call | solution.py:226
  65.1 5.9 %close_steps.1 = (f32[512,1024]{1,0:T(8,128)S(1)}, bf16[512,1024]{1,0:T(8,128)(2,1)S(1)}) custom-call(s32[2,2]{1,0:T(2,128)S(1)} %copy-done.2, bf16[32,72,512]{2,1,0:T(8,128)(2,1)S(1)} %all-to-all-done.own, bf16[32,72,512]{2,1,0:T(8,128)(2,1)S(1)} %collective-permute-done.9.other, bf16[1024,1024]{1,0:T(8,128)(2,1)S(1)} %get-tuple-element.33.v1, ...), custom_call_target="tpu_custom_call" | custom-call | flops 8000000000 | bytes 10000000 | tf_op jit(solution)/shard_map/close_steps/pallas_call | solution.py:251
  71.9 1.2 early.1.half
  73.9 1.4 %late.1 = bf16[32,72,512]{2,1,0:T(8,128)(2,1)S(1)} custom-call(s32[2,2]{1,0:T(2,128)S(1)} %copy-done.2, s32[1]{0:T(128)S(6)} %copy.30.count, bf16[512,1024]{1,0:T(8,128)(2,1)S(1)} %copy-done.1, bf16[512,1024]{1,0:T(8,128)(2,1)S(1)} %collective-permute-done.10.remote, bf16[16,72,512]{2,1,0:T(8,128)(2,1)S(1)} %early.1.half), custom_call_target="tpu_custom_call" | custom-call | tf_op jit(solution)/shard_map/late/pallas_call | solution.py:290
  75.3 37.9 %all_to_all.10.got = bf16[32,72,512]{2,1,0:T(8,128)(2,1)S(1)} all-to-all(bf16[32,72,512]{2,1,0:T(8,128)(2,1)S(1)} %late.1), channel_id=1, replica_groups=mesh['zl'=2,'core'=2,'zh'=4,'x'=4,'y'=4] {'zl','x','y'}, dimensions={0} | all-to-all | bytes 4718592 | tf_op jit(solution)/shard_map/all_to_all | solution.py:381
  113.2 1.8 %gather.1 = (f32[24,768]{1,0:T(8,128)S(1)}, bf16[24,768]{1,0:T(8,128)(2,1)S(1)}, bf16[24,768]{1,0:T(8,128)(2,1)S(1)}, bf16[24,768]{1,0:T(8,128)(2,1)S(1)}) custom-call(s32[4,4,2,2]{3,2,1,0:T(2,128)S(1)} %pad_add_fusion.peers, bf16[32,72,512]{2,1,0:T(8,128)(2,1)S(1)} %all_to_all.10.got), custom_call_target="tpu_custom_call" | custom-call | tf_op jit(solution)/shard_map/gather/pallas_call | solution.py:329
  115.0 2.7 %collective-permute-start.12 = (bf16[24,768]{1,0:T(8,128)(2,1)S(1)}, bf16[24,768]{1,0:T(8,128)(2,1)S(1)}, u32[]{:S(2)}, u32[]{:S(2)}) collective-permute-start(bf16[24,768]{1,0:T(8,128)(2,1)S(1)} %get-tuple-element.40), channel_id=1, source_target_pairs={{0,32},{16,48},{32,0},{48,16},{1,33},{17,49},{33,1},{49,17},{2,34}... | collective-permute-start | bytes 110600 | tf_op jit(solution)/shard_map/ppermute | solution.py:358
  117.7 3.6 %collective-permute-start.13 = (bf16[24,768]{1,0:T(8,128)(2,1)S(1)}, bf16[24,768]{1,0:T(8,128)(2,1)S(1)}, u32[]{:S(2)}, u32[]{:S(2)}) collective-permute-start(bf16[24,768]{1,0:T(8,128)(2,1)S(1)} %get-tuple-element.41), channel_id=1, source_target_pairs={{0,16},{16,32},{32,48},{48,0},{1,17},{17,33},{33,49},{49,1},{2,18}... | collective-permute-start | bytes 110600 | tf_op jit(solution)/shard_map/ppermute | solution.py:358
  121.3 1.8 %collective-permute-done.12.one = bf16[24,768]{1,0:T(8,128)(2,1)S(1)} collective-permute-done((bf16[24,768]{1,0:T(8,128)(2,1)S(1)}, bf16[24,768]{1,0:T(8,128)(2,1)S(1)}, u32[]{:S(2)}, u32[]{:S(2)}) %collective-permute-start.12) | collective-permute-done | bytes 36896 | tf_op jit(solution)/shard_map/ppermute | solution.py:358
  123.2 4.6 %collective-permute-done.14.three = bf16[24,768]{1,0:T(8,128)(2,1)S(1)} collective-permute-done((bf16[24,768]{1,0:T(8,128)(2,1)S(1)}, bf16[24,768]{1,0:T(8,128)(2,1)S(1)}, u32[]{:S(2)}, u32[]{:S(2)}) %collective-permute-start.14) | collective-permute-done | bytes 36896 | tf_op jit(solution)/shard_map/ppermute | solution.py:358
  (40 shorter events, 11.2 us)
Async XLA Ops:
  0.0 12.2 %collective-permute-start = (s32[2,2]{1,0:T(2,128)}, s32[2,2]{1,0:T(2,128)S(1)}, u32[]{:S(2)}, u32[]{:S(2)}) collective-permute-start(s32[2,2]{1,0:T(2,128)} %tiles.9), channel_id=1, source_target_pairs={{0,1},{1,2},{2,3},{3,0},{4,5},{5,6},{6,7},{7,4},{8,9},{9,10},{10,1... | collective-permute-start | bytes 56 | tf_op jit(solution)/shard_map/ppermute | solution.py:358
  1.6 13.4 %collective-permute-start.1 = (s32[2,2]{1,0:T(2,128)}, s32[2,2]{1,0:T(2,128)S(1)}, u32[]{:S(2)}, u32[]{:S(2)}) collective-permute-start(s32[2,2]{1,0:T(2,128)} %tiles.9), channel_id=1, source_target_pairs={{0,2},{1,3},{2,0},{3,1},{4,6},{5,7},{6,4},{7,5},{8,10},{9,11},{10,... | collective-permute-start | bytes 56 | tf_op jit(solution)/shard_map/ppermute | solution.py:358
  4.5 10.5 %collective-permute-start.2 = (s32[2,2]{1,0:T(2,128)}, s32[2,2]{1,0:T(2,128)S(1)}, u32[]{:S(2)}, u32[]{:S(2)}) collective-permute-start(s32[2,2]{1,0:T(2,128)} %tiles.9), channel_id=1, source_target_pairs={{0,3},{1,0},{2,1},{3,2},{4,7},{5,4},{6,5},{7,6},{8,11},{9,8},{10,9... | collective-permute-start | bytes 56 | tf_op jit(solution)/shard_map/ppermute | solution.py:358
  6.6 17.6 %collective-permute-start.6 = (bf16[24,768]{1,0:T(8,128)(2,1)S(1)}, bf16[24,768]{1,0:T(8,128)(2,1)S(1)}, u32[]{:S(2)}, u32[]{:S(2)}) collective-permute-start(bf16[24,768]{1,0:T(8,128)(2,1)S(1)} %reshape.3.own), channel_id=1, source_target_pairs={{0,16},{16,32},{32,48},{48,0},{1,17},{17,33},{33,49},{49,1},{2,18}... | collective-permute-start | bytes 110600 | tf_op jit(solution)/shard_map/ppermute | solution.py:358
  11.2 13.1 %collective-permute-start.7 = (bf16[24,768]{1,0:T(8,128)(2,1)S(1)}, bf16[24,768]{1,0:T(8,128)(2,1)S(1)}, u32[]{:S(2)}, u32[]{:S(2)}) collective-permute-start(bf16[24,768]{1,0:T(8,128)(2,1)S(1)} %reshape.3.own), channel_id=1, source_target_pairs={{0,32},{16,48},{32,0},{48,16},{1,33},{17,49},{33,1},{49,17},{2,34}... | collective-permute-start | bytes 110600 | tf_op jit(solution)/shard_map/ppermute | solution.py:358
  12.2 12.1 %collective-permute-start.8 = (bf16[24,768]{1,0:T(8,128)(2,1)S(1)}, bf16[24,768]{1,0:T(8,128)(2,1)S(1)}, u32[]{:S(2)}, u32[]{:S(2)}) collective-permute-start(bf16[24,768]{1,0:T(8,128)(2,1)S(1)} %reshape.3.own), channel_id=1, source_target_pairs={{0,48},{16,0},{32,16},{48,32},{1,49},{17,1},{33,17},{49,33},{2,50}... | collective-permute-start | bytes 110600 | tf_op jit(solution)/shard_map/ppermute | solution.py:358
  15.7 4.9 %collective-permute-start.3 = (s32[4,2,2]{2,1,0:T(2,128)S(1)}, s32[4,2,2]{2,1,0:T(2,128)S(1)}, u32[]{:S(2)}, u32[]{:S(2)}) collective-permute-start(s32[4,2,2]{2,1,0:T(2,128)S(1)} %pad_add_fusion.1), channel_id=1, source_target_pairs={{0,4},{4,8},{8,12},{12,0},{1,5},{5,9},{9,13},{13,1},{2,6},{6,10},{... | collective-permute-start | bytes 200 | tf_op jit(solution)/shard_map/ppermute | solution.py:358
  17.2 5.1 %collective-permute-start.4 = (s32[4,2,2]{2,1,0:T(2,128)S(1)}, s32[4,2,2]{2,1,0:T(2,128)S(1)}, u32[]{:S(2)}, u32[]{:S(2)}) collective-permute-start(s32[4,2,2]{2,1,0:T(2,128)S(1)} %pad_add_fusion.1), channel_id=1, source_target_pairs={{0,8},{4,12},{8,0},{12,4},{1,9},{5,13},{9,1},{13,5},{2,10},{6,14},... | collective-permute-start | bytes 200 | tf_op jit(solution)/shard_map/ppermute | solution.py:358
  20.6 3.6 %collective-permute-start.5 = (s32[4,2,2]{2,1,0:T(2,128)S(1)}, s32[4,2,2]{2,1,0:T(2,128)S(1)}, u32[]{:S(2)}, u32[]{:S(2)}) collective-permute-start(s32[4,2,2]{2,1,0:T(2,128)S(1)} %pad_add_fusion.1), channel_id=1, source_target_pairs={{0,12},{4,0},{8,4},{12,8},{1,13},{5,1},{9,5},{13,9},{2,14},{6,2},{... | collective-permute-start | bytes 200 | tf_op jit(solution)/shard_map/ppermute | solution.py:358
  27.0 5.0 %copy-start.2 = (s32[2,2]{1,0:T(2,128)S(1)}, s32[2,2]{1,0:T(2,128)}, u32[]{:S(2)}) copy-start(s32[2,2]{1,0:T(2,128)} %tiles.9) | copy-start | bytes 52
  27.0 5.0 %copy-start.4 = (bf16[2,512,512]{2,1,0:T(8,128)(2,1)S(1)}, bf16[2,512,512]{2,1,0:T(8,128)(2,1)}, u32[]{:S(2)}) copy-start(bf16[2,512,512]{2,1,0:T(8,128)(2,1)} %rows) | copy-start | bytes 3145732
  27.0 32.5 %all-to-all-start = ((bf16[32,72,512]{2,1,0:T(8,128)(2,1)}), bf16[32,72,512]{2,1,0:T(8,128)(2,1)S(1)}, u32[]{:S(2)}, u32[]{:S(2)}) async-start(bf16[32,72,512]{2,1,0:T(8,128)(2,1)} %pack.1), calls=%async_computation | async-start | bytes 4718592 | tf_op jit(solution)/shard_map/all_to_all | solution.py:368
  32.0 1.6 %copy-start.3 = (bf16[2,2,512,512]{3,2,1,0:T(8,128)(2,1)S(1)}, bf16[2,2,512,512]{3,2,1,0:T(8,128)(2,1)}, u32[]{:S(2)}) copy-start(bf16[2,2,512,512]{3,2,1,0:T(8,128)(2,1)} %cot.1) | copy-start | bytes 6291460
  33.6 1.2 copy-start.5
  34.8 1.2 copy-start.6
  39.4 1.0 copy-start
  41.4 1.0 copy-start.8
  59.4 5.6 %collective-permute-start.9 = (bf16[32,72,512]{2,1,0:T(8,128)(2,1)S(1)}, bf16[32,72,512]{2,1,0:T(8,128)(2,1)S(1)}, u32[]{:S(2)}, u32[]{:S(2)}) collective-permute-start(bf16[32,72,512]{2,1,0:T(8,128)(2,1)S(1)} %all-to-all-done.own), channel_id=1, source_target_pairs={{0,64},{64,0},{1,65},{65,1},{2,66},{66,2},{3,67},{67,3},{4,68},{68... | collective-permute-start | bytes 7077896 | tf_op jit(solution)/shard_map/ppermute | solution.py:358
  64.5 7.5 %collective-permute-start.11 = (bf16[512,1024]{1,0:T(8,128)(2,1)S(1)}, bf16[512,1024]{1,0:T(8,128)(2,1)S(1)}, u32[]{:S(2)}, u32[]{:S(2)}) collective-permute-start(bf16[512,1024]{1,0:T(8,128)(2,1)S(1)} %get-tuple-element.38), channel_id=1, source_target_pairs={{0,64},{64,0},{1,65},{65,1},{2,66},{66,2},{3,67},{67,3},{4,68},{68... | collective-permute-start | bytes 3145736 | tf_op jit(solution)/shard_map/ppermute | solution.py:358
  70.9 3.0 %collective-permute-start.10 = (bf16[512,1024]{1,0:T(8,128)(2,1)S(1)}, bf16[512,1024]{1,0:T(8,128)(2,1)S(1)}, u32[]{:S(2)}, u32[]{:S(2)}) collective-permute-start(bf16[512,1024]{1,0:T(8,128)(2,1)S(1)} %get-tuple-element.36), channel_id=1, source_target_pairs={{0,64},{64,0},{1,65},{65,1},{2,66},{66,2},{3,67},{67,3},{4,68},{68... | collective-permute-start | bytes 3145736 | tf_op jit(solution)/shard_map/ppermute | solution.py:358
  71.9 2.0 %copy-start.1 = (bf16[512,1024]{1,0:T(8,128)(2,1)S(1)}, bf16[512,1024]{1,0:T(8,128)(2,1)}, u32[]{:S(2)}) copy-start(bf16[512,1024]{1,0:T(8,128)(2,1)} %copy-done) | copy-start | bytes 3145732
  115.0 8.2 %collective-permute-start.12 = (bf16[24,768]{1,0:T(8,128)(2,1)S(1)}, bf16[24,768]{1,0:T(8,128)(2,1)S(1)}, u32[]{:S(2)}, u32[]{:S(2)}) collective-permute-start(bf16[24,768]{1,0:T(8,128)(2,1)S(1)} %get-tuple-element.40), channel_id=1, source_target_pairs={{0,32},{16,48},{32,0},{48,16},{1,33},{17,49},{33,1},{49,17},{2,34}... | collective-permute-start | bytes 110600 | tf_op jit(solution)/shard_map/ppermute | solution.py:358
  117.7 5.5 %collective-permute-start.13 = (bf16[24,768]{1,0:T(8,128)(2,1)S(1)}, bf16[24,768]{1,0:T(8,128)(2,1)S(1)}, u32[]{:S(2)}, u32[]{:S(2)}) collective-permute-start(bf16[24,768]{1,0:T(8,128)(2,1)S(1)} %get-tuple-element.41), channel_id=1, source_target_pairs={{0,16},{16,32},{32,48},{48,0},{1,17},{17,33},{33,49},{49,1},{2,18}... | collective-permute-start | bytes 110600 | tf_op jit(solution)/shard_map/ppermute | solution.py:358
  121.3 6.5 %collective-permute-start.14 = (bf16[24,768]{1,0:T(8,128)(2,1)S(1)}, bf16[24,768]{1,0:T(8,128)(2,1)S(1)}, u32[]{:S(2)}, u32[]{:S(2)}) collective-permute-start(bf16[24,768]{1,0:T(8,128)(2,1)S(1)} %get-tuple-element.42), channel_id=1, source_target_pairs={{0,48},{16,0},{32,16},{48,32},{1,49},{17,1},{33,17},{49,33},{2,50}... | collective-permute-start | bytes 110600 | tf_op jit(solution)/shard_map/ppermute | solution.py:358
  (1 other events, 1.0 us)

commit v9 on v8

--- a/solution.py
+++ b/solution.py
@@ -165,7 +165,7 @@
     lax.fori_loop(0, 4, place, 0)
 
 
-def form_contrib(local, remote, contrib, out, sign, used, row_tile):
+def form_contrib(local, remote, contrib, out, sign, used, row_tile, formed=None):
     ar = local[:, 0:W].astype(F32)
     ai = local[:, W:].astype(F32)
     br = remote[:, 0:W].astype(F32)
@@ -182,6 +182,8 @@
         ]
         for y in range(4):
             out[plane * 4 + y] = jnp.concatenate([b[12 * y : 12 * y + 12] for b in blocks]).astype(BF)
+            if formed is not None:
+                formed(plane * 4 + y)
         return carry
 
     lax.fori_loop(0, 4, cut, 0)
@@ -279,11 +281,23 @@
     )(tiles, count, local, remote)
 
 
-def late_kernel(tiles, count, local, remote, half, out, contrib):
+def late_kernel(tiles, count, local, remote, half, out, contrib, chunks, sems):
     core, sign, row_tile = role(tiles)
     used = lax.axis_index("zl") < count[0]
-    out[pl.ds((1 - core) * 16, 16)] = half[...]
-    form_contrib(local, remote, contrib, out.at[pl.ds(core * 16, 16)], sign, used, row_tile)
+    whole = pltpu.make_async_copy(half, out.at[pl.ds((1 - core) * 16, 16)], sems.at[16])
+    whole.start()
+
+    def moved(i):
+        return pltpu.make_async_copy(chunks.at[i], out.at[core * 16 + i], sems.at[i])
+
+    form_contrib(local, remote, contrib, chunks, sign, used, row_tile, lambda i: moved(i).start())
+
+    def settle(i, carry):
+        moved(i).wait()
+        return carry
+
+    lax.fori_loop(0, 16, settle, 0)
+    whole.wait()
 
 
 def late(tiles, count, local, remote, half):
@@ -291,8 +305,8 @@
         late_kernel,
         out_shape=jax.ShapeDtypeStruct((32, 72, W), BF),
         in_specs=[SMEM] * 2 + [VMEM] * 3,
-        out_specs=VMEM,
-        scratch_shapes=WORK[:1],
+        out_specs=HBM,
+        scratch_shapes=WORK[:1] + [pltpu.VMEM((16, 72, W), BF), pltpu.SemaphoreType.DMA((17,))],
         compiler_params=params(24),
         name="late",
     )(tiles, count, local, remote, half)
@@ -378,6 +392,7 @@
     last_away = turn(last, "core", 1, 2)
     half = early(window_tiles, slot_count, middle, first_away)
     contrib = late(window_tiles, slot_count, state, last_away, half)
+    contrib = pltpu.with_memory_space_constraint(contrib, pltpu.HBM)
     got = lax.all_to_all(contrib, ("zl", "x", "y"), 0, 0, tiled=True)
     here, *away = gather(peers, got)
     total = last_sum(here, [turn(away[hops - 1], "zh", hops, 4) for hops in (2, 1, 3)])

time: 129 us -> 132 us (1.023)
  Pallas kernels: 22 us -> 25 us
    pallas_call x1, Pallas kernels: 1.42 us -> 3.51 us  [late(): pl.pallas_call(late_kernel, out_shape=jax.ShapeDtypeStruct((32, 72, W), B...]
where the time goes in v9:
time: 132 us
  blocking collectives  38 us (29%)
  starting transfers between devices  32.2 us (24%)
  waiting for transfers between devices  26.4 us (20%)
  Pallas kernels  25 us (19%)
  local copies, waits for them, and re-layouts  7.79 us (6%)
  other arithmetic  1.38 us (1%)
    all_to_all x1, blocking collectives, on_device(): got = lax.all_to_all(contrib, ('zl', 'x', 'y'), 0, 0, tiled=True)  38 us
    ppermute x15, starting transfers between devices, turn(): lax.ppermute(value, axis, [(i, (i + step) % count) for i in range(count)])  27.1 us
    all_to_all x1, waiting for transfers between devices, on_device(): own = lax.all_to_all(sent, ('zl', 'x', 'y'), 0, 0, tiled=True)  17 us
    ppermute x15, waiting for transfers between devices, turn(): lax.ppermute(value, axis, [(i, (i + step) % count) for i in range(count)])  9.34 us
    unnamed x19, local copies, waits for them, and re-layouts  7.77 us
    pallas_call x1, Pallas kernels, close_steps(): pl.pallas_call(close_kernel, out_shape=[STATE, SENT], in_specs=[SMEM] + [...  5.87 us
    pallas_call x1, Pallas kernels, open_step(): pl.pallas_call(open_kernel, out_shape=[STATE, SENT, SQUARE, SQUARE], in_s...  5.02 us
    all_to_all x1, starting transfers between devices, on_device(): own = lax.all_to_all(sent, ('zl', 'x', 'y'), 0, 0, tiled=True)  5 us
  transfers between devices with their start and end apart: 16, of which 6 were waited for; matrix products, arithmetic and copies ran while one was open for 2% of the time, Pallas kernels for 12%

profile of v9, /device:TPU:64, one launch (start us, length us, event | category | flops | bytes accessed | tf_op | source)
XLA Modules:
  0.0 131.5 jit_solution(2125412438104389945)
XLA Ops:
  0.0 1.6 %collective-permute-start = (s32[2,2]{1,0:T(2,128)}, s32[2,2]{1,0:T(2,128)S(1)}, u32[]{:S(2)}, u32[]{:S(2)}) collective-permute-start(s32[2,2]{1,0:T(2,128)} %tiles.9), channel_id=1, source_target_pairs={{0,1},{1,2},{2,3},{3,0},{4,5},{5,6},{6,7},{7,4},{8,9},{9,10},{10,1... | collective-permute-start | bytes 56 | tf_op jit(solution)/shard_map/ppermute | solution.py:372
  1.6 2.9 %collective-permute-start.1 = (s32[2,2]{1,0:T(2,128)}, s32[2,2]{1,0:T(2,128)S(1)}, u32[]{:S(2)}, u32[]{:S(2)}) collective-permute-start(s32[2,2]{1,0:T(2,128)} %tiles.9), channel_id=1, source_target_pairs={{0,2},{1,3},{2,0},{3,1},{4,6},{5,7},{6,4},{7,5},{8,10},{9,11},{10,... | collective-permute-start | bytes 56 | tf_op jit(solution)/shard_map/ppermute | solution.py:372
  4.5 1.3 %collective-permute-start.2 = (s32[2,2]{1,0:T(2,128)}, s32[2,2]{1,0:T(2,128)S(1)}, u32[]{:S(2)}, u32[]{:S(2)}) collective-permute-start(s32[2,2]{1,0:T(2,128)} %tiles.9), channel_id=1, source_target_pairs={{0,3},{1,0},{2,1},{3,2},{4,7},{5,4},{6,5},{7,6},{8,11},{9,8},{10,9... | collective-permute-start | bytes 56 | tf_op jit(solution)/shard_map/ppermute | solution.py:372
  6.6 4.6 %collective-permute-start.6 = (bf16[24,768]{1,0:T(8,128)(2,1)S(1)}, bf16[24,768]{1,0:T(8,128)(2,1)S(1)}, u32[]{:S(2)}, u32[]{:S(2)}) collective-permute-start(bf16[24,768]{1,0:T(8,128)(2,1)S(1)} %reshape.3.own), channel_id=1, source_target_pairs={{0,16},{16,32},{32,48},{48,0},{1,17},{17,33},{33,49},{49,1},{2,18}... | collective-permute-start | bytes 110600 | tf_op jit(solution)/shard_map/ppermute | solution.py:372
  12.2 2.8 %collective-permute-start.8 = (bf16[24,768]{1,0:T(8,128)(2,1)S(1)}, bf16[24,768]{1,0:T(8,128)(2,1)S(1)}, u32[]{:S(2)}, u32[]{:S(2)}) collective-permute-start(bf16[24,768]{1,0:T(8,128)(2,1)S(1)} %reshape.3.own), channel_id=1, source_target_pairs={{0,48},{16,0},{32,16},{48,32},{1,49},{17,1},{33,17},{49,33},{2,50}... | collective-permute-start | bytes 110600 | tf_op jit(solution)/shard_map/ppermute | solution.py:372
  15.7 1.5 %collective-permute-start.3 = (s32[4,2,2]{2,1,0:T(2,128)S(1)}, s32[4,2,2]{2,1,0:T(2,128)S(1)}, u32[]{:S(2)}, u32[]{:S(2)}) collective-permute-start(s32[4,2,2]{2,1,0:T(2,128)S(1)} %pad_add_fusion.1), channel_id=1, source_target_pairs={{0,4},{4,8},{8,12},{12,0},{1,5},{5,9},{9,13},{13,1},{2,6},{6,10},{... | collective-permute-start | bytes 200 | tf_op jit(solution)/shard_map/ppermute | solution.py:372
  17.2 2.7 %collective-permute-start.4 = (s32[4,2,2]{2,1,0:T(2,128)S(1)}, s32[4,2,2]{2,1,0:T(2,128)S(1)}, u32[]{:S(2)}, u32[]{:S(2)}) collective-permute-start(s32[4,2,2]{2,1,0:T(2,128)S(1)} %pad_add_fusion.1), channel_id=1, source_target_pairs={{0,8},{4,12},{8,0},{12,4},{1,9},{5,13},{9,1},{13,5},{2,10},{6,14},... | collective-permute-start | bytes 200 | tf_op jit(solution)/shard_map/ppermute | solution.py:372
  20.6 1.5 %collective-permute-start.5 = (s32[4,2,2]{2,1,0:T(2,128)S(1)}, s32[4,2,2]{2,1,0:T(2,128)S(1)}, u32[]{:S(2)}, u32[]{:S(2)}) collective-permute-start(s32[4,2,2]{2,1,0:T(2,128)S(1)} %pad_add_fusion.1), channel_id=1, source_target_pairs={{0,12},{4,0},{8,4},{12,8},{1,13},{5,1},{9,5},{13,9},{2,14},{6,2},{... | collective-permute-start | bytes 200 | tf_op jit(solution)/shard_map/ppermute | solution.py:372
  22.3 1.9 %collective-permute-done.5 = s32[4,2,2]{2,1,0:T(2,128)S(1)} collective-permute-done((s32[4,2,2]{2,1,0:T(2,128)S(1)}, s32[4,2,2]{2,1,0:T(2,128)S(1)}, u32[]{:S(2)}, u32[]{:S(2)}) %collective-permute-start.5) | collective-permute-done | bytes 96 | tf_op jit(solution)/shard_map/ppermute | solution.py:372
  24.3 2.7 %pack.1 = bf16[32,72,512]{2,1,0:T(8,128)(2,1)} custom-call(s32[4,4,2,2]{3,2,1,0:T(2,128)S(1)} %pad_add_fusion.peers, bf16[24,768]{1,0:T(8,128)(2,1)S(1)} %reshape.3.own, bf16[24,768]{1,0:T(8,128)(2,1)S(1)} %collective-permute-done.6.one, bf16[24,768]{1,0:T(8,128)(2,1)S(1)} %collective-permute-done.7.two, bf16[24,768]{1,0:T(8,128)(2,1)S(1)} %collective-permute-done.8.three), custom_call_target="tpu_custom_call" | custom-call | tf_op jit(solution)/shard_map/pack/pallas_call | solution.py:139
  27.0 5.0 %all-to-all-start = ((bf16[32,72,512]{2,1,0:T(8,128)(2,1)}), bf16[32,72,512]{2,1,0:T(8,128)(2,1)S(1)}, u32[]{:S(2)}, u32[]{:S(2)}) async-start(bf16[32,72,512]{2,1,0:T(8,128)(2,1)} %pack.1), calls=%async_computation | async-start | bytes 4718592 | tf_op jit(solution)/shard_map/all_to_all | solution.py:382
  32.0 1.6 %copy-done.3 = bf16[2,2,512,512]{3,2,1,0:T(8,128)(2,1)S(1)} copy-done((bf16[2,2,512,512]{3,2,1,0:T(8,128)(2,1)S(1)}, bf16[2,2,512,512]{3,2,1,0:T(8,128)(2,1)}, u32[]{:S(2)}) %copy-start.3) | copy-done | bytes 2097176
  36.1 3.4 %prep.1 = (bf16[512,1024]{1,0:T(8,128)(2,1)S(1)}, bf16[512,1024]{1,0:T(8,128)(2,1)S(1)}, bf16[512,1024]{1,0:T(8,128)(2,1)S(1)}) custom-call(s32[2,2]{1,0:T(2,128)S(1)} %copy-done.2, bf16[2,512,512]{2,1,0:T(8,128)(2,1)S(1)} %copy-done.4, bf16[2,512,512]{2,1,0:T(8,128)(2,1)S(1)} %copy-done.5, bf16[2,512,512]{2,1,0:T(8,128)(2,1)S(1)} %copy-done.6, ...), custom_call_target="tpu_custom_call" | custom-call | flops 4000000000 | bytes 20000000 | tf_op jit(solution)/shard_map/prep/pallas_call | solution.py:92
  42.4 17.0 %all-to-all-done.own = bf16[32,72,512]{2,1,0:T(8,128)(2,1)S(1)} async-done(((bf16[32,72,512]{2,1,0:T(8,128)(2,1)}), bf16[32,72,512]{2,1,0:T(8,128)(2,1)S(1)}, u32[]{:S(2)}, u32[]{:S(2)}) %all-to-all-start) | async-done | bytes 2359328 | tf_op jit(solution)/shard_map/all_to_all | solution.py:382
  59.5 5.0 %open_step.1 = (f32[512,1024]{1,0:T(8,128)S(1)}, bf16[512,1024]{1,0:T(8,128)(2,1)S(1)}, bf16[1024,1024]{1,0:T(8,128)(2,1)S(1)}, bf16[1024,1024]{1,0:T(8,128)(2,1)S(1)}) custom-call(s32[2,2]{1,0:T(2,128)S(1)} %copy-done.2, bf16[32,72,512]{2,1,0:T(8,128)(2,1)S(1)} %all-to-all-done.own, bf16[512,1024]{1,0:T(8,128)(2,1)} %copy-done.7, ...), custom_call_target="tpu_custom_call" | custom-call | flops 4000000000 | bytes 10000000 | tf_op jit(solution)/shard_map/open_step/pallas_call | solution.py:228
  65.1 5.9 %close_steps.1 = (f32[512,1024]{1,0:T(8,128)S(1)}, bf16[512,1024]{1,0:T(8,128)(2,1)S(1)}) custom-call(s32[2,2]{1,0:T(2,128)S(1)} %copy-done.2, bf16[32,72,512]{2,1,0:T(8,128)(2,1)S(1)} %all-to-all-done.own, bf16[32,72,512]{2,1,0:T(8,128)(2,1)S(1)} %collective-permute-done.9.other, bf16[1024,1024]{1,0:T(8,128)(2,1)S(1)} %get-tuple-element.33.v1, ...), custom_call_target="tpu_custom_call" | custom-call | flops 8000000000 | bytes 10000000 | tf_op jit(solution)/shard_map/close_steps/pallas_call | solution.py:253
  71.9 1.2 early.1.half
  73.9 3.5 %late.1 = bf16[32,72,512]{2,1,0:T(8,128)(2,1)S(1)} custom-call(s32[2,2]{1,0:T(2,128)S(1)} %copy-done.2, s32[1]{0:T(128)S(6)} %copy.30.count, bf16[512,1024]{1,0:T(8,128)(2,1)S(1)} %copy-done.1, bf16[512,1024]{1,0:T(8,128)(2,1)S(1)} %collective-permute-done.10.remote, bf16[16,72,512]{2,1,0:T(8,128)(2,1)S(1)} %early.1.half), custom_call_target="tpu_custom_call" | custom-call | tf_op jit(solution)/shard_map/late/pallas_call | solution.py:304
  77.4 38.0 %all_to_all.10.got = bf16[32,72,512]{2,1,0:T(8,128)(2,1)} all-to-all(bf16[32,72,512]{2,1,0:T(8,128)(2,1)S(1)} %late.1), channel_id=1, replica_groups=mesh['zl'=2,'core'=2,'zh'=4,'x'=4,'y'=4] {'zl','x','y'}, dimensions={0} | all-to-all | bytes 4718592 | tf_op jit(solution)/shard_map/all_to_all | solution.py:396
  115.4 2.6 %gather.1 = (f32[24,768]{1,0:T(8,128)S(1)}, bf16[24,768]{1,0:T(8,128)(2,1)S(1)}, bf16[24,768]{1,0:T(8,128)(2,1)S(1)}, bf16[24,768]{1,0:T(8,128)(2,1)S(1)}) custom-call(s32[4,4,2,2]{3,2,1,0:T(2,128)S(1)} %pad_add_fusion.peers, bf16[32,72,512]{2,1,0:T(8,128)(2,1)} %all_to_all.10.got), custom_call_target="tpu_custom_call" | custom-call | tf_op jit(solution)/shard_map/gather/pallas_call | solution.py:343
  118.1 2.7 %collective-permute-start.12 = (bf16[24,768]{1,0:T(8,128)(2,1)S(1)}, bf16[24,768]{1,0:T(8,128)(2,1)S(1)}, u32[]{:S(2)}, u32[]{:S(2)}) collective-permute-start(bf16[24,768]{1,0:T(8,128)(2,1)S(1)} %get-tuple-element.40), channel_id=1, source_target_pairs={{0,32},{16,48},{32,0},{48,16},{1,33},{17,49},{33,1},{49,17},{2,34}... | collective-permute-start | bytes 110600 | tf_op jit(solution)/shard_map/ppermute | solution.py:372
  120.7 3.6 %collective-permute-start.13 = (bf16[24,768]{1,0:T(8,128)(2,1)S(1)}, bf16[24,768]{1,0:T(8,128)(2,1)S(1)}, u32[]{:S(2)}, u32[]{:S(2)}) collective-permute-start(bf16[24,768]{1,0:T(8,128)(2,1)S(1)} %get-tuple-element.41), channel_id=1, source_target_pairs={{0,16},{16,32},{32,48},{48,0},{1,17},{17,33},{33,49},{49,1},{2,18}... | collective-permute-start | bytes 110600 | tf_op jit(solution)/shard_map/ppermute | solution.py:372
  124.4 1.8 %collective-permute-done.12.one = bf16[24,768]{1,0:T(8,128)(2,1)S(1)} collective-permute-done((bf16[24,768]{1,0:T(8,128)(2,1)S(1)}, bf16[24,768]{1,0:T(8,128)(2,1)S(1)}, u32[]{:S(2)}, u32[]{:S(2)}) %collective-permute-start.12) | collective-permute-done | bytes 36896 | tf_op jit(solution)/shard_map/ppermute | solution.py:372
  126.2 4.6 %collective-permute-done.14.three = bf16[24,768]{1,0:T(8,128)(2,1)S(1)} collective-permute-done((bf16[24,768]{1,0:T(8,128)(2,1)S(1)}, bf16[24,768]{1,0:T(8,128)(2,1)S(1)}, u32[]{:S(2)}, u32[]{:S(2)}) %collective-permute-start.14) | collective-permute-done | bytes 36896 | tf_op jit(solution)/shard_map/ppermute | solution.py:372
  (40 shorter events, 11.2 us)
Async XLA Ops:
  0.0 12.2 %collective-permute-start = (s32[2,2]{1,0:T(2,128)}, s32[2,2]{1,0:T(2,128)S(1)}, u32[]{:S(2)}, u32[]{:S(2)}) collective-permute-start(s32[2,2]{1,0:T(2,128)} %tiles.9), channel_id=1, source_target_pairs={{0,1},{1,2},{2,3},{3,0},{4,5},{5,6},{6,7},{7,4},{8,9},{9,10},{10,1... | collective-permute-start | bytes 56 | tf_op jit(solution)/shard_map/ppermute | solution.py:372
  1.6 13.4 %collective-permute-start.1 = (s32[2,2]{1,0:T(2,128)}, s32[2,2]{1,0:T(2,128)S(1)}, u32[]{:S(2)}, u32[]{:S(2)}) collective-permute-start(s32[2,2]{1,0:T(2,128)} %tiles.9), channel_id=1, source_target_pairs={{0,2},{1,3},{2,0},{3,1},{4,6},{5,7},{6,4},{7,5},{8,10},{9,11},{10,... | collective-permute-start | bytes 56 | tf_op jit(solution)/shard_map/ppermute | solution.py:372
  4.5 10.5 %collective-permute-start.2 = (s32[2,2]{1,0:T(2,128)}, s32[2,2]{1,0:T(2,128)S(1)}, u32[]{:S(2)}, u32[]{:S(2)}) collective-permute-start(s32[2,2]{1,0:T(2,128)} %tiles.9), channel_id=1, source_target_pairs={{0,3},{1,0},{2,1},{3,2},{4,7},{5,4},{6,5},{7,6},{8,11},{9,8},{10,9... | collective-permute-start | bytes 56 | tf_op jit(solution)/shard_map/ppermute | solution.py:372
  6.6 17.6 %collective-permute-start.6 = (bf16[24,768]{1,0:T(8,128)(2,1)S(1)}, bf16[24,768]{1,0:T(8,128)(2,1)S(1)}, u32[]{:S(2)}, u32[]{:S(2)}) collective-permute-start(bf16[24,768]{1,0:T(8,128)(2,1)S(1)} %reshape.3.own), channel_id=1, source_target_pairs={{0,16},{16,32},{32,48},{48,0},{1,17},{17,33},{33,49},{49,1},{2,18}... | collective-permute-start | bytes 110600 | tf_op jit(solution)/shard_map/ppermute | solution.py:372
  11.2 13.1 %collective-permute-start.7 = (bf16[24,768]{1,0:T(8,128)(2,1)S(1)}, bf16[24,768]{1,0:T(8,128)(2,1)S(1)}, u32[]{:S(2)}, u32[]{:S(2)}) collective-permute-start(bf16[24,768]{1,0:T(8,128)(2,1)S(1)} %reshape.3.own), channel_id=1, source_target_pairs={{0,32},{16,48},{32,0},{48,16},{1,33},{17,49},{33,1},{49,17},{2,34}... | collective-permute-start | bytes 110600 | tf_op jit(solution)/shard_map/ppermute | solution.py:372
  12.2 12.1 %collective-permute-start.8 = (bf16[24,768]{1,0:T(8,128)(2,1)S(1)}, bf16[24,768]{1,0:T(8,128)(2,1)S(1)}, u32[]{:S(2)}, u32[]{:S(2)}) collective-permute-start(bf16[24,768]{1,0:T(8,128)(2,1)S(1)} %reshape.3.own), channel_id=1, source_target_pairs={{0,48},{16,0},{32,16},{48,32},{1,49},{17,1},{33,17},{49,33},{2,50}... | collective-permute-start | bytes 110600 | tf_op jit(solution)/shard_map/ppermute | solution.py:372
  15.7 4.9 %collective-permute-start.3 = (s32[4,2,2]{2,1,0:T(2,128)S(1)}, s32[4,2,2]{2,1,0:T(2,128)S(1)}, u32[]{:S(2)}, u32[]{:S(2)}) collective-permute-start(s32[4,2,2]{2,1,0:T(2,128)S(1)} %pad_add_fusion.1), channel_id=1, source_target_pairs={{0,4},{4,8},{8,12},{12,0},{1,5},{5,9},{9,13},{13,1},{2,6},{6,10},{... | collective-permute-start | bytes 200 | tf_op jit(solution)/shard_map/ppermute | solution.py:372
  17.2 5.1 %collective-permute-start.4 = (s32[4,2,2]{2,1,0:T(2,128)S(1)}, s32[4,2,2]{2,1,0:T(2,128)S(1)}, u32[]{:S(2)}, u32[]{:S(2)}) collective-permute-start(s32[4,2,2]{2,1,0:T(2,128)S(1)} %pad_add_fusion.1), channel_id=1, source_target_pairs={{0,8},{4,12},{8,0},{12,4},{1,9},{5,13},{9,1},{13,5},{2,10},{6,14},... | collective-permute-start | bytes 200 | tf_op jit(solution)/shard_map/ppermute | solution.py:372
  20.6 3.6 %collective-permute-start.5 = (s32[4,2,2]{2,1,0:T(2,128)S(1)}, s32[4,2,2]{2,1,0:T(2,128)S(1)}, u32[]{:S(2)}, u32[]{:S(2)}) collective-permute-start(s32[4,2,2]{2,1,0:T(2,128)S(1)} %pad_add_fusion.1), channel_id=1, source_target_pairs={{0,12},{4,0},{8,4},{12,8},{1,13},{5,1},{9,5},{13,9},{2,14},{6,2},{... | collective-permute-start | bytes 200 | tf_op jit(solution)/shard_map/ppermute | solution.py:372
  27.0 5.0 %copy-start.2 = (s32[2,2]{1,0:T(2,128)S(1)}, s32[2,2]{1,0:T(2,128)}, u32[]{:S(2)}) copy-start(s32[2,2]{1,0:T(2,128)} %tiles.9) | copy-start | bytes 52
  27.0 5.0 %copy-start.4 = (bf16[2,512,512]{2,1,0:T(8,128)(2,1)S(1)}, bf16[2,512,512]{2,1,0:T(8,128)(2,1)}, u32[]{:S(2)}) copy-start(bf16[2,512,512]{2,1,0:T(8,128)(2,1)} %rows) | copy-start | bytes 3145732
  27.0 32.5 %all-to-all-start = ((bf16[32,72,512]{2,1,0:T(8,128)(2,1)}), bf16[32,72,512]{2,1,0:T(8,128)(2,1)S(1)}, u32[]{:S(2)}, u32[]{:S(2)}) async-start(bf16[32,72,512]{2,1,0:T(8,128)(2,1)} %pack.1), calls=%async_computation | async-start | bytes 4718592 | tf_op jit(solution)/shard_map/all_to_all | solution.py:382
  32.0 1.6 %copy-start.3 = (bf16[2,2,512,512]{3,2,1,0:T(8,128)(2,1)S(1)}, bf16[2,2,512,512]{3,2,1,0:T(8,128)(2,1)}, u32[]{:S(2)}) copy-start(bf16[2,2,512,512]{3,2,1,0:T(8,128)(2,1)} %cot.1) | copy-start | bytes 6291460
  33.6 1.2 copy-start.5
  34.8 1.2 copy-start.6
  39.4 1.0 copy-start
  41.4 1.0 copy-start.8
  59.4 5.6 %collective-permute-start.9 = (bf16[32,72,512]{2,1,0:T(8,128)(2,1)S(1)}, bf16[32,72,512]{2,1,0:T(8,128)(2,1)S(1)}, u32[]{:S(2)}, u32[]{:S(2)}) collective-permute-start(bf16[32,72,512]{2,1,0:T(8,128)(2,1)S(1)} %all-to-all-done.own), channel_id=1, source_target_pairs={{0,64},{64,0},{1,65},{65,1},{2,66},{66,2},{3,67},{67,3},{4,68},{68... | collective-permute-start | bytes 7077896 | tf_op jit(solution)/shard_map/ppermute | solution.py:372
  64.5 7.5 %collective-permute-start.11 = (bf16[512,1024]{1,0:T(8,128)(2,1)S(1)}, bf16[512,1024]{1,0:T(8,128)(2,1)S(1)}, u32[]{:S(2)}, u32[]{:S(2)}) collective-permute-start(bf16[512,1024]{1,0:T(8,128)(2,1)S(1)} %get-tuple-element.38), channel_id=1, source_target_pairs={{0,64},{64,0},{1,65},{65,1},{2,66},{66,2},{3,67},{67,3},{4,68},{68... | collective-permute-start | bytes 3145736 | tf_op jit(solution)/shard_map/ppermute | solution.py:372
  70.9 3.0 %collective-permute-start.10 = (bf16[512,1024]{1,0:T(8,128)(2,1)S(1)}, bf16[512,1024]{1,0:T(8,128)(2,1)S(1)}, u32[]{:S(2)}, u32[]{:S(2)}) collective-permute-start(bf16[512,1024]{1,0:T(8,128)(2,1)S(1)} %get-tuple-element.36), channel_id=1, source_target_pairs={{0,64},{64,0},{1,65},{65,1},{2,66},{66,2},{3,67},{67,3},{4,68},{68... | collective-permute-start | bytes 3145736 | tf_op jit(solution)/shard_map/ppermute | solution.py:372
  71.9 2.0 %copy-start.1 = (bf16[512,1024]{1,0:T(8,128)(2,1)S(1)}, bf16[512,1024]{1,0:T(8,128)(2,1)}, u32[]{:S(2)}) copy-start(bf16[512,1024]{1,0:T(8,128)(2,1)} %copy-done) | copy-start | bytes 3145732
  118.1 8.2 %collective-permute-start.12 = (bf16[24,768]{1,0:T(8,128)(2,1)S(1)}, bf16[24,768]{1,0:T(8,128)(2,1)S(1)}, u32[]{:S(2)}, u32[]{:S(2)}) collective-permute-start(bf16[24,768]{1,0:T(8,128)(2,1)S(1)} %get-tuple-element.40), channel_id=1, source_target_pairs={{0,32},{16,48},{32,0},{48,16},{1,33},{17,49},{33,1},{49,17},{2,34}... | collective-permute-start | bytes 110600 | tf_op jit(solution)/shard_map/ppermute | solution.py:372
  120.7 5.5 %collective-permute-start.13 = (bf16[24,768]{1,0:T(8,128)(2,1)S(1)}, bf16[24,768]{1,0:T(8,128)(2,1)S(1)}, u32[]{:S(2)}, u32[]{:S(2)}) collective-permute-start(bf16[24,768]{1,0:T(8,128)(2,1)S(1)} %get-tuple-element.41), channel_id=1, source_target_pairs={{0,16},{16,32},{32,48},{48,0},{1,17},{17,33},{33,49},{49,1},{2,18}... | collective-permute-start | bytes 110600 | tf_op jit(solution)/shard_map/ppermute | solution.py:372
  124.4 6.5 %collective-permute-start.14 = (bf16[24,768]{1,0:T(8,128)(2,1)S(1)}, bf16[24,768]{1,0:T(8,128)(2,1)S(1)}, u32[]{:S(2)}, u32[]{:S(2)}) collective-permute-start(bf16[24,768]{1,0:T(8,128)(2,1)S(1)} %get-tuple-element.42), channel_id=1, source_target_pairs={{0,48},{16,0},{32,16},{48,32},{1,49},{17,1},{33,17},{49,33},{2,50}... | collective-permute-start | bytes 110600 | tf_op jit(solution)/shard_map/ppermute | solution.py:372
  (1 other events, 1.0 us)

commit v10 on v8

--- a/solution.py
+++ b/solution.py
@@ -8,6 +8,7 @@
 TILE = 32
 W = 512
 OBJ = 768
+COLS = (OBJ - W) // TILE + 1
 PAD = 64
 ROWS = 640
 BF = jnp.bfloat16
@@ -110,29 +111,31 @@
     lane = lax.broadcasted_iota(jnp.int32, (72, 256), 1)
     y = lax.axis_index("y")
 
-    def moved(i):
-        return pltpu.make_async_copy(chunks.at[i], out.at[i], sems.at[i])
-
-    def target(t, carry):
+    for first in range(2):
+        rows = slice(24 * first, 24 * first + 72)
+        rest = held[rows, 256:512].astype(BF)
+        for tile in range(COLS):
+            chunks[first * COLS + tile, :, 0:256] = jnp.where(lane < tile * TILE, held[rows, 512:768], held[rows, 0:256]).astype(BF)
+            chunks[first * COLS + tile, :, 256:512] = rest
+
+    def moved(t, slot):
         ahead, below = t // 4, lax.rem(t, 4)
-        place = lax.rem(x - ahead + 4, 4) * 4 + lax.rem(y - below + 4, 4)
+        place = slot * 16 + lax.rem(x - ahead + 4, 4) * 4 + lax.rem(y - below + 4, 4)
+        kind = first_interval(peers[ahead, below, slot, 0], x) * COLS + peers[ahead, below, slot, 1]
+        return pltpu.make_async_copy(chunks.at[kind], out.at[place], sems.at[place])
+
+    def send(t, carry):
         for slot in range(2):
-            first = first_interval(peers[ahead, below, slot, 0], x)
-            rows = pl.ds(pl.multiple_of(first * 24, 8), 72)
-            wrapped = lane < peers[ahead, below, slot, 1] * TILE
-            low = held[rows, 0:256]
-            high = held[rows, 512:768]
-            chunks[slot * 16 + place, :, 0:256] = jnp.where(wrapped, high, low).astype(BF)
-            chunks[slot * 16 + place, :, 256:512] = held[rows, 256:512].astype(BF)
-            moved(slot * 16 + place).start()
+            moved(t, slot).start()
         return carry
 
-    def settle(i, carry):
-        moved(i).wait()
+    def settle(t, carry):
+        for slot in range(2):
+            moved(t, slot).wait()
         return carry
 
-    lax.fori_loop(0, 16, target, 0)
-    lax.fori_loop(0, 32, settle, 0)
+    lax.fori_loop(0, 16, send, 0)
+    lax.fori_loop(0, 16, settle, 0)
 
 
 def pack(peers, own, others):
@@ -143,7 +146,7 @@
         out_specs=HBM,
         scratch_shapes=[
             pltpu.VMEM((96, OBJ), F32),
-            pltpu.VMEM((32, 72, W), BF),
+            pltpu.VMEM((2 * COLS, 72, W), BF),
             pltpu.SemaphoreType.DMA((32,)),
         ],
         compiler_params=params(16),

time: 129 us -> 129 us (level)
  no operation moved by 1% of the time
where the time goes in v10:
time: 129 us; the launch traced here: 128 us
  blocking collectives  37.9 us (29%)
  starting transfers between devices  32.2 us (25%)
  waiting for transfers between devices  26.4 us (20%)
  Pallas kernels  22 us (17%)
  local copies, waits for them, and re-layouts  7.79 us (6%)
  other arithmetic  1.38 us (1%)
    all_to_all x1, blocking collectives, on_device(): got = lax.all_to_all(contrib, ('zl', 'x', 'y'), 0, 0, tiled=True)  37.9 us
    ppermute x15, starting transfers between devices, turn(): lax.ppermute(value, axis, [(i, (i + step) % count) for i in range(count)])  27.1 us
    all_to_all x1, waiting for transfers between devices, on_device(): own = lax.all_to_all(sent, ('zl', 'x', 'y'), 0, 0, tiled=True)  17 us
    ppermute x15, waiting for transfers between devices, turn(): lax.ppermute(value, axis, [(i, (i + step) % count) for i in range(count)])  9.34 us
    unnamed x19, local copies, waits for them, and re-layouts  7.77 us
    pallas_call x1, Pallas kernels, close_steps(): pl.pallas_call(close_kernel, out_shape=[STATE, SENT], in_specs=[SMEM] + [...  5.87 us
    all_to_all x1, starting transfers between devices, on_device(): own = lax.all_to_all(sent, ('zl', 'x', 'y'), 0, 0, tiled=True)  5.02 us
    pallas_call x1, Pallas kernels, open_step(): pl.pallas_call(open_kernel, out_shape=[STATE, SENT, SQUARE, SQUARE], in_s...  5.02 us
  transfers between devices with their start and end apart: 16, of which 6 were waited for; matrix products, arithmetic and copies ran while one was open for 2% of the time, Pallas kernels for 12%

profile of v10, /device:TPU:64, one launch (start us, length us, event | category | flops | bytes accessed | tf_op | source)
XLA Modules:
  0.0 128.4 jit_solution(18386465293393049628)
XLA Ops:
  0.0 1.6 %collective-permute-start = (s32[2,2]{1,0:T(2,128)}, s32[2,2]{1,0:T(2,128)S(1)}, u32[]{:S(2)}, u32[]{:S(2)}) collective-permute-start(s32[2,2]{1,0:T(2,128)} %tiles.9), channel_id=1, source_target_pairs={{0,1},{1,2},{2,3},{3,0},{4,5},{5,6},{6,7},{7,4},{8,9},{9,10},{10,1... | collective-permute-start | bytes 56 | tf_op jit(solution)/shard_map/ppermute | solution.py:361
  1.6 2.9 %collective-permute-start.1 = (s32[2,2]{1,0:T(2,128)}, s32[2,2]{1,0:T(2,128)S(1)}, u32[]{:S(2)}, u32[]{:S(2)}) collective-permute-start(s32[2,2]{1,0:T(2,128)} %tiles.9), channel_id=1, source_target_pairs={{0,2},{1,3},{2,0},{3,1},{4,6},{5,7},{6,4},{7,5},{8,10},{9,11},{10,... | collective-permute-start | bytes 56 | tf_op jit(solution)/shard_map/ppermute | solution.py:361
  4.5 1.3 %collective-permute-start.2 = (s32[2,2]{1,0:T(2,128)}, s32[2,2]{1,0:T(2,128)S(1)}, u32[]{:S(2)}, u32[]{:S(2)}) collective-permute-start(s32[2,2]{1,0:T(2,128)} %tiles.9), channel_id=1, source_target_pairs={{0,3},{1,0},{2,1},{3,2},{4,7},{5,4},{6,5},{7,6},{8,11},{9,8},{10,9... | collective-permute-start | bytes 56 | tf_op jit(solution)/shard_map/ppermute | solution.py:361
  6.6 4.6 %collective-permute-start.6 = (bf16[24,768]{1,0:T(8,128)(2,1)S(1)}, bf16[24,768]{1,0:T(8,128)(2,1)S(1)}, u32[]{:S(2)}, u32[]{:S(2)}) collective-permute-start(bf16[24,768]{1,0:T(8,128)(2,1)S(1)} %reshape.3.own), channel_id=1, source_target_pairs={{0,16},{16,32},{32,48},{48,0},{1,17},{17,33},{33,49},{49,1},{2,18}... | collective-permute-start | bytes 110600 | tf_op jit(solution)/shard_map/ppermute | solution.py:361
  12.2 2.8 %collective-permute-start.8 = (bf16[24,768]{1,0:T(8,128)(2,1)S(1)}, bf16[24,768]{1,0:T(8,128)(2,1)S(1)}, u32[]{:S(2)}, u32[]{:S(2)}) collective-permute-start(bf16[24,768]{1,0:T(8,128)(2,1)S(1)} %reshape.3.own), channel_id=1, source_target_pairs={{0,48},{16,0},{32,16},{48,32},{1,49},{17,1},{33,17},{49,33},{2,50}... | collective-permute-start | bytes 110600 | tf_op jit(solution)/shard_map/ppermute | solution.py:361
  15.7 1.5 %collective-permute-start.3 = (s32[4,2,2]{2,1,0:T(2,128)S(1)}, s32[4,2,2]{2,1,0:T(2,128)S(1)}, u32[]{:S(2)}, u32[]{:S(2)}) collective-permute-start(s32[4,2,2]{2,1,0:T(2,128)S(1)} %pad_add_fusion.1), channel_id=1, source_target_pairs={{0,4},{4,8},{8,12},{12,0},{1,5},{5,9},{9,13},{13,1},{2,6},{6,10},{... | collective-permute-start | bytes 200 | tf_op jit(solution)/shard_map/ppermute | solution.py:361
  17.2 2.7 %collective-permute-start.4 = (s32[4,2,2]{2,1,0:T(2,128)S(1)}, s32[4,2,2]{2,1,0:T(2,128)S(1)}, u32[]{:S(2)}, u32[]{:S(2)}) collective-permute-start(s32[4,2,2]{2,1,0:T(2,128)S(1)} %pad_add_fusion.1), channel_id=1, source_target_pairs={{0,8},{4,12},{8,0},{12,4},{1,9},{5,13},{9,1},{13,5},{2,10},{6,14},... | collective-permute-start | bytes 200 | tf_op jit(solution)/shard_map/ppermute | solution.py:361
  20.6 1.5 %collective-permute-start.5 = (s32[4,2,2]{2,1,0:T(2,128)S(1)}, s32[4,2,2]{2,1,0:T(2,128)S(1)}, u32[]{:S(2)}, u32[]{:S(2)}) collective-permute-start(s32[4,2,2]{2,1,0:T(2,128)S(1)} %pad_add_fusion.1), channel_id=1, source_target_pairs={{0,12},{4,0},{8,4},{12,8},{1,13},{5,1},{9,5},{13,9},{2,14},{6,2},{... | collective-permute-start | bytes 200 | tf_op jit(solution)/shard_map/ppermute | solution.py:361
  22.3 1.9 %collective-permute-done.5 = s32[4,2,2]{2,1,0:T(2,128)S(1)} collective-permute-done((s32[4,2,2]{2,1,0:T(2,128)S(1)}, s32[4,2,2]{2,1,0:T(2,128)S(1)}, u32[]{:S(2)}, u32[]{:S(2)}) %collective-permute-start.5) | collective-permute-done | bytes 96 | tf_op jit(solution)/shard_map/ppermute | solution.py:361
  24.3 2.7 %pack.1 = bf16[32,72,512]{2,1,0:T(8,128)(2,1)} custom-call(s32[4,4,2,2]{3,2,1,0:T(2,128)S(1)} %pad_add_fusion.peers, bf16[24,768]{1,0:T(8,128)(2,1)S(1)} %reshape.3.own, bf16[24,768]{1,0:T(8,128)(2,1)S(1)} %collective-permute-done.6.one, bf16[24,768]{1,0:T(8,128)(2,1)S(1)} %collective-permute-done.7.two, bf16[24,768]{1,0:T(8,128)(2,1)S(1)} %collective-permute-done.8.three), custom_call_target="tpu_custom_call" | custom-call | tf_op jit(solution)/shard_map/pack/pallas_call | solution.py:142
  27.0 5.0 %all-to-all-start = ((bf16[32,72,512]{2,1,0:T(8,128)(2,1)}), bf16[32,72,512]{2,1,0:T(8,128)(2,1)S(1)}, u32[]{:S(2)}, u32[]{:S(2)}) async-start(bf16[32,72,512]{2,1,0:T(8,128)(2,1)} %pack.1), calls=%async_computation | async-start | bytes 4718592 | tf_op jit(solution)/shard_map/all_to_all | solution.py:371
  32.0 1.6 %copy-done.3 = bf16[2,2,512,512]{3,2,1,0:T(8,128)(2,1)S(1)} copy-done((bf16[2,2,512,512]{3,2,1,0:T(8,128)(2,1)S(1)}, bf16[2,2,512,512]{3,2,1,0:T(8,128)(2,1)}, u32[]{:S(2)}) %copy-start.3) | copy-done | bytes 2097176
  36.1 3.4 %prep.1 = (bf16[512,1024]{1,0:T(8,128)(2,1)S(1)}, bf16[512,1024]{1,0:T(8,128)(2,1)S(1)}, bf16[512,1024]{1,0:T(8,128)(2,1)S(1)}) custom-call(s32[2,2]{1,0:T(2,128)S(1)} %copy-done.2, bf16[2,512,512]{2,1,0:T(8,128)(2,1)S(1)} %copy-done.4, bf16[2,512,512]{2,1,0:T(8,128)(2,1)S(1)} %copy-done.5, bf16[2,512,512]{2,1,0:T(8,128)(2,1)S(1)} %copy-done.6, ...), custom_call_target="tpu_custom_call" | custom-call | flops 4000000000 | bytes 20000000 | tf_op jit(solution)/shard_map/prep/pallas_call | solution.py:93
  42.4 17.0 %all-to-all-done.own = bf16[32,72,512]{2,1,0:T(8,128)(2,1)S(1)} async-done(((bf16[32,72,512]{2,1,0:T(8,128)(2,1)}), bf16[32,72,512]{2,1,0:T(8,128)(2,1)S(1)}, u32[]{:S(2)}, u32[]{:S(2)}) %all-to-all-start) | async-done | bytes 2359328 | tf_op jit(solution)/shard_map/all_to_all | solution.py:371
  59.4 5.0 %open_step.1 = (f32[512,1024]{1,0:T(8,128)S(1)}, bf16[512,1024]{1,0:T(8,128)(2,1)S(1)}, bf16[1024,1024]{1,0:T(8,128)(2,1)S(1)}, bf16[1024,1024]{1,0:T(8,128)(2,1)S(1)}) custom-call(s32[2,2]{1,0:T(2,128)S(1)} %copy-done.2, bf16[32,72,512]{2,1,0:T(8,128)(2,1)S(1)} %all-to-all-done.own, bf16[512,1024]{1,0:T(8,128)(2,1)} %copy-done.7, ...), custom_call_target="tpu_custom_call" | custom-call | flops 4000000000 | bytes 10000000 | tf_op jit(solution)/shard_map/open_step/pallas_call | solution.py:229
  65.1 5.9 %close_steps.1 = (f32[512,1024]{1,0:T(8,128)S(1)}, bf16[512,1024]{1,0:T(8,128)(2,1)S(1)}) custom-call(s32[2,2]{1,0:T(2,128)S(1)} %copy-done.2, bf16[32,72,512]{2,1,0:T(8,128)(2,1)S(1)} %all-to-all-done.own, bf16[32,72,512]{2,1,0:T(8,128)(2,1)S(1)} %collective-permute-done.9.other, bf16[1024,1024]{1,0:T(8,128)(2,1)S(1)} %get-tuple-element.33.v1, ...), custom_call_target="tpu_custom_call" | custom-call | flops 8000000000 | bytes 10000000 | tf_op jit(solution)/shard_map/close_steps/pallas_call | solution.py:254
  71.9 1.2 early.1.half
  73.9 1.4 %late.1 = bf16[32,72,512]{2,1,0:T(8,128)(2,1)S(1)} custom-call(s32[2,2]{1,0:T(2,128)S(1)} %copy-done.2, s32[1]{0:T(128)S(6)} %copy.30.count, bf16[512,1024]{1,0:T(8,128)(2,1)S(1)} %copy-done.1, bf16[512,1024]{1,0:T(8,128)(2,1)S(1)} %collective-permute-done.10.remote, bf16[16,72,512]{2,1,0:T(8,128)(2,1)S(1)} %early.1.half), custom_call_target="tpu_custom_call" | custom-call | tf_op jit(solution)/shard_map/late/pallas_call | solution.py:293
  75.3 37.9 %all_to_all.10.got = bf16[32,72,512]{2,1,0:T(8,128)(2,1)S(1)} all-to-all(bf16[32,72,512]{2,1,0:T(8,128)(2,1)S(1)} %late.1), channel_id=1, replica_groups=mesh['zl'=2,'core'=2,'zh'=4,'x'=4,'y'=4] {'zl','x','y'}, dimensions={0} | all-to-all | bytes 4718592 | tf_op jit(solution)/shard_map/all_to_all | solution.py:384
  113.2 1.8 %gather.1 = (f32[24,768]{1,0:T(8,128)S(1)}, bf16[24,768]{1,0:T(8,128)(2,1)S(1)}, bf16[24,768]{1,0:T(8,128)(2,1)S(1)}, bf16[24,768]{1,0:T(8,128)(2,1)S(1)}) custom-call(s32[4,4,2,2]{3,2,1,0:T(2,128)S(1)} %pad_add_fusion.peers, bf16[32,72,512]{2,1,0:T(8,128)(2,1)S(1)} %all_to_all.10.got), custom_call_target="tpu_custom_call" | custom-call | tf_op jit(solution)/shard_map/gather/pallas_call | solution.py:332
  115.0 2.7 %collective-permute-start.12 = (bf16[24,768]{1,0:T(8,128)(2,1)S(1)}, bf16[24,768]{1,0:T(8,128)(2,1)S(1)}, u32[]{:S(2)}, u32[]{:S(2)}) collective-permute-start(bf16[24,768]{1,0:T(8,128)(2,1)S(1)} %get-tuple-element.40), channel_id=1, source_target_pairs={{0,32},{16,48},{32,0},{48,16},{1,33},{17,49},{33,1},{49,17},{2,34}... | collective-permute-start | bytes 110600 | tf_op jit(solution)/shard_map/ppermute | solution.py:361
  117.7 3.6 %collective-permute-start.13 = (bf16[24,768]{1,0:T(8,128)(2,1)S(1)}, bf16[24,768]{1,0:T(8,128)(2,1)S(1)}, u32[]{:S(2)}, u32[]{:S(2)}) collective-permute-start(bf16[24,768]{1,0:T(8,128)(2,1)S(1)} %get-tuple-element.41), channel_id=1, source_target_pairs={{0,16},{16,32},{32,48},{48,0},{1,17},{17,33},{33,49},{49,1},{2,18}... | collective-permute-start | bytes 110600 | tf_op jit(solution)/shard_map/ppermute | solution.py:361
  121.3 1.8 %collective-permute-done.12.one = bf16[24,768]{1,0:T(8,128)(2,1)S(1)} collective-permute-done((bf16[24,768]{1,0:T(8,128)(2,1)S(1)}, bf16[24,768]{1,0:T(8,128)(2,1)S(1)}, u32[]{:S(2)}, u32[]{:S(2)}) %collective-permute-start.12) | collective-permute-done | bytes 36896 | tf_op jit(solution)/shard_map/ppermute | solution.py:361
  123.1 4.6 %collective-permute-done.14.three = bf16[24,768]{1,0:T(8,128)(2,1)S(1)} collective-permute-done((bf16[24,768]{1,0:T(8,128)(2,1)S(1)}, bf16[24,768]{1,0:T(8,128)(2,1)S(1)}, u32[]{:S(2)}, u32[]{:S(2)}) %collective-permute-start.14) | collective-permute-done | bytes 36896 | tf_op jit(solution)/shard_map/ppermute | solution.py:361
  (40 shorter events, 11.2 us)
Async XLA Ops:
  0.0 12.2 %collective-permute-start = (s32[2,2]{1,0:T(2,128)}, s32[2,2]{1,0:T(2,128)S(1)}, u32[]{:S(2)}, u32[]{:S(2)}) collective-permute-start(s32[2,2]{1,0:T(2,128)} %tiles.9), channel_id=1, source_target_pairs={{0,1},{1,2},{2,3},{3,0},{4,5},{5,6},{6,7},{7,4},{8,9},{9,10},{10,1... | collective-permute-start | bytes 56 | tf_op jit(solution)/shard_map/ppermute | solution.py:361
  1.6 13.4 %collective-permute-start.1 = (s32[2,2]{1,0:T(2,128)}, s32[2,2]{1,0:T(2,128)S(1)}, u32[]{:S(2)}, u32[]{:S(2)}) collective-permute-start(s32[2,2]{1,0:T(2,128)} %tiles.9), channel_id=1, source_target_pairs={{0,2},{1,3},{2,0},{3,1},{4,6},{5,7},{6,4},{7,5},{8,10},{9,11},{10,... | collective-permute-start | bytes 56 | tf_op jit(solution)/shard_map/ppermute | solution.py:361
  4.5 10.5 %collective-permute-start.2 = (s32[2,2]{1,0:T(2,128)}, s32[2,2]{1,0:T(2,128)S(1)}, u32[]{:S(2)}, u32[]{:S(2)}) collective-permute-start(s32[2,2]{1,0:T(2,128)} %tiles.9), channel_id=1, source_target_pairs={{0,3},{1,0},{2,1},{3,2},{4,7},{5,4},{6,5},{7,6},{8,11},{9,8},{10,9... | collective-permute-start | bytes 56 | tf_op jit(solution)/shard_map/ppermute | solution.py:361
  6.6 17.6 %collective-permute-start.6 = (bf16[24,768]{1,0:T(8,128)(2,1)S(1)}, bf16[24,768]{1,0:T(8,128)(2,1)S(1)}, u32[]{:S(2)}, u32[]{:S(2)}) collective-permute-start(bf16[24,768]{1,0:T(8,128)(2,1)S(1)} %reshape.3.own), channel_id=1, source_target_pairs={{0,16},{16,32},{32,48},{48,0},{1,17},{17,33},{33,49},{49,1},{2,18}... | collective-permute-start | bytes 110600 | tf_op jit(solution)/shard_map/ppermute | solution.py:361
  11.2 13.1 %collective-permute-start.7 = (bf16[24,768]{1,0:T(8,128)(2,1)S(1)}, bf16[24,768]{1,0:T(8,128)(2,1)S(1)}, u32[]{:S(2)}, u32[]{:S(2)}) collective-permute-start(bf16[24,768]{1,0:T(8,128)(2,1)S(1)} %reshape.3.own), channel_id=1, source_target_pairs={{0,32},{16,48},{32,0},{48,16},{1,33},{17,49},{33,1},{49,17},{2,34}... | collective-permute-start | bytes 110600 | tf_op jit(solution)/shard_map/ppermute | solution.py:361
  12.2 12.1 %collective-permute-start.8 = (bf16[24,768]{1,0:T(8,128)(2,1)S(1)}, bf16[24,768]{1,0:T(8,128)(2,1)S(1)}, u32[]{:S(2)}, u32[]{:S(2)}) collective-permute-start(bf16[24,768]{1,0:T(8,128)(2,1)S(1)} %reshape.3.own), channel_id=1, source_target_pairs={{0,48},{16,0},{32,16},{48,32},{1,49},{17,1},{33,17},{49,33},{2,50}... | collective-permute-start | bytes 110600 | tf_op jit(solution)/shard_map/ppermute | solution.py:361
  15.7 4.9 %collective-permute-start.3 = (s32[4,2,2]{2,1,0:T(2,128)S(1)}, s32[4,2,2]{2,1,0:T(2,128)S(1)}, u32[]{:S(2)}, u32[]{:S(2)}) collective-permute-start(s32[4,2,2]{2,1,0:T(2,128)S(1)} %pad_add_fusion.1), channel_id=1, source_target_pairs={{0,4},{4,8},{8,12},{12,0},{1,5},{5,9},{9,13},{13,1},{2,6},{6,10},{... | collective-permute-start | bytes 200 | tf_op jit(solution)/shard_map/ppermute | solution.py:361
  17.2 5.1 %collective-permute-start.4 = (s32[4,2,2]{2,1,0:T(2,128)S(1)}, s32[4,2,2]{2,1,0:T(2,128)S(1)}, u32[]{:S(2)}, u32[]{:S(2)}) collective-permute-start(s32[4,2,2]{2,1,0:T(2,128)S(1)} %pad_add_fusion.1), channel_id=1, source_target_pairs={{0,8},{4,12},{8,0},{12,4},{1,9},{5,13},{9,1},{13,5},{2,10},{6,14},... | collective-permute-start | bytes 200 | tf_op jit(solution)/shard_map/ppermute | solution.py:361
  20.6 3.6 %collective-permute-start.5 = (s32[4,2,2]{2,1,0:T(2,128)S(1)}, s32[4,2,2]{2,1,0:T(2,128)S(1)}, u32[]{:S(2)}, u32[]{:S(2)}) collective-permute-start(s32[4,2,2]{2,1,0:T(2,128)S(1)} %pad_add_fusion.1), channel_id=1, source_target_pairs={{0,12},{4,0},{8,4},{12,8},{1,13},{5,1},{9,5},{13,9},{2,14},{6,2},{... | collective-permute-start | bytes 200 | tf_op jit(solution)/shard_map/ppermute | solution.py:361
  26.9 5.1 %copy-start.2 = (s32[2,2]{1,0:T(2,128)S(1)}, s32[2,2]{1,0:T(2,128)}, u32[]{:S(2)}) copy-start(s32[2,2]{1,0:T(2,128)} %tiles.9) | copy-start | bytes 52
  27.0 5.1 %copy-start.4 = (bf16[2,512,512]{2,1,0:T(8,128)(2,1)S(1)}, bf16[2,512,512]{2,1,0:T(8,128)(2,1)}, u32[]{:S(2)}) copy-start(bf16[2,512,512]{2,1,0:T(8,128)(2,1)} %rows) | copy-start | bytes 3145732
  27.0 32.5 %all-to-all-start = ((bf16[32,72,512]{2,1,0:T(8,128)(2,1)}), bf16[32,72,512]{2,1,0:T(8,128)(2,1)S(1)}, u32[]{:S(2)}, u32[]{:S(2)}) async-start(bf16[32,72,512]{2,1,0:T(8,128)(2,1)} %pack.1), calls=%async_computation | async-start | bytes 4718592 | tf_op jit(solution)/shard_map/all_to_all | solution.py:371
  32.0 1.6 %copy-start.3 = (bf16[2,2,512,512]{3,2,1,0:T(8,128)(2,1)S(1)}, bf16[2,2,512,512]{3,2,1,0:T(8,128)(2,1)}, u32[]{:S(2)}) copy-start(bf16[2,2,512,512]{3,2,1,0:T(8,128)(2,1)} %cot.1) | copy-start | bytes 6291460
  33.6 1.2 copy-start.5
  34.8 1.2 copy-start.6
  39.4 1.0 copy-start
  41.4 1.0 copy-start.8
  59.4 5.6 %collective-permute-start.9 = (bf16[32,72,512]{2,1,0:T(8,128)(2,1)S(1)}, bf16[32,72,512]{2,1,0:T(8,128)(2,1)S(1)}, u32[]{:S(2)}, u32[]{:S(2)}) collective-permute-start(bf16[32,72,512]{2,1,0:T(8,128)(2,1)S(1)} %all-to-all-done.own), channel_id=1, source_target_pairs={{0,64},{64,0},{1,65},{65,1},{2,66},{66,2},{3,67},{67,3},{4,68},{68... | collective-permute-start | bytes 7077896 | tf_op jit(solution)/shard_map/ppermute | solution.py:361
  64.5 7.5 %collective-permute-start.11 = (bf16[512,1024]{1,0:T(8,128)(2,1)S(1)}, bf16[512,1024]{1,0:T(8,128)(2,1)S(1)}, u32[]{:S(2)}, u32[]{:S(2)}) collective-permute-start(bf16[512,1024]{1,0:T(8,128)(2,1)S(1)} %get-tuple-element.38), channel_id=1, source_target_pairs={{0,64},{64,0},{1,65},{65,1},{2,66},{66,2},{3,67},{67,3},{4,68},{68... | collective-permute-start | bytes 3145736 | tf_op jit(solution)/shard_map/ppermute | solution.py:361
  70.9 3.0 %collective-permute-start.10 = (bf16[512,1024]{1,0:T(8,128)(2,1)S(1)}, bf16[512,1024]{1,0:T(8,128)(2,1)S(1)}, u32[]{:S(2)}, u32[]{:S(2)}) collective-permute-start(bf16[512,1024]{1,0:T(8,128)(2,1)S(1)} %get-tuple-element.36), channel_id=1, source_target_pairs={{0,64},{64,0},{1,65},{65,1},{2,66},{66,2},{3,67},{67,3},{4,68},{68... | collective-permute-start | bytes 3145736 | tf_op jit(solution)/shard_map/ppermute | solution.py:361
  71.9 2.0 %copy-start.1 = (bf16[512,1024]{1,0:T(8,128)(2,1)S(1)}, bf16[512,1024]{1,0:T(8,128)(2,1)}, u32[]{:S(2)}) copy-start(bf16[512,1024]{1,0:T(8,128)(2,1)} %copy-done) | copy-start | bytes 3145732
  115.0 8.2 %collective-permute-start.12 = (bf16[24,768]{1,0:T(8,128)(2,1)S(1)}, bf16[24,768]{1,0:T(8,128)(2,1)S(1)}, u32[]{:S(2)}, u32[]{:S(2)}) collective-permute-start(bf16[24,768]{1,0:T(8,128)(2,1)S(1)} %get-tuple-element.40), channel_id=1, source_target_pairs={{0,32},{16,48},{32,0},{48,16},{1,33},{17,49},{33,1},{49,17},{2,34}... | collective-permute-start | bytes 110600 | tf_op jit(solution)/shard_map/ppermute | solution.py:361
  117.7 5.5 %collective-permute-start.13 = (bf16[24,768]{1,0:T(8,128)(2,1)S(1)}, bf16[24,768]{1,0:T(8,128)(2,1)S(1)}, u32[]{:S(2)}, u32[]{:S(2)}) collective-permute-start(bf16[24,768]{1,0:T(8,128)(2,1)S(1)} %get-tuple-element.41), channel_id=1, source_target_pairs={{0,16},{16,32},{32,48},{48,0},{1,17},{17,33},{33,49},{49,1},{2,18}... | collective-permute-start | bytes 110600 | tf_op jit(solution)/shard_map/ppermute | solution.py:361
  121.3 6.5 %collective-permute-start.14 = (bf16[24,768]{1,0:T(8,128)(2,1)S(1)}, bf16[24,768]{1,0:T(8,128)(2,1)S(1)}, u32[]{:S(2)}, u32[]{:S(2)}) collective-permute-start(bf16[24,768]{1,0:T(8,128)(2,1)S(1)} %get-tuple-element.42), channel_id=1, source_target_pairs={{0,48},{16,0},{32,16},{48,32},{1,49},{17,1},{33,17},{49,33},{2,50}... | collective-permute-start | bytes 110600 | tf_op jit(solution)/shard_map/ppermute | solution.py:361
  (1 other events, 1.0 us)

commit v11 on v10

--- a/solution.py
+++ b/solution.py
@@ -102,7 +102,8 @@
     )(tiles, rows, cols, probe, cot)
 
 
-def pack_kernel(peers, own, one, two, three, out, held, chunks, sems):
+def pack_kernel(line0, line1, line2, line3, own, one, two, three, out, held, chunks, sems):
+    peers = (line0, line1, line2, line3)
     zh = lax.axis_index("zh")
     x = lax.axis_index("x")
     for hops, piece in enumerate((own, one, two, three)):
@@ -118,31 +119,32 @@
             chunks[first * COLS + tile, :, 0:256] = jnp.where(lane < tile * TILE, held[rows, 512:768], held[rows, 0:256]).astype(BF)
             chunks[first * COLS + tile, :, 256:512] = rest
 
-    def moved(t, slot):
-        ahead, below = t // 4, lax.rem(t, 4)
+    def moved(ahead, below, slot):
         place = slot * 16 + lax.rem(x - ahead + 4, 4) * 4 + lax.rem(y - below + 4, 4)
-        kind = first_interval(peers[ahead, below, slot, 0], x) * COLS + peers[ahead, below, slot, 1]
+        kind = first_interval(peers[ahead][below, slot, 0], x) * COLS + peers[ahead][below, slot, 1]
         return pltpu.make_async_copy(chunks.at[kind], out.at[place], sems.at[place])
 
-    def send(t, carry):
-        for slot in range(2):
-            moved(t, slot).start()
+    def send(below, carry):
+        for ahead in range(4):
+            for slot in range(2):
+                moved(ahead, below, slot).start()
         return carry
 
-    def settle(t, carry):
-        for slot in range(2):
-            moved(t, slot).wait()
+    def settle(below, carry):
+        for ahead in range(4):
+            for slot in range(2):
+                moved(ahead, below, slot).wait()
         return carry
 
-    lax.fori_loop(0, 16, send, 0)
-    lax.fori_loop(0, 16, settle, 0)
+    lax.fori_loop(0, 4, send, 0)
+    lax.fori_loop(0, 4, settle, 0)
 
 
 def pack(peers, own, others):
     return pl.pallas_call(
         pack_kernel,
         out_shape=jax.ShapeDtypeStruct((32, 72, W), BF),
-        in_specs=[SMEM] + [VMEM] * 4,
+        in_specs=[SMEM] * 4 + [VMEM] * 4,
         out_specs=HBM,
         scratch_shapes=[
             pltpu.VMEM((96, OBJ), F32),
@@ -151,7 +153,7 @@
         ],
         compiler_params=params(16),
         name="pack",
-    )(peers, own, *others)
+    )(*peers, own, *others)
 
 
 def place_patch(source, base, patch, row_tile):
@@ -301,28 +303,29 @@
     )(tiles, count, local, remote, half)
 
 
-def gather_kernel(peers, got, own, one, two, three, total):
+def gather_kernel(line0, line1, line2, line3, got, own, one, two, three, total):
+    peers = (line0, line1, line2, line3)
     zh = lax.axis_index("zh")
     x = lax.axis_index("x")
     total[...] = jnp.zeros((96, OBJ), F32)
     lane = lax.broadcasted_iota(jnp.int32, (72, 256), 1)
     y = lax.axis_index("y")
 
-    def source(t, carry):
-        ahead, below = t // 4, lax.rem(t, 4)
-        place = lax.rem(x - ahead + 4, 4) * 4 + lax.rem(y - below + 4, 4)
-        for slot in range(2):
-            first = first_interval(peers[ahead, below, slot, 0], x)
-            rows = pl.ds(pl.multiple_of(first * 24, 8), 72)
-            wrapped = lane < peers[ahead, below, slot, 1] * TILE
-            value = got[slot * 16 + place].astype(F32)
-            low = value[:, 0:256]
-            total[rows, 0:256] += jnp.where(wrapped, 0.0, low)
-            total[rows, 512:768] += jnp.where(wrapped, low, 0.0)
-            total[rows, 256:512] += value[:, 256:512]
+    def source(below, carry):
+        for ahead in range(4):
+            place = lax.rem(x - ahead + 4, 4) * 4 + lax.rem(y - below + 4, 4)
+            for slot in range(2):
+                first = first_interval(peers[ahead][below, slot, 0], x)
+                rows = pl.ds(pl.multiple_of(first * 24, 8), 72)
+                wrapped = lane < peers[ahead][below, slot, 1] * TILE
+                value = got[slot * 16 + place].astype(F32)
+                low = value[:, 0:256]
+                total[rows, 0:256] += jnp.where(wrapped, 0.0, low)
+                total[rows, 512:768] += jnp.where(wrapped, low, 0.0)
+                total[rows, 256:512] += value[:, 256:512]
         return carry
 
-    lax.fori_loop(0, 16, source, 0)
+    lax.fori_loop(0, 4, source, 0)
     for step, out in enumerate((own, one, two, three)):
         place = lax.rem(zh + step, 4)
         out[...] = total[pl.ds(pl.multiple_of(place * 24, 8), 24), :].astype(out.dtype)
@@ -332,12 +335,12 @@
     return pl.pallas_call(
         gather_kernel,
         out_shape=[jax.ShapeDtypeStruct((24, OBJ), F32)] + [jax.ShapeDtypeStruct((24, OBJ), BF)] * 3,
-        in_specs=[SMEM, VMEM],
+        in_specs=[SMEM] * 4 + [VMEM],
         out_specs=[VMEM] * 4,
         scratch_shapes=[pltpu.VMEM((96, OBJ), F32)],
         compiler_params=params(16),
         name="gather",
-    )(peers, got)
+    )(*peers, got)
 
 
 def last_kernel(own, one, two, three, out):
@@ -364,9 +367,9 @@
 def on_device(probe_wave, prop_rows, prop_cols, transmission, exit_cotangent, window_tiles, slot_count):
     line = jnp.stack([window_tiles] + [turn(window_tiles, "y", hops, 4) for hops in (1, 2, 3)])
     piece = transmission.reshape(24, OBJ)
-    others = [turn(piece, "zh", hops, 4) for hops in (1, 2, 3)]
-    peers = jnp.stack([line] + [turn(line, "x", hops, 4) for hops in (1, 2, 3)])
-    sent = pack(peers, piece, others)
+    two, one, three = [turn(piece, "zh", hops, 4) for hops in (2, 1, 3)]
+    peers = [line] + [turn(line, "x", hops, 4) for hops in (1, 2, 3)]
+    sent = pack(peers, piece, (one, two, three))
     sent, rows = lax.optimization_barrier((sent, prop_rows))
     own = lax.all_to_all(sent, ("zl", "x", "y"), 0, 0, tiled=True)
     mats = prep(window_tiles, rows, prop_cols, probe_wave, exit_cotangent)

time: 129 us -> 128 us (level)
  transfers between devices with their start and end apart: 16 -> 16, of which waited for: 6 -> 8; matrix products, arithmetic and copies ran while one was open for 2% -> 1% of each run, Pallas kernels for 12% -> 12%
where the time goes in v11:
time: 128 us
  blocking collectives  37.5 us (29%)
  starting transfers between devices  32.6 us (25%)
  waiting for transfers between devices  26.7 us (21%)
  Pallas kernels  21.8 us (17%)
  local copies, waits for them, and re-layouts  7.79 us (6%)
    all_to_all x1, blocking collectives, on_device(): got = lax.all_to_all(contrib, ('zl', 'x', 'y'), 0, 0, tiled=True)  37.5 us
    ppermute x15, starting transfers between devices, turn(): lax.ppermute(value, axis, [(i, (i + step) % count) for i in range(count)])  27.5 us
    all_to_all x1, waiting for transfers between devices, on_device(): own = lax.all_to_all(sent, ('zl', 'x', 'y'), 0, 0, tiled=True)  16.8 us
    ppermute x15, waiting for transfers between devices, turn(): lax.ppermute(value, axis, [(i, (i + step) % count) for i in range(count)])  9.84 us
    unnamed x19, local copies, waits for them, and re-layouts  7.77 us
    pallas_call x1, Pallas kernels, close_steps(): pl.pallas_call(close_kernel, out_shape=[STATE, SENT], in_specs=[SMEM] + [...  5.86 us
    all_to_all x1, starting transfers between devices, on_device(): own = lax.all_to_all(sent, ('zl', 'x', 'y'), 0, 0, tiled=True)  5.13 us
    pallas_call x1, Pallas kernels, open_step(): pl.pallas_call(open_kernel, out_shape=[STATE, SENT, SQUARE, SQUARE], in_s...  5.02 us
  transfers between devices with their start and end apart: 16, of which 8 were waited for; matrix products, arithmetic and copies ran while one was open for 1% of the time, Pallas kernels for 12%

profile of v11, /device:TPU:64, one launch (start us, length us, event | category | flops | bytes accessed | tf_op | source)
XLA Modules:
  0.0 127.7 jit_solution(18206943822072861000)
XLA Ops:
  0.0 1.6 %collective-permute-start = (s32[2,2]{1,0:T(2,128)}, s32[2,2]{1,0:T(2,128)S(1)}, u32[]{:S(2)}, u32[]{:S(2)}) collective-permute-start(s32[2,2]{1,0:T(2,128)} %tiles.9), channel_id=1, source_target_pairs={{0,1},{1,2},{2,3},{3,0},{4,5},{5,6},{6,7},{7,4},{8,9},{9,10},{10,1... | collective-permute-start | bytes 56 | tf_op jit(solution)/shard_map/ppermute | solution.py:364
  1.6 2.9 %collective-permute-start.1 = (s32[2,2]{1,0:T(2,128)}, s32[2,2]{1,0:T(2,128)S(1)}, u32[]{:S(2)}, u32[]{:S(2)}) collective-permute-start(s32[2,2]{1,0:T(2,128)} %tiles.9), channel_id=1, source_target_pairs={{0,2},{1,3},{2,0},{3,1},{4,6},{5,7},{6,4},{7,5},{8,10},{9,11},{10,... | collective-permute-start | bytes 56 | tf_op jit(solution)/shard_map/ppermute | solution.py:364
  4.5 1.3 %collective-permute-start.2 = (s32[2,2]{1,0:T(2,128)}, s32[2,2]{1,0:T(2,128)S(1)}, u32[]{:S(2)}, u32[]{:S(2)}) collective-permute-start(s32[2,2]{1,0:T(2,128)} %tiles.9), channel_id=1, source_target_pairs={{0,3},{1,0},{2,1},{3,2},{4,7},{5,4},{6,5},{7,6},{8,11},{9,8},{10,9... | collective-permute-start | bytes 56 | tf_op jit(solution)/shard_map/ppermute | solution.py:364
  6.6 4.6 %collective-permute-start.6 = (bf16[24,768]{1,0:T(8,128)(2,1)S(1)}, bf16[24,768]{1,0:T(8,128)(2,1)S(1)}, u32[]{:S(2)}, u32[]{:S(2)}) collective-permute-start(bf16[24,768]{1,0:T(8,128)(2,1)S(1)} %reshape.3.own), channel_id=1, source_target_pairs={{0,16},{16,32},{32,48},{48,0},{1,17},{17,33},{33,49},{49,1},{2,18}... | collective-permute-start | bytes 110600 | tf_op jit(solution)/shard_map/ppermute | solution.py:364
  12.2 2.8 %collective-permute-start.8 = (bf16[24,768]{1,0:T(8,128)(2,1)S(1)}, bf16[24,768]{1,0:T(8,128)(2,1)S(1)}, u32[]{:S(2)}, u32[]{:S(2)}) collective-permute-start(bf16[24,768]{1,0:T(8,128)(2,1)S(1)} %reshape.3.own), channel_id=1, source_target_pairs={{0,48},{16,0},{32,16},{48,32},{1,49},{17,1},{33,17},{49,33},{2,50}... | collective-permute-start | bytes 110600 | tf_op jit(solution)/shard_map/ppermute | solution.py:364
  15.7 1.5 %collective-permute-start.3 = (s32[4,2,2]{2,1,0:T(2,128)S(1)}, s32[4,2,2]{2,1,0:T(2,128)S(1)}, u32[]{:S(2)}, u32[]{:S(2)}) collective-permute-start(s32[4,2,2]{2,1,0:T(2,128)S(1)} %pad_add_fusion.line0), channel_id=1, source_target_pairs={{0,4},{4,8},{8,12},{12,0},{1,5},{5,9},{9,13},{13,1},{2,6},{6,10},{... | collective-permute-start | bytes 200 | tf_op jit(solution)/shard_map/ppermute | solution.py:364
  17.2 2.7 %collective-permute-start.4 = (s32[4,2,2]{2,1,0:T(2,128)S(1)}, s32[4,2,2]{2,1,0:T(2,128)S(1)}, u32[]{:S(2)}, u32[]{:S(2)}) collective-permute-start(s32[4,2,2]{2,1,0:T(2,128)S(1)} %pad_add_fusion.line0), channel_id=1, source_target_pairs={{0,8},{4,12},{8,0},{12,4},{1,9},{5,13},{9,1},{13,5},{2,10},{6,14},... | collective-permute-start | bytes 200 | tf_op jit(solution)/shard_map/ppermute | solution.py:364
  20.5 1.5 %collective-permute-start.5 = (s32[4,2,2]{2,1,0:T(2,128)S(1)}, s32[4,2,2]{2,1,0:T(2,128)S(1)}, u32[]{:S(2)}, u32[]{:S(2)}) collective-permute-start(s32[4,2,2]{2,1,0:T(2,128)S(1)} %pad_add_fusion.line0), channel_id=1, source_target_pairs={{0,12},{4,0},{8,4},{12,8},{1,13},{5,1},{9,5},{13,9},{2,14},{6,2},{... | collective-permute-start | bytes 200 | tf_op jit(solution)/shard_map/ppermute | solution.py:364
  22.3 1.8 %collective-permute-done.5.line3 = s32[4,2,2]{2,1,0:T(2,128)S(1)} collective-permute-done((s32[4,2,2]{2,1,0:T(2,128)S(1)}, s32[4,2,2]{2,1,0:T(2,128)S(1)}, u32[]{:S(2)}, u32[]{:S(2)}) %collective-permute-start.5) | collective-permute-done | bytes 96 | tf_op jit(solution)/shard_map/ppermute | solution.py:364
  24.1 2.6 %pack.1 = bf16[32,72,512]{2,1,0:T(8,128)(2,1)} custom-call(s32[4,2,2]{2,1,0:T(2,128)S(1)} %pad_add_fusion.line0, s32[4,2,2]{2,1,0:T(2,128)S(1)} %collective-permute-done.3.line1, s32[4,2,2]{2,1,0:T(2,128)S(1)} %collective-permute-done.4.line2, s32[4,2,2]{2,1,0:T(2,128)S(1)} %collective-permute-done.5.line3, bf16[24,768]{1,0:T(8,128)(2,1)S(1)} %reshape.3.own, ...), custom_call_target="tpu_custom_call" | custom-call | tf_op jit(solution)/shard_map/pack/pallas_call | solution.py:144
  26.8 5.1 %all-to-all-start = ((bf16[32,72,512]{2,1,0:T(8,128)(2,1)}), bf16[32,72,512]{2,1,0:T(8,128)(2,1)S(1)}, u32[]{:S(2)}, u32[]{:S(2)}) async-start(bf16[32,72,512]{2,1,0:T(8,128)(2,1)} %pack.1), calls=%async_computation | async-start | bytes 4718592 | tf_op jit(solution)/shard_map/all_to_all | solution.py:374
  32.0 1.6 %copy-done.3 = bf16[2,2,512,512]{3,2,1,0:T(8,128)(2,1)S(1)} copy-done((bf16[2,2,512,512]{3,2,1,0:T(8,128)(2,1)S(1)}, bf16[2,2,512,512]{3,2,1,0:T(8,128)(2,1)}, u32[]{:S(2)}) %copy-start.3) | copy-done | bytes 2097176
  36.0 3.4 %prep.1 = (bf16[512,1024]{1,0:T(8,128)(2,1)S(1)}, bf16[512,1024]{1,0:T(8,128)(2,1)S(1)}, bf16[512,1024]{1,0:T(8,128)(2,1)S(1)}) custom-call(s32[2,2]{1,0:T(2,128)S(1)} %copy-done.2, bf16[2,512,512]{2,1,0:T(8,128)(2,1)S(1)} %copy-done.4, bf16[2,512,512]{2,1,0:T(8,128)(2,1)S(1)} %copy-done.5, bf16[2,512,512]{2,1,0:T(8,128)(2,1)S(1)} %copy-done.6, ...), custom_call_target="tpu_custom_call" | custom-call | flops 4000000000 | bytes 20000000 | tf_op jit(solution)/shard_map/prep/pallas_call | solution.py:93
  42.3 16.8 %all-to-all-done.own = bf16[32,72,512]{2,1,0:T(8,128)(2,1)S(1)} async-done(((bf16[32,72,512]{2,1,0:T(8,128)(2,1)}), bf16[32,72,512]{2,1,0:T(8,128)(2,1)S(1)}, u32[]{:S(2)}, u32[]{:S(2)}) %all-to-all-start) | async-done | bytes 2359328 | tf_op jit(solution)/shard_map/all_to_all | solution.py:374
  59.2 5.0 %open_step.1 = (f32[512,1024]{1,0:T(8,128)S(1)}, bf16[512,1024]{1,0:T(8,128)(2,1)S(1)}, bf16[1024,1024]{1,0:T(8,128)(2,1)S(1)}, bf16[1024,1024]{1,0:T(8,128)(2,1)S(1)}) custom-call(s32[2,2]{1,0:T(2,128)S(1)} %copy-done.2, bf16[32,72,512]{2,1,0:T(8,128)(2,1)S(1)} %all-to-all-done.own, bf16[512,1024]{1,0:T(8,128)(2,1)} %copy-done.7, ...), custom_call_target="tpu_custom_call" | custom-call | flops 4000000000 | bytes 10000000 | tf_op jit(solution)/shard_map/open_step/pallas_call | solution.py:231
  64.8 5.9 %close_steps.1 = (f32[512,1024]{1,0:T(8,128)S(1)}, bf16[512,1024]{1,0:T(8,128)(2,1)S(1)}) custom-call(s32[2,2]{1,0:T(2,128)S(1)} %copy-done.2, bf16[32,72,512]{2,1,0:T(8,128)(2,1)S(1)} %all-to-all-done.own, bf16[32,72,512]{2,1,0:T(8,128)(2,1)S(1)} %collective-permute-done.9.other, bf16[1024,1024]{1,0:T(8,128)(2,1)S(1)} %get-tuple-element.33.v1, ...), custom_call_target="tpu_custom_call" | custom-call | flops 8000000000 | bytes 10000000 | tf_op jit(solution)/shard_map/close_steps/pallas_call | solution.py:256
  71.7 1.2 early.1.half
  73.6 1.4 %late.1 = bf16[32,72,512]{2,1,0:T(8,128)(2,1)S(1)} custom-call(s32[2,2]{1,0:T(2,128)S(1)} %copy-done.2, s32[1]{0:T(128)S(6)} %copy.10.count, bf16[512,1024]{1,0:T(8,128)(2,1)S(1)} %copy-done.1, bf16[512,1024]{1,0:T(8,128)(2,1)S(1)} %collective-permute-done.10.remote, bf16[16,72,512]{2,1,0:T(8,128)(2,1)S(1)} %early.1.half), custom_call_target="tpu_custom_call" | custom-call | tf_op jit(solution)/shard_map/late/pallas_call | solution.py:295
  75.1 37.5 %all_to_all.10.got = bf16[32,72,512]{2,1,0:T(8,128)(2,1)S(1)} all-to-all(bf16[32,72,512]{2,1,0:T(8,128)(2,1)S(1)} %late.1), channel_id=1, replica_groups=mesh['zl'=2,'core'=2,'zh'=4,'x'=4,'y'=4] {'zl','x','y'}, dimensions={0} | all-to-all | bytes 4718592 | tf_op jit(solution)/shard_map/all_to_all | solution.py:387
  112.5 1.6 %gather.1 = (f32[24,768]{1,0:T(8,128)S(1)}, bf16[24,768]{1,0:T(8,128)(2,1)S(1)}, bf16[24,768]{1,0:T(8,128)(2,1)S(1)}, bf16[24,768]{1,0:T(8,128)(2,1)S(1)}) custom-call(s32[4,2,2]{2,1,0:T(2,128)S(1)} %pad_add_fusion.line0, s32[4,2,2]{2,1,0:T(2,128)S(1)} %collective-permute-done.3.line1, s32[4,2,2]{2,1,0:T(2,128)S(1)} %collective-permute-done.4.line2, ...), custom_call_target="tpu_custom_call" | custom-call | tf_op jit(solution)/shard_map/gather/pallas_call | solution.py:335
  114.1 3.4 %collective-permute-start.12 = (bf16[24,768]{1,0:T(8,128)(2,1)S(1)}, bf16[24,768]{1,0:T(8,128)(2,1)S(1)}, u32[]{:S(2)}, u32[]{:S(2)}) collective-permute-start(bf16[24,768]{1,0:T(8,128)(2,1)S(1)} %get-tuple-element.40), channel_id=1, source_target_pairs={{0,32},{16,48},{32,0},{48,16},{1,33},{17,49},{33,1},{49,17},{2,34}... | collective-permute-start | bytes 110600 | tf_op jit(solution)/shard_map/ppermute | solution.py:364
  117.5 3.1 %collective-permute-start.13 = (bf16[24,768]{1,0:T(8,128)(2,1)S(1)}, bf16[24,768]{1,0:T(8,128)(2,1)S(1)}, u32[]{:S(2)}, u32[]{:S(2)}) collective-permute-start(bf16[24,768]{1,0:T(8,128)(2,1)S(1)} %get-tuple-element.41), channel_id=1, source_target_pairs={{0,16},{16,32},{32,48},{48,0},{1,17},{17,33},{33,49},{49,1},{2,18}... | collective-permute-start | bytes 110600 | tf_op jit(solution)/shard_map/ppermute | solution.py:364
  120.6 1.5 %collective-permute-done.12.one = bf16[24,768]{1,0:T(8,128)(2,1)S(1)} collective-permute-done((bf16[24,768]{1,0:T(8,128)(2,1)S(1)}, bf16[24,768]{1,0:T(8,128)(2,1)S(1)}, u32[]{:S(2)}, u32[]{:S(2)}) %collective-permute-start.12) | collective-permute-done | bytes 36896 | tf_op jit(solution)/shard_map/ppermute | solution.py:364
  122.9 4.2 %collective-permute-done.14.three = bf16[24,768]{1,0:T(8,128)(2,1)S(1)} collective-permute-done((bf16[24,768]{1,0:T(8,128)(2,1)S(1)}, bf16[24,768]{1,0:T(8,128)(2,1)S(1)}, u32[]{:S(2)}, u32[]{:S(2)}) %collective-permute-start.14) | collective-permute-done | bytes 36896 | tf_op jit(solution)/shard_map/ppermute | solution.py:364
  (38 shorter events, 11.8 us)
Async XLA Ops:
  0.0 12.2 %collective-permute-start = (s32[2,2]{1,0:T(2,128)}, s32[2,2]{1,0:T(2,128)S(1)}, u32[]{:S(2)}, u32[]{:S(2)}) collective-permute-start(s32[2,2]{1,0:T(2,128)} %tiles.9), channel_id=1, source_target_pairs={{0,1},{1,2},{2,3},{3,0},{4,5},{5,6},{6,7},{7,4},{8,9},{9,10},{10,1... | collective-permute-start | bytes 56 | tf_op jit(solution)/shard_map/ppermute | solution.py:364
  1.6 13.4 %collective-permute-start.1 = (s32[2,2]{1,0:T(2,128)}, s32[2,2]{1,0:T(2,128)S(1)}, u32[]{:S(2)}, u32[]{:S(2)}) collective-permute-start(s32[2,2]{1,0:T(2,128)} %tiles.9), channel_id=1, source_target_pairs={{0,2},{1,3},{2,0},{3,1},{4,6},{5,7},{6,4},{7,5},{8,10},{9,11},{10,... | collective-permute-start | bytes 56 | tf_op jit(solution)/shard_map/ppermute | solution.py:364
  4.5 10.5 %collective-permute-start.2 = (s32[2,2]{1,0:T(2,128)}, s32[2,2]{1,0:T(2,128)S(1)}, u32[]{:S(2)}, u32[]{:S(2)}) collective-permute-start(s32[2,2]{1,0:T(2,128)} %tiles.9), channel_id=1, source_target_pairs={{0,3},{1,0},{2,1},{3,2},{4,7},{5,4},{6,5},{7,6},{8,11},{9,8},{10,9... | collective-permute-start | bytes 56 | tf_op jit(solution)/shard_map/ppermute | solution.py:364
  6.6 17.5 %collective-permute-start.6 = (bf16[24,768]{1,0:T(8,128)(2,1)S(1)}, bf16[24,768]{1,0:T(8,128)(2,1)S(1)}, u32[]{:S(2)}, u32[]{:S(2)}) collective-permute-start(bf16[24,768]{1,0:T(8,128)(2,1)S(1)} %reshape.3.own), channel_id=1, source_target_pairs={{0,16},{16,32},{32,48},{48,0},{1,17},{17,33},{33,49},{49,1},{2,18}... | collective-permute-start | bytes 110600 | tf_op jit(solution)/shard_map/ppermute | solution.py:364
  11.2 13.0 %collective-permute-start.7 = (bf16[24,768]{1,0:T(8,128)(2,1)S(1)}, bf16[24,768]{1,0:T(8,128)(2,1)S(1)}, u32[]{:S(2)}, u32[]{:S(2)}) collective-permute-start(bf16[24,768]{1,0:T(8,128)(2,1)S(1)} %reshape.3.own), channel_id=1, source_target_pairs={{0,32},{16,48},{32,0},{48,16},{1,33},{17,49},{33,1},{49,17},{2,34}... | collective-permute-start | bytes 110600 | tf_op jit(solution)/shard_map/ppermute | solution.py:364
  12.2 12.0 %collective-permute-start.8 = (bf16[24,768]{1,0:T(8,128)(2,1)S(1)}, bf16[24,768]{1,0:T(8,128)(2,1)S(1)}, u32[]{:S(2)}, u32[]{:S(2)}) collective-permute-start(bf16[24,768]{1,0:T(8,128)(2,1)S(1)} %reshape.3.own), channel_id=1, source_target_pairs={{0,48},{16,0},{32,16},{48,32},{1,49},{17,1},{33,17},{49,33},{2,50}... | collective-permute-start | bytes 110600 | tf_op jit(solution)/shard_map/ppermute | solution.py:364
  15.7 4.8 %collective-permute-start.3 = (s32[4,2,2]{2,1,0:T(2,128)S(1)}, s32[4,2,2]{2,1,0:T(2,128)S(1)}, u32[]{:S(2)}, u32[]{:S(2)}) collective-permute-start(s32[4,2,2]{2,1,0:T(2,128)S(1)} %pad_add_fusion.line0), channel_id=1, source_target_pairs={{0,4},{4,8},{8,12},{12,0},{1,5},{5,9},{9,13},{13,1},{2,6},{6,10},{... | collective-permute-start | bytes 200 | tf_op jit(solution)/shard_map/ppermute | solution.py:364
  17.2 5.1 %collective-permute-start.4 = (s32[4,2,2]{2,1,0:T(2,128)S(1)}, s32[4,2,2]{2,1,0:T(2,128)S(1)}, u32[]{:S(2)}, u32[]{:S(2)}) collective-permute-start(s32[4,2,2]{2,1,0:T(2,128)S(1)} %pad_add_fusion.line0), channel_id=1, source_target_pairs={{0,8},{4,12},{8,0},{12,4},{1,9},{5,13},{9,1},{13,5},{2,10},{6,14},... | collective-permute-start | bytes 200 | tf_op jit(solution)/shard_map/ppermute | solution.py:364
  20.5 3.6 %collective-permute-start.5 = (s32[4,2,2]{2,1,0:T(2,128)S(1)}, s32[4,2,2]{2,1,0:T(2,128)S(1)}, u32[]{:S(2)}, u32[]{:S(2)}) collective-permute-start(s32[4,2,2]{2,1,0:T(2,128)S(1)} %pad_add_fusion.line0), channel_id=1, source_target_pairs={{0,12},{4,0},{8,4},{12,8},{1,13},{5,1},{9,5},{13,9},{2,14},{6,2},{... | collective-permute-start | bytes 200 | tf_op jit(solution)/shard_map/ppermute | solution.py:364
  26.8 5.2 %copy-start.2 = (s32[2,2]{1,0:T(2,128)S(1)}, s32[2,2]{1,0:T(2,128)}, u32[]{:S(2)}) copy-start(s32[2,2]{1,0:T(2,128)} %tiles.9) | copy-start | bytes 52
  26.8 5.2 %copy-start.4 = (bf16[2,512,512]{2,1,0:T(8,128)(2,1)S(1)}, bf16[2,512,512]{2,1,0:T(8,128)(2,1)}, u32[]{:S(2)}) copy-start(bf16[2,512,512]{2,1,0:T(8,128)(2,1)} %rows) | copy-start | bytes 3145732
  26.8 32.4 %all-to-all-start = ((bf16[32,72,512]{2,1,0:T(8,128)(2,1)}), bf16[32,72,512]{2,1,0:T(8,128)(2,1)S(1)}, u32[]{:S(2)}, u32[]{:S(2)}) async-start(bf16[32,72,512]{2,1,0:T(8,128)(2,1)} %pack.1), calls=%async_computation | async-start | bytes 4718592 | tf_op jit(solution)/shard_map/all_to_all | solution.py:374
  32.0 1.6 %copy-start.3 = (bf16[2,2,512,512]{3,2,1,0:T(8,128)(2,1)S(1)}, bf16[2,2,512,512]{3,2,1,0:T(8,128)(2,1)}, u32[]{:S(2)}) copy-start(bf16[2,2,512,512]{3,2,1,0:T(8,128)(2,1)} %cot.1) | copy-start | bytes 6291460
  33.6 1.2 copy-start.5
  34.8 1.2 copy-start.6
  39.4 1.0 copy-start
  41.3 1.0 copy-start.8
  59.2 5.6 %collective-permute-start.9 = (bf16[32,72,512]{2,1,0:T(8,128)(2,1)S(1)}, bf16[32,72,512]{2,1,0:T(8,128)(2,1)S(1)}, u32[]{:S(2)}, u32[]{:S(2)}) collective-permute-start(bf16[32,72,512]{2,1,0:T(8,128)(2,1)S(1)} %all-to-all-done.own), channel_id=1, source_target_pairs={{0,64},{64,0},{1,65},{65,1},{2,66},{66,2},{3,67},{67,3},{4,68},{68... | collective-permute-start | bytes 7077896 | tf_op jit(solution)/shard_map/ppermute | solution.py:364
  64.2 7.5 %collective-permute-start.11 = (bf16[512,1024]{1,0:T(8,128)(2,1)S(1)}, bf16[512,1024]{1,0:T(8,128)(2,1)S(1)}, u32[]{:S(2)}, u32[]{:S(2)}) collective-permute-start(bf16[512,1024]{1,0:T(8,128)(2,1)S(1)} %get-tuple-element.38), channel_id=1, source_target_pairs={{0,64},{64,0},{1,65},{65,1},{2,66},{66,2},{3,67},{67,3},{4,68},{68... | collective-permute-start | bytes 3145736 | tf_op jit(solution)/shard_map/ppermute | solution.py:364
  70.7 3.0 %collective-permute-start.10 = (bf16[512,1024]{1,0:T(8,128)(2,1)S(1)}, bf16[512,1024]{1,0:T(8,128)(2,1)S(1)}, u32[]{:S(2)}, u32[]{:S(2)}) collective-permute-start(bf16[512,1024]{1,0:T(8,128)(2,1)S(1)} %get-tuple-element.36), channel_id=1, source_target_pairs={{0,64},{64,0},{1,65},{65,1},{2,66},{66,2},{3,67},{67,3},{4,68},{68... | collective-permute-start | bytes 3145736 | tf_op jit(solution)/shard_map/ppermute | solution.py:364
  71.7 2.0 %copy-start.1 = (bf16[512,1024]{1,0:T(8,128)(2,1)S(1)}, bf16[512,1024]{1,0:T(8,128)(2,1)}, u32[]{:S(2)}) copy-start(bf16[512,1024]{1,0:T(8,128)(2,1)} %copy-done) | copy-start | bytes 3145732
  114.1 8.0 %collective-permute-start.12 = (bf16[24,768]{1,0:T(8,128)(2,1)S(1)}, bf16[24,768]{1,0:T(8,128)(2,1)S(1)}, u32[]{:S(2)}, u32[]{:S(2)}) collective-permute-start(bf16[24,768]{1,0:T(8,128)(2,1)S(1)} %get-tuple-element.40), channel_id=1, source_target_pairs={{0,32},{16,48},{32,0},{48,16},{1,33},{17,49},{33,1},{49,17},{2,34}... | collective-permute-start | bytes 110600 | tf_op jit(solution)/shard_map/ppermute | solution.py:364
  117.5 5.4 %collective-permute-start.13 = (bf16[24,768]{1,0:T(8,128)(2,1)S(1)}, bf16[24,768]{1,0:T(8,128)(2,1)S(1)}, u32[]{:S(2)}, u32[]{:S(2)}) collective-permute-start(bf16[24,768]{1,0:T(8,128)(2,1)S(1)} %get-tuple-element.41), channel_id=1, source_target_pairs={{0,16},{16,32},{32,48},{48,0},{1,17},{17,33},{33,49},{49,1},{2,18}... | collective-permute-start | bytes 110600 | tf_op jit(solution)/shard_map/ppermute | solution.py:364
  120.6 6.5 %collective-permute-start.14 = (bf16[24,768]{1,0:T(8,128)(2,1)S(1)}, bf16[24,768]{1,0:T(8,128)(2,1)S(1)}, u32[]{:S(2)}, u32[]{:S(2)}) collective-permute-start(bf16[24,768]{1,0:T(8,128)(2,1)S(1)} %get-tuple-element.42), channel_id=1, source_target_pairs={{0,48},{16,0},{32,16},{48,32},{1,49},{17,1},{33,17},{49,33},{2,50}... | collective-permute-start | bytes 110600 | tf_op jit(solution)/shard_map/ppermute | solution.py:364
  (1 other events, 1.0 us)

commit v12 on v11

--- a/solution.py
+++ b/solution.py
@@ -209,7 +209,7 @@
     m[W:, W:] = m[0:W, 0:W]
 
 
-def open_kernel(tiles, own, m1, m2, state, after, sent, v1, v2, patch, left, right, held, sems):
+def open_kernel(tiles, own, m1, m2, state, after, sent, v1, v2, spare, patch, left, right, held, sems):
     core, sign, row_tile = role(tiles)
     copies = [pltpu.make_async_copy(a, b, sems.at[i]) for i, (a, b) in enumerate([(state, held), (m1, v1.at[0:W]), (m2, v2.at[0:W])])]
     for copy in copies:
@@ -217,6 +217,7 @@
     place_patch(own, core * 16, patch, row_tile)
     copies[0].wait()
     form_left(held, patch, sign, left)
+    place_patch(own, (1 - core) * 16, spare, row_tile)
     copies[1].wait()
     complete(v1)
     sweep(v1, left, right)
@@ -230,9 +231,9 @@
 def open_step(tiles, own, m1, m2, state):
     return pl.pallas_call(
         open_kernel,
-        out_shape=[STATE, SENT, SQUARE, SQUARE],
+        out_shape=[STATE, SENT, SQUARE, SQUARE, jax.ShapeDtypeStruct((2, ROWS, W), F32)],
         in_specs=[SMEM, VMEM] + [HBM] * 3,
-        out_specs=[VMEM] * 4,
+        out_specs=[VMEM] * 5,
         scratch_shapes=WORK + [pltpu.VMEM((W, 2 * W), BF), pltpu.SemaphoreType.DMA((3,))],
         compiler_params=params(24),
         cost_estimate=pl.CostEstimate(flops=4 * 10**9, transcendentals=0, bytes_accessed=10**7),
@@ -240,19 +241,18 @@
     )(tiles, own, m1, m2, state)
 
 
-def close_kernel(tiles, own, other, v1, v2, state, middle, sent, patch, left, right):
+def close_kernel(tiles, spare, other, v1, v2, state, middle, sent, patch, left, right):
     core, sign, row_tile = role(tiles)
     place_patch(other, core * 16, patch, row_tile)
     form_left(state, patch, sign, left)
     sweep(v1, left, right)
     middle[...] = jnp.dot(right[...], v2[...], preferred_element_type=F32)
-    place_patch(own, (1 - core) * 16, patch, row_tile)
-    form_left(middle, patch, sign, left)
+    form_left(middle, spare, sign, left)
     sweep(v1, left, right)
     sent[...] = jnp.dot(right[...], v2[...], preferred_element_type=F32).astype(BF)
 
 
-def close_steps(tiles, own, other, m1, m2, state):
+def close_steps(tiles, spare, other, m1, m2, state):
     return pl.pallas_call(
         close_kernel,
         out_shape=[STATE, SENT],
@@ -262,7 +262,7 @@
         compiler_params=params(24),
         cost_estimate=pl.CostEstimate(flops=8 * 10**9, transcendentals=0, bytes_accessed=10**7),
         name="close_steps",
-    )(tiles, own, other, m1, m2, state)
+    )(tiles, spare, other, m1, m2, state)
 
 
 def early_kernel(tiles, count, local, remote, out, contrib):
@@ -378,9 +378,9 @@
     m2 = pltpu.with_memory_space_constraint(m2, pltpu.HBM)
     kept = pltpu.with_memory_space_constraint(state, pltpu.HBM)
     other = turn(own, "core", 1, 2)
-    after, first, m1, m2 = open_step(window_tiles, own, m1, m2, kept)
+    after, first, m1, m2, spare = open_step(window_tiles, own, m1, m2, kept)
     first_away = turn(first, "core", 1, 2)
-    middle, last = close_steps(window_tiles, own, other, m1, m2, after)
+    middle, last = close_steps(window_tiles, spare, other, m1, m2, after)
     last_away = turn(last, "core", 1, 2)
     half = early(window_tiles, slot_count, middle, first_away)
     contrib = late(window_tiles, slot_count, state, last_away, half)

time: 128 us -> 128 us (level)
  no operation moved by 1% of the time
where the time goes in v12:
time: 128 us
  blocking collectives  37.5 us (29%)
  starting transfers between devices  32.6 us (25%)
  waiting for transfers between devices  26.7 us (21%)
  Pallas kernels  21.5 us (17%)
  local copies, waits for them, and re-layouts  7.79 us (6%)
    all_to_all x1, blocking collectives, on_device(): got = lax.all_to_all(contrib, ('zl', 'x', 'y'), 0, 0, tiled=True)  37.5 us
    ppermute x15, starting transfers between devices, turn(): lax.ppermute(value, axis, [(i, (i + step) % count) for i in range(count)])  27.4 us
    all_to_all x1, waiting for transfers between devices, on_device(): own = lax.all_to_all(sent, ('zl', 'x', 'y'), 0, 0, tiled=True)  16.8 us
    ppermute x15, waiting for transfers between devices, turn(): lax.ppermute(value, axis, [(i, (i + step) % count) for i in range(count)])  9.85 us
    unnamed x19, local copies, waits for them, and re-layouts  7.77 us
    pallas_call x1, Pallas kernels, close_steps(): pl.pallas_call(close_kernel, out_shape=[STATE, SENT], in_specs=[SMEM] + [...  5.73 us
    all_to_all x1, starting transfers between devices, on_device(): own = lax.all_to_all(sent, ('zl', 'x', 'y'), 0, 0, tiled=True)  5.13 us
    pallas_call x1, Pallas kernels, open_step(): pl.pallas_call(open_kernel, out_shape=[STATE, SENT, SQUARE, SQUARE, jax.S...  4.92 us
  transfers between devices with their start and end apart: 16, of which 8 were waited for; matrix products, arithmetic and copies ran while one was open for 1% of the time, Pallas kernels for 12%

profile of v12, /device:TPU:64, one launch (start us, length us, event | category | flops | bytes accessed | tf_op | source)
XLA Modules:
  0.0 127.5 jit_solution(145392476100828177)
XLA Ops:
  0.0 1.6 %collective-permute-start = (s32[2,2]{1,0:T(2,128)}, s32[2,2]{1,0:T(2,128)S(1)}, u32[]{:S(2)}, u32[]{:S(2)}) collective-permute-start(s32[2,2]{1,0:T(2,128)} %tiles.9), channel_id=1, source_target_pairs={{0,1},{1,2},{2,3},{3,0},{4,5},{5,6},{6,7},{7,4},{8,9},{9,10},{10,1... | collective-permute-start | bytes 56 | tf_op jit(solution)/shard_map/ppermute | solution.py:364
  1.6 2.9 %collective-permute-start.1 = (s32[2,2]{1,0:T(2,128)}, s32[2,2]{1,0:T(2,128)S(1)}, u32[]{:S(2)}, u32[]{:S(2)}) collective-permute-start(s32[2,2]{1,0:T(2,128)} %tiles.9), channel_id=1, source_target_pairs={{0,2},{1,3},{2,0},{3,1},{4,6},{5,7},{6,4},{7,5},{8,10},{9,11},{10,... | collective-permute-start | bytes 56 | tf_op jit(solution)/shard_map/ppermute | solution.py:364
  4.5 1.3 %collective-permute-start.2 = (s32[2,2]{1,0:T(2,128)}, s32[2,2]{1,0:T(2,128)S(1)}, u32[]{:S(2)}, u32[]{:S(2)}) collective-permute-start(s32[2,2]{1,0:T(2,128)} %tiles.9), channel_id=1, source_target_pairs={{0,3},{1,0},{2,1},{3,2},{4,7},{5,4},{6,5},{7,6},{8,11},{9,8},{10,9... | collective-permute-start | bytes 56 | tf_op jit(solution)/shard_map/ppermute | solution.py:364
  6.6 4.6 %collective-permute-start.6 = (bf16[24,768]{1,0:T(8,128)(2,1)S(1)}, bf16[24,768]{1,0:T(8,128)(2,1)S(1)}, u32[]{:S(2)}, u32[]{:S(2)}) collective-permute-start(bf16[24,768]{1,0:T(8,128)(2,1)S(1)} %reshape.3.own), channel_id=1, source_target_pairs={{0,16},{16,32},{32,48},{48,0},{1,17},{17,33},{33,49},{49,1},{2,18}... | collective-permute-start | bytes 110600 | tf_op jit(solution)/shard_map/ppermute | solution.py:364
  12.2 2.8 %collective-permute-start.8 = (bf16[24,768]{1,0:T(8,128)(2,1)S(1)}, bf16[24,768]{1,0:T(8,128)(2,1)S(1)}, u32[]{:S(2)}, u32[]{:S(2)}) collective-permute-start(bf16[24,768]{1,0:T(8,128)(2,1)S(1)} %reshape.3.own), channel_id=1, source_target_pairs={{0,48},{16,0},{32,16},{48,32},{1,49},{17,1},{33,17},{49,33},{2,50}... | collective-permute-start | bytes 110600 | tf_op jit(solution)/shard_map/ppermute | solution.py:364
  15.7 1.5 %collective-permute-start.3 = (s32[4,2,2]{2,1,0:T(2,128)S(1)}, s32[4,2,2]{2,1,0:T(2,128)S(1)}, u32[]{:S(2)}, u32[]{:S(2)}) collective-permute-start(s32[4,2,2]{2,1,0:T(2,128)S(1)} %pad_add_fusion.line0), channel_id=1, source_target_pairs={{0,4},{4,8},{8,12},{12,0},{1,5},{5,9},{9,13},{13,1},{2,6},{6,10},{... | collective-permute-start | bytes 200 | tf_op jit(solution)/shard_map/ppermute | solution.py:364
  17.2 2.7 %collective-permute-start.4 = (s32[4,2,2]{2,1,0:T(2,128)S(1)}, s32[4,2,2]{2,1,0:T(2,128)S(1)}, u32[]{:S(2)}, u32[]{:S(2)}) collective-permute-start(s32[4,2,2]{2,1,0:T(2,128)S(1)} %pad_add_fusion.line0), channel_id=1, source_target_pairs={{0,8},{4,12},{8,0},{12,4},{1,9},{5,13},{9,1},{13,5},{2,10},{6,14},... | collective-permute-start | bytes 200 | tf_op jit(solution)/shard_map/ppermute | solution.py:364
  20.5 1.5 %collective-permute-start.5 = (s32[4,2,2]{2,1,0:T(2,128)S(1)}, s32[4,2,2]{2,1,0:T(2,128)S(1)}, u32[]{:S(2)}, u32[]{:S(2)}) collective-permute-start(s32[4,2,2]{2,1,0:T(2,128)S(1)} %pad_add_fusion.line0), channel_id=1, source_target_pairs={{0,12},{4,0},{8,4},{12,8},{1,13},{5,1},{9,5},{13,9},{2,14},{6,2},{... | collective-permute-start | bytes 200 | tf_op jit(solution)/shard_map/ppermute | solution.py:364
  22.3 1.8 %collective-permute-done.5.line3 = s32[4,2,2]{2,1,0:T(2,128)S(1)} collective-permute-done((s32[4,2,2]{2,1,0:T(2,128)S(1)}, s32[4,2,2]{2,1,0:T(2,128)S(1)}, u32[]{:S(2)}, u32[]{:S(2)}) %collective-permute-start.5) | collective-permute-done | bytes 96 | tf_op jit(solution)/shard_map/ppermute | solution.py:364
  24.1 2.6 %pack.1 = bf16[32,72,512]{2,1,0:T(8,128)(2,1)} custom-call(s32[4,2,2]{2,1,0:T(2,128)S(1)} %pad_add_fusion.line0, s32[4,2,2]{2,1,0:T(2,128)S(1)} %collective-permute-done.3.line1, s32[4,2,2]{2,1,0:T(2,128)S(1)} %collective-permute-done.4.line2, s32[4,2,2]{2,1,0:T(2,128)S(1)} %collective-permute-done.5.line3, bf16[24,768]{1,0:T(8,128)(2,1)S(1)} %reshape.3.own, ...), custom_call_target="tpu_custom_call" | custom-call | tf_op jit(solution)/shard_map/pack/pallas_call | solution.py:144
  26.8 5.1 %all-to-all-start = ((bf16[32,72,512]{2,1,0:T(8,128)(2,1)}), bf16[32,72,512]{2,1,0:T(8,128)(2,1)S(1)}, u32[]{:S(2)}, u32[]{:S(2)}) async-start(bf16[32,72,512]{2,1,0:T(8,128)(2,1)} %pack.1), calls=%async_computation | async-start | bytes 4718592 | tf_op jit(solution)/shard_map/all_to_all | solution.py:374
  32.0 1.6 %copy-done.3 = bf16[2,2,512,512]{3,2,1,0:T(8,128)(2,1)S(1)} copy-done((bf16[2,2,512,512]{3,2,1,0:T(8,128)(2,1)S(1)}, bf16[2,2,512,512]{3,2,1,0:T(8,128)(2,1)}, u32[]{:S(2)}) %copy-start.3) | copy-done | bytes 2097176
  36.0 3.4 %prep.1 = (bf16[512,1024]{1,0:T(8,128)(2,1)S(1)}, bf16[512,1024]{1,0:T(8,128)(2,1)S(1)}, bf16[512,1024]{1,0:T(8,128)(2,1)S(1)}) custom-call(s32[2,2]{1,0:T(2,128)S(1)} %copy-done.2, bf16[2,512,512]{2,1,0:T(8,128)(2,1)S(1)} %copy-done.4, bf16[2,512,512]{2,1,0:T(8,128)(2,1)S(1)} %copy-done.5, bf16[2,512,512]{2,1,0:T(8,128)(2,1)S(1)} %copy-done.6, ...), custom_call_target="tpu_custom_call" | custom-call | flops 4000000000 | bytes 20000000 | tf_op jit(solution)/shard_map/prep/pallas_call | solution.py:93
  42.3 16.8 %all-to-all-done.own = bf16[32,72,512]{2,1,0:T(8,128)(2,1)S(1)} async-done(((bf16[32,72,512]{2,1,0:T(8,128)(2,1)}), bf16[32,72,512]{2,1,0:T(8,128)(2,1)S(1)}, u32[]{:S(2)}, u32[]{:S(2)}) %all-to-all-start) | async-done | bytes 2359328 | tf_op jit(solution)/shard_map/all_to_all | solution.py:374
  59.2 4.9 %open_step.1 = (f32[512,1024]{1,0:T(8,128)S(1)}, bf16[512,1024]{1,0:T(8,128)(2,1)S(1)}, bf16[1024,1024]{1,0:T(8,128)(2,1)S(1)}, bf16[1024,1024]{1,0:T(8,128)(2,1)S(1)}, f32[2,640,512]{2,1,0:T(8,128)S(1)}) custom-call(s32[2,2]{1,0:T(2,128)S(1)} %copy-done.2, bf16[32,72,512]{2,1,0:T(8,128)(2,1)S(1)} %all-to-all-done.own, bf16[512,1024]{1,0:T(8,128)(2,1)} %copy-done.7, ...), custom_call_target="tpu_custom_call" | custom-call | flops 4000000000 | bytes 10000000 | tf_op jit(solution)/shard_map/open_step/pallas_call | solution.py:232
  64.7 5.7 %close_steps.1 = (f32[512,1024]{1,0:T(8,128)S(1)}, bf16[512,1024]{1,0:T(8,128)(2,1)S(1)}) custom-call(s32[2,2]{1,0:T(2,128)S(1)} %copy-done.2, f32[2,640,512]{2,1,0:T(8,128)S(1)} %get-tuple-element.34.spare, bf16[32,72,512]{2,1,0:T(8,128)(2,1)S(1)} %collective-permute-done.9.other, bf16[1024,1024]{1,0:T(8,128)(2,1)S(1)} %get-tuple-element.35.v1, ...), custom_call_target="tpu_custom_call" | custom-call | flops 8000000000 | bytes 10000000 | tf_op jit(solution)/shard_map/close_steps/pallas_call | solution.py:256
  71.4 1.2 early.1.half
  73.4 1.4 %late.1 = bf16[32,72,512]{2,1,0:T(8,128)(2,1)S(1)} custom-call(s32[2,2]{1,0:T(2,128)S(1)} %copy-done.2, s32[1]{0:T(128)S(6)} %copy.10.count, bf16[512,1024]{1,0:T(8,128)(2,1)S(1)} %copy-done.1, bf16[512,1024]{1,0:T(8,128)(2,1)S(1)} %collective-permute-done.10.remote, bf16[16,72,512]{2,1,0:T(8,128)(2,1)S(1)} %early.1.half), custom_call_target="tpu_custom_call" | custom-call | tf_op jit(solution)/shard_map/late/pallas_call | solution.py:295
  74.8 37.5 %all_to_all.10.got = bf16[32,72,512]{2,1,0:T(8,128)(2,1)S(1)} all-to-all(bf16[32,72,512]{2,1,0:T(8,128)(2,1)S(1)} %late.1), channel_id=1, replica_groups=mesh['zl'=2,'core'=2,'zh'=4,'x'=4,'y'=4] {'zl','x','y'}, dimensions={0} | all-to-all | bytes 4718592 | tf_op jit(solution)/shard_map/all_to_all | solution.py:387
  112.3 1.6 %gather.1 = (f32[24,768]{1,0:T(8,128)S(1)}, bf16[24,768]{1,0:T(8,128)(2,1)S(1)}, bf16[24,768]{1,0:T(8,128)(2,1)S(1)}, bf16[24,768]{1,0:T(8,128)(2,1)S(1)}) custom-call(s32[4,2,2]{2,1,0:T(2,128)S(1)} %pad_add_fusion.line0, s32[4,2,2]{2,1,0:T(2,128)S(1)} %collective-permute-done.3.line1, s32[4,2,2]{2,1,0:T(2,128)S(1)} %collective-permute-done.4.line2, ...), custom_call_target="tpu_custom_call" | custom-call | tf_op jit(solution)/shard_map/gather/pallas_call | solution.py:335
  113.8 3.4 %collective-permute-start.12 = (bf16[24,768]{1,0:T(8,128)(2,1)S(1)}, bf16[24,768]{1,0:T(8,128)(2,1)S(1)}, u32[]{:S(2)}, u32[]{:S(2)}) collective-permute-start(bf16[24,768]{1,0:T(8,128)(2,1)S(1)} %get-tuple-element.42), channel_id=1, source_target_pairs={{0,32},{16,48},{32,0},{48,16},{1,33},{17,49},{33,1},{49,17},{2,34}... | collective-permute-start | bytes 110600 | tf_op jit(solution)/shard_map/ppermute | solution.py:364
  117.2 3.1 %collective-permute-start.13 = (bf16[24,768]{1,0:T(8,128)(2,1)S(1)}, bf16[24,768]{1,0:T(8,128)(2,1)S(1)}, u32[]{:S(2)}, u32[]{:S(2)}) collective-permute-start(bf16[24,768]{1,0:T(8,128)(2,1)S(1)} %get-tuple-element.43), channel_id=1, source_target_pairs={{0,16},{16,32},{32,48},{48,0},{1,17},{17,33},{33,49},{49,1},{2,18}... | collective-permute-start | bytes 110600 | tf_op jit(solution)/shard_map/ppermute | solution.py:364
  120.4 1.5 %collective-permute-done.12.one = bf16[24,768]{1,0:T(8,128)(2,1)S(1)} collective-permute-done((bf16[24,768]{1,0:T(8,128)(2,1)S(1)}, bf16[24,768]{1,0:T(8,128)(2,1)S(1)}, u32[]{:S(2)}, u32[]{:S(2)}) %collective-permute-start.12) | collective-permute-done | bytes 36896 | tf_op jit(solution)/shard_map/ppermute | solution.py:364
  122.6 4.2 %collective-permute-done.14.three = bf16[24,768]{1,0:T(8,128)(2,1)S(1)} collective-permute-done((bf16[24,768]{1,0:T(8,128)(2,1)S(1)}, bf16[24,768]{1,0:T(8,128)(2,1)S(1)}, u32[]{:S(2)}, u32[]{:S(2)}) %collective-permute-start.14) | collective-permute-done | bytes 36896 | tf_op jit(solution)/shard_map/ppermute | solution.py:364
  (38 shorter events, 11.8 us)
Async XLA Ops:
  0.0 12.2 %collective-permute-start = (s32[2,2]{1,0:T(2,128)}, s32[2,2]{1,0:T(2,128)S(1)}, u32[]{:S(2)}, u32[]{:S(2)}) collective-permute-start(s32[2,2]{1,0:T(2,128)} %tiles.9), channel_id=1, source_target_pairs={{0,1},{1,2},{2,3},{3,0},{4,5},{5,6},{6,7},{7,4},{8,9},{9,10},{10,1... | collective-permute-start | bytes 56 | tf_op jit(solution)/shard_map/ppermute | solution.py:364
  1.6 13.4 %collective-permute-start.1 = (s32[2,2]{1,0:T(2,128)}, s32[2,2]{1,0:T(2,128)S(1)}, u32[]{:S(2)}, u32[]{:S(2)}) collective-permute-start(s32[2,2]{1,0:T(2,128)} %tiles.9), channel_id=1, source_target_pairs={{0,2},{1,3},{2,0},{3,1},{4,6},{5,7},{6,4},{7,5},{8,10},{9,11},{10,... | collective-permute-start | bytes 56 | tf_op jit(solution)/shard_map/ppermute | solution.py:364
  4.5 10.5 %collective-permute-start.2 = (s32[2,2]{1,0:T(2,128)}, s32[2,2]{1,0:T(2,128)S(1)}, u32[]{:S(2)}, u32[]{:S(2)}) collective-permute-start(s32[2,2]{1,0:T(2,128)} %tiles.9), channel_id=1, source_target_pairs={{0,3},{1,0},{2,1},{3,2},{4,7},{5,4},{6,5},{7,6},{8,11},{9,8},{10,9... | collective-permute-start | bytes 56 | tf_op jit(solution)/shard_map/ppermute | solution.py:364
  6.6 17.5 %collective-permute-start.6 = (bf16[24,768]{1,0:T(8,128)(2,1)S(1)}, bf16[24,768]{1,0:T(8,128)(2,1)S(1)}, u32[]{:S(2)}, u32[]{:S(2)}) collective-permute-start(bf16[24,768]{1,0:T(8,128)(2,1)S(1)} %reshape.3.own), channel_id=1, source_target_pairs={{0,16},{16,32},{32,48},{48,0},{1,17},{17,33},{33,49},{49,1},{2,18}... | collective-permute-start | bytes 110600 | tf_op jit(solution)/shard_map/ppermute | solution.py:364
  11.2 13.0 %collective-permute-start.7 = (bf16[24,768]{1,0:T(8,128)(2,1)S(1)}, bf16[24,768]{1,0:T(8,128)(2,1)S(1)}, u32[]{:S(2)}, u32[]{:S(2)}) collective-permute-start(bf16[24,768]{1,0:T(8,128)(2,1)S(1)} %reshape.3.own), channel_id=1, source_target_pairs={{0,32},{16,48},{32,0},{48,16},{1,33},{17,49},{33,1},{49,17},{2,34}... | collective-permute-start | bytes 110600 | tf_op jit(solution)/shard_map/ppermute | solution.py:364
  12.2 12.0 %collective-permute-start.8 = (bf16[24,768]{1,0:T(8,128)(2,1)S(1)}, bf16[24,768]{1,0:T(8,128)(2,1)S(1)}, u32[]{:S(2)}, u32[]{:S(2)}) collective-permute-start(bf16[24,768]{1,0:T(8,128)(2,1)S(1)} %reshape.3.own), channel_id=1, source_target_pairs={{0,48},{16,0},{32,16},{48,32},{1,49},{17,1},{33,17},{49,33},{2,50}... | collective-permute-start | bytes 110600 | tf_op jit(solution)/shard_map/ppermute | solution.py:364
  15.7 4.8 %collective-permute-start.3 = (s32[4,2,2]{2,1,0:T(2,128)S(1)}, s32[4,2,2]{2,1,0:T(2,128)S(1)}, u32[]{:S(2)}, u32[]{:S(2)}) collective-permute-start(s32[4,2,2]{2,1,0:T(2,128)S(1)} %pad_add_fusion.line0), channel_id=1, source_target_pairs={{0,4},{4,8},{8,12},{12,0},{1,5},{5,9},{9,13},{13,1},{2,6},{6,10},{... | collective-permute-start | bytes 200 | tf_op jit(solution)/shard_map/ppermute | solution.py:364
  17.2 5.1 %collective-permute-start.4 = (s32[4,2,2]{2,1,0:T(2,128)S(1)}, s32[4,2,2]{2,1,0:T(2,128)S(1)}, u32[]{:S(2)}, u32[]{:S(2)}) collective-permute-start(s32[4,2,2]{2,1,0:T(2,128)S(1)} %pad_add_fusion.line0), channel_id=1, source_target_pairs={{0,8},{4,12},{8,0},{12,4},{1,9},{5,13},{9,1},{13,5},{2,10},{6,14},... | collective-permute-start | bytes 200 | tf_op jit(solution)/shard_map/ppermute | solution.py:364
  20.5 3.6 %collective-permute-start.5 = (s32[4,2,2]{2,1,0:T(2,128)S(1)}, s32[4,2,2]{2,1,0:T(2,128)S(1)}, u32[]{:S(2)}, u32[]{:S(2)}) collective-permute-start(s32[4,2,2]{2,1,0:T(2,128)S(1)} %pad_add_fusion.line0), channel_id=1, source_target_pairs={{0,12},{4,0},{8,4},{12,8},{1,13},{5,1},{9,5},{13,9},{2,14},{6,2},{... | collective-permute-start | bytes 200 | tf_op jit(solution)/shard_map/ppermute | solution.py:364
  26.8 5.2 %copy-start.2 = (s32[2,2]{1,0:T(2,128)S(1)}, s32[2,2]{1,0:T(2,128)}, u32[]{:S(2)}) copy-start(s32[2,2]{1,0:T(2,128)} %tiles.9) | copy-start | bytes 52
  26.8 5.2 %copy-start.4 = (bf16[2,512,512]{2,1,0:T(8,128)(2,1)S(1)}, bf16[2,512,512]{2,1,0:T(8,128)(2,1)}, u32[]{:S(2)}) copy-start(bf16[2,512,512]{2,1,0:T(8,128)(2,1)} %rows) | copy-start | bytes 3145732
  26.8 32.4 %all-to-all-start = ((bf16[32,72,512]{2,1,0:T(8,128)(2,1)}), bf16[32,72,512]{2,1,0:T(8,128)(2,1)S(1)}, u32[]{:S(2)}, u32[]{:S(2)}) async-start(bf16[32,72,512]{2,1,0:T(8,128)(2,1)} %pack.1), calls=%async_computation | async-start | bytes 4718592 | tf_op jit(solution)/shard_map/all_to_all | solution.py:374
  32.0 1.6 %copy-start.3 = (bf16[2,2,512,512]{3,2,1,0:T(8,128)(2,1)S(1)}, bf16[2,2,512,512]{3,2,1,0:T(8,128)(2,1)}, u32[]{:S(2)}) copy-start(bf16[2,2,512,512]{3,2,1,0:T(8,128)(2,1)} %cot.1) | copy-start | bytes 6291460
  33.6 1.2 copy-start.5
  34.8 1.2 copy-start.6
  39.4 1.0 copy-start
  41.3 1.0 copy-start.8
  59.2 5.5 %collective-permute-start.9 = (bf16[32,72,512]{2,1,0:T(8,128)(2,1)S(1)}, bf16[32,72,512]{2,1,0:T(8,128)(2,1)S(1)}, u32[]{:S(2)}, u32[]{:S(2)}) collective-permute-start(bf16[32,72,512]{2,1,0:T(8,128)(2,1)S(1)} %all-to-all-done.own), channel_id=1, source_target_pairs={{0,64},{64,0},{1,65},{65,1},{2,66},{66,2},{3,67},{67,3},{4,68},{68... | collective-permute-start | bytes 7077896 | tf_op jit(solution)/shard_map/ppermute | solution.py:364
  64.1 7.3 %collective-permute-start.11 = (bf16[512,1024]{1,0:T(8,128)(2,1)S(1)}, bf16[512,1024]{1,0:T(8,128)(2,1)S(1)}, u32[]{:S(2)}, u32[]{:S(2)}) collective-permute-start(bf16[512,1024]{1,0:T(8,128)(2,1)S(1)} %get-tuple-element.40), channel_id=1, source_target_pairs={{0,64},{64,0},{1,65},{65,1},{2,66},{66,2},{3,67},{67,3},{4,68},{68... | collective-permute-start | bytes 3145736 | tf_op jit(solution)/shard_map/ppermute | solution.py:364
  70.4 3.0 %collective-permute-start.10 = (bf16[512,1024]{1,0:T(8,128)(2,1)S(1)}, bf16[512,1024]{1,0:T(8,128)(2,1)S(1)}, u32[]{:S(2)}, u32[]{:S(2)}) collective-permute-start(bf16[512,1024]{1,0:T(8,128)(2,1)S(1)} %get-tuple-element.38), channel_id=1, source_target_pairs={{0,64},{64,0},{1,65},{65,1},{2,66},{66,2},{3,67},{67,3},{4,68},{68... | collective-permute-start | bytes 3145736 | tf_op jit(solution)/shard_map/ppermute | solution.py:364
  71.4 2.0 %copy-start.1 = (bf16[512,1024]{1,0:T(8,128)(2,1)S(1)}, bf16[512,1024]{1,0:T(8,128)(2,1)}, u32[]{:S(2)}) copy-start(bf16[512,1024]{1,0:T(8,128)(2,1)} %copy-done) | copy-start | bytes 3145732
  113.8 8.0 %collective-permute-start.12 = (bf16[24,768]{1,0:T(8,128)(2,1)S(1)}, bf16[24,768]{1,0:T(8,128)(2,1)S(1)}, u32[]{:S(2)}, u32[]{:S(2)}) collective-permute-start(bf16[24,768]{1,0:T(8,128)(2,1)S(1)} %get-tuple-element.42), channel_id=1, source_target_pairs={{0,32},{16,48},{32,0},{48,16},{1,33},{17,49},{33,1},{49,17},{2,34}... | collective-permute-start | bytes 110600 | tf_op jit(solution)/shard_map/ppermute | solution.py:364
  117.2 5.4 %collective-permute-start.13 = (bf16[24,768]{1,0:T(8,128)(2,1)S(1)}, bf16[24,768]{1,0:T(8,128)(2,1)S(1)}, u32[]{:S(2)}, u32[]{:S(2)}) collective-permute-start(bf16[24,768]{1,0:T(8,128)(2,1)S(1)} %get-tuple-element.43), channel_id=1, source_target_pairs={{0,16},{16,32},{32,48},{48,0},{1,17},{17,33},{33,49},{49,1},{2,18}... | collective-permute-start | bytes 110600 | tf_op jit(solution)/shard_map/ppermute | solution.py:364
  120.4 6.5 %collective-permute-start.14 = (bf16[24,768]{1,0:T(8,128)(2,1)S(1)}, bf16[24,768]{1,0:T(8,128)(2,1)S(1)}, u32[]{:S(2)}, u32[]{:S(2)}) collective-permute-start(bf16[24,768]{1,0:T(8,128)(2,1)S(1)} %get-tuple-element.44), channel_id=1, source_target_pairs={{0,48},{16,0},{32,16},{48,32},{1,49},{17,1},{33,17},{49,33},{2,50}... | collective-permute-start | bytes 110600 | tf_op jit(solution)/shard_map/ppermute | solution.py:364
  (1 other events, 1.0 us)

commit v13 on v12

--- a/solution.py
+++ b/solution.py
@@ -219,10 +219,10 @@
     form_left(held, patch, sign, left)
     place_patch(own, (1 - core) * 16, spare, row_tile)
     copies[1].wait()
+    copies[2].wait()
     complete(v1)
+    complete(v2)
     sweep(v1, left, right)
-    copies[2].wait()
-    complete(v2)
     value = jnp.dot(right[...], v2[...], preferred_element_type=F32)
     after[...] = value
     sent[...] = value.astype(BF)

time: 128 us -> 128 us (level)
  no operation moved by 1% of the time
where the time goes in v13:
time: 128 us; the launch traced here: 127 us
  blocking collectives  37.5 us (29%)
  starting transfers between devices  32.6 us (25%)
  waiting for transfers between devices  26.7 us (21%)
  Pallas kernels  21.4 us (17%)
  local copies, waits for them, and re-layouts  7.79 us (6%)
    all_to_all x1, blocking collectives, on_device(): got = lax.all_to_all(contrib, ('zl', 'x', 'y'), 0, 0, tiled=True)  37.5 us
    ppermute x15, starting transfers between devices, turn(): lax.ppermute(value, axis, [(i, (i + step) % count) for i in range(count)])  27.5 us
    all_to_all x1, waiting for transfers between devices, on_device(): own = lax.all_to_all(sent, ('zl', 'x', 'y'), 0, 0, tiled=True)  16.8 us
    ppermute x15, waiting for transfers between devices, turn(): lax.ppermute(value, axis, [(i, (i + step) % count) for i in range(count)])  9.84 us
    unnamed x19, local copies, waits for them, and re-layouts  7.77 us
    pallas_call x1, Pallas kernels, close_steps(): pl.pallas_call(close_kernel, out_shape=[STATE, SENT], in_specs=[SMEM] + [...  5.72 us
    all_to_all x1, starting transfers between devices, on_device(): own = lax.all_to_all(sent, ('zl', 'x', 'y'), 0, 0, tiled=True)  5.13 us
    pallas_call x1, Pallas kernels, open_step(): pl.pallas_call(open_kernel, out_shape=[STATE, SENT, SQUARE, SQUARE, jax.S...  4.77 us
  transfers between devices with their start and end apart: 16, of which 8 were waited for; matrix products, arithmetic and copies ran while one was open for 1% of the time, Pallas kernels for 12%

profile of v13, /device:TPU:64, one launch (start us, length us, event | category | flops | bytes accessed | tf_op | source)
XLA Modules:
  0.0 127.3 jit_solution(13380418884696689283)
XLA Ops:
  0.0 1.6 %collective-permute-start = (s32[2,2]{1,0:T(2,128)}, s32[2,2]{1,0:T(2,128)S(1)}, u32[]{:S(2)}, u32[]{:S(2)}) collective-permute-start(s32[2,2]{1,0:T(2,128)} %tiles.9), channel_id=1, source_target_pairs={{0,1},{1,2},{2,3},{3,0},{4,5},{5,6},{6,7},{7,4},{8,9},{9,10},{10,1... | collective-permute-start | bytes 56 | tf_op jit(solution)/shard_map/ppermute | solution.py:364
  1.6 2.9 %collective-permute-start.1 = (s32[2,2]{1,0:T(2,128)}, s32[2,2]{1,0:T(2,128)S(1)}, u32[]{:S(2)}, u32[]{:S(2)}) collective-permute-start(s32[2,2]{1,0:T(2,128)} %tiles.9), channel_id=1, source_target_pairs={{0,2},{1,3},{2,0},{3,1},{4,6},{5,7},{6,4},{7,5},{8,10},{9,11},{10,... | collective-permute-start | bytes 56 | tf_op jit(solution)/shard_map/ppermute | solution.py:364
  4.5 1.3 %collective-permute-start.2 = (s32[2,2]{1,0:T(2,128)}, s32[2,2]{1,0:T(2,128)S(1)}, u32[]{:S(2)}, u32[]{:S(2)}) collective-permute-start(s32[2,2]{1,0:T(2,128)} %tiles.9), channel_id=1, source_target_pairs={{0,3},{1,0},{2,1},{3,2},{4,7},{5,4},{6,5},{7,6},{8,11},{9,8},{10,9... | collective-permute-start | bytes 56 | tf_op jit(solution)/shard_map/ppermute | solution.py:364
  6.6 4.6 %collective-permute-start.6 = (bf16[24,768]{1,0:T(8,128)(2,1)S(1)}, bf16[24,768]{1,0:T(8,128)(2,1)S(1)}, u32[]{:S(2)}, u32[]{:S(2)}) collective-permute-start(bf16[24,768]{1,0:T(8,128)(2,1)S(1)} %reshape.3.own), channel_id=1, source_target_pairs={{0,16},{16,32},{32,48},{48,0},{1,17},{17,33},{33,49},{49,1},{2,18}... | collective-permute-start | bytes 110600 | tf_op jit(solution)/shard_map/ppermute | solution.py:364
  12.2 2.8 %collective-permute-start.8 = (bf16[24,768]{1,0:T(8,128)(2,1)S(1)}, bf16[24,768]{1,0:T(8,128)(2,1)S(1)}, u32[]{:S(2)}, u32[]{:S(2)}) collective-permute-start(bf16[24,768]{1,0:T(8,128)(2,1)S(1)} %reshape.3.own), channel_id=1, source_target_pairs={{0,48},{16,0},{32,16},{48,32},{1,49},{17,1},{33,17},{49,33},{2,50}... | collective-permute-start | bytes 110600 | tf_op jit(solution)/shard_map/ppermute | solution.py:364
  15.7 1.5 %collective-permute-start.3 = (s32[4,2,2]{2,1,0:T(2,128)S(1)}, s32[4,2,2]{2,1,0:T(2,128)S(1)}, u32[]{:S(2)}, u32[]{:S(2)}) collective-permute-start(s32[4,2,2]{2,1,0:T(2,128)S(1)} %pad_add_fusion.line0), channel_id=1, source_target_pairs={{0,4},{4,8},{8,12},{12,0},{1,5},{5,9},{9,13},{13,1},{2,6},{6,10},{... | collective-permute-start | bytes 200 | tf_op jit(solution)/shard_map/ppermute | solution.py:364
  17.2 2.7 %collective-permute-start.4 = (s32[4,2,2]{2,1,0:T(2,128)S(1)}, s32[4,2,2]{2,1,0:T(2,128)S(1)}, u32[]{:S(2)}, u32[]{:S(2)}) collective-permute-start(s32[4,2,2]{2,1,0:T(2,128)S(1)} %pad_add_fusion.line0), channel_id=1, source_target_pairs={{0,8},{4,12},{8,0},{12,4},{1,9},{5,13},{9,1},{13,5},{2,10},{6,14},... | collective-permute-start | bytes 200 | tf_op jit(solution)/shard_map/ppermute | solution.py:364
  20.5 1.5 %collective-permute-start.5 = (s32[4,2,2]{2,1,0:T(2,128)S(1)}, s32[4,2,2]{2,1,0:T(2,128)S(1)}, u32[]{:S(2)}, u32[]{:S(2)}) collective-permute-start(s32[4,2,2]{2,1,0:T(2,128)S(1)} %pad_add_fusion.line0), channel_id=1, source_target_pairs={{0,12},{4,0},{8,4},{12,8},{1,13},{5,1},{9,5},{13,9},{2,14},{6,2},{... | collective-permute-start | bytes 200 | tf_op jit(solution)/shard_map/ppermute | solution.py:364
  22.3 1.8 %collective-permute-done.5.line3 = s32[4,2,2]{2,1,0:T(2,128)S(1)} collective-permute-done((s32[4,2,2]{2,1,0:T(2,128)S(1)}, s32[4,2,2]{2,1,0:T(2,128)S(1)}, u32[]{:S(2)}, u32[]{:S(2)}) %collective-permute-start.5) | collective-permute-done | bytes 96 | tf_op jit(solution)/shard_map/ppermute | solution.py:364
  24.1 2.6 %pack.1 = bf16[32,72,512]{2,1,0:T(8,128)(2,1)} custom-call(s32[4,2,2]{2,1,0:T(2,128)S(1)} %pad_add_fusion.line0, s32[4,2,2]{2,1,0:T(2,128)S(1)} %collective-permute-done.3.line1, s32[4,2,2]{2,1,0:T(2,128)S(1)} %collective-permute-done.4.line2, s32[4,2,2]{2,1,0:T(2,128)S(1)} %collective-permute-done.5.line3, bf16[24,768]{1,0:T(8,128)(2,1)S(1)} %reshape.3.own, ...), custom_call_target="tpu_custom_call" | custom-call | tf_op jit(solution)/shard_map/pack/pallas_call | solution.py:144
  26.8 5.1 %all-to-all-start = ((bf16[32,72,512]{2,1,0:T(8,128)(2,1)}), bf16[32,72,512]{2,1,0:T(8,128)(2,1)S(1)}, u32[]{:S(2)}, u32[]{:S(2)}) async-start(bf16[32,72,512]{2,1,0:T(8,128)(2,1)} %pack.1), calls=%async_computation | async-start | bytes 4718592 | tf_op jit(solution)/shard_map/all_to_all | solution.py:374
  32.0 1.6 %copy-done.3 = bf16[2,2,512,512]{3,2,1,0:T(8,128)(2,1)S(1)} copy-done((bf16[2,2,512,512]{3,2,1,0:T(8,128)(2,1)S(1)}, bf16[2,2,512,512]{3,2,1,0:T(8,128)(2,1)}, u32[]{:S(2)}) %copy-start.3) | copy-done | bytes 2097176
  36.0 3.4 %prep.1 = (bf16[512,1024]{1,0:T(8,128)(2,1)S(1)}, bf16[512,1024]{1,0:T(8,128)(2,1)S(1)}, bf16[512,1024]{1,0:T(8,128)(2,1)S(1)}) custom-call(s32[2,2]{1,0:T(2,128)S(1)} %copy-done.2, bf16[2,512,512]{2,1,0:T(8,128)(2,1)S(1)} %copy-done.4, bf16[2,512,512]{2,1,0:T(8,128)(2,1)S(1)} %copy-done.5, bf16[2,512,512]{2,1,0:T(8,128)(2,1)S(1)} %copy-done.6, ...), custom_call_target="tpu_custom_call" | custom-call | flops 4000000000 | bytes 20000000 | tf_op jit(solution)/shard_map/prep/pallas_call | solution.py:93
  42.3 16.8 %all-to-all-done.own = bf16[32,72,512]{2,1,0:T(8,128)(2,1)S(1)} async-done(((bf16[32,72,512]{2,1,0:T(8,128)(2,1)}), bf16[32,72,512]{2,1,0:T(8,128)(2,1)S(1)}, u32[]{:S(2)}, u32[]{:S(2)}) %all-to-all-start) | async-done | bytes 2359328 | tf_op jit(solution)/shard_map/all_to_all | solution.py:374
  59.2 4.8 %open_step.1 = (f32[512,1024]{1,0:T(8,128)S(1)}, bf16[512,1024]{1,0:T(8,128)(2,1)S(1)}, bf16[1024,1024]{1,0:T(8,128)(2,1)S(1)}, bf16[1024,1024]{1,0:T(8,128)(2,1)S(1)}, f32[2,640,512]{2,1,0:T(8,128)S(1)}) custom-call(s32[2,2]{1,0:T(2,128)S(1)} %copy-done.2, bf16[32,72,512]{2,1,0:T(8,128)(2,1)S(1)} %all-to-all-done.own, bf16[512,1024]{1,0:T(8,128)(2,1)} %copy-done.7, ...), custom_call_target="tpu_custom_call" | custom-call | flops 4000000000 | bytes 10000000 | tf_op jit(solution)/shard_map/open_step/pallas_call | solution.py:232
  64.5 5.7 %close_steps.1 = (f32[512,1024]{1,0:T(8,128)S(1)}, bf16[512,1024]{1,0:T(8,128)(2,1)S(1)}) custom-call(s32[2,2]{1,0:T(2,128)S(1)} %copy-done.2, f32[2,640,512]{2,1,0:T(8,128)S(1)} %get-tuple-element.34.spare, bf16[32,72,512]{2,1,0:T(8,128)(2,1)S(1)} %collective-permute-done.9.other, bf16[1024,1024]{1,0:T(8,128)(2,1)S(1)} %get-tuple-element.35.v1, ...), custom_call_target="tpu_custom_call" | custom-call | flops 8000000000 | bytes 10000000 | tf_op jit(solution)/shard_map/close_steps/pallas_call | solution.py:256
  71.3 1.2 early.1.half
  73.2 1.4 %late.1 = bf16[32,72,512]{2,1,0:T(8,128)(2,1)S(1)} custom-call(s32[2,2]{1,0:T(2,128)S(1)} %copy-done.2, s32[1]{0:T(128)S(6)} %copy.10.count, bf16[512,1024]{1,0:T(8,128)(2,1)S(1)} %copy-done.1, bf16[512,1024]{1,0:T(8,128)(2,1)S(1)} %collective-permute-done.10.remote, bf16[16,72,512]{2,1,0:T(8,128)(2,1)S(1)} %early.1.half), custom_call_target="tpu_custom_call" | custom-call | tf_op jit(solution)/shard_map/late/pallas_call | solution.py:295
  74.7 37.5 %all_to_all.10.got = bf16[32,72,512]{2,1,0:T(8,128)(2,1)S(1)} all-to-all(bf16[32,72,512]{2,1,0:T(8,128)(2,1)S(1)} %late.1), channel_id=1, replica_groups=mesh['zl'=2,'core'=2,'zh'=4,'x'=4,'y'=4] {'zl','x','y'}, dimensions={0} | all-to-all | bytes 4718592 | tf_op jit(solution)/shard_map/all_to_all | solution.py:387
  112.1 1.6 %gather.1 = (f32[24,768]{1,0:T(8,128)S(1)}, bf16[24,768]{1,0:T(8,128)(2,1)S(1)}, bf16[24,768]{1,0:T(8,128)(2,1)S(1)}, bf16[24,768]{1,0:T(8,128)(2,1)S(1)}) custom-call(s32[4,2,2]{2,1,0:T(2,128)S(1)} %pad_add_fusion.line0, s32[4,2,2]{2,1,0:T(2,128)S(1)} %collective-permute-done.3.line1, s32[4,2,2]{2,1,0:T(2,128)S(1)} %collective-permute-done.4.line2, ...), custom_call_target="tpu_custom_call" | custom-call | tf_op jit(solution)/shard_map/gather/pallas_call | solution.py:335
  113.7 3.4 %collective-permute-start.12 = (bf16[24,768]{1,0:T(8,128)(2,1)S(1)}, bf16[24,768]{1,0:T(8,128)(2,1)S(1)}, u32[]{:S(2)}, u32[]{:S(2)}) collective-permute-start(bf16[24,768]{1,0:T(8,128)(2,1)S(1)} %get-tuple-element.42), channel_id=1, source_target_pairs={{0,32},{16,48},{32,0},{48,16},{1,33},{17,49},{33,1},{49,17},{2,34}... | collective-permute-start | bytes 110600 | tf_op jit(solution)/shard_map/ppermute | solution.py:364
  117.1 3.1 %collective-permute-start.13 = (bf16[24,768]{1,0:T(8,128)(2,1)S(1)}, bf16[24,768]{1,0:T(8,128)(2,1)S(1)}, u32[]{:S(2)}, u32[]{:S(2)}) collective-permute-start(bf16[24,768]{1,0:T(8,128)(2,1)S(1)} %get-tuple-element.43), channel_id=1, source_target_pairs={{0,16},{16,32},{32,48},{48,0},{1,17},{17,33},{33,49},{49,1},{2,18}... | collective-permute-start | bytes 110600 | tf_op jit(solution)/shard_map/ppermute | solution.py:364
  120.2 1.5 %collective-permute-done.12.one = bf16[24,768]{1,0:T(8,128)(2,1)S(1)} collective-permute-done((bf16[24,768]{1,0:T(8,128)(2,1)S(1)}, bf16[24,768]{1,0:T(8,128)(2,1)S(1)}, u32[]{:S(2)}, u32[]{:S(2)}) %collective-permute-start.12) | collective-permute-done | bytes 36896 | tf_op jit(solution)/shard_map/ppermute | solution.py:364
  122.5 4.2 %collective-permute-done.14.three = bf16[24,768]{1,0:T(8,128)(2,1)S(1)} collective-permute-done((bf16[24,768]{1,0:T(8,128)(2,1)S(1)}, bf16[24,768]{1,0:T(8,128)(2,1)S(1)}, u32[]{:S(2)}, u32[]{:S(2)}) %collective-permute-start.14) | collective-permute-done | bytes 36896 | tf_op jit(solution)/shard_map/ppermute | solution.py:364
  (38 shorter events, 11.8 us)
Async XLA Ops:
  0.0 12.2 %collective-permute-start = (s32[2,2]{1,0:T(2,128)}, s32[2,2]{1,0:T(2,128)S(1)}, u32[]{:S(2)}, u32[]{:S(2)}) collective-permute-start(s32[2,2]{1,0:T(2,128)} %tiles.9), channel_id=1, source_target_pairs={{0,1},{1,2},{2,3},{3,0},{4,5},{5,6},{6,7},{7,4},{8,9},{9,10},{10,1... | collective-permute-start | bytes 56 | tf_op jit(solution)/shard_map/ppermute | solution.py:364
  1.6 13.4 %collective-permute-start.1 = (s32[2,2]{1,0:T(2,128)}, s32[2,2]{1,0:T(2,128)S(1)}, u32[]{:S(2)}, u32[]{:S(2)}) collective-permute-start(s32[2,2]{1,0:T(2,128)} %tiles.9), channel_id=1, source_target_pairs={{0,2},{1,3},{2,0},{3,1},{4,6},{5,7},{6,4},{7,5},{8,10},{9,11},{10,... | collective-permute-start | bytes 56 | tf_op jit(solution)/shard_map/ppermute | solution.py:364
  4.5 10.5 %collective-permute-start.2 = (s32[2,2]{1,0:T(2,128)}, s32[2,2]{1,0:T(2,128)S(1)}, u32[]{:S(2)}, u32[]{:S(2)}) collective-permute-start(s32[2,2]{1,0:T(2,128)} %tiles.9), channel_id=1, source_target_pairs={{0,3},{1,0},{2,1},{3,2},{4,7},{5,4},{6,5},{7,6},{8,11},{9,8},{10,9... | collective-permute-start | bytes 56 | tf_op jit(solution)/shard_map/ppermute | solution.py:364
  6.6 17.5 %collective-permute-start.6 = (bf16[24,768]{1,0:T(8,128)(2,1)S(1)}, bf16[24,768]{1,0:T(8,128)(2,1)S(1)}, u32[]{:S(2)}, u32[]{:S(2)}) collective-permute-start(bf16[24,768]{1,0:T(8,128)(2,1)S(1)} %reshape.3.own), channel_id=1, source_target_pairs={{0,16},{16,32},{32,48},{48,0},{1,17},{17,33},{33,49},{49,1},{2,18}... | collective-permute-start | bytes 110600 | tf_op jit(solution)/shard_map/ppermute | solution.py:364
  11.2 13.0 %collective-permute-start.7 = (bf16[24,768]{1,0:T(8,128)(2,1)S(1)}, bf16[24,768]{1,0:T(8,128)(2,1)S(1)}, u32[]{:S(2)}, u32[]{:S(2)}) collective-permute-start(bf16[24,768]{1,0:T(8,128)(2,1)S(1)} %reshape.3.own), channel_id=1, source_target_pairs={{0,32},{16,48},{32,0},{48,16},{1,33},{17,49},{33,1},{49,17},{2,34}... | collective-permute-start | bytes 110600 | tf_op jit(solution)/shard_map/ppermute | solution.py:364
  12.2 12.0 %collective-permute-start.8 = (bf16[24,768]{1,0:T(8,128)(2,1)S(1)}, bf16[24,768]{1,0:T(8,128)(2,1)S(1)}, u32[]{:S(2)}, u32[]{:S(2)}) collective-permute-start(bf16[24,768]{1,0:T(8,128)(2,1)S(1)} %reshape.3.own), channel_id=1, source_target_pairs={{0,48},{16,0},{32,16},{48,32},{1,49},{17,1},{33,17},{49,33},{2,50}... | collective-permute-start | bytes 110600 | tf_op jit(solution)/shard_map/ppermute | solution.py:364
  15.7 4.8 %collective-permute-start.3 = (s32[4,2,2]{2,1,0:T(2,128)S(1)}, s32[4,2,2]{2,1,0:T(2,128)S(1)}, u32[]{:S(2)}, u32[]{:S(2)}) collective-permute-start(s32[4,2,2]{2,1,0:T(2,128)S(1)} %pad_add_fusion.line0), channel_id=1, source_target_pairs={{0,4},{4,8},{8,12},{12,0},{1,5},{5,9},{9,13},{13,1},{2,6},{6,10},{... | collective-permute-start | bytes 200 | tf_op jit(solution)/shard_map/ppermute | solution.py:364
  17.2 5.1 %collective-permute-start.4 = (s32[4,2,2]{2,1,0:T(2,128)S(1)}, s32[4,2,2]{2,1,0:T(2,128)S(1)}, u32[]{:S(2)}, u32[]{:S(2)}) collective-permute-start(s32[4,2,2]{2,1,0:T(2,128)S(1)} %pad_add_fusion.line0), channel_id=1, source_target_pairs={{0,8},{4,12},{8,0},{12,4},{1,9},{5,13},{9,1},{13,5},{2,10},{6,14},... | collective-permute-start | bytes 200 | tf_op jit(solution)/shard_map/ppermute | solution.py:364
  20.5 3.6 %collective-permute-start.5 = (s32[4,2,2]{2,1,0:T(2,128)S(1)}, s32[4,2,2]{2,1,0:T(2,128)S(1)}, u32[]{:S(2)}, u32[]{:S(2)}) collective-permute-start(s32[4,2,2]{2,1,0:T(2,128)S(1)} %pad_add_fusion.line0), channel_id=1, source_target_pairs={{0,12},{4,0},{8,4},{12,8},{1,13},{5,1},{9,5},{13,9},{2,14},{6,2},{... | collective-permute-start | bytes 200 | tf_op jit(solution)/shard_map/ppermute | solution.py:364
  26.8 5.2 %copy-start.2 = (s32[2,2]{1,0:T(2,128)S(1)}, s32[2,2]{1,0:T(2,128)}, u32[]{:S(2)}) copy-start(s32[2,2]{1,0:T(2,128)} %tiles.9) | copy-start | bytes 52
  26.8 5.2 %copy-start.4 = (bf16[2,512,512]{2,1,0:T(8,128)(2,1)S(1)}, bf16[2,512,512]{2,1,0:T(8,128)(2,1)}, u32[]{:S(2)}) copy-start(bf16[2,512,512]{2,1,0:T(8,128)(2,1)} %rows) | copy-start | bytes 3145732
  26.8 32.4 %all-to-all-start = ((bf16[32,72,512]{2,1,0:T(8,128)(2,1)}), bf16[32,72,512]{2,1,0:T(8,128)(2,1)S(1)}, u32[]{:S(2)}, u32[]{:S(2)}) async-start(bf16[32,72,512]{2,1,0:T(8,128)(2,1)} %pack.1), calls=%async_computation | async-start | bytes 4718592 | tf_op jit(solution)/shard_map/all_to_all | solution.py:374
  32.0 1.6 %copy-start.3 = (bf16[2,2,512,512]{3,2,1,0:T(8,128)(2,1)S(1)}, bf16[2,2,512,512]{3,2,1,0:T(8,128)(2,1)}, u32[]{:S(2)}) copy-start(bf16[2,2,512,512]{3,2,1,0:T(8,128)(2,1)} %cot.1) | copy-start | bytes 6291460
  33.6 1.2 copy-start.5
  34.8 1.2 copy-start.6
  39.4 1.0 copy-start
  41.3 1.0 copy-start.8
  59.2 5.4 %collective-permute-start.9 = (bf16[32,72,512]{2,1,0:T(8,128)(2,1)S(1)}, bf16[32,72,512]{2,1,0:T(8,128)(2,1)S(1)}, u32[]{:S(2)}, u32[]{:S(2)}) collective-permute-start(bf16[32,72,512]{2,1,0:T(8,128)(2,1)S(1)} %all-to-all-done.own), channel_id=1, source_target_pairs={{0,64},{64,0},{1,65},{65,1},{2,66},{66,2},{3,67},{67,3},{4,68},{68... | collective-permute-start | bytes 7077896 | tf_op jit(solution)/shard_map/ppermute | solution.py:364
  63.9 7.3 %collective-permute-start.11 = (bf16[512,1024]{1,0:T(8,128)(2,1)S(1)}, bf16[512,1024]{1,0:T(8,128)(2,1)S(1)}, u32[]{:S(2)}, u32[]{:S(2)}) collective-permute-start(bf16[512,1024]{1,0:T(8,128)(2,1)S(1)} %get-tuple-element.40), channel_id=1, source_target_pairs={{0,64},{64,0},{1,65},{65,1},{2,66},{66,2},{3,67},{67,3},{4,68},{68... | collective-permute-start | bytes 3145736 | tf_op jit(solution)/shard_map/ppermute | solution.py:364
  70.3 3.0 %collective-permute-start.10 = (bf16[512,1024]{1,0:T(8,128)(2,1)S(1)}, bf16[512,1024]{1,0:T(8,128)(2,1)S(1)}, u32[]{:S(2)}, u32[]{:S(2)}) collective-permute-start(bf16[512,1024]{1,0:T(8,128)(2,1)S(1)} %get-tuple-element.38), channel_id=1, source_target_pairs={{0,64},{64,0},{1,65},{65,1},{2,66},{66,2},{3,67},{67,3},{4,68},{68... | collective-permute-start | bytes 3145736 | tf_op jit(solution)/shard_map/ppermute | solution.py:364
  71.3 2.0 %copy-start.1 = (bf16[512,1024]{1,0:T(8,128)(2,1)S(1)}, bf16[512,1024]{1,0:T(8,128)(2,1)}, u32[]{:S(2)}) copy-start(bf16[512,1024]{1,0:T(8,128)(2,1)} %copy-done) | copy-start | bytes 3145732
  113.7 8.0 %collective-permute-start.12 = (bf16[24,768]{1,0:T(8,128)(2,1)S(1)}, bf16[24,768]{1,0:T(8,128)(2,1)S(1)}, u32[]{:S(2)}, u32[]{:S(2)}) collective-permute-start(bf16[24,768]{1,0:T(8,128)(2,1)S(1)} %get-tuple-element.42), channel_id=1, source_target_pairs={{0,32},{16,48},{32,0},{48,16},{1,33},{17,49},{33,1},{49,17},{2,34}... | collective-permute-start | bytes 110600 | tf_op jit(solution)/shard_map/ppermute | solution.py:364
  117.1 5.4 %collective-permute-start.13 = (bf16[24,768]{1,0:T(8,128)(2,1)S(1)}, bf16[24,768]{1,0:T(8,128)(2,1)S(1)}, u32[]{:S(2)}, u32[]{:S(2)}) collective-permute-start(bf16[24,768]{1,0:T(8,128)(2,1)S(1)} %get-tuple-element.43), channel_id=1, source_target_pairs={{0,16},{16,32},{32,48},{48,0},{1,17},{17,33},{33,49},{49,1},{2,18}... | collective-permute-start | bytes 110600 | tf_op jit(solution)/shard_map/ppermute | solution.py:364
  120.2 6.5 %collective-permute-start.14 = (bf16[24,768]{1,0:T(8,128)(2,1)S(1)}, bf16[24,768]{1,0:T(8,128)(2,1)S(1)}, u32[]{:S(2)}, u32[]{:S(2)}) collective-permute-start(bf16[24,768]{1,0:T(8,128)(2,1)S(1)} %get-tuple-element.44), channel_id=1, source_target_pairs={{0,48},{16,0},{32,16},{48,32},{1,49},{17,1},{33,17},{49,33},{2,50}... | collective-permute-start | bytes 110600 | tf_op jit(solution)/shard_map/ppermute | solution.py:364
  (1 other events, 1.0 us)
